TPU v7x, 32 devices: a whole 2x2x4 slice. The times are simulated.
32 devices in a mesh: dp: 8 (over z, x), ctx: 2 (over y), tp: 2 (over core).
Axes of the slice: x: 2, y: 2, z: 4, core: 2. Of those that a mesh axis runs over, the one named last changes fastest.
Arguments:
- inputs: bfloat16 [4096, 768], P(('dp', 'ctx')), may hold values from -6 to 6
- qkv_weight: bfloat16 [3, 768, 768], P(None, 'dp', 'tp'), may hold values from -0.21875 to 0.21875
- out_weight: bfloat16 [768, 768], P('tp', 'dp'), may hold values from -2.5 to 2.5
- up_weight: bfloat16 [768, 3072], P('dp', 'tp'), may hold values from -0.21875 to 0.21875
- down_weight: bfloat16 [3072, 768], P('tp', 'dp'), may hold values from -0.109375 to 0.109375
- norm_gains: bfloat16 [2, 768], P(None, 'dp'), may hold values from 0.099609375 to 1.8984375
- norm_biases: bfloat16 [2, 768], P(None, 'dp'), may hold values from -3 to 3
- lengths: int32 [8, 1], P('dp'), may hold values from 4 to 8, as said below
- random_blocks: int32 [64, 12, 3], P(('dp', 'ctx'), 'tp'), may hold values from 0 to 4095
- out_grad: bfloat16 [4096, 768], P(('dp', 'ctx')), may hold values from -6 to 6
Outputs:
- output: bfloat16 [4096, 768], P(('dp', 'ctx'))
- input_grad: bfloat16 [4096, 768], P(('dp', 'ctx'))
- qkv_grad: float32 [3, 768, 768], P(None, 'dp', 'tp')
- proj_grad: float32 [768, 768], P('tp', 'dp')
- up_grad: float32 [768, 3072], P('dp', 'tp')
- down_grad: float32 [3072, 768], P('tp', 'dp')
- gains_grad: float32 [2, 768], P(None, 'dp')
- biases_grad: float32 [2, 768], P(None, 'dp')
Inputs may be any that keep to these rules, and one draw needn't show every extreme that they name: Each of a group's 1 sequence has 4 blocks or more, a group's lengths sum to 8, and the first group's first sequence has the most, 8 blocks.
All inputs are finite; a program needn't handle non-finite values.
Results may differ from a plain program's by a relative error of at most 0.02.
Values may be sent and summed in bfloat16 or wider, within the bound.
No kernel may reach another device: no remote copies, remote signals or barrier semaphores. Data moves between devices by JAX's collectives and lax.ppermute only.
A program may use at most 128 MiB of HBM per device.

v0:
```python
import math

import jax
import jax.numpy as jnp
from jax import lax
from jax.sharding import PartitionSpec as P

HD = 64
BLOCK = 64


eps = 1e-06


def layer_norm(values, gain, shift):
    row_mean = jnp.mean(values, axis=-1, keepdims=True)
    centred = values - row_mean
    spread = jnp.mean(centred * centred, axis=-1, keepdims=True)
    return centred * lax.rsqrt(spread + eps) * gain + shift


def gelu_tanh(values):
    return jax.nn.gelu(values, approximate=True)


def contract(form, left, right):
    return jnp.einsum(form, left, right, preferred_element_type=jnp.float32)


def block_table(blocks, lengths_row, offsets):
    seq_ends = jnp.cumsum(lengths_row)
    starts = seq_ends - lengths_row
    inside = ((blocks[:, None] >= starts[None, :]) & (blocks[:, None] < seq_ends[None, :])).astype(
        jnp.int32
    )
    seq_first = jnp.sum(inside * starts[None, :], axis=1)
    seq_count = jnp.sum(inside * lengths_row[None, :], axis=1)
    position = blocks - seq_first
    has_before = position > 0
    has_behind = position < seq_count - 1
    before = jnp.where(has_before, blocks - 1, blocks)
    behind = jnp.where(has_behind, blocks + 1, blocks)
    fixed_ids = jnp.stack([before, blocks, behind, seq_first, seq_first + 1], axis=-1)
    random_ids = seq_first[:, None, None] + offsets % seq_count[:, None, None]
    head_count = offsets.shape[1]
    key_table = jnp.concatenate(
        [jnp.broadcast_to(fixed_ids[:, None, :], (blocks.shape[0], head_count, 5)), random_ids],
        axis=-1,
    )
    always = jnp.ones_like(has_before)
    usable = jnp.stack(
        [has_before, always, has_behind, always, always] + [always] * offsets.shape[2], axis=-1
    )
    return (key_table, usable)


def scores_of(query, key_sel, usable, scale):
    raw = contract("bqhd,bhkcd->bhqkc", query, key_sel)
    return jnp.where(usable[:, None, None, :, None], raw * scale, -1e30)


def per_device(
    inputs,
    qkv_weight,
    out_weight,
    up_weight,
    down_weight,
    norm_gains,
    norm_biases,
    lengths,
    random_blocks,
    out_grad,
):
    w_qkv, w_out, w_up, w_down, gains_low, biases_low = (
        lax.all_gather(qkv_weight, "dp", axis=1, tiled=True),
        lax.all_gather(out_weight, "dp", axis=1, tiled=True),
        lax.all_gather(up_weight, "dp", axis=0, tiled=True),
        lax.all_gather(down_weight, "dp", axis=1, tiled=True),
        lax.all_gather(norm_gains, "dp", axis=1, tiled=True),
        lax.all_gather(norm_biases, "dp", axis=1, tiled=True),
    )
    gains = gains_low.astype(jnp.float32)
    biases = biases_low.astype(jnp.float32)
    rows = inputs.shape[0]
    own_blocks = rows // BLOCK
    local_width = w_qkv.shape[2]
    local_heads = local_width // HD
    scale = 1.0 / math.sqrt(HD)
    x_float = inputs.astype(jnp.float32)
    projected = contract("td,kde->kte", inputs, w_qkv)
    q_low = projected[0].astype(jnp.bfloat16)
    k_low = projected[1].astype(jnp.bfloat16)
    v_low = projected[2].astype(jnp.bfloat16)
    key_all, value_all = (
        lax.all_gather(k_low, "ctx", axis=0, tiled=True),
        lax.all_gather(v_low, "ctx", axis=0, tiled=True),
    )
    group_blocks = key_all.shape[0] // BLOCK
    first_block = lax.axis_index("ctx") * own_blocks
    blocks = first_block + jnp.arange(own_blocks, dtype=jnp.int32)
    key_table, usable = block_table(blocks, lengths[0], random_blocks)
    head_pick = jnp.arange(local_heads, dtype=jnp.int32)[None, :, None]
    key_blocks = key_all.reshape(group_blocks, BLOCK, local_heads, HD)
    value_blocks = value_all.reshape(group_blocks, BLOCK, local_heads, HD)
    key_sel = key_blocks[key_table, :, head_pick, :]
    value_sel = value_blocks[key_table, :, head_pick, :]
    query = q_low.reshape(own_blocks, BLOCK, local_heads, HD)
    scores = scores_of(query, key_sel, usable, scale)
    top = jnp.max(scores, axis=(3, 4), keepdims=True)
    log_total = top + jnp.log(jnp.sum(jnp.exp(scores - top), axis=(3, 4), keepdims=True))
    probs = jnp.exp(scores - log_total)
    probs_low = probs.astype(jnp.bfloat16)
    attended = (
        contract("bhqkc,bhkcd->bqhd", probs_low, value_sel)
        .reshape(rows, local_width)
        .astype(jnp.bfloat16)
    )
    attn_sum = lax.psum(
        jnp.dot(attended, w_out, preferred_element_type=jnp.float32).astype(jnp.bfloat16), "tp"
    ).astype(jnp.float32)
    first_sum = x_float + attn_sum
    normed, norm_pull = jax.vjp(layer_norm, first_sum, gains[0], biases[0])
    normed_low = normed.astype(jnp.bfloat16)
    hidden = jnp.dot(normed_low, w_up, preferred_element_type=jnp.float32)
    activated, gelu_pull = jax.vjp(gelu_tanh, hidden)
    act_low = activated.astype(jnp.bfloat16)
    mlp_sum = lax.psum(
        jnp.dot(act_low, w_down, preferred_element_type=jnp.float32).astype(jnp.bfloat16), "tp"
    ).astype(jnp.float32)
    second_sum = normed + mlp_sum
    result, final_pull = jax.vjp(layer_norm, second_sum, gains[1], biases[1])
    d_second, d_gain_two, d_bias_two = final_pull(out_grad.astype(jnp.float32))
    d_mlp = d_second.astype(jnp.bfloat16)
    grad_down = contract("tf,td->fd", act_low, d_mlp)
    d_act = contract("td,fd->tf", d_mlp, w_down)
    d_hidden = gelu_pull(d_act)[0].astype(jnp.bfloat16)
    grad_up = contract("td,tf->df", normed_low, d_hidden)
    d_normed = d_second + lax.psum(
        contract("tf,df->td", d_hidden, w_up).astype(jnp.bfloat16), "tp"
    ).astype(jnp.float32)
    d_first, d_gain_one, d_bias_one = norm_pull(d_normed)
    d_attn = d_first.astype(jnp.bfloat16)
    grad_proj = contract("te,td->ed", attended, d_attn)
    d_attended = (
        contract("td,ed->te", d_attn, w_out)
        .astype(jnp.bfloat16)
        .reshape(own_blocks, BLOCK, local_heads, HD)
    )
    scores = scores_of(query, key_sel, usable, scale)
    probs = jnp.exp(scores - log_total)
    probs_low = probs.astype(jnp.bfloat16)
    d_probs = contract("bqhd,bhkcd->bhqkc", d_attended, value_sel)
    d_scores = probs * (d_probs - jnp.sum(probs * d_probs, axis=(3, 4), keepdims=True))
    d_raw = (d_scores * scale).astype(jnp.bfloat16)
    d_query = (
        contract("bhqkc,bhkcd->bqhd", d_raw, key_sel)
        .reshape(rows, local_width)
        .astype(jnp.bfloat16)
    )
    d_key_sel = contract("bhqkc,bqhd->bhkcd", d_raw, query)
    d_value_sel = contract("bhqkc,bqhd->bhkcd", probs_low, d_attended)
    empty = jnp.zeros((group_blocks, BLOCK, local_heads, HD), jnp.float32)
    d_key_all = (
        empty.at[key_table, :, head_pick, :]
        .add(d_key_sel)
        .reshape(group_blocks * BLOCK, local_width)
    )
    d_value_all = (
        empty.at[key_table, :, head_pick, :]
        .add(d_value_sel)
        .reshape(group_blocks * BLOCK, local_width)
    )
    d_key, d_value = (
        lax.psum_scatter(
            d_key_all.astype(jnp.bfloat16), "ctx", scatter_dimension=0, tiled=True
        ).astype(jnp.float32),
        lax.psum_scatter(
            d_value_all.astype(jnp.bfloat16), "ctx", scatter_dimension=0, tiled=True
        ).astype(jnp.float32),
    )
    d_projected = jnp.stack([d_query, d_key.astype(jnp.bfloat16), d_value.astype(jnp.bfloat16)])
    grad_qkv = contract("td,kte->kde", inputs, d_projected)
    d_inputs = d_first + lax.psum(
        contract("kte,kde->td", d_projected, w_qkv).astype(jnp.bfloat16), "tp"
    ).astype(jnp.float32)
    grad_gains = jnp.stack([d_gain_one, d_gain_two])
    grad_biases = jnp.stack([d_bias_one, d_bias_two])
    shared = (
        lax.psum_scatter(
            grad_qkv.astype(jnp.bfloat16), "dp", scatter_dimension=1, tiled=True
        ).astype(jnp.float32),
        lax.psum_scatter(
            grad_proj.astype(jnp.bfloat16), "dp", scatter_dimension=1, tiled=True
        ).astype(jnp.float32),
        lax.psum_scatter(
            grad_up.astype(jnp.bfloat16), "dp", scatter_dimension=0, tiled=True
        ).astype(jnp.float32),
        lax.psum_scatter(
            grad_down.astype(jnp.bfloat16), "dp", scatter_dimension=1, tiled=True
        ).astype(jnp.float32),
        lax.psum_scatter(
            grad_gains.astype(jnp.bfloat16), "dp", scatter_dimension=1, tiled=True
        ).astype(jnp.float32),
        lax.psum_scatter(
            grad_biases.astype(jnp.bfloat16), "dp", scatter_dimension=1, tiled=True
        ).astype(jnp.float32),
    )
    totals = (
        lax.psum(shared[0].astype(jnp.bfloat16), "ctx").astype(jnp.float32),
        lax.psum(shared[1].astype(jnp.bfloat16), "ctx").astype(jnp.float32),
        lax.psum(shared[2].astype(jnp.bfloat16), "ctx").astype(jnp.float32),
        lax.psum(shared[3].astype(jnp.bfloat16), "ctx").astype(jnp.float32),
        lax.psum(shared[4].astype(jnp.bfloat16), "ctx").astype(jnp.float32),
        lax.psum(shared[5].astype(jnp.bfloat16), "ctx").astype(jnp.float32),
    )
    return (
        result.astype(jnp.bfloat16),
        d_inputs.astype(jnp.bfloat16),
        totals[0],
        totals[1],
        totals[2],
        totals[3],
        totals[4],
        totals[5],
    )


def solution(mesh):
    return jax.shard_map(
        per_device,
        mesh=mesh,
        in_specs=(
            P(("dp", "ctx"), None),
            P(None, "dp", "tp"),
            P("tp", "dp"),
            P("dp", "tp"),
            P("tp", "dp"),
            P(None, "dp"),
            P(None, "dp"),
            P("dp", None),
            P(("dp", "ctx"), "tp", None),
            P(("dp", "ctx"), None),
        ),
        out_specs=(
            P(("dp", "ctx"), None),
            P(("dp", "ctx"), None),
            P(None, "dp", "tp"),
            P("tp", "dp"),
            P("dp", "tp"),
            P("tp", "dp"),
            P(None, "dp"),
            P(None, "dp"),
        ),
        check_vma=False,
    )
```

profile of v0, /device:TPU:0, one launch (start us, length us, event | category | flops | bytes accessed | tf_op | source)
XLA Modules:
  0.0 850.5 jit_solution(17683783043665351817)
XLA Ops:
  10.7 36.1 %all_gather.27 = bf16[384,768]{0,1:T(8,128)(2,1)} all-gather(bf16[384,96]{0,1:T(8,128)(2,1)} %param.12), channel_id=1, replica_groups=mesh['dp'=8,'ctx'=2,'tp'=2] {'dp'}, dimensions={1}, use_global_device_ids=true | all-gather | bytes 663552 | tf_op jit(solution)/shard_map/all_gather | solution.py:76
  46.8 13.7 %all-gather.8.cloned.1.call-done = bf16[3,768,384]{2,1,0:T(8,128)(2,1)} async-done(((bf16[3,96,384]{2,1,0:T(8,128)(2,1)}), bf16[3,768,384]{2,1,0:T(8,128)(2,1)}) %all-gather.8.cloned.1.call-update) | async-done | bytes 1769488 | tf_op jit(solution)/shard_map/all_gather | solution.py:75
  63.5 6.8 all-gather.1
  72.6 3.4 gather_fusion.1
  80.3 6.5 all-gather
  87.9 3.7 gather_fusion
  91.5 5.6 fusion.14
  100.4 19.4 %all-gather.2 = bf16[8,96,2]{1,2,0:T(2,128)(2,1)S(1)} all-gather(bf16[1,96,2]{1,2,0:T(2,128)(2,1)S(1)} %bitcast.123), channel_id=1, replica_groups=mesh['dp'=8,'ctx'=2,'tp'=2] {'dp'}, dimensions={0}, use_global_device_ids=true | all-gather | bytes 3456 | tf_op jit(solution)/shard_map/all_gather | solution.py:79
  119.9 16.2 %all-gather.3 = bf16[8,96,2]{1,2,0:T(2,128)(2,1)S(1)} all-gather(bf16[1,96,2]{1,2,0:T(2,128)(2,1)S(1)} %bitcast.124), channel_id=1, replica_groups=mesh['dp'=8,'ctx'=2,'tp'=2] {'dp'}, dimensions={0}, use_global_device_ids=true | all-gather | bytes 3456 | tf_op jit(solution)/shard_map/all_gather | solution.py:80
  138.7 34.7 %all-gather.10.cloned.1.call-done = bf16[768,1536]{1,0:T(8,128)(2,1)} async-done(((bf16[96,1536]{1,0:T(8,128)(2,1)}), bf16[768,1536]{1,0:T(8,128)(2,1)}) %all-gather.10.cloned.1.call-update) | async-done | bytes 2359312 | tf_op jit(solution)/shard_map/all_gather | solution.py:77
  176.1 50.2 %all-gather.12.cloned.1.call-done = bf16[1536,768]{0,1:T(8,128)(2,1)} async-done(((bf16[1536,96]{0,1:T(8,128)(2,1)}), bf16[1536,768]{0,1:T(8,128)(2,1)}) %all-gather.12.cloned.1.call-update) | async-done | bytes 2359312 | tf_op jit(solution)/shard_map/all_gather | solution.py:78
  226.3 3.5 convolution_convert_fusion.5
  229.9 17.1 %all-reduce.10.cloned.1.call-done = bf16[256,768]{1,0:T(8,128)(2,1)} async-done(((bf16[256,768]{1,0:T(8,128)(2,1)}), bf16[256,768]{1,0:T(8,128)(2,1)}) %all-reduce.10.cloned.1.call-update) | async-done | bytes 393232 | tf_op jit(solution)/shard_map/psum | solution.py:127
  254.7 19.5 %all-reduce.12.cloned.1.call-done = bf16[256,768]{1,0:T(8,128)(2,1)} async-done(((bf16[256,768]{1,0:T(8,128)(2,1)}), bf16[256,768]{1,0:T(8,128)(2,1)}) %all-reduce.12.cloned.1.call-update) | async-done | bytes 393232 | tf_op jit(solution)/shard_map/psum | solution.py:138
  279.8 5.8 multiply_reduce_fusion
  287.9 3.6 fusion.55
  291.7 21.6 %scatter_fusion = f32[8,64,6,64]{3,1,2,0:T(8,128)S(1)} fusion(f32[8,64,6,64]{3,1,2,0:T(8,128)S(1)} %broadcast_in_dim.38.clone.1, s32[192]{0:T(256)S(1)} %reshape.312, f32[192,64,64]{2,1,0:T(8,128)} %bitcast.109), kind=kCustom, calls=%fused_computation.2 | custom fusion | flops 786432 | bytes 9438720 | tf_op jit(solution)/shard_map/scatter-add | solution.py:165
  315.4 6.8 fusion.24
  322.4 21.6 %scatter_fusion.1 = f32[8,64,6,64]{3,1,2,0:T(8,128)S(1)} fusion(f32[8,64,6,64]{3,1,2,0:T(8,128)S(1)} %broadcast_in_dim.38.clone, s32[192]{0:T(256)S(1)} %reshape.312, f32[192,64,64]{2,1,0:T(8,128)} %bitcast.108), kind=kCustom, calls=%fused_computation.3 | custom fusion | flops 786432 | bytes 9438720 | tf_op jit(solution)/shard_map/scatter-add | solution.py:170
  348.6 3.8 fusion.13
  354.1 8.7 %reduce-scatter.17.cloned.1.call-done = bf16[256,384]{1,0:T(8,128)(2,1)} async-done(((bf16[512,384]{1,0:T(8,128)(2,1)}), bf16[256,384]{1,0:T(8,128)(2,1)}) %reduce-scatter.17.cloned.1.call-update) | async-done | bytes 196624 | tf_op jit(solution)/shard_map/reduce_scatter | solution.py:177
  364.4 3.4 copy.124
  372.6 3.8 convolution_convert_fusion
  385.7 51.8 %reduce-scatter.25.cloned.1.call-done = bf16[96,1152]{1,0:T(8,128)(2,1)} async-done(((bf16[768,1152]{1,0:T(8,128)(2,1)}), bf16[96,1152]{1,0:T(8,128)(2,1)}) %reduce-scatter.25.cloned.1.call-update) | async-done | bytes 221200
  439.4 62.8 %reduce-scatter.19.cloned.1.call-done = bf16[384,96]{0,1:T(8,128)(2,1)} async-done(((bf16[384,768]{0,1:T(8,128)(2,1)}), bf16[384,96]{0,1:T(8,128)(2,1)}) %reduce-scatter.19.cloned.1.call-update) | async-done | bytes 73744 | tf_op jit(solution)/shard_map/reduce_scatter | solution.py:192
  502.2 72.1 %reduce-scatter.23.cloned.1.call-done = bf16[1536,96]{0,1:T(8,128)(2,1)} async-done(((bf16[1536,768]{0,1:T(8,128)(2,1)}), bf16[1536,96]{0,1:T(8,128)(2,1)}) %reduce-scatter.23.cloned.1.call-update) | async-done | bytes 294928 | tf_op jit(solution)/shard_map/reduce_scatter | solution.py:198
  574.3 71.8 %reduce-scatter.21.cloned.1.call-done = bf16[96,1536]{1,0:T(8,128)(2,1)} async-done(((bf16[768,1536]{1,0:T(8,128)(2,1)}), bf16[96,1536]{1,0:T(8,128)(2,1)}) %reduce-scatter.21.cloned.1.call-update) | async-done | bytes 294928 | tf_op jit(solution)/shard_map/reduce_scatter | solution.py:195
  646.2 64.3 %reduce-scatter.27.cloned.1.call-done = bf16[96,2]{1,0:T(8,128)(2,1)} async-done(((bf16[768,2]{1,0:T(8,128)(2,1)}), bf16[96,2]{1,0:T(8,128)(2,1)}) %reduce-scatter.27.cloned.1.call-update) | async-done | bytes 400
  711.3 62.8 %reduce-scatter.29.cloned.1.call-done = bf16[96,2]{1,0:T(8,128)(2,1)} async-done(((bf16[768,2]{1,0:T(8,128)(2,1)}), bf16[96,2]{1,0:T(8,128)(2,1)}) %reduce-scatter.29.cloned.1.call-update) | async-done | bytes 400
  774.9 4.9 all-reduce
  781.0 13.5 %all-reduce.14.cloned.1.call-done = bf16[256,768]{1,0:T(8,128)(2,1)} async-done(((bf16[256,768]{1,0:T(8,128)(2,1)}), bf16[256,768]{1,0:T(8,128)(2,1)}) %all-reduce.14.cloned.1.call-update) | async-done | bytes 393232 | tf_op jit(solution)/shard_map/psum | solution.py:183
  796.4 40.9 %all-reduce.16.cloned.1.call-done = (bf16[3,96,384]{1,2,0:T(8,128)(2,1)}, bf16[384,96]{0,1:T(8,128)(2,1)}, bf16[96,1536]{1,0:T(8,128)(2,1)}, bf16[1536,96]{0,1:T(8,128)(2,1)}) async-done(((bf16[3,96,384]{1,2,0:T(8,128)(2,1)}, bf16[384,96]{0,1:T(8,128)(2,1)}, bf16[96,1536]{1,0:T(8,128)(2,1)}, bf16[1536,96]{0,1:T(8,128)(2,1)}), (bf16[3,96,384]{1,2,0:T(8,128)(2,1)}, bf16[384,96]{0,1:T(8,128)(2,1)}, ...) | async-done | bytes 884752 | tf_op jit(solution)/shard_map/psum | solution.py:209
  (213 shorter events, 74.1 us)
Async XLA Ops:
  7.2 53.4 %all-gather.8.cloned.1.call-start = ((), (), s32[]{:S(2)}) async-start(), calls=%async_computation.8 | async-start | bytes 1990656 | tf_op jit(solution)/shard_map/all_gather | solution.py:75
  7.9 128.3 %all-reduce.8.cloned.1.call-start = ((), (), s32[]{:S(2)}) async-start(), calls=%async_computation.9 | async-start | bytes 786432 | tf_op jit(solution)/shard_map/psum | solution.py:118
  91.5 6.2 copy-start.11
  97.2 22.7 %copy-start.33 = (bf16[2,96]{1,0:T(2,128)(2,1)S(1)}, bf16[2,96]{1,0:T(2,128)(2,1)}, u32[]{:S(2)}) copy-start(bf16[2,96]{1,0:T(2,128)(2,1)} %param.16) | copy-start | bytes 1156
  97.2 39.0 %copy-start.4 = (bf16[256,768]{1,0:T(8,128)(2,1)S(1)}, bf16[256,768]{1,0:T(8,128)(2,1)}, u32[]{:S(2)}) copy-start(bf16[256,768]{1,0:T(8,128)(2,1)} %param.10) | copy-start | bytes 1179652
  97.8 78.3 %copy-start.16 = (bf16[256,384]{0,1:T(8,128)(2,1)}, bf16[256,384]{0,1:T(8,128)(2,1)S(1)}, u32[]{:S(2)}) copy-start(bf16[256,384]{0,1:T(8,128)(2,1)S(1)} %convert_element_type.176) | copy-start | bytes 589828
  99.0 74.4 %all-gather.10.cloned.1.call-start = ((), (), s32[]{:S(2)}) async-start(), calls=%async_computation.10 | async-start | bytes 2654208 | tf_op jit(solution)/shard_map/all_gather | solution.py:77
  99.7 126.6 %all-gather.12.cloned.1.call-start = ((), (), s32[]{:S(2)}) async-start(), calls=%async_computation.11 | async-start | bytes 2654208 | tf_op jit(solution)/shard_map/all_gather | solution.py:78
  100.3 146.7 %all-reduce.10.cloned.1.call-start = ((), (), s32[]{:S(2)}) async-start(), calls=%async_computation.12 | async-start | bytes 786432 | tf_op jit(solution)/shard_map/psum | solution.py:127
  138.6 137.6 %copy-start.23 = (f32[256]{0:T(256)}, f32[256]{0:T(256)S(1)}, u32[]{:S(2)}) copy-start(f32[256]{0:T(256)S(1)} %fusion.36) | copy-start | bytes 3076
  176.1 50.2 %copy-start.38 = (f32[256,1536]{1,0:T(8,128)}, f32[256,1536]{1,0:T(8,128)S(1)}, u32[]{:S(2)}) copy-start(f32[256,1536]{1,0:T(8,128)S(1)} %fusion.46) | copy-start | bytes 4718596
  176.1 70.9 %copy-start.5 = (bf16[256,768]{1,0:T(8,128)(2,1)S(1)}, bf16[256,768]{1,0:T(8,128)(2,1)}, u32[]{:S(2)}) copy-start(bf16[256,768]{1,0:T(8,128)(2,1)} %all-reduce.8.cloned.1.call-done) | copy-start | bytes 1179652
  229.8 18.9 %copy-start.14 = (bf16[256,768]{1,0:T(8,128)(2,1)S(1)}, bf16[256,768]{1,0:T(8,128)(2,1)}, u32[]{:S(2)}) copy-start(bf16[256,768]{1,0:T(8,128)(2,1)} %param.19) | copy-start | bytes 1179652
  229.8 44.3 %all-reduce.12.cloned.1.call-start = ((), (), s32[]{:S(2)}) async-start(), calls=%async_computation.13 | async-start | bytes 786432 | tf_op jit(solution)/shard_map/psum | solution.py:138
  250.7 25.5 %copy-start.9 = (f32[256,768]{1,0:T(8,128)}, f32[256,768]{1,0:T(8,128)S(1)}, u32[]{:S(2)}) copy-start(f32[256,768]{1,0:T(8,128)S(1)} %get-tuple-element.58) | copy-start | bytes 2359300
  250.7 25.5 %copy-start.27 = (f32[256]{0:T(256)}, f32[256]{0:T(256)S(1)}, u32[]{:S(2)}) copy-start(f32[256]{0:T(256)S(1)} %negate_multiply_fusion.1) | copy-start | bytes 3076
  252.7 23.5 %copy-start.18 = (bf16[256,1536]{1,0:T(8,128)(2,1)}, bf16[256,1536]{1,0:T(8,128)(2,1)S(1)}, u32[]{:S(2)}) copy-start(bf16[256,1536]{1,0:T(8,128)(2,1)S(1)} %fusion.8) | copy-start | bytes 2359300
  254.3 99.7 %reduce-scatter.15.cloned.1.call-start = ((), (), s32[]{:S(2)}) async-start(), calls=%async_computation.14 | async-start | bytes 589824 | tf_op jit(solution)/shard_map/reduce_scatter | solution.py:174
  279.5 6.2 slice-start
  279.8 5.9 slice-start.1
  315.4 47.3 %reduce-scatter.17.cloned.1.call-start = ((), (), s32[]{:S(2)}) async-start(), calls=%async_computation.15 | async-start | bytes 589824 | tf_op jit(solution)/shard_map/reduce_scatter | solution.py:177
  344.2 4.3 copy-start.2
  348.3 89.2 %reduce-scatter.25.cloned.1.call-start = ((), (), s32[]{:S(2)}) async-start(), calls=%async_computation.20 | async-start | bytes 1990656
  371.1 131.1 %reduce-scatter.19.cloned.1.call-start = ((), (), s32[]{:S(2)}) async-start(), calls=%async_computation.17 | async-start | bytes 663552 | tf_op jit(solution)/shard_map/reduce_scatter | solution.py:192
  372.5 201.8 %reduce-scatter.23.cloned.1.call-start = ((), (), s32[]{:S(2)}) async-start(), calls=%async_computation.19 | async-start | bytes 2654208 | tf_op jit(solution)/shard_map/reduce_scatter | solution.py:198
  376.4 3.7 copy-start.15
  376.5 269.7 %reduce-scatter.21.cloned.1.call-start = ((), (), s32[]{:S(2)}) async-start(), calls=%async_computation.18 | async-start | bytes 2654208 | tf_op jit(solution)/shard_map/reduce_scatter | solution.py:195
  380.1 330.4 %reduce-scatter.27.cloned.1.call-start = ((), (), s32[]{:S(2)}) async-start(), calls=%async_computation.21 | async-start | bytes 221184
  381.6 392.5 %reduce-scatter.29.cloned.1.call-start = ((), (), s32[]{:S(2)}) async-start(), calls=%async_computation.22 | async-start | bytes 221184
  382.6 412.0 %all-reduce.14.cloned.1.call-start = ((), (), s32[]{:S(2)}) async-start(), calls=%async_computation.16 | async-start | bytes 786432 | tf_op jit(solution)/shard_map/psum | solution.py:183
  385.6 451.7 %all-reduce.16.cloned.1.call-start = ((), (), s32[]{:S(2)}) async-start(), calls=%async_computation.23 | async-start | bytes 1916928 | tf_op jit(solution)/shard_map/psum | solution.py:209
  837.3 5.6 copy-start.21
  (26 other events, 55.2 us)
Sparse Core Ops, SparseCore 0:
  10.2 50.3 all-gather.7
  99.1 18.5 all-reduce.7
  120.1 53.2 all-gather.9
  175.6 50.6 all-gather.11
  229.9 17.0 all-reduce.9
  254.4 19.6 all-reduce.11
  315.5 14.2 reduce-scatter.14
  348.4 14.2 reduce-scatter.16
  371.2 66.1 reduce-scatter.24
  441.1 60.9 reduce-scatter.18
  506.1 68.1 reduce-scatter.22
  578.1 68.0 reduce-scatter.20
  650.3 60.0 reduce-scatter.26
  713.9 60.1 reduce-scatter.28
  777.0 17.4 all-reduce.13
  797.5 39.7 all-reduce.15
where the time goes:
time: 858 us; the launch traced here: 851 us
  waiting for transfers between devices  586 us (68%)
  blocking collectives  89.9 us (10%)
  other arithmetic  66.2 us (8%)
  matrix products  51.8 us (6%)
  local copies, waits for them, and re-layouts  39.5 us (5%)
  between operations  15.8 us (2%)
    unnamed x19, waiting for transfers between devices  181 us
    reduce_scatter x1, waiting for transfers between devices, per_device(): lax.psum_scatter(grad_down.astype(jnp.bfloat16), 'dp', scatter_dimension=...  72.1 us
    reduce_scatter x1, waiting for transfers between devices, per_device(): lax.psum_scatter(grad_up.astype(jnp.bfloat16), 'dp', scatter_dimension=0,...  71.8 us
    reduce_scatter x1, waiting for transfers between devices, per_device(): lax.psum_scatter(grad_proj.astype(jnp.bfloat16), 'dp', scatter_dimension=...  62.8 us
    all_gather x1, waiting for transfers between devices, per_device(): lax.all_gather(down_weight, 'dp', axis=1, tiled=True)  50.2 us
    dot_general x15, matrix products, contract(): return jnp.einsum(form, left, right, preferred_element_type=jnp.float32)  44.5 us
    psum x1, waiting for transfers between devices, per_device(): lax.psum(shared[0].astype(jnp.bfloat16), 'ctx').astype(jnp.float32)  40.9 us
    all_gather x1, blocking collectives, per_device(): lax.all_gather(out_weight, 'dp', axis=1, tiled=True)  36.1 us
  transfers between devices with their start and end apart: 16, of which 14 were waited for; matrix products, arithmetic and copies ran while one was open for 8% of the time, Pallas kernels for 0%

commit v1 on v0

--- a/solution.py
+++ b/solution.py
@@ -1,3 +1,4 @@
+import functools
 import math
 
 import jax
@@ -225,9 +226,210 @@
     )
 
 
+def rows_device(
+    dims,
+    inputs,
+    qkv_weight,
+    out_weight,
+    up_weight,
+    down_weight,
+    norm_gains,
+    norm_biases,
+    lengths,
+    random_blocks,
+    out_grad,
+):
+    n_dp = dims["dp"]
+    n_out = n_dp // 2
+    dp = lax.axis_index("dp")
+    c = lax.axis_index("ctx")
+    t = lax.axis_index("tp")
+    z = dp // 2
+    x = dp % 2
+    f32, bf16 = jnp.float32, jnp.bfloat16
+    pair = [(0, 1), (1, 0)]
+    across_x = [(i, i ^ 1) for i in range(n_dp)]
+
+    def across_z(s):
+        return [(i, ((i // 2 + s) % n_out) * 2 + i % 2) for i in range(n_dp)]
+
+    def swap_tp(v):
+        return lax.ppermute(v, "tp", pair)
+
+    def swap_ctx(v):
+        return lax.ppermute(v, "ctx", pair)
+
+    def gather_dp(v):
+        near = [v] + [lax.ppermute(v, "dp", across_z(s)) for s in range(1, n_out)]
+        far = [lax.ppermute(p, "dp", across_x) for p in near]
+        order = [0] + [n_out - s for s in range(1, n_out)]
+        near = jnp.stack([near[s] for s in order])
+        far = jnp.stack([far[s] for s in order])
+        both = jnp.stack([jnp.where(x == 0, near, far), jnp.where(x == 0, far, near)], axis=1)
+        both = jnp.roll(both, z, axis=0)
+        return both.reshape(n_dp * v.shape[0], v.shape[1])
+
+    def scatter_dp(g):
+        rows = g.shape[0] // n_dp
+        g = g.astype(bf16).reshape(n_out, 2, rows, g.shape[1])
+        away = lax.dynamic_index_in_dim(g, 1 - x, 1, False)
+        own = lax.dynamic_index_in_dim(g, x, 1, False)
+        half = (own.astype(f32) + lax.ppermute(away, "dp", across_x).astype(f32)).astype(bf16)
+        total = lax.dynamic_index_in_dim(half, z, 0, False).astype(f32)
+        for s in range(1, n_out):
+            piece = lax.dynamic_index_in_dim(half, (z + s) % n_out, 0, False)
+            total = total + lax.ppermute(piece, "dp", across_z(s)).astype(f32)
+        return total.astype(bf16)
+
+    rows = inputs.shape[0]
+    part = rows // 2
+    width = inputs.shape[1]
+    shard = qkv_weight.shape[1]
+    cols = qkv_weight.shape[2] // 2
+    units = up_weight.shape[1] // 2
+    heads = cols // HD
+    own_blocks = rows // BLOCK
+    per = own_blocks // 2
+
+    def own_cols(w):
+        n = w.shape[-1] // 2
+        return lax.dynamic_slice_in_dim(w, c * n, n, w.ndim - 1)
+
+    small = jnp.concatenate([norm_gains, norm_biases], axis=0)
+    w1 = jnp.concatenate(
+        [own_cols(qkv_weight[0]), own_cols(qkv_weight[1]), own_cols(qkv_weight[2]), jnp.pad(small.T, ((0, 0), (0, 60)))],
+        axis=1,
+    )
+    w_out_t = own_cols(out_weight.T)
+    w_up = own_cols(up_weight)
+    w_down_t = own_cols(down_weight.T)
+    w1 = gather_dp(w1)
+    w_out_t = gather_dp(w_out_t)
+    w_up = gather_dp(w_up)
+    w_down_t = gather_dp(w_down_t)
+    w_qkv = w1[:, : 3 * cols]
+    vecs = w1[:, 3 * cols : 3 * cols + 4].T.astype(f32)
+
+    def gather_rows(v):
+        halves = v.reshape(2, part, v.shape[1])
+        near = swap_ctx(lax.dynamic_index_in_dim(halves, t, 0, False))
+        far = swap_tp(near)
+        other = jnp.where(t == 0, jnp.stack([near, far]), jnp.stack([far, near]))
+        return jnp.where(c == 0, jnp.stack([halves, other], 1), jnp.stack([other, halves], 1)).reshape(4 * part, v.shape[1])
+
+    x_all = gather_rows(inputs)
+    e_own = lax.dynamic_index_in_dim(out_grad.reshape(2, part, width), t, 0, False)
+    e_far = swap_ctx(e_own)
+    e_mine = jnp.where(c == 0, jnp.concatenate([e_own, e_far]), jnp.concatenate([e_far, e_own])).astype(f32)
+
+    picks = random_blocks.reshape(own_blocks, 2, heads, 3)
+    picks_own = lax.dynamic_index_in_dim(picks, c, 1, False)
+    picks_far = swap_ctx(lax.dynamic_index_in_dim(picks, 1 - c, 1, False))
+    picks = jnp.where(c == 0, jnp.concatenate([picks_own, picks_far]), jnp.concatenate([picks_far, picks_own]))
+    blocks = jnp.arange(2 * own_blocks, dtype=jnp.int32)
+    table, usable = block_table(blocks, lengths[0], picks)
+    named = (table[..., None] == blocks) & usable[:, None, :, None]
+    counts = jnp.sum(named.astype(f32), axis=2)
+    order = [cc * own_blocks + tt * per + i for tt in range(2) for cc in range(2) for i in range(per)]
+    order = jnp.array(order)
+    counts = counts[order][:, :, order]
+    bias = jnp.where(counts > 0, jnp.log(jnp.maximum(counts, 1.0)), -1e30)
+    bias = jnp.repeat(jnp.repeat(bias.transpose(1, 0, 2), BLOCK, 1), BLOCK, 2)
+    scale = 1.0 / math.sqrt(HD)
+
+    qkv = jnp.dot(x_all, w_qkv, preferred_element_type=f32).astype(bf16)
+    q, k, v = [qkv[:, i * cols : (i + 1) * cols].reshape(-1, heads, HD) for i in range(3)]
+    scores = contract("qhd,khd->hqk", q, k) * scale + bias
+    top = jnp.max(scores, axis=2, keepdims=True)
+    log_total = top + jnp.log(jnp.sum(jnp.exp(scores - top), axis=2, keepdims=True))
+    probs = jnp.exp(scores - log_total)
+    o = contract("hqk,khd->qhd", probs.astype(bf16), v).reshape(-1, cols).astype(bf16)
+
+    def mine(s):
+        return lax.dynamic_index_in_dim(s.reshape(2, s.shape[0] // 2, s.shape[1]), t, 0, False)
+
+    def theirs(s):
+        return lax.dynamic_index_in_dim(s.reshape(2, s.shape[0] // 2, s.shape[1]), 1 - t, 0, False)
+
+    def sum_row(s):
+        s = s.astype(bf16)
+        s = (mine(s).astype(f32) + swap_tp(theirs(s)).astype(f32)).astype(bf16)
+        return s.astype(f32) + swap_ctx(s).astype(f32)
+
+    def spread(s):
+        far = swap_tp(s)
+        return jnp.where(t == 0, jnp.concatenate([s, far]), jnp.concatenate([far, s]))
+
+    a = sum_row(contract("te,de->td", o, w_out_t))
+    y1, norm_pull = jax.vjp(layer_norm, mine(x_all).astype(f32) + a, vecs[0], vecs[2])
+    y1_low = spread(y1.astype(bf16))
+    hid = jnp.dot(y1_low, w_up, preferred_element_type=f32)
+    act, gelu_pull = jax.vjp(gelu_tanh, hid)
+    u = act.astype(bf16)
+    m = sum_row(contract("tf,df->td", u, w_down_t))
+    result, final_pull = jax.vjp(layer_norm, y1 + m, vecs[1], vecs[3])
+    dz2, dg2, dc2 = final_pull(e_mine)
+    dm = spread(dz2.astype(bf16))
+
+    def keep(s):
+        near = lax.dynamic_index_in_dim(s.reshape(2, part, s.shape[1]), c, 0, False)
+        far = swap_tp(near)
+        return jnp.where(t == 0, jnp.concatenate([near, far]), jnp.concatenate([far, near]))
+
+    output = keep(result.astype(bf16))
+    grad_down_t = contract("td,tf->df", dm, u)
+    du = jnp.dot(dm, w_down_t, preferred_element_type=f32)
+    dhid = gelu_pull(du)[0].astype(bf16)
+    grad_up = contract("td,tf->df", y1_low, dhid)
+    dy1 = dz2 + sum_row(contract("tf,df->td", dhid, w_up))
+    dz1, dg1, dc1 = norm_pull(dy1)
+    da = spread(dz1.astype(bf16))
+    grad_out_t = contract("td,te->de", da, o)
+    do = jnp.dot(da, w_out_t, preferred_element_type=f32).astype(bf16).reshape(-1, heads, HD)
+    dp_ = contract("qhd,khd->hqk", do, v)
+    ds = probs * (dp_ - jnp.sum(probs * dp_, axis=2, keepdims=True))
+    dr = (ds * scale).astype(bf16)
+    dq = contract("hqk,khd->qhd", dr, k).astype(bf16)
+    dk = contract("hqk,qhd->khd", dr, q).astype(bf16)
+    dv = contract("hqk,qhd->khd", probs.astype(bf16), do).astype(bf16)
+    dqkv = jnp.concatenate([g.reshape(-1, cols) for g in (dq, dk, dv)], axis=1)
+    grad_qkv = contract("td,te->de", x_all, dqkv)
+    vec_grads = jnp.stack([dg1, dg2, dc1, dc2])
+    vec_grads = vec_grads + swap_tp(vec_grads)
+    grad_1 = jnp.concatenate([grad_qkv, jnp.pad(vec_grads.T, ((0, 0), (0, 60)))], axis=1)
+    dx = contract("te,de->td", dqkv, w_qkv).astype(bf16)
+    dx = (mine(dx).astype(f32) + swap_tp(theirs(dx)).astype(f32)).astype(bf16).reshape(2, part, width)
+    dx_own = lax.dynamic_index_in_dim(dx, c, 0, False).astype(f32)
+    dx_far = swap_ctx(lax.dynamic_index_in_dim(dx, 1 - c, 0, False)).astype(f32)
+    dz1_own = lax.dynamic_index_in_dim(dz1.reshape(2, part, width), c, 0, False)
+    dx = (dz1_own + dx_own + dx_far).astype(bf16)
+    dx_tp = swap_tp(dx)
+    input_grad = jnp.where(t == 0, jnp.concatenate([dx, dx_tp]), jnp.concatenate([dx_tp, dx]))
+
+    def both_ctx(g):
+        far = swap_ctx(g)
+        return jnp.where(c == 0, jnp.concatenate([g, far], 1), jnp.concatenate([far, g], 1))
+
+    grad_down = both_ctx(scatter_dp(grad_down_t)).astype(f32).T
+    grad_up = both_ctx(scatter_dp(grad_up)).astype(f32)
+    grad_out = both_ctx(scatter_dp(grad_out_t)).astype(f32).T
+    grad_1 = scatter_dp(grad_1)
+    far_1 = swap_ctx(grad_1)
+    lo = jnp.where(c == 0, grad_1, far_1).astype(f32)
+    hi = jnp.where(c == 0, far_1, grad_1).astype(f32)
+    grad_qkv = jnp.stack(
+        [jnp.concatenate([lo[:, i * cols : (i + 1) * cols], hi[:, i * cols : (i + 1) * cols]], 1) for i in range(3)]
+    )
+    vec = grad_1[:, 3 * cols : 3 * cols + 4].astype(f32).T
+    return (output, input_grad, grad_qkv, grad_out, grad_up, grad_down, vec[:2], vec[2:])
+
+
 def solution(mesh):
+    dims = dict(mesh.shape)
+    fast = dims["ctx"] == 2 and dims["tp"] == 2 and dims["dp"] % 2 == 0
+    step = functools.partial(rows_device, dims) if fast else per_device
     return jax.shard_map(
-        per_device,
+        step,
         mesh=mesh,
         in_specs=(
             P(("dp", "ctx"), None),

time: 858 us -> 246 us (0.29)
  waiting for transfers between devices: 586 us -> 79.8 us
  blocking collectives: 89.9 us -> 0 us
  starting transfers between devices: 1.12 us -> 81.1 us
  other arithmetic: 66.2 us -> 24.7 us
  matrix products: 51.8 us -> 32.5 us
  local copies, waits for them, and re-layouts: 39.5 us -> 25.1 us
  between operations: 15.8 us -> 2.45 us
    reduce_scatter x5 -> x0, waiting for transfers between devices: 215 us -> none  [the longest x1 72.1 us: per_device(): lax.psum_scatter(grad_down.astype(jnp.bfloat16), 'dp', scatter_dimension=...]
    unnamed x19 -> x0, waiting for transfers between devices: 181 us -> none
    all_gather x3 -> x0, waiting for transfers between devices: 98.7 us -> none  [the longest x1 50.2 us: per_device(): lax.all_gather(down_weight, 'dp', axis=1, tiled=True)]
    psum x5 -> x0, waiting for transfers between devices: 91 us -> none  [the longest x1 40.9 us: per_device(): lax.psum(shared[0].astype(jnp.bfloat16), 'ctx').astype(jnp.float32)]
    all_gather x5 -> x0, blocking collectives: 85 us -> none  [the longest x1 36.1 us: per_device(): lax.all_gather(out_weight, 'dp', axis=1, tiled=True)]
    ppermute x0 -> x66, starting transfers between devices: none -> 81.1 us  [the longest x12 27.8 us: gather_dp(): near = [v] + [lax.ppermute(v, 'dp', across_z(s)) for s in range(1, n_out)]]
    ppermute x0 -> x66, waiting for transfers between devices: none -> 79.8 us  [the longest x12 21.8 us: scatter_dp(): total = total + lax.ppermute(piece, 'dp', across_z(s)).astype(f32)]
    scatter-add x2 -> x0, other arithmetic: 43.3 us -> none  [the longest x1 21.6 us: per_device(): d_value_all = empty.at[key_table, :, head_pick, :].add(d_value_sel).resha...]
  transfers between devices with their start and end apart: 16 -> 66, of which waited for: 14 -> 28; matrix products, arithmetic and copies ran while one was open for 8% -> 26% of each run, Pallas kernels for 0% -> 0%
where the time goes in v1:
time: 246 us
  starting transfers between devices  81.1 us (33%)
  waiting for transfers between devices  79.8 us (32%)
  matrix products  32.5 us (13%)
  local copies, waits for them, and re-layouts  25.1 us (10%)
  other arithmetic  24.7 us (10%)
    ppermute x12, starting transfers between devices, gather_dp(): near = [v] + [lax.ppermute(v, 'dp', across_z(s)) for s in range(1, n_out)]  27.8 us
    dot_general x14, matrix products, contract(): return jnp.einsum(form, left, right, preferred_element_type=jnp.float32)  25.3 us
    ppermute x12, waiting for transfers between devices, scatter_dp(): total = total + lax.ppermute(piece, 'dp', across_z(s)).astype(f32)  21.8 us
    ppermute x4, waiting for transfers between devices, scatter_dp(): lax.ppermute(away, 'dp', across_x).astype(f32)  21.7 us
    ppermute x11, waiting for transfers between devices, swap_ctx(): return lax.ppermute(v, 'ctx', pair)  21 us
    ppermute x12, starting transfers between devices, scatter_dp(): total = total + lax.ppermute(piece, 'dp', across_z(s)).astype(f32)  18.4 us
    ppermute x16, starting transfers between devices, gather_dp(): far = [lax.ppermute(p, 'dp', across_x) for p in near]  17.8 us
    ppermute x16, waiting for transfers between devices, gather_dp(): far = [lax.ppermute(p, 'dp', across_x) for p in near]  11.6 us
  transfers between devices with their start and end apart: 66, of which 28 were waited for; matrix products, arithmetic and copies ran while one was open for 26% of the time, Pallas kernels for 0%

profile of v1, /device:TPU:0, one launch (start us, length us, event | category | flops | bytes accessed | tf_op | source)
XLA Modules:
  0.0 245.7 jit_solution(6704972294798809182)
XLA Ops:
  1.7 3.1 %collective-permute-start.12 = (bf16[96,192]{1,0:T(8,128)(2,1)S(1)}, bf16[96,192]{1,0:T(8,128)(2,1)S(1)}, u32[]{:S(2)}, u32[]{:S(2)}) collective-permute-start(bf16[96,192]{1,0:T(8,128)(2,1)S(1)} %get-tuple-element.110), channel_id=1, source_target_pairs={{0,8},{4,12},{8,16},{12,20},{16,24},{20,28},{24,0},{28,4},{1,9},{5... | collective-permute-start | bytes 110600 | tf_op jit(solution)/shard_map/ppermute | solution.py:263
  4.8 2.6 %collective-permute-start.11 = (bf16[96,192]{1,0:T(8,128)(2,1)S(1)}, bf16[96,192]{1,0:T(8,128)(2,1)S(1)}, u32[]{:S(2)}, u32[]{:S(2)}) collective-permute-start(bf16[96,192]{1,0:T(8,128)(2,1)S(1)} %get-tuple-element.110), channel_id=1, source_target_pairs={{0,16},{4,20},{8,24},{12,28},{16,0},{20,4},{24,8},{28,12},{1,17},{... | collective-permute-start | bytes 110600 | tf_op jit(solution)/shard_map/ppermute | solution.py:263
  19.3 2.9 %collective-permute-start.2 = (bf16[96,640]{1,0:T(8,128)(2,1)S(1)}, bf16[96,640]{1,0:T(8,128)(2,1)S(1)}, u32[]{:S(2)}, u32[]{:S(2)}) collective-permute-start(bf16[96,640]{1,0:T(8,128)(2,1)S(1)} %fusion.78), channel_id=1, source_target_pairs={{0,24},{4,28},{8,0},{12,4},{16,8},{20,12},{24,16},{28,20},{1,25},{... | collective-permute-start | bytes 368648 | tf_op jit(solution)/shard_map/ppermute | solution.py:263
  44.4 2.5 %collective-permute-start.21 = (bf16[96,768]{1,0:T(8,128)(2,1)S(1)}, bf16[96,768]{1,0:T(8,128)(2,1)S(1)}, u32[]{:S(2)}, u32[]{:S(2)}) collective-permute-start(bf16[96,768]{1,0:T(8,128)(2,1)S(1)} %constant_dynamic-slice_fusion.2), channel_id=1, source_target_pairs={{0,16},{4,20},{8,24},{12,28},{16,0},{20,4},{24,8},{28,12},{1,17},{... | collective-permute-start | bytes 442376 | tf_op jit(solution)/shard_map/ppermute | solution.py:263
  52.7 4.0 %collective-permute-start.29 = (bf16[96,768]{1,0:T(8,128)(2,1)S(1)}, bf16[96,768]{1,0:T(8,128)(2,1)S(1)}, u32[]{:S(2)}, u32[]{:S(2)}) collective-permute-start(bf16[96,768]{1,0:T(8,128)(2,1)S(1)} %get-tuple-element.94), channel_id=1, source_target_pairs={{0,8},{4,12},{8,16},{12,20},{16,24},{20,28},{24,0},{28,4},{1,9},{5... | collective-permute-start | bytes 442376 | tf_op jit(solution)/shard_map/ppermute | solution.py:263
  56.7 2.1 collective-permute-start.28
  60.0 6.0 %collective-permute-start.27 = (bf16[96,768]{1,0:T(8,128)(2,1)S(1)}, bf16[96,768]{1,0:T(8,128)(2,1)S(1)}, u32[]{:S(2)}, u32[]{:S(2)}) collective-permute-start(bf16[96,768]{1,0:T(8,128)(2,1)S(1)} %get-tuple-element.94), channel_id=1, source_target_pairs={{0,24},{4,28},{8,0},{12,4},{16,8},{20,12},{24,16},{28,20},{1,25},{... | collective-permute-start | bytes 442376 | tf_op jit(solution)/shard_map/ppermute | solution.py:263
  78.2 2.7 %collective-permute-done.18 = bf16[256,768]{1,0:T(8,128)(2,1)S(1)} collective-permute-done((bf16[256,768]{1,0:T(8,128)(2,1)S(1)}, bf16[256,768]{1,0:T(8,128)(2,1)S(1)}, u32[]{:S(2)}, u32[]{:S(2)}) %collective-permute-start.18) | collective-permute-done | bytes 393248 | tf_op jit(solution)/shard_map/ppermute | solution.py:260
  81.7 2.1 collective-permute-done.33
  83.8 2.9 %collective-permute-done.32 = bf16[96,768]{1,0:T(8,128)(2,1)S(1)} collective-permute-done((bf16[96,768]{1,0:T(8,128)(2,1)S(1)}, bf16[96,768]{1,0:T(8,128)(2,1)S(1)}, u32[]{:S(2)}, u32[]{:S(2)}) %collective-permute-start.32) | collective-permute-done | bytes 147488 | tf_op jit(solution)/shard_map/ppermute | solution.py:264
  96.1 9.8 %collective-permute-done.35 = bf16[256,768]{1,0:T(8,128)(2,1)S(1)} collective-permute-done((bf16[256,768]{1,0:T(8,128)(2,1)S(1)}, bf16[256,768]{1,0:T(8,128)(2,1)S(1)}, u32[]{:S(2)}, u32[]{:S(2)}) %collective-permute-start.35) | collective-permute-done | bytes 393248 | tf_op jit(solution)/shard_map/ppermute | solution.py:260
  106.5 2.8 %collective-permute-done.37 = bf16[128,768]{1,0:T(8,128)(2,1)S(1)} collective-permute-done((bf16[128,768]{1,0:T(8,128)(2,1)S(1)}, bf16[128,768]{1,0:T(8,128)(2,1)S(1)}, u32[]{:S(2)}, u32[]{:S(2)}) %collective-permute-start.37) | collective-permute-done | bytes 196640 | tf_op jit(solution)/shard_map/ppermute | solution.py:260
  113.8 2.3 copy.99
  117.5 2.1 maximum_select_fusion.5
  119.5 3.8 %fusion.17 = bf16[512,768]{1,0:T(8,128)(2,1)S(1)} fusion(f32[512,768]{1,0:T(8,128)} %copy-done.38, bf16[768,768]{1,0:T(8,128)(2,1)} %bitcast.267, bf16[256,768]{1,0:T(8,128)(2,1)} %collective-permute-done.38, bf16[256,768]{1,0:T(8,128)(2,1)} %add_convert_fusion.1, pred[]{:T(512)S(6)} %eq.73), kind=kOutput, calls=%fused_computation.32 | convolution fusion | flops 615383040 | bytes 4325377 | tf_op jit(solution)/shard_map/dot_general | solution.py:381
  126.9 2.4 convolution_convert_fusion
  131.0 10.6 %collective-permute-done.56 = bf16[4,96,768]{2,1,0:T(8,128)(2,1)S(1)} collective-permute-done((bf16[4,96,768]{2,1,0:T(8,128)(2,1)S(1)}, bf16[4,96,768]{2,1,0:T(8,128)(2,1)S(1)}, u32[]{:S(2)}, u32[]{:S(2)}) %collective-permute-start.56) | collective-permute-done | bytes 589856 | tf_op jit(solution)/shard_map/ppermute | solution.py:277
  141.8 3.8 %collective-permute-start.57 = (bf16[96,768]{1,0:T(8,128)(2,1)S(1)}, bf16[96,768]{1,0:T(8,128)(2,1)S(1)}, u32[]{:S(2)}, u32[]{:S(2)}) collective-permute-start(bf16[96,768]{1,0:T(8,128)(2,1)S(1)} %get-tuple-element.80), channel_id=1, source_target_pairs={{0,8},{4,12},{8,16},{12,20},{16,24},{20,28},{24,0},{28,4},{1,9},{5... | collective-permute-start | bytes 442376 | tf_op jit(solution)/shard_map/ppermute | solution.py:281
  147.1 6.6 %collective-permute-done.61 = bf16[4,96,768]{2,1,0:T(8,128)(2,1)S(1)} collective-permute-done((bf16[4,96,768]{2,1,0:T(8,128)(2,1)S(1)}, bf16[4,96,768]{2,1,0:T(8,128)(2,1)S(1)}, u32[]{:S(2)}, u32[]{:S(2)}) %collective-permute-start.61) | collective-permute-done | bytes 589856 | tf_op jit(solution)/shard_map/ppermute | solution.py:277
  153.9 3.8 %collective-permute-start.62 = (bf16[96,768]{1,0:T(8,128)(2,1)S(1)}, bf16[96,768]{1,0:T(8,128)(2,1)S(1)}, u32[]{:S(2)}, u32[]{:S(2)}) collective-permute-start(bf16[96,768]{1,0:T(8,128)(2,1)S(1)} %get-tuple-element.77), channel_id=1, source_target_pairs={{0,8},{4,12},{8,16},{12,20},{16,24},{20,28},{24,0},{28,4},{1,9},{5... | collective-permute-start | bytes 442376 | tf_op jit(solution)/shard_map/ppermute | solution.py:281
  160.9 2.2 collective-permute-done.62
  163.2 2.1 collective-permute-done.64
  165.2 6.3 %collective-permute-done.63 = bf16[96,768]{1,0:T(8,128)(2,1)S(1)} collective-permute-done((bf16[96,768]{1,0:T(8,128)(2,1)S(1)}, bf16[96,768]{1,0:T(8,128)(2,1)S(1)}, u32[]{:S(2)}, u32[]{:S(2)}) %collective-permute-start.63) | collective-permute-done | bytes 147488 | tf_op jit(solution)/shard_map/ppermute | solution.py:281
  185.1 2.3 fusion.110
  187.4 5.1 %fusion.32 = bf16[3,64,512]{2,1,0:T(8,128)(2,1)} fusion(bf16[512,3,64]{0,2,1:T(8,128)(2,1)} %bitcast.278, f32[3,512,512]{1,2,0:T(8,128)} %fusion.110, f32[3,512,512]{1,2,0:T(8,128)S(1)} %get-tuple-element.116, f32[3,512]{1,0:T(4,128)S(1)} %log_add_fusion), kind=kOutput, calls=%fused_computation.64 | convolution fusion | flops 106268672 | bytes 6690816 | tf_op jit(solution)/shard_map/hqk,khd->qhd/dot_general | solution.py:28
  192.5 5.1 %fusion.35 = bf16[3,64,512]{2,1,0:T(8,128)(2,1)} fusion(bf16[512,3,64]{0,2,1:T(8,128)(2,1)} %bitcast.276, f32[3,512,512]{1,2,0:T(8,128)} %fusion.110, f32[3,512,512]{1,2,0:T(8,128)S(1)} %get-tuple-element.116, f32[3,512]{1,0:T(4,128)S(1)} %log_add_fusion), kind=kOutput, calls=%fused_computation.65 | convolution fusion | flops 106268672 | bytes 6690816 | tf_op jit(solution)/shard_map/hqk,qhd->khd/dot_general | solution.py:28
  206.7 2.5 %collective-permute-done.51 = bf16[4,96,192]{2,1,0:T(8,128)(2,1)S(1)} collective-permute-done((bf16[4,96,192]{2,1,0:T(8,128)(2,1)}, bf16[4,96,192]{2,1,0:T(8,128)(2,1)S(1)}, u32[]{:S(2)}, u32[]{:S(2)}) %collective-permute-start.51) | collective-permute-done | bytes 147488 | tf_op jit(solution)/shard_map/ppermute | solution.py:277
  209.4 3.8 %collective-permute-start.54 = (bf16[96,192]{1,0:T(8,128)(2,1)S(1)}, bf16[96,192]{1,0:T(8,128)(2,1)S(1)}, u32[]{:S(2)}, u32[]{:S(2)}) collective-permute-start(bf16[96,192]{1,0:T(8,128)(2,1)S(1)} %get-tuple-element.107), channel_id=1, source_target_pairs={{0,24},{4,28},{8,0},{12,4},{16,8},{20,12},{24,16},{28,20},{1,25},{... | collective-permute-start | bytes 110600 | tf_op jit(solution)/shard_map/ppermute | solution.py:281
  226.8 3.8 %collective-permute-start.49 = (bf16[96,640]{1,0:T(8,128)(2,1)S(1)}, bf16[96,640]{1,0:T(8,128)(2,1)S(1)}, u32[]{:S(2)}, u32[]{:S(2)}) collective-permute-start(bf16[96,640]{1,0:T(8,128)(2,1)S(1)} %get-tuple-element.87), channel_id=1, source_target_pairs={{0,24},{4,28},{8,0},{12,4},{16,8},{20,12},{24,16},{28,20},{1,25},{... | collective-permute-start | bytes 368648 | tf_op jit(solution)/shard_map/ppermute | solution.py:281
  230.7 3.0 %collective-permute-done.47 = bf16[96,640]{1,0:T(8,128)(2,1)S(1)} collective-permute-done((bf16[96,640]{1,0:T(8,128)(2,1)S(1)}, bf16[96,640]{1,0:T(8,128)(2,1)S(1)}, u32[]{:S(2)}, u32[]{:S(2)}) %collective-permute-start.47) | collective-permute-done | bytes 122912 | tf_op jit(solution)/shard_map/ppermute | solution.py:281
  233.7 4.8 %collective-permute-done.48 = bf16[96,640]{1,0:T(8,128)(2,1)S(1)} collective-permute-done((bf16[96,640]{1,0:T(8,128)(2,1)S(1)}, bf16[96,640]{1,0:T(8,128)(2,1)S(1)}, u32[]{:S(2)}, u32[]{:S(2)}) %collective-permute-start.48) | collective-permute-done | bytes 122912 | tf_op jit(solution)/shard_map/ppermute | solution.py:281
  241.0 2.6 %collective-permute-done.50 = bf16[96,640]{1,0:T(8,128)(2,1)S(1)} collective-permute-done((bf16[96,640]{1,0:T(8,128)(2,1)S(1)}, bf16[96,640]{1,0:T(8,128)(2,1)S(1)}, u32[]{:S(2)}, u32[]{:S(2)}) %collective-permute-start.50) | collective-permute-done | bytes 122912 | tf_op jit(solution)/shard_map/ppermute | solution.py:260
  (328 shorter events, 120.9 us)
Async XLA Ops:
  1.7 15.2 %collective-permute-start.12 = (bf16[96,192]{1,0:T(8,128)(2,1)S(1)}, bf16[96,192]{1,0:T(8,128)(2,1)S(1)}, u32[]{:S(2)}, u32[]{:S(2)}) collective-permute-start(bf16[96,192]{1,0:T(8,128)(2,1)S(1)} %get-tuple-element.110), channel_id=1, source_target_pairs={{0,8},{4,12},{8,16},{12,20},{16,24},{20,28},{24,0},{28,4},{1,9},{5... | collective-permute-start | bytes 110600 | tf_op jit(solution)/shard_map/ppermute | solution.py:263
  4.8 14.1 %collective-permute-start.11 = (bf16[96,192]{1,0:T(8,128)(2,1)S(1)}, bf16[96,192]{1,0:T(8,128)(2,1)S(1)}, u32[]{:S(2)}, u32[]{:S(2)}) collective-permute-start(bf16[96,192]{1,0:T(8,128)(2,1)S(1)} %get-tuple-element.110), channel_id=1, source_target_pairs={{0,16},{4,20},{8,24},{12,28},{16,0},{20,4},{24,8},{28,12},{1,17},{... | collective-permute-start | bytes 110600 | tf_op jit(solution)/shard_map/ppermute | solution.py:263
  7.4 11.9 %collective-permute-start.10 = (bf16[96,192]{1,0:T(8,128)(2,1)S(1)}, bf16[96,192]{1,0:T(8,128)(2,1)S(1)}, u32[]{:S(2)}, u32[]{:S(2)}) collective-permute-start(bf16[96,192]{1,0:T(8,128)(2,1)S(1)} %get-tuple-element.110), channel_id=1, source_target_pairs={{0,24},{4,28},{8,0},{12,4},{16,8},{20,12},{24,16},{28,20},{1,25},{... | collective-permute-start | bytes 110600 | tf_op jit(solution)/shard_map/ppermute | solution.py:263
  8.7 13.4 %collective-permute-start.13 = (bf16[96,192]{1,0:T(8,128)(2,1)S(1)}, bf16[96,192]{1,0:T(8,128)(2,1)S(1)}, u32[]{:S(2)}, u32[]{:S(2)}) collective-permute-start(bf16[96,192]{1,0:T(8,128)(2,1)S(1)} %get-tuple-element.110), channel_id=1, source_target_pairs={{0,4},{4,0},{8,12},{12,8},{16,20},{20,16},{24,28},{28,24},{1,5},{5... | collective-permute-start | bytes 110600 | tf_op jit(solution)/shard_map/ppermute | solution.py:264
  15.9 12.9 %collective-permute-start.4 = (bf16[96,640]{1,0:T(8,128)(2,1)S(1)}, bf16[96,640]{1,0:T(8,128)(2,1)S(1)}, u32[]{:S(2)}, u32[]{:S(2)}) collective-permute-start(bf16[96,640]{1,0:T(8,128)(2,1)S(1)} %fusion.78), channel_id=1, source_target_pairs={{0,8},{4,12},{8,16},{12,20},{16,24},{20,28},{24,0},{28,4},{1,9},{5... | collective-permute-start | bytes 368648 | tf_op jit(solution)/shard_map/ppermute | solution.py:263
  18.9 11.0 %collective-permute-start.3 = (bf16[96,640]{1,0:T(8,128)(2,1)S(1)}, bf16[96,640]{1,0:T(8,128)(2,1)S(1)}, u32[]{:S(2)}, u32[]{:S(2)}) collective-permute-start(bf16[96,640]{1,0:T(8,128)(2,1)S(1)} %fusion.78), channel_id=1, source_target_pairs={{0,16},{4,20},{8,24},{12,28},{16,0},{20,4},{24,8},{28,12},{1,17},{... | collective-permute-start | bytes 368648 | tf_op jit(solution)/shard_map/ppermute | solution.py:263
  19.3 11.5 %collective-permute-start.2 = (bf16[96,640]{1,0:T(8,128)(2,1)S(1)}, bf16[96,640]{1,0:T(8,128)(2,1)S(1)}, u32[]{:S(2)}, u32[]{:S(2)}) collective-permute-start(bf16[96,640]{1,0:T(8,128)(2,1)S(1)} %fusion.78), channel_id=1, source_target_pairs={{0,24},{4,28},{8,0},{12,4},{16,8},{20,12},{24,16},{28,20},{1,25},{... | collective-permute-start | bytes 368648 | tf_op jit(solution)/shard_map/ppermute | solution.py:263
  43.1 13.6 %collective-permute-start.17 = (bf16[256,768]{1,0:T(8,128)(2,1)}, bf16[256,768]{1,0:T(8,128)(2,1)}, u32[]{:S(2)}, u32[]{:S(2)}) collective-permute-start(bf16[256,768]{1,0:T(8,128)(2,1)} %dynamic-slice_bitcast_fusion.5), channel_id=1, source_target_pairs={{0,1},{1,0},{2,3},{3,2},{4,5},{5,4},{6,7},{7,6},{8,9},{9,8},{10,11... | collective-permute-start | bytes 1179656 | tf_op jit(solution)/shard_map/ppermute | solution.py:257
  44.4 15.6 %collective-permute-start.21 = (bf16[96,768]{1,0:T(8,128)(2,1)S(1)}, bf16[96,768]{1,0:T(8,128)(2,1)S(1)}, u32[]{:S(2)}, u32[]{:S(2)}) collective-permute-start(bf16[96,768]{1,0:T(8,128)(2,1)S(1)} %constant_dynamic-slice_fusion.2), channel_id=1, source_target_pairs={{0,16},{4,20},{8,24},{12,28},{16,0},{20,4},{24,8},{28,12},{1,17},{... | collective-permute-start | bytes 442376 | tf_op jit(solution)/shard_map/ppermute | solution.py:263
  46.9 19.1 %collective-permute-start.20 = (bf16[96,768]{1,0:T(8,128)(2,1)S(1)}, bf16[96,768]{1,0:T(8,128)(2,1)S(1)}, u32[]{:S(2)}, u32[]{:S(2)}) collective-permute-start(bf16[96,768]{1,0:T(8,128)(2,1)S(1)} %constant_dynamic-slice_fusion.2), channel_id=1, source_target_pairs={{0,24},{4,28},{8,0},{12,4},{16,8},{20,12},{24,16},{28,20},{1,25},{... | collective-permute-start | bytes 442376 | tf_op jit(solution)/shard_map/ppermute | solution.py:263
  48.7 18.8 %collective-permute-start.23 = (bf16[96,768]{1,0:T(8,128)(2,1)S(1)}, bf16[96,768]{1,0:T(8,128)(2,1)S(1)}, u32[]{:S(2)}, u32[]{:S(2)}) collective-permute-start(bf16[96,768]{1,0:T(8,128)(2,1)S(1)} %constant_dynamic-slice_fusion.2), channel_id=1, source_target_pairs={{0,4},{4,0},{8,12},{12,8},{16,20},{20,16},{24,28},{28,24},{1,5},{5... | collective-permute-start | bytes 442376 | tf_op jit(solution)/shard_map/ppermute | solution.py:264
  52.7 15.4 %collective-permute-start.29 = (bf16[96,768]{1,0:T(8,128)(2,1)S(1)}, bf16[96,768]{1,0:T(8,128)(2,1)S(1)}, u32[]{:S(2)}, u32[]{:S(2)}) collective-permute-start(bf16[96,768]{1,0:T(8,128)(2,1)S(1)} %get-tuple-element.94), channel_id=1, source_target_pairs={{0,8},{4,12},{8,16},{12,20},{16,24},{20,28},{24,0},{28,4},{1,9},{5... | collective-permute-start | bytes 442376 | tf_op jit(solution)/shard_map/ppermute | solution.py:263
  56.7 14.2 %collective-permute-start.28 = (bf16[96,768]{1,0:T(8,128)(2,1)S(1)}, bf16[96,768]{1,0:T(8,128)(2,1)S(1)}, u32[]{:S(2)}, u32[]{:S(2)}) collective-permute-start(bf16[96,768]{1,0:T(8,128)(2,1)S(1)} %get-tuple-element.94), channel_id=1, source_target_pairs={{0,16},{4,20},{8,24},{12,28},{16,0},{20,4},{24,8},{28,12},{1,17},{... | collective-permute-start | bytes 442376 | tf_op jit(solution)/shard_map/ppermute | solution.py:263
  60.0 13.8 %collective-permute-start.27 = (bf16[96,768]{1,0:T(8,128)(2,1)S(1)}, bf16[96,768]{1,0:T(8,128)(2,1)S(1)}, u32[]{:S(2)}, u32[]{:S(2)}) collective-permute-start(bf16[96,768]{1,0:T(8,128)(2,1)S(1)} %get-tuple-element.94), channel_id=1, source_target_pairs={{0,24},{4,28},{8,0},{12,4},{16,8},{20,12},{24,16},{28,20},{1,25},{... | collective-permute-start | bytes 442376 | tf_op jit(solution)/shard_map/ppermute | solution.py:263
  70.9 9.9 %collective-permute-start.18 = (bf16[256,768]{1,0:T(8,128)(2,1)S(1)}, bf16[256,768]{1,0:T(8,128)(2,1)S(1)}, u32[]{:S(2)}, u32[]{:S(2)}) collective-permute-start(bf16[256,768]{1,0:T(8,128)(2,1)S(1)} %fusion.51), channel_id=1, source_target_pairs={{0,2},{2,0},{1,3},{3,1},{4,6},{6,4},{5,7},{7,5},{8,10},{10,8},{9,1... | collective-permute-start | bytes 1179656 | tf_op jit(solution)/shard_map/ppermute | solution.py:260
  75.9 10.8 %collective-permute-start.32 = (bf16[96,768]{1,0:T(8,128)(2,1)S(1)}, bf16[96,768]{1,0:T(8,128)(2,1)S(1)}, u32[]{:S(2)}, u32[]{:S(2)}) collective-permute-start(bf16[96,768]{1,0:T(8,128)(2,1)S(1)} %collective-permute-done.28), channel_id=1, source_target_pairs={{0,4},{4,0},{8,12},{12,8},{16,20},{20,16},{24,28},{28,24},{1,5},{5... | collective-permute-start | bytes 442376 | tf_op jit(solution)/shard_map/ppermute | solution.py:264
  77.0 11.2 %collective-permute-start.31 = (bf16[96,768]{1,0:T(8,128)(2,1)S(1)}, bf16[96,768]{1,0:T(8,128)(2,1)S(1)}, u32[]{:S(2)}, u32[]{:S(2)}) collective-permute-start(bf16[96,768]{1,0:T(8,128)(2,1)S(1)} %collective-permute-done.27), channel_id=1, source_target_pairs={{0,4},{4,0},{8,12},{12,8},{16,20},{20,16},{24,28},{28,24},{1,5},{5... | collective-permute-start | bytes 442376 | tf_op jit(solution)/shard_map/ppermute | solution.py:264
  93.9 12.0 %collective-permute-start.35 = (bf16[256,768]{1,0:T(8,128)(2,1)S(1)}, bf16[256,768]{1,0:T(8,128)(2,1)S(1)}, u32[]{:S(2)}, u32[]{:S(2)}) collective-permute-start(bf16[256,768]{1,0:T(8,128)(2,1)S(1)} %fusion.50), channel_id=1, source_target_pairs={{0,2},{2,0},{1,3},{3,1},{4,6},{6,4},{5,7},{7,5},{8,10},{10,8},{9,1... | collective-permute-start | bytes 1179656 | tf_op jit(solution)/shard_map/ppermute | solution.py:260
  94.5 14.8 %collective-permute-start.37 = (bf16[128,768]{1,0:T(8,128)(2,1)S(1)}, bf16[128,768]{1,0:T(8,128)(2,1)S(1)}, u32[]{:S(2)}, u32[]{:S(2)}) collective-permute-start(bf16[128,768]{1,0:T(8,128)(2,1)S(1)} %dynamic-slice_bitcast_fusion.7), channel_id=1, source_target_pairs={{0,2},{2,0},{1,3},{3,1},{4,6},{6,4},{5,7},{7,5},{8,10},{10,8},{9,1... | collective-permute-start | bytes 589832 | tf_op jit(solution)/shard_map/ppermute | solution.py:260
  125.4 16.2 %collective-permute-start.56 = (bf16[4,96,768]{2,1,0:T(8,128)(2,1)S(1)}, bf16[4,96,768]{2,1,0:T(8,128)(2,1)S(1)}, u32[]{:S(2)}, u32[]{:S(2)}) collective-permute-start(bf16[4,96,768]{2,1,0:T(8,128)(2,1)S(1)} %dynamic-slice_bitcast_fusion.1), channel_id=1, source_target_pairs={{0,4},{4,0},{8,12},{12,8},{16,20},{20,16},{24,28},{28,24},{1,5},{5... | collective-permute-start | bytes 1769480 | tf_op jit(solution)/shard_map/ppermute | solution.py:277
  129.4 24.2 %collective-permute-start.61 = (bf16[4,96,768]{2,1,0:T(8,128)(2,1)S(1)}, bf16[4,96,768]{2,1,0:T(8,128)(2,1)S(1)}, u32[]{:S(2)}, u32[]{:S(2)}) collective-permute-start(bf16[4,96,768]{2,1,0:T(8,128)(2,1)S(1)} %dynamic-slice_bitcast_fusion), channel_id=1, source_target_pairs={{0,4},{4,0},{8,12},{12,8},{16,20},{20,16},{24,28},{28,24},{1,5},{5... | collective-permute-start | bytes 1769480 | tf_op jit(solution)/shard_map/ppermute | solution.py:277
  130.4 43.0 %collective-permute-start.40 = (bf16[256,768]{1,0:T(8,128)(2,1)S(1)}, bf16[256,768]{1,0:T(8,128)(2,1)S(1)}, u32[]{:S(2)}, u32[]{:S(2)}) collective-permute-start(bf16[256,768]{1,0:T(8,128)(2,1)S(1)} %fusion.49), channel_id=1, source_target_pairs={{0,2},{2,0},{1,3},{3,1},{4,6},{6,4},{5,7},{7,5},{8,10},{10,8},{9,1... | collective-permute-start | bytes 1179656 | tf_op jit(solution)/shard_map/ppermute | solution.py:260
  141.8 15.9 %collective-permute-start.57 = (bf16[96,768]{1,0:T(8,128)(2,1)S(1)}, bf16[96,768]{1,0:T(8,128)(2,1)S(1)}, u32[]{:S(2)}, u32[]{:S(2)}) collective-permute-start(bf16[96,768]{1,0:T(8,128)(2,1)S(1)} %get-tuple-element.80), channel_id=1, source_target_pairs={{0,8},{4,12},{8,16},{12,20},{16,24},{20,28},{24,0},{28,4},{1,9},{5... | collective-permute-start | bytes 442376 | tf_op jit(solution)/shard_map/ppermute | solution.py:281
  145.6 12.9 %collective-permute-start.59 = (bf16[96,768]{1,0:T(8,128)(2,1)S(1)}, bf16[96,768]{1,0:T(8,128)(2,1)S(1)}, u32[]{:S(2)}, u32[]{:S(2)}) collective-permute-start(bf16[96,768]{1,0:T(8,128)(2,1)S(1)} %get-tuple-element.81), channel_id=1, source_target_pairs={{0,24},{4,28},{8,0},{12,4},{16,8},{20,12},{24,16},{28,20},{1,25},{... | collective-permute-start | bytes 442376 | tf_op jit(solution)/shard_map/ppermute | solution.py:281
  146.4 12.9 %collective-permute-start.58 = (bf16[96,768]{1,0:T(8,128)(2,1)S(1)}, bf16[96,768]{1,0:T(8,128)(2,1)S(1)}, u32[]{:S(2)}, u32[]{:S(2)}) collective-permute-start(bf16[96,768]{1,0:T(8,128)(2,1)S(1)} %get-tuple-element.82), channel_id=1, source_target_pairs={{0,16},{4,20},{8,24},{12,28},{16,0},{20,4},{24,8},{28,12},{1,17},{... | collective-permute-start | bytes 442376 | tf_op jit(solution)/shard_map/ppermute | solution.py:281
  153.9 9.2 %collective-permute-start.62 = (bf16[96,768]{1,0:T(8,128)(2,1)S(1)}, bf16[96,768]{1,0:T(8,128)(2,1)S(1)}, u32[]{:S(2)}, u32[]{:S(2)}) collective-permute-start(bf16[96,768]{1,0:T(8,128)(2,1)S(1)} %get-tuple-element.77), channel_id=1, source_target_pairs={{0,8},{4,12},{8,16},{12,20},{16,24},{20,28},{24,0},{28,4},{1,9},{5... | collective-permute-start | bytes 442376 | tf_op jit(solution)/shard_map/ppermute | solution.py:281
  158.5 13.0 %collective-permute-start.63 = (bf16[96,768]{1,0:T(8,128)(2,1)S(1)}, bf16[96,768]{1,0:T(8,128)(2,1)S(1)}, u32[]{:S(2)}, u32[]{:S(2)}) collective-permute-start(bf16[96,768]{1,0:T(8,128)(2,1)S(1)} %get-tuple-element.79), channel_id=1, source_target_pairs={{0,16},{4,20},{8,24},{12,28},{16,0},{20,4},{24,8},{28,12},{1,17},{... | collective-permute-start | bytes 442376 | tf_op jit(solution)/shard_map/ppermute | solution.py:281
  160.0 19.9 %collective-permute-start.60 = (bf16[96,768]{1,0:T(8,128)(2,1)}, bf16[96,768]{1,0:T(8,128)(2,1)}, u32[]{:S(2)}, u32[]{:S(2)}) collective-permute-start(bf16[96,768]{1,0:T(8,128)(2,1)} %fusion.71), channel_id=1, source_target_pairs={{0,2},{2,0},{1,3},{3,1},{4,6},{6,4},{5,7},{7,5},{8,10},{10,8},{9,1... | collective-permute-start | bytes 442376 | tf_op jit(solution)/shard_map/ppermute | solution.py:260
  172.2 47.0 %collective-permute-start.65 = (bf16[96,768]{1,0:T(8,128)(2,1)}, bf16[96,768]{1,0:T(8,128)(2,1)}, u32[]{:S(2)}, u32[]{:S(2)}) collective-permute-start(bf16[96,768]{1,0:T(8,128)(2,1)} %fusion.68), channel_id=1, source_target_pairs={{0,2},{2,0},{1,3},{3,1},{4,6},{6,4},{5,7},{7,5},{8,10},{10,8},{9,1... | collective-permute-start | bytes 442376 | tf_op jit(solution)/shard_map/ppermute | solution.py:260
  205.8 17.5 %collective-permute-start.42 = (bf16[256,768]{1,0:T(8,128)(2,1)S(1)}, bf16[256,768]{1,0:T(8,128)(2,1)S(1)}, u32[]{:S(2)}, u32[]{:S(2)}) collective-permute-start(bf16[256,768]{1,0:T(8,128)(2,1)S(1)} %dynamic-slice_bitcast_fusion.2), channel_id=1, source_target_pairs={{0,1},{1,0},{2,3},{3,2},{4,5},{5,4},{6,7},{7,6},{8,9},{9,8},{10,11... | collective-permute-start | bytes 1179656 | tf_op jit(solution)/shard_map/ppermute | solution.py:257
  215.3 11.2 %collective-permute-start.46 = (bf16[4,96,640]{2,1,0:T(8,128)(2,1)S(1)}, bf16[4,96,640]{2,1,0:T(8,128)(2,1)S(1)}, u32[]{:S(2)}, u32[]{:S(2)}) collective-permute-start(bf16[4,96,640]{2,1,0:T(8,128)(2,1)S(1)} %fusion.55), channel_id=1, source_target_pairs={{0,4},{4,0},{8,12},{12,8},{16,20},{20,16},{24,28},{28,24},{1,5},{5... | collective-permute-start | bytes 1474568 | tf_op jit(solution)/shard_map/ppermute | solution.py:277
  230.7 14.2 %collective-permute-start.44 = (bf16[128,768]{1,0:T(8,128)(2,1)S(1)}, bf16[128,768]{1,0:T(8,128)(2,1)S(1)}, u32[]{:S(2)}, u32[]{:S(2)}) collective-permute-start(bf16[128,768]{1,0:T(8,128)(2,1)S(1)} %fusion.64), channel_id=1, source_target_pairs={{0,1},{1,0},{2,3},{3,2},{4,5},{5,4},{6,7},{7,6},{8,9},{9,8},{10,11... | collective-permute-start | bytes 589832 | tf_op jit(solution)/shard_map/ppermute | solution.py:257
  (74 other events, 551.5 us)

commit v2 on v1

--- a/solution.py
+++ b/solution.py
@@ -4,6 +4,8 @@
 import jax
 import jax.numpy as jnp
 from jax import lax
+from jax.experimental import pallas as pl
+from jax.experimental.pallas import tpu as pltpu
 from jax.sharding import PartitionSpec as P
 
 HD = 64
@@ -226,6 +228,211 @@
     )
 
 
+def mul(left, right, left_dim, right_dim):
+    dims = (((left_dim,), (right_dim,)), ((), ()))
+    return lax.dot_general(left, right, dims, preferred_element_type=jnp.float32)
+
+
+def call(body, outs, *args, scratch=(), flops=0):
+    specs = [pl.BlockSpec(memory_space=pltpu.SMEM)] + [pl.BlockSpec(memory_space=pltpu.VMEM)] * (len(args) - 1)
+    shapes = [jax.ShapeDtypeStruct(shape, dtype) for shape, dtype in outs]
+    size = sum(math.prod(a.shape) * a.dtype.itemsize for a in list(args) + shapes)
+    return pl.pallas_call(
+        body,
+        out_shape=shapes,
+        in_specs=specs,
+        out_specs=[pl.BlockSpec(memory_space=pltpu.VMEM)] * len(shapes),
+        scratch_shapes=[pltpu.VMEM(shape, dtype) for shape, dtype in scratch],
+        compiler_params=pltpu.CompilerParams(vmem_limit_bytes=48 << 20),
+        cost_estimate=pl.CostEstimate(flops=flops, bytes_accessed=size, transcendentals=0),
+    )(*args)
+
+
+def head_masks(width):
+    lane = lax.broadcasted_iota(jnp.int32, (1, width), 1)
+    return [(lane >= h * HD) & (lane < (h + 1) * HD) for h in range(width // HD)]
+
+
+def only(values, mask):
+    return jnp.where(mask, values, jnp.zeros_like(values))
+
+
+def biased(raw, bias, scale):
+    blocks = bias.shape[0]
+    size = raw.shape[0] // blocks
+    return jnp.concatenate(
+        [raw[j * size : (j + 1) * size] * scale + bias[j : j + 1] for j in range(blocks)], axis=0
+    )
+
+
+def attend_body(at, x_ref, w_ref, bias_ref, o_ref, qkv_ref, lse_ref, vec_ref, p_scr, v_scr):
+    width = o_ref.shape[1]
+    rows = x_ref.shape[0]
+    scale = 1.0 / math.sqrt(HD)
+    w = w_ref[...]
+    qkv = mul(x_ref[...], w, 1, 0).astype(jnp.bfloat16)
+    qkv_ref[...] = qkv[:, : 3 * width]
+    vec = w[:, 3 * width :]
+    unit = (
+        lax.broadcasted_iota(jnp.int32, (8, vec.shape[1]), 0) == lax.broadcasted_iota(jnp.int32, (8, vec.shape[1]), 1)
+    ).astype(jnp.bfloat16)
+    vec_ref[...] = mul(unit, vec, 1, 1)
+    q, k, v = [qkv[:, i * width : (i + 1) * width] for i in range(3)]
+    lse_ref[...] = jnp.zeros_like(lse_ref)
+    blocks = bias_ref.shape[0] // (width // HD)
+    for h, mask in enumerate(head_masks(width)):
+        s = biased(mul(k, only(q, mask), 1, 1), bias_ref[h * blocks : (h + 1) * blocks, :], scale)
+        top = jnp.max(s, axis=0, keepdims=True)
+        e = jnp.exp(s - top)
+        total = jnp.sum(e, axis=0, keepdims=True)
+        lse_ref[h : h + 1, :] = top + jnp.log(total)
+        p_scr[h * rows : (h + 1) * rows, :] = (e * (1.0 / total)).astype(jnp.bfloat16)
+        v_scr[h * rows : (h + 1) * rows, :] = only(v, mask)
+    o_ref[...] = mul(p_scr[...], v_scr[...], 0, 0).astype(jnp.bfloat16)
+
+
+def split_rows(at, value_of, mine_ref, theirs_ref):
+    half = mine_ref.shape[0]
+    t = at[3]
+    theirs_ref[...] = value_of(pl.ds((1 - t) * half, half)).astype(theirs_ref.dtype)
+    mine_ref[...] = value_of(pl.ds(t * half, half))
+
+
+def project_body(at, o_ref, w_ref, mine_ref, theirs_ref):
+    split_rows(at, lambda rows: mul(o_ref[rows, :], w_ref[...], 1, 1), mine_ref, theirs_ref)
+
+
+def norm_parts(z):
+    centred = z - jnp.mean(z, axis=1, keepdims=True)
+    r = lax.rsqrt(jnp.mean(centred * centred, axis=1, keepdims=True) + eps)
+    return centred * r, r
+
+
+def norm_back(e2, n, r):
+    return r * (e2 - jnp.mean(e2, axis=1, keepdims=True) - n * jnp.mean(e2 * n, axis=1, keepdims=True))
+
+
+def norm_one_body(at, x_ref, a_ref, far_ref, vec_ref, n_ref, r_ref, low_ref):
+    half = n_ref.shape[0]
+    z = x_ref[pl.ds(at[3] * half, half), :].astype(jnp.float32)
+    z = z + (a_ref[...].astype(jnp.float32) + far_ref[...].astype(jnp.float32))
+    n, r = norm_parts(z)
+    n_ref[...] = n
+    r_ref[...] = jnp.broadcast_to(r, r_ref.shape)
+    low_ref[...] = (n * vec_ref[0:1, :] + vec_ref[2:3, :]).astype(jnp.bfloat16)
+
+
+def join(at, near_ref, far_ref, all_ref):
+    half = near_ref.shape[0]
+    t = at[3]
+    all_ref[pl.ds(t * half, half), :] = near_ref[...]
+    all_ref[pl.ds((1 - t) * half, half), :] = far_ref[...]
+
+
+def ffn_body(at, near_ref, far_ref, up_ref, down_ref, y_ref, u_ref, slope_ref, mine_ref, theirs_ref):
+    join(at, near_ref, far_ref, y_ref)
+    hid = mul(y_ref[...], up_ref[...], 1, 0)
+    root = math.sqrt(2.0 / math.pi)
+    square = hid * hid
+    bent = jnp.tanh(root * (hid + 0.044715 * (square * hid)))
+    u_ref[...] = (0.5 * hid * (1.0 + bent)).astype(jnp.bfloat16)
+    slope = 0.5 * (1.0 + bent) + 0.5 * hid * (1.0 - bent * bent) * (root * (1.0 + 3 * 0.044715 * square))
+    slope_ref[...] = slope.astype(jnp.bfloat16)
+    split_rows(at, lambda rows: mul(u_ref[rows, :], down_ref[...], 1, 1), mine_ref, theirs_ref)
+
+
+def norm_two_body(at, n1_ref, m_ref, far_ref, e_ref, e_far_ref, vec_ref, out_ref, dz_ref, low_ref, grad_ref, e_scr, out_scr):
+    part = e_far_ref.shape[0]
+    c, t = at[2], at[3]
+    e_scr[pl.ds(c * part, part), :] = e_ref[pl.ds(t * part, part), :].astype(jnp.float32)
+    e_scr[pl.ds((1 - c) * part, part), :] = e_far_ref[...].astype(jnp.float32)
+    y1 = n1_ref[...] * vec_ref[0:1, :] + vec_ref[2:3, :]
+    z = y1 + (m_ref[...].astype(jnp.float32) + far_ref[...].astype(jnp.float32))
+    n, r = norm_parts(z)
+    out_scr[...] = n * vec_ref[1:2, :] + vec_ref[3:4, :]
+    out_ref[...] = out_scr[pl.ds(c * part, part), :].astype(jnp.bfloat16)
+    e = e_scr[...]
+    dz = norm_back(e * vec_ref[1:2, :], n, r)
+    dz_ref[...] = dz
+    low_ref[...] = dz.astype(jnp.bfloat16)
+    grad_ref[...] = jnp.zeros_like(grad_ref)
+    grad_ref[1:2, :] = jnp.sum(e * n, axis=0, keepdims=True)
+    grad_ref[3:4, :] = jnp.sum(e, axis=0, keepdims=True)
+
+
+def ffn_back_body(at, near_ref, far_ref, slope_ref, down_ref, up_ref, dm_ref, dhid_ref, mine_ref, theirs_ref):
+    join(at, near_ref, far_ref, dm_ref)
+    du = mul(dm_ref[...], down_ref[...], 1, 0)
+    dhid_ref[...] = (du * slope_ref[...].astype(jnp.float32)).astype(jnp.bfloat16)
+    split_rows(at, lambda rows: mul(dhid_ref[rows, :], up_ref[...], 1, 1), mine_ref, theirs_ref)
+
+
+def deal(at, grad, own_ref, away_ref, scr):
+    shard = own_ref.shape[1]
+    scr[...] = grad
+    x = at[1]
+    for i in range(own_ref.shape[0]):
+        away_ref[i] = scr[pl.ds((2 * i + 1 - x) * shard, shard), :].astype(away_ref.dtype)
+        own_ref[i] = scr[pl.ds((2 * i + x) * shard, shard), :].astype(own_ref.dtype)
+
+
+def grad_body(at, left_ref, right_ref, own_ref, away_ref, scr):
+    deal(at, mul(left_ref[...], right_ref[...], 0, 0), own_ref, away_ref, scr)
+
+
+def norm_one_back_body(at, dz2_ref, d_ref, far_ref, n_ref, r_ref, vec_ref, grad2_ref, dz_ref, low_ref, grad_ref):
+    dy = dz2_ref[...] + (d_ref[...].astype(jnp.float32) + far_ref[...].astype(jnp.float32))
+    n = n_ref[...]
+    dz = norm_back(dy * vec_ref[0:1, :], n, r_ref[:, 0:1])
+    dz_ref[...] = dz
+    low_ref[...] = dz.astype(jnp.bfloat16)
+    grad_ref[...] = grad2_ref[...]
+    grad_ref[0:1, :] = jnp.sum(dy * n, axis=0, keepdims=True)
+    grad_ref[2:3, :] = jnp.sum(dy, axis=0, keepdims=True)
+
+
+def attend_back_body(
+    at, near_ref, far_ref, w_out_ref, w_ref, qkv_ref, o_ref, lse_ref, bias_ref, x_ref, vec_ref, vec_far_ref,
+    own_ref, away_ref, own_o_ref, away_o_ref, mine_ref, theirs_ref,
+    da_scr, p_scr, dr_scr, q_scr, do_scr, all_scr, grad_scr, grad_o_scr,
+):
+    width = o_ref.shape[1]
+    rows = x_ref.shape[0]
+    scale = 1.0 / math.sqrt(HD)
+    join(at, near_ref, far_ref, da_scr)
+    da = da_scr[...]
+    deal(at, mul(da, o_ref[...], 0, 0), own_o_ref, away_o_ref, grad_o_scr)
+    do = mul(da, w_out_ref[...], 1, 0).astype(jnp.bfloat16)
+    q, k, v = [qkv_ref[:, i * width : (i + 1) * width] for i in range(3)]
+    blocks = bias_ref.shape[0] // (width // HD)
+    dq = jnp.zeros((rows, width), jnp.float32)
+    for h, mask in enumerate(head_masks(width)):
+        q_h, do_h = only(q, mask), only(do, mask)
+        s = biased(mul(k, q_h, 1, 1), bias_ref[h * blocks : (h + 1) * blocks, :], scale)
+        p = jnp.exp(s - lse_ref[h : h + 1, :])
+        dp = mul(v, do_h, 1, 1)
+        pd = p * dp
+        ds = pd - p * jnp.sum(pd, axis=0, keepdims=True)
+        dr = (ds * scale).astype(jnp.bfloat16)
+        p_scr[:, h * rows : (h + 1) * rows] = p.astype(jnp.bfloat16)
+        dr_scr[:, h * rows : (h + 1) * rows] = dr
+        q_scr[h * rows : (h + 1) * rows, :] = q_h
+        do_scr[h * rows : (h + 1) * rows, :] = do_h
+        dq = dq + mul(dr, only(k, mask), 0, 0)
+    all_scr[:, 0:width] = dq.astype(jnp.bfloat16)
+    all_scr[:, width : 2 * width] = mul(dr_scr[...], q_scr[...], 1, 0).astype(jnp.bfloat16)
+    all_scr[:, 2 * width : 3 * width] = mul(p_scr[...], do_scr[...], 1, 0).astype(jnp.bfloat16)
+    vec = (vec_ref[...] + vec_far_ref[...]).astype(jnp.bfloat16)
+    extra = grad_scr.shape[1] - 3 * width
+    unit = (
+        lax.broadcasted_iota(jnp.int32, (8, extra), 0) == lax.broadcasted_iota(jnp.int32, (8, extra), 1)
+    ).astype(jnp.bfloat16)
+    grad = jnp.concatenate([mul(x_ref[...], all_scr[...], 0, 0), mul(vec, unit, 0, 0)], axis=1)
+    deal(at, grad, own_ref, away_ref, grad_scr)
+    w = w_ref[:, 0 : 3 * width]
+    split_rows(at, lambda r: mul(all_scr[r, :], w, 1, 1), mine_ref, theirs_ref)
+
+
 def rows_device(
     dims,
     inputs,
@@ -246,6 +453,7 @@
     t = lax.axis_index("tp")
     z = dp // 2
     x = dp % 2
+    at = jnp.stack([z, x, c, t]).astype(jnp.int32)
     f32, bf16 = jnp.float32, jnp.bfloat16
     pair = [(0, 1), (1, 0)]
     across_x = [(i, i ^ 1) for i in range(n_dp)]
@@ -261,19 +469,16 @@
 
     def gather_dp(v):
         near = [v] + [lax.ppermute(v, "dp", across_z(s)) for s in range(1, n_out)]
-        far = [lax.ppermute(p, "dp", across_x) for p in near]
         order = [0] + [n_out - s for s in range(1, n_out)]
+        first = lax.ppermute(v, "dp", across_x)
         near = jnp.stack([near[s] for s in order])
-        far = jnp.stack([far[s] for s in order])
+        rest = lax.ppermute(near[1:], "dp", across_x)
+        far = jnp.concatenate([first[None], rest])
         both = jnp.stack([jnp.where(x == 0, near, far), jnp.where(x == 0, far, near)], axis=1)
         both = jnp.roll(both, z, axis=0)
         return both.reshape(n_dp * v.shape[0], v.shape[1])
 
-    def scatter_dp(g):
-        rows = g.shape[0] // n_dp
-        g = g.astype(bf16).reshape(n_out, 2, rows, g.shape[1])
-        away = lax.dynamic_index_in_dim(g, 1 - x, 1, False)
-        own = lax.dynamic_index_in_dim(g, x, 1, False)
+    def scatter_dp(own, away):
         half = (own.astype(f32) + lax.ppermute(away, "dp", across_x).astype(f32)).astype(bf16)
         total = lax.dynamic_index_in_dim(half, z, 0, False).astype(f32)
         for s in range(1, n_out):
@@ -290,16 +495,15 @@
     heads = cols // HD
     own_blocks = rows // BLOCK
     per = own_blocks // 2
+    total_rows = 2 * rows
+    pad = -(3 * cols + 4) % 128
 
     def own_cols(w):
         n = w.shape[-1] // 2
         return lax.dynamic_slice_in_dim(w, c * n, n, w.ndim - 1)
 
     small = jnp.concatenate([norm_gains, norm_biases], axis=0)
-    w1 = jnp.concatenate(
-        [own_cols(qkv_weight[0]), own_cols(qkv_weight[1]), own_cols(qkv_weight[2]), jnp.pad(small.T, ((0, 0), (0, 60)))],
-        axis=1,
-    )
+    w1 = jnp.concatenate([own_cols(qkv_weight[i]) for i in range(3)] + [jnp.pad(small.T, ((0, 0), (0, pad)))], axis=1)
     w_out_t = own_cols(out_weight.T)
     w_up = own_cols(up_weight)
     w_down_t = own_cols(down_weight.T)
@@ -307,113 +511,108 @@
     w_out_t = gather_dp(w_out_t)
     w_up = gather_dp(w_up)
     w_down_t = gather_dp(w_down_t)
-    w_qkv = w1[:, : 3 * cols]
-    vecs = w1[:, 3 * cols : 3 * cols + 4].T.astype(f32)
-
-    def gather_rows(v):
-        halves = v.reshape(2, part, v.shape[1])
-        near = swap_ctx(lax.dynamic_index_in_dim(halves, t, 0, False))
-        far = swap_tp(near)
-        other = jnp.where(t == 0, jnp.stack([near, far]), jnp.stack([far, near]))
-        return jnp.where(c == 0, jnp.stack([halves, other], 1), jnp.stack([other, halves], 1)).reshape(4 * part, v.shape[1])
-
-    x_all = gather_rows(inputs)
-    e_own = lax.dynamic_index_in_dim(out_grad.reshape(2, part, width), t, 0, False)
-    e_far = swap_ctx(e_own)
-    e_mine = jnp.where(c == 0, jnp.concatenate([e_own, e_far]), jnp.concatenate([e_far, e_own])).astype(f32)
+
+    halves = inputs.reshape(2, part, width)
+    near = swap_ctx(lax.dynamic_index_in_dim(halves, t, 0, False))
+    far = swap_tp(near)
+    other = jnp.where(t == 0, jnp.stack([near, far]), jnp.stack([far, near]))
+    x_all = jnp.where(c == 0, jnp.stack([halves, other], 1), jnp.stack([other, halves], 1)).reshape(total_rows, width)
+    e_far = swap_ctx(lax.dynamic_index_in_dim(out_grad.reshape(2, part, width), t, 0, False))
 
     picks = random_blocks.reshape(own_blocks, 2, heads, 3)
     picks_own = lax.dynamic_index_in_dim(picks, c, 1, False)
     picks_far = swap_ctx(lax.dynamic_index_in_dim(picks, 1 - c, 1, False))
-    picks = jnp.where(c == 0, jnp.concatenate([picks_own, picks_far]), jnp.concatenate([picks_far, picks_own]))
+    picks = jnp.where(c == 0, jnp.stack([picks_own, picks_far]), jnp.stack([picks_far, picks_own]))
+    picks = picks.reshape(2 * own_blocks, heads, 3)
     blocks = jnp.arange(2 * own_blocks, dtype=jnp.int32)
     table, usable = block_table(blocks, lengths[0], picks)
     named = (table[..., None] == blocks) & usable[:, None, :, None]
     counts = jnp.sum(named.astype(f32), axis=2)
-    order = [cc * own_blocks + tt * per + i for tt in range(2) for cc in range(2) for i in range(per)]
-    order = jnp.array(order)
-    counts = counts[order][:, :, order]
+    counts = counts.reshape(2, 2, per, heads, 2, 2, per).transpose(3, 5, 4, 6, 1, 0, 2)
     bias = jnp.where(counts > 0, jnp.log(jnp.maximum(counts, 1.0)), -1e30)
-    bias = jnp.repeat(jnp.repeat(bias.transpose(1, 0, 2), BLOCK, 1), BLOCK, 2)
-    scale = 1.0 / math.sqrt(HD)
-
-    qkv = jnp.dot(x_all, w_qkv, preferred_element_type=f32).astype(bf16)
-    q, k, v = [qkv[:, i * cols : (i + 1) * cols].reshape(-1, heads, HD) for i in range(3)]
-    scores = contract("qhd,khd->hqk", q, k) * scale + bias
-    top = jnp.max(scores, axis=2, keepdims=True)
-    log_total = top + jnp.log(jnp.sum(jnp.exp(scores - top), axis=2, keepdims=True))
-    probs = jnp.exp(scores - log_total)
-    o = contract("hqk,khd->qhd", probs.astype(bf16), v).reshape(-1, cols).astype(bf16)
-
-    def mine(s):
-        return lax.dynamic_index_in_dim(s.reshape(2, s.shape[0] // 2, s.shape[1]), t, 0, False)
-
-    def theirs(s):
-        return lax.dynamic_index_in_dim(s.reshape(2, s.shape[0] // 2, s.shape[1]), 1 - t, 0, False)
-
-    def sum_row(s):
-        s = s.astype(bf16)
-        s = (mine(s).astype(f32) + swap_tp(theirs(s)).astype(f32)).astype(bf16)
-        return s.astype(f32) + swap_ctx(s).astype(f32)
-
-    def spread(s):
-        far = swap_tp(s)
-        return jnp.where(t == 0, jnp.concatenate([s, far]), jnp.concatenate([far, s]))
-
-    a = sum_row(contract("te,de->td", o, w_out_t))
-    y1, norm_pull = jax.vjp(layer_norm, mine(x_all).astype(f32) + a, vecs[0], vecs[2])
-    y1_low = spread(y1.astype(bf16))
-    hid = jnp.dot(y1_low, w_up, preferred_element_type=f32)
-    act, gelu_pull = jax.vjp(gelu_tanh, hid)
-    u = act.astype(bf16)
-    m = sum_row(contract("tf,df->td", u, w_down_t))
-    result, final_pull = jax.vjp(layer_norm, y1 + m, vecs[1], vecs[3])
-    dz2, dg2, dc2 = final_pull(e_mine)
-    dm = spread(dz2.astype(bf16))
-
-    def keep(s):
-        near = lax.dynamic_index_in_dim(s.reshape(2, part, s.shape[1]), c, 0, False)
-        far = swap_tp(near)
-        return jnp.where(t == 0, jnp.concatenate([near, far]), jnp.concatenate([far, near]))
-
-    output = keep(result.astype(bf16))
-    grad_down_t = contract("td,tf->df", dm, u)
-    du = jnp.dot(dm, w_down_t, preferred_element_type=f32)
-    dhid = gelu_pull(du)[0].astype(bf16)
-    grad_up = contract("td,tf->df", y1_low, dhid)
-    dy1 = dz2 + sum_row(contract("tf,df->td", dhid, w_up))
-    dz1, dg1, dc1 = norm_pull(dy1)
-    da = spread(dz1.astype(bf16))
-    grad_out_t = contract("td,te->de", da, o)
-    do = jnp.dot(da, w_out_t, preferred_element_type=f32).astype(bf16).reshape(-1, heads, HD)
-    dp_ = contract("qhd,khd->hqk", do, v)
-    ds = probs * (dp_ - jnp.sum(probs * dp_, axis=2, keepdims=True))
-    dr = (ds * scale).astype(bf16)
-    dq = contract("hqk,khd->qhd", dr, k).astype(bf16)
-    dk = contract("hqk,qhd->khd", dr, q).astype(bf16)
-    dv = contract("hqk,qhd->khd", probs.astype(bf16), do).astype(bf16)
-    dqkv = jnp.concatenate([g.reshape(-1, cols) for g in (dq, dk, dv)], axis=1)
-    grad_qkv = contract("td,te->de", x_all, dqkv)
-    vec_grads = jnp.stack([dg1, dg2, dc1, dc2])
-    vec_grads = vec_grads + swap_tp(vec_grads)
-    grad_1 = jnp.concatenate([grad_qkv, jnp.pad(vec_grads.T, ((0, 0), (0, 60)))], axis=1)
-    dx = contract("te,de->td", dqkv, w_qkv).astype(bf16)
-    dx = (mine(dx).astype(f32) + swap_tp(theirs(dx)).astype(f32)).astype(bf16).reshape(2, part, width)
+    bias = bias.reshape(heads * 2 * own_blocks, 2 * own_blocks, 1)
+    bias = jnp.broadcast_to(bias, bias.shape[:2] + (BLOCK,)).reshape(-1, total_rows)
+
+    low = [((rows, width), bf16)]
+    wide = [((rows, width), f32)]
+    o, qkv, lse, vecs = call(
+        attend_body,
+        [((total_rows, cols), bf16), ((total_rows, 3 * cols), bf16), ((8, total_rows), f32), ((8, width), f32)],
+        at, x_all, w1, bias,
+        scratch=[((heads * total_rows, total_rows), bf16), ((heads * total_rows, cols), bf16)],
+        flops=10**9,
+    )
+
+    def sum_row(mine, theirs):
+        s = (mine + swap_tp(theirs).astype(f32)).astype(bf16)
+        return s, swap_ctx(s)
+
+    a, a_far = sum_row(*call(project_body, wide + low, at, o, w_out_t))
+    n1, r1, y_low = call(norm_one_body, wide + [((rows, 128), f32)] + low, at, x_all, a, a_far, vecs)
+    flat = [((total_rows, units), bf16)]
+    y_all, u, slope, mine, theirs = call(
+        ffn_body, [((total_rows, width), bf16)] + flat * 2 + wide + low, at, y_low, swap_tp(y_low), w_up, w_down_t,
+        flops=10**9,
+    )
+    m, m_far = sum_row(mine, theirs)
+    out, dz2, dm_low, grad2 = call(
+        norm_two_body,
+        [((part, width), bf16)] + wide + low + [((8, width), f32)],
+        at, n1, m, m_far, out_grad, e_far, vecs,
+        scratch=wide * 2,
+    )
+    dm_all, dhid, mine, theirs = call(
+        ffn_back_body, [((total_rows, width), bf16)] + flat + wide + low,
+        at, dm_low, swap_tp(dm_low), slope, w_down_t, w_up,
+        flops=10**9,
+    )
+    d, d_far = sum_row(mine, theirs)
+
+    def dealt(n):
+        return [((n_out, shard, n), f32), ((n_out, shard, n), bf16)]
+
+    down_own, down_away = call(grad_body, dealt(units), at, dm_all, u, scratch=[((width, units), f32)])
+    up_own, up_away = call(grad_body, dealt(units), at, y_all, dhid, scratch=[((width, units), f32)])
+    dz1, da_low, grad1 = call(
+        norm_one_back_body, wide + low + [((8, width), f32)], at, dz2, d, d_far, n1, r1, vecs, grad2
+    )
+    qkv_own, qkv_away, o_own, o_away, mine, theirs = call(
+        attend_back_body,
+        dealt(w1.shape[1]) + dealt(cols) + wide + low,
+        at, da_low, swap_tp(da_low), w_out_t, w1, qkv, o, lse, bias, x_all, grad1, swap_tp(grad1),
+        scratch=[
+            ((total_rows, width), bf16),
+            ((total_rows, heads * total_rows), bf16),
+            ((total_rows, heads * total_rows), bf16),
+            ((heads * total_rows, cols), bf16),
+            ((heads * total_rows, cols), bf16),
+            ((total_rows, 3 * cols), bf16),
+            ((width, w1.shape[1]), f32),
+            ((width, cols), f32),
+        ],
+        flops=2 * 10**9,
+    )
+    dx = (mine + swap_tp(theirs).astype(f32)).astype(bf16).reshape(2, part, width)
     dx_own = lax.dynamic_index_in_dim(dx, c, 0, False).astype(f32)
     dx_far = swap_ctx(lax.dynamic_index_in_dim(dx, 1 - c, 0, False)).astype(f32)
     dz1_own = lax.dynamic_index_in_dim(dz1.reshape(2, part, width), c, 0, False)
     dx = (dz1_own + dx_own + dx_far).astype(bf16)
-    dx_tp = swap_tp(dx)
-    input_grad = jnp.where(t == 0, jnp.concatenate([dx, dx_tp]), jnp.concatenate([dx_tp, dx]))
+
+    def both_tp(near):
+        far = swap_tp(near)
+        return jnp.where(t == 0, jnp.concatenate([near, far]), jnp.concatenate([far, near]))
+
+    output = both_tp(out)
+    input_grad = both_tp(dx)
 
     def both_ctx(g):
         far = swap_ctx(g)
         return jnp.where(c == 0, jnp.concatenate([g, far], 1), jnp.concatenate([far, g], 1))
 
-    grad_down = both_ctx(scatter_dp(grad_down_t)).astype(f32).T
-    grad_up = both_ctx(scatter_dp(grad_up)).astype(f32)
-    grad_out = both_ctx(scatter_dp(grad_out_t)).astype(f32).T
-    grad_1 = scatter_dp(grad_1)
+    grad_down = both_ctx(scatter_dp(down_own, down_away)).astype(f32).T
+    grad_up = both_ctx(scatter_dp(up_own, up_away)).astype(f32)
+    grad_out = both_ctx(scatter_dp(o_own, o_away)).astype(f32).T
+    grad_1 = scatter_dp(qkv_own, qkv_away)
     far_1 = swap_ctx(grad_1)
     lo = jnp.where(c == 0, grad_1, far_1).astype(f32)
     hi = jnp.where(c == 0, far_1, grad_1).astype(f32)

time: 246 us -> 220 us (0.89)
  matrix products: 32.5 us -> 0 us
  Pallas kernels: 0 us -> 26.4 us
  waiting for transfers between devices: 79.8 us -> 91.1 us
  local copies, waits for them, and re-layouts: 25.1 us -> 13.9 us
  starting transfers between devices: 81.1 us -> 71.3 us
  other arithmetic: 24.7 us -> 15 us
    dot_general x18 -> x0, matrix products: 32.5 us -> none  [the longest x14 25.3 us: contract(): return jnp.einsum(form, left, right, preferred_element_type=jnp.float32)]
    pallas_call x0 -> x10, Pallas kernels: none -> 26.4 us  [call(): pl.pallas_call(body, out_shape=shapes, in_specs=specs, out_specs=[pl.Bloc...]
    ppermute x16 -> x8, waiting for transfers between devices: 11.6 us -> 24.9 us  [the longest x4 22.4 us: gather_dp(): first = lax.ppermute(v, 'dp', across_x)]
    ppermute x12, waiting for transfers between devices: 21.8 us -> 8.64 us  [scatter_dp(): total = total + lax.ppermute(piece, 'dp', across_z(s)).astype(f32)]
    ppermute x16 -> x8, starting transfers between devices: 17.8 us -> 7.42 us  [the longest x4 5.39 us: gather_dp(): first = lax.ppermute(v, 'dp', across_x)]
    ppermute x12, waiting for transfers between devices: 2.03 us -> 11.6 us  [gather_dp(): near = [v] + [lax.ppermute(v, 'dp', across_z(s)) for s in range(1, n_out)]]
    ppermute x12, starting transfers between devices: 18.4 us -> 25.2 us  [scatter_dp(): total = total + lax.ppermute(piece, 'dp', across_z(s)).astype(f32)]
    ppermute x11, waiting for transfers between devices: 1.74 us -> 7.32 us  [swap_tp(): return lax.ppermute(v, 'tp', pair)]
  transfers between devices with their start and end apart: 66 -> 58, of which waited for: 28 -> 24; matrix products, arithmetic and copies ran while one was open for 26% -> 9% of each run, Pallas kernels for 0% -> 8%
where the time goes in v2:
time: 220 us
  waiting for transfers between devices  91.1 us (41%)
  starting transfers between devices  71.3 us (32%)
  Pallas kernels  26.4 us (12%)
  other arithmetic  15 us (7%)
  local copies, waits for them, and re-layouts  13.9 us (6%)
    pallas_call x10, Pallas kernels, call(): pl.pallas_call(body, out_shape=shapes, in_specs=specs, out_specs=[pl.Bloc...  26.4 us
    ppermute x12, starting transfers between devices, scatter_dp(): total = total + lax.ppermute(piece, 'dp', across_z(s)).astype(f32)  25.2 us
    ppermute x12, starting transfers between devices, gather_dp(): near = [v] + [lax.ppermute(v, 'dp', across_z(s)) for s in range(1, n_out)]  23 us
    ppermute x4, waiting for transfers between devices, gather_dp(): first = lax.ppermute(v, 'dp', across_x)  22.4 us
    ppermute x4, waiting for transfers between devices, scatter_dp(): lax.ppermute(away, 'dp', across_x).astype(f32)  21.3 us
    ppermute x11, waiting for transfers between devices, swap_ctx(): return lax.ppermute(v, 'ctx', pair)  17.4 us
    ppermute x11, starting transfers between devices, swap_ctx(): return lax.ppermute(v, 'ctx', pair)  12.2 us
    ppermute x12, waiting for transfers between devices, gather_dp(): near = [v] + [lax.ppermute(v, 'dp', across_z(s)) for s in range(1, n_out)]  11.6 us
  transfers between devices with their start and end apart: 58, of which 24 were waited for; matrix products, arithmetic and copies ran while one was open for 9% of the time, Pallas kernels for 8%

profile of v2, /device:TPU:0, one launch (start us, length us, event | category | flops | bytes accessed | tf_op | source)
XLA Modules:
  0.0 219.7 jit_solution(3385502799226679499)
XLA Ops:
  3.5 5.0 %collective-permute-start.2 = (bf16[96,640]{1,0:T(8,128)(2,1)}, bf16[96,640]{1,0:T(8,128)(2,1)S(1)}, u32[]{:S(2)}, u32[]{:S(2)}) collective-permute-start(bf16[96,640]{1,0:T(8,128)(2,1)} %fusion.24), channel_id=1, source_target_pairs={{0,24},{4,28},{8,0},{12,4},{16,8},{20,12},{24,16},{28,20},{1,25},{... | collective-permute-start | bytes 368648 | tf_op jit(solution)/shard_map/ppermute | solution.py:471
  12.1 2.9 %collective-permute-start.8 = (bf16[96,192]{1,0:T(8,128)(2,1)S(1)}, bf16[96,192]{1,0:T(8,128)(2,1)S(1)}, u32[]{:S(2)}, u32[]{:S(2)}) collective-permute-start(bf16[96,192]{1,0:T(8,128)(2,1)S(1)} %get-tuple-element.137), channel_id=1, source_target_pairs={{0,24},{4,28},{8,0},{12,4},{16,8},{20,12},{24,16},{28,20},{1,25},{... | collective-permute-start | bytes 110600 | tf_op jit(solution)/shard_map/ppermute | solution.py:471
  19.1 4.0 %collective-permute-start.10 = (bf16[96,192]{1,0:T(8,128)(2,1)S(1)}, bf16[96,192]{1,0:T(8,128)(2,1)S(1)}, u32[]{:S(2)}, u32[]{:S(2)}) collective-permute-start(bf16[96,192]{1,0:T(8,128)(2,1)S(1)} %get-tuple-element.137), channel_id=1, source_target_pairs={{0,8},{4,12},{8,16},{12,20},{16,24},{20,28},{24,0},{28,4},{1,9},{5... | collective-permute-start | bytes 110600 | tf_op jit(solution)/shard_map/ppermute | solution.py:471
  24.0 2.6 %collective-permute-start.21 = (bf16[96,768]{1,0:T(8,128)(2,1)}, bf16[96,768]{1,0:T(8,128)(2,1)S(1)}, u32[]{:S(2)}, u32[]{:S(2)}) collective-permute-start(bf16[96,768]{1,0:T(8,128)(2,1)} %get-tuple-element.121), channel_id=1, source_target_pairs={{0,24},{4,28},{8,0},{12,4},{16,8},{20,12},{24,16},{28,20},{1,25},{... | collective-permute-start | bytes 442376 | tf_op jit(solution)/shard_map/ppermute | solution.py:471
  30.4 2.0 collective-permute-done.11
  33.3 2.4 %collective-permute-done.12 = bf16[3,96,192]{2,1,0:T(8,128)(2,1)S(1)} collective-permute-done((bf16[3,96,192]{2,1,0:T(8,128)(2,1)S(1)}, bf16[3,96,192]{2,1,0:T(8,128)(2,1)S(1)}, u32[]{:S(2)}, u32[]{:S(2)}) %collective-permute-start.12) | collective-permute-done | bytes 110624 | tf_op jit(solution)/shard_map/ppermute | solution.py:475
  39.3 6.5 %collective-permute-done.5 = bf16[96,640]{1,0:T(8,128)(2,1)S(1)} collective-permute-done((bf16[96,640]{1,0:T(8,128)(2,1)}, bf16[96,640]{1,0:T(8,128)(2,1)S(1)}, u32[]{:S(2)}, u32[]{:S(2)}) %collective-permute-start.5) | collective-permute-done | bytes 122912 | tf_op jit(solution)/shard_map/ppermute | solution.py:473
  46.6 3.3 %shard_map.161 = (bf16[512,192]{1,0:T(8,128)(2,1)S(1)}, bf16[512,576]{1,0:T(8,128)(2,1)S(1)}, f32[8,512]{1,0:T(8,128)S(1)}, f32[8,768]{1,0:T(8,128)S(1)}) custom-call(s32[4]{0:T(128)S(1)} %pad_add_fusion.1.at, bf16[512,768]{1,0:T(8,128)(2,1)S(1)} %bitcast.161, bf16[768,640]{1,0:T(8,128)(2,1)S(1)} %bitcast.166, f32[24,512]{1,0:T(8,128)S(1)} %reshape.944.bias_ref), custom_call_target="tpu_custom_call" | custom-call | flops 1000000000 | bytes 2646032 | tf_op jit(solution)/shard_map/pallas_call | solution.py:240
  52.4 3.7 %collective-permute-start.16 = (bf16[96,768]{1,0:T(8,128)(2,1)S(1)}, bf16[96,768]{1,0:T(8,128)(2,1)S(1)}, u32[]{:S(2)}, u32[]{:S(2)}) collective-permute-start(bf16[96,768]{1,0:T(8,128)(2,1)S(1)} %constant_dynamic-slice_fusion), channel_id=1, source_target_pairs={{0,24},{4,28},{8,0},{12,4},{16,8},{20,12},{24,16},{28,20},{1,25},{... | collective-permute-start | bytes 442376 | tf_op jit(solution)/shard_map/ppermute | solution.py:471
  60.4 9.3 %collective-permute-done.17 = bf16[96,768]{1,0:T(8,128)(2,1)S(1)} collective-permute-done((bf16[96,768]{1,0:T(8,128)(2,1)S(1)}, bf16[96,768]{1,0:T(8,128)(2,1)S(1)}, u32[]{:S(2)}, u32[]{:S(2)}) %collective-permute-start.17) | collective-permute-done | bytes 147488 | tf_op jit(solution)/shard_map/ppermute | solution.py:471
  70.7 2.0 collective-permute-start.24
  72.8 13.3 %collective-permute-done.24 = bf16[96,768]{1,0:T(8,128)(2,1)S(1)} collective-permute-done((bf16[96,768]{1,0:T(8,128)(2,1)}, bf16[96,768]{1,0:T(8,128)(2,1)S(1)}, u32[]{:S(2)}, u32[]{:S(2)}) %collective-permute-start.24) | collective-permute-done | bytes 147488 | tf_op jit(solution)/shard_map/ppermute | solution.py:473
  90.9 3.8 %shard_map.164 = (bf16[512,768]{1,0:T(8,128)(2,1)S(1)}, bf16[512,768]{1,0:T(8,128)(2,1)S(1)}, bf16[512,768]{1,0:T(8,128)(2,1)S(1)}, f32[256,768]{1,0:T(8,128)S(1)}, bf16[256,768]{1,0:T(8,128)(2,1)S(1)}) custom-call(s32[4]{0:T(128)S(1)} %pad_add_fusion.1.at, bf16[256,768]{1,0:T(8,128)(2,1)S(1)} %get-tuple-element.49.near_ref, ...), custom_call_target="tpu_custom_call" | custom-call | flops 1000000000 | bytes 6684688 | tf_op jit(solution)/shard_map/pallas_call | solution.py:240
  99.5 13.2 %collective-permute-done.28.e_far_ref = bf16[128,768]{1,0:T(8,128)(2,1)S(1)} collective-permute-done((bf16[128,768]{1,0:T(8,128)(2,1)S(1)}, bf16[128,768]{1,0:T(8,128)(2,1)S(1)}, u32[]{:S(2)}, u32[]{:S(2)}) %collective-permute-start.28) | collective-permute-done | bytes 196640 | tf_op jit(solution)/shard_map/ppermute | solution.py:468
  112.8 2.0 shard_map.165
  117.5 3.6 %shard_map.166 = (bf16[512,768]{1,0:T(8,128)(2,1)S(1)}, bf16[512,768]{1,0:T(8,128)(2,1)S(1)}, f32[256,768]{1,0:T(8,128)S(1)}, bf16[256,768]{1,0:T(8,128)(2,1)}) custom-call(s32[4]{0:T(128)S(1)} %pad_add_fusion.1.at, bf16[256,768]{1,0:T(8,128)(2,1)S(1)} %get-tuple-element.54.near_ref, bf16[256,768]{1,0:T(8,128)(2,1)S(1)} %collective-permute-done.30.far_ref, ...), custom_call_target="tpu_custom_call" | custom-call | flops 1000000000 | bytes 6684688 | tf_op jit(solution)/shard_map/pallas_call | solution.py:240
  123.0 2.3 %shard_map.170 = (f32[4,96,768]{2,1,0:T(8,128)S(1)}, bf16[4,96,768]{2,1,0:T(8,128)(2,1)}) custom-call(s32[4]{0:T(128)S(1)} %pad_add_fusion.1.at, bf16[512,768]{1,0:T(8,128)(2,1)S(1)} %get-tuple-element.75.left_ref, bf16[512,768]{1,0:T(8,128)(2,1)S(1)} %get-tuple-element.76.right_ref), custom_call_target="tpu_custom_call" | custom-call | bytes 3342352 | tf_op jit(solution)/shard_map/pallas_call | solution.py:240
  127.9 2.1 maximum_select_fusion.2
  136.0 5.8 %collective-permute-done.53 = bf16[4,96,768]{2,1,0:T(8,128)(2,1)} collective-permute-done((bf16[4,96,768]{2,1,0:T(8,128)(2,1)}, bf16[4,96,768]{2,1,0:T(8,128)(2,1)}, u32[]{:S(2)}, u32[]{:S(2)}) %collective-permute-start.53) | collective-permute-done | bytes 589856 | tf_op jit(solution)/shard_map/ppermute | solution.py:482
  144.4 2.0 collective-permute-start.55
  146.4 2.8 %collective-permute-start.56 = (bf16[96,768]{1,0:T(8,128)(2,1)S(1)}, bf16[96,768]{1,0:T(8,128)(2,1)S(1)}, u32[]{:S(2)}, u32[]{:S(2)}) collective-permute-start(bf16[96,768]{1,0:T(8,128)(2,1)S(1)} %get-tuple-element.110), channel_id=1, source_target_pairs={{0,24},{4,28},{8,0},{12,4},{16,8},{20,12},{24,16},{28,20},{1,25},{... | collective-permute-start | bytes 442376 | tf_op jit(solution)/shard_map/ppermute | solution.py:486
  150.4 3.3 %collective-permute-done.48 = bf16[4,96,768]{2,1,0:T(8,128)(2,1)S(1)} collective-permute-done((bf16[4,96,768]{2,1,0:T(8,128)(2,1)S(1)}, bf16[4,96,768]{2,1,0:T(8,128)(2,1)S(1)}, u32[]{:S(2)}, u32[]{:S(2)}) %collective-permute-start.48) | collective-permute-done | bytes 589856 | tf_op jit(solution)/shard_map/ppermute | solution.py:482
  155.3 3.6 %collective-permute-start.50 = (bf16[96,768]{1,0:T(8,128)(2,1)S(1)}, bf16[96,768]{1,0:T(8,128)(2,1)S(1)}, u32[]{:S(2)}, u32[]{:S(2)}) collective-permute-start(bf16[96,768]{1,0:T(8,128)(2,1)S(1)} %get-tuple-element.114), channel_id=1, source_target_pairs={{0,16},{4,20},{8,24},{12,28},{16,0},{20,4},{24,8},{28,12},{1,17},{... | collective-permute-start | bytes 442376 | tf_op jit(solution)/shard_map/ppermute | solution.py:486
  158.9 5.2 %collective-permute-start.51 = (bf16[96,768]{1,0:T(8,128)(2,1)S(1)}, bf16[96,768]{1,0:T(8,128)(2,1)S(1)}, u32[]{:S(2)}, u32[]{:S(2)}) collective-permute-start(bf16[96,768]{1,0:T(8,128)(2,1)S(1)} %get-tuple-element.113), channel_id=1, source_target_pairs={{0,24},{4,28},{8,0},{12,4},{16,8},{20,12},{24,16},{28,20},{1,25},{... | collective-permute-start | bytes 442376 | tf_op jit(solution)/shard_map/ppermute | solution.py:486
  166.2 7.0 %shard_map.168 = (f32[4,96,640]{2,1,0:T(8,128)}, bf16[4,96,640]{2,1,0:T(8,128)(2,1)S(1)}, f32[4,96,192]{2,1,0:T(8,128)S(1)}, bf16[4,96,192]{2,1,0:T(8,128)(2,1)S...) custom-call(s32[4]{0:T(128)S(1)} %pad_add_fusion.1.at, bf16[256,768]{1,0:T(8,128)(2,1)S(1)} %get-tuple-element.61.near_ref, ...), custom_call_target="tpu_custom_call" | custom-call | flops 2000000000 | bytes 6848528 | tf_op jit(solution)/shard_map/pallas_call | solution.py:240
  175.1 4.7 %collective-permute-done.43 = bf16[4,96,192]{2,1,0:T(8,128)(2,1)S(1)} collective-permute-done((bf16[4,96,192]{2,1,0:T(8,128)(2,1)S(1)}, bf16[4,96,192]{2,1,0:T(8,128)(2,1)S(1)}, u32[]{:S(2)}, u32[]{:S(2)}) %collective-permute-start.43) | collective-permute-done | bytes 147488 | tf_op jit(solution)/shard_map/ppermute | solution.py:482
  180.0 2.3 %collective-permute-start.44 = (bf16[96,192]{1,0:T(8,128)(2,1)S(1)}, bf16[96,192]{1,0:T(8,128)(2,1)S(1)}, u32[]{:S(2)}, u32[]{:S(2)}) collective-permute-start(bf16[96,192]{1,0:T(8,128)(2,1)S(1)} %get-tuple-element.133), channel_id=1, source_target_pairs={{0,8},{4,12},{8,16},{12,20},{16,24},{20,28},{24,0},{28,4},{1,9},{5... | collective-permute-start | bytes 110600 | tf_op jit(solution)/shard_map/ppermute | solution.py:486
  182.3 2.4 %collective-permute-start.46 = (bf16[96,192]{1,0:T(8,128)(2,1)S(1)}, bf16[96,192]{1,0:T(8,128)(2,1)S(1)}, u32[]{:S(2)}, u32[]{:S(2)}) collective-permute-start(bf16[96,192]{1,0:T(8,128)(2,1)S(1)} %get-tuple-element.134), channel_id=1, source_target_pairs={{0,24},{4,28},{8,0},{12,4},{16,8},{20,12},{24,16},{28,20},{1,25},{... | collective-permute-start | bytes 110600 | tf_op jit(solution)/shard_map/ppermute | solution.py:486
  193.9 7.4 %collective-permute-done.38 = bf16[4,96,640]{2,1,0:T(8,128)(2,1)S(1)} collective-permute-done((bf16[4,96,640]{2,1,0:T(8,128)(2,1)S(1)}, bf16[4,96,640]{2,1,0:T(8,128)(2,1)S(1)}, u32[]{:S(2)}, u32[]{:S(2)}) %collective-permute-start.38) | collective-permute-done | bytes 491552 | tf_op jit(solution)/shard_map/ppermute | solution.py:482
  205.7 3.2 %collective-permute-done.39 = bf16[96,640]{1,0:T(8,128)(2,1)S(1)} collective-permute-done((bf16[96,640]{1,0:T(8,128)(2,1)S(1)}, bf16[96,640]{1,0:T(8,128)(2,1)S(1)}, u32[]{:S(2)}, u32[]{:S(2)}) %collective-permute-start.39) | collective-permute-done | bytes 122912 | tf_op jit(solution)/shard_map/ppermute | solution.py:486
  208.9 3.6 %collective-permute-done.40 = bf16[96,640]{1,0:T(8,128)(2,1)S(1)} collective-permute-done((bf16[96,640]{1,0:T(8,128)(2,1)S(1)}, bf16[96,640]{1,0:T(8,128)(2,1)S(1)}, u32[]{:S(2)}, u32[]{:S(2)}) %collective-permute-start.40) | collective-permute-done | bytes 122912 | tf_op jit(solution)/shard_map/ppermute | solution.py:486
  214.8 2.8 %collective-permute-done.42 = bf16[96,640]{1,0:T(8,128)(2,1)S(1)} collective-permute-done((bf16[96,640]{1,0:T(8,128)(2,1)S(1)}, bf16[96,640]{1,0:T(8,128)(2,1)S(1)}, u32[]{:S(2)}, u32[]{:S(2)}) %collective-permute-start.42) | collective-permute-done | bytes 122912 | tf_op jit(solution)/shard_map/ppermute | solution.py:468
  (240 shorter events, 77.3 us)
Async XLA Ops:
  3.5 24.6 %collective-permute-start.2 = (bf16[96,640]{1,0:T(8,128)(2,1)}, bf16[96,640]{1,0:T(8,128)(2,1)S(1)}, u32[]{:S(2)}, u32[]{:S(2)}) collective-permute-start(bf16[96,640]{1,0:T(8,128)(2,1)} %fusion.24), channel_id=1, source_target_pairs={{0,24},{4,28},{8,0},{12,4},{16,8},{20,12},{24,16},{28,20},{1,25},{... | collective-permute-start | bytes 368648 | tf_op jit(solution)/shard_map/ppermute | solution.py:471
  8.6 19.7 %collective-permute-start.3 = (bf16[96,640]{1,0:T(8,128)(2,1)}, bf16[96,640]{1,0:T(8,128)(2,1)S(1)}, u32[]{:S(2)}, u32[]{:S(2)}) collective-permute-start(bf16[96,640]{1,0:T(8,128)(2,1)} %fusion.24), channel_id=1, source_target_pairs={{0,16},{4,20},{8,24},{12,28},{16,0},{20,4},{24,8},{28,12},{1,17},{... | collective-permute-start | bytes 368648 | tf_op jit(solution)/shard_map/ppermute | solution.py:471
  8.6 21.2 %collective-permute-start.4 = (bf16[96,640]{1,0:T(8,128)(2,1)}, bf16[96,640]{1,0:T(8,128)(2,1)S(1)}, u32[]{:S(2)}, u32[]{:S(2)}) collective-permute-start(bf16[96,640]{1,0:T(8,128)(2,1)} %fusion.24), channel_id=1, source_target_pairs={{0,8},{4,12},{8,16},{12,20},{16,24},{20,28},{24,0},{28,4},{1,9},{5... | collective-permute-start | bytes 368648 | tf_op jit(solution)/shard_map/ppermute | solution.py:471
  24.0 32.1 %collective-permute-start.21 = (bf16[96,768]{1,0:T(8,128)(2,1)}, bf16[96,768]{1,0:T(8,128)(2,1)S(1)}, u32[]{:S(2)}, u32[]{:S(2)}) collective-permute-start(bf16[96,768]{1,0:T(8,128)(2,1)} %get-tuple-element.121), channel_id=1, source_target_pairs={{0,24},{4,28},{8,0},{12,4},{16,8},{20,12},{24,16},{28,20},{1,25},{... | collective-permute-start | bytes 442376 | tf_op jit(solution)/shard_map/ppermute | solution.py:471
  28.2 27.9 %collective-permute-start.22 = (bf16[96,768]{1,0:T(8,128)(2,1)}, bf16[96,768]{1,0:T(8,128)(2,1)S(1)}, u32[]{:S(2)}, u32[]{:S(2)}) collective-permute-start(bf16[96,768]{1,0:T(8,128)(2,1)} %get-tuple-element.121), channel_id=1, source_target_pairs={{0,16},{4,20},{8,24},{12,28},{16,0},{20,4},{24,8},{28,12},{1,17},{... | collective-permute-start | bytes 442376 | tf_op jit(solution)/shard_map/ppermute | solution.py:471
  32.4 25.3 %collective-permute-start.23 = (bf16[96,768]{1,0:T(8,128)(2,1)}, bf16[96,768]{1,0:T(8,128)(2,1)S(1)}, u32[]{:S(2)}, u32[]{:S(2)}) collective-permute-start(bf16[96,768]{1,0:T(8,128)(2,1)} %get-tuple-element.121), channel_id=1, source_target_pairs={{0,8},{4,12},{8,16},{12,20},{16,24},{20,28},{24,0},{28,4},{1,9},{5... | collective-permute-start | bytes 442376 | tf_op jit(solution)/shard_map/ppermute | solution.py:471
  52.3 18.1 %collective-permute-start.13 = (bf16[256,768]{1,0:T(8,128)(2,1)S(1)}, bf16[256,768]{1,0:T(8,128)(2,1)S(1)}, u32[]{:S(2)}, u32[]{:S(2)}) collective-permute-start(bf16[256,768]{1,0:T(8,128)(2,1)S(1)} %get-tuple-element.46), channel_id=1, source_target_pairs={{0,1},{1,0},{2,3},{3,2},{4,5},{5,4},{6,7},{7,6},{8,9},{9,8},{10,11... | collective-permute-start | bytes 1179656 | tf_op jit(solution)/shard_map/ppermute | solution.py:465
  56.1 13.6 %collective-permute-start.17 = (bf16[96,768]{1,0:T(8,128)(2,1)S(1)}, bf16[96,768]{1,0:T(8,128)(2,1)S(1)}, u32[]{:S(2)}, u32[]{:S(2)}) collective-permute-start(bf16[96,768]{1,0:T(8,128)(2,1)S(1)} %constant_dynamic-slice_fusion), channel_id=1, source_target_pairs={{0,16},{4,20},{8,24},{12,28},{16,0},{20,4},{24,8},{28,12},{1,17},{... | collective-permute-start | bytes 442376 | tf_op jit(solution)/shard_map/ppermute | solution.py:471
  56.1 13.6 %collective-permute-start.18 = (bf16[96,768]{1,0:T(8,128)(2,1)S(1)}, bf16[96,768]{1,0:T(8,128)(2,1)S(1)}, u32[]{:S(2)}, u32[]{:S(2)}) collective-permute-start(bf16[96,768]{1,0:T(8,128)(2,1)S(1)} %constant_dynamic-slice_fusion), channel_id=1, source_target_pairs={{0,8},{4,12},{8,16},{12,20},{16,24},{20,28},{24,0},{28,4},{1,9},{5... | collective-permute-start | bytes 442376 | tf_op jit(solution)/shard_map/ppermute | solution.py:471
  57.8 28.3 %collective-permute-start.25 = (bf16[3,96,768]{2,1,0:T(8,128)(2,1)S(1)}, bf16[3,96,768]{2,1,0:T(8,128)(2,1)S(1)}, u32[]{:S(2)}, u32[]{:S(2)}) collective-permute-start(bf16[3,96,768]{2,1,0:T(8,128)(2,1)S(1)} %pad_maximum_fusion.6), channel_id=1, source_target_pairs={{0,4},{4,0},{8,12},{12,8},{16,20},{20,16},{24,28},{28,24},{1,5},{5... | collective-permute-start | bytes 1327112 | tf_op jit(solution)/shard_map/ppermute | solution.py:475
  69.7 18.1 %collective-permute-start.20 = (bf16[3,96,768]{2,1,0:T(8,128)(2,1)S(1)}, bf16[3,96,768]{2,1,0:T(8,128)(2,1)S(1)}, u32[]{:S(2)}, u32[]{:S(2)}) collective-permute-start(bf16[3,96,768]{2,1,0:T(8,128)(2,1)S(1)} %pad_maximum_fusion.5), channel_id=1, source_target_pairs={{0,4},{4,0},{8,12},{12,8},{16,20},{20,16},{24,28},{28,24},{1,5},{5... | collective-permute-start | bytes 1327112 | tf_op jit(solution)/shard_map/ppermute | solution.py:475
  70.5 15.7 %collective-permute-start.14 = (bf16[256,768]{1,0:T(8,128)(2,1)S(1)}, bf16[256,768]{1,0:T(8,128)(2,1)S(1)}, u32[]{:S(2)}, u32[]{:S(2)}) collective-permute-start(bf16[256,768]{1,0:T(8,128)(2,1)S(1)} %add_convert_fusion.6.a_ref), channel_id=1, source_target_pairs={{0,2},{2,0},{1,3},{3,1},{4,6},{6,4},{5,7},{7,5},{8,10},{10,8},{9,1... | collective-permute-start | bytes 1179656 | tf_op jit(solution)/shard_map/ppermute | solution.py:468
  70.7 15.3 %collective-permute-start.24 = (bf16[96,768]{1,0:T(8,128)(2,1)}, bf16[96,768]{1,0:T(8,128)(2,1)S(1)}, u32[]{:S(2)}, u32[]{:S(2)}) collective-permute-start(bf16[96,768]{1,0:T(8,128)(2,1)} %get-tuple-element.121), channel_id=1, source_target_pairs={{0,4},{4,0},{8,12},{12,8},{16,20},{20,16},{24,28},{28,24},{1,5},{5... | collective-permute-start | bytes 442376 | tf_op jit(solution)/shard_map/ppermute | solution.py:473
  72.7 15.1 %collective-permute-start.19 = (bf16[96,768]{1,0:T(8,128)(2,1)S(1)}, bf16[96,768]{1,0:T(8,128)(2,1)S(1)}, u32[]{:S(2)}, u32[]{:S(2)}) collective-permute-start(bf16[96,768]{1,0:T(8,128)(2,1)S(1)} %constant_dynamic-slice_fusion), channel_id=1, source_target_pairs={{0,4},{4,0},{8,12},{12,8},{16,20},{20,16},{24,28},{28,24},{1,5},{5... | collective-permute-start | bytes 442376 | tf_op jit(solution)/shard_map/ppermute | solution.py:473
  97.4 15.4 %collective-permute-start.27 = (bf16[256,768]{1,0:T(8,128)(2,1)S(1)}, bf16[256,768]{1,0:T(8,128)(2,1)S(1)}, u32[]{:S(2)}, u32[]{:S(2)}) collective-permute-start(bf16[256,768]{1,0:T(8,128)(2,1)S(1)} %add_convert_fusion.5.m_ref), channel_id=1, source_target_pairs={{0,2},{2,0},{1,3},{3,1},{4,6},{6,4},{5,7},{7,5},{8,10},{10,8},{9,1... | collective-permute-start | bytes 1179656 | tf_op jit(solution)/shard_map/ppermute | solution.py:468
  98.4 14.4 %collective-permute-start.28 = (bf16[128,768]{1,0:T(8,128)(2,1)S(1)}, bf16[128,768]{1,0:T(8,128)(2,1)S(1)}, u32[]{:S(2)}, u32[]{:S(2)}) collective-permute-start(bf16[128,768]{1,0:T(8,128)(2,1)S(1)} %dynamic-slice_bitcast_fusion.1), channel_id=1, source_target_pairs={{0,2},{2,0},{1,3},{3,1},{4,6},{6,4},{5,7},{7,5},{8,10},{10,8},{9,1... | collective-permute-start | bytes 589832 | tf_op jit(solution)/shard_map/ppermute | solution.py:468
  122.8 11.0 %collective-permute-start.31 = (bf16[256,768]{1,0:T(8,128)(2,1)}, bf16[256,768]{1,0:T(8,128)(2,1)}, u32[]{:S(2)}, u32[]{:S(2)}) collective-permute-start(bf16[256,768]{1,0:T(8,128)(2,1)} %get-tuple-element.57), channel_id=1, source_target_pairs={{0,1},{1,0},{2,3},{3,2},{4,5},{5,4},{6,7},{7,6},{8,9},{9,8},{10,11... | collective-permute-start | bytes 1179656 | tf_op jit(solution)/shard_map/ppermute | solution.py:465
  125.3 16.5 %collective-permute-start.53 = (bf16[4,96,768]{2,1,0:T(8,128)(2,1)}, bf16[4,96,768]{2,1,0:T(8,128)(2,1)}, u32[]{:S(2)}, u32[]{:S(2)}) collective-permute-start(bf16[4,96,768]{2,1,0:T(8,128)(2,1)} %get-tuple-element.78), channel_id=1, source_target_pairs={{0,4},{4,0},{8,12},{12,8},{16,20},{20,16},{24,28},{28,24},{1,5},{5... | collective-permute-start | bytes 1769480 | tf_op jit(solution)/shard_map/ppermute | solution.py:482
  132.6 21.2 %collective-permute-start.48 = (bf16[4,96,768]{2,1,0:T(8,128)(2,1)S(1)}, bf16[4,96,768]{2,1,0:T(8,128)(2,1)S(1)}, u32[]{:S(2)}, u32[]{:S(2)}) collective-permute-start(bf16[4,96,768]{2,1,0:T(8,128)(2,1)S(1)} %get-tuple-element.74), channel_id=1, source_target_pairs={{0,4},{4,0},{8,12},{12,8},{16,20},{20,16},{24,28},{28,24},{1,5},{5... | collective-permute-start | bytes 1769480 | tf_op jit(solution)/shard_map/ppermute | solution.py:482
  134.9 14.3 %collective-permute-start.32 = (bf16[256,768]{1,0:T(8,128)(2,1)S(1)}, bf16[256,768]{1,0:T(8,128)(2,1)S(1)}, u32[]{:S(2)}, u32[]{:S(2)}) collective-permute-start(bf16[256,768]{1,0:T(8,128)(2,1)S(1)} %add_convert_fusion.4.d_ref), channel_id=1, source_target_pairs={{0,2},{2,0},{1,3},{3,1},{4,6},{6,4},{5,7},{7,5},{8,10},{10,8},{9,1... | collective-permute-start | bytes 1179656 | tf_op jit(solution)/shard_map/ppermute | solution.py:468
  143.1 12.2 %collective-permute-start.54 = (bf16[96,768]{1,0:T(8,128)(2,1)S(1)}, bf16[96,768]{1,0:T(8,128)(2,1)S(1)}, u32[]{:S(2)}, u32[]{:S(2)}) collective-permute-start(bf16[96,768]{1,0:T(8,128)(2,1)S(1)} %get-tuple-element.109), channel_id=1, source_target_pairs={{0,8},{4,12},{8,16},{12,20},{16,24},{20,28},{24,0},{28,4},{1,9},{5... | collective-permute-start | bytes 442376 | tf_op jit(solution)/shard_map/ppermute | solution.py:486
  144.4 14.5 %collective-permute-start.55 = (bf16[96,768]{1,0:T(8,128)(2,1)S(1)}, bf16[96,768]{1,0:T(8,128)(2,1)S(1)}, u32[]{:S(2)}, u32[]{:S(2)}) collective-permute-start(bf16[96,768]{1,0:T(8,128)(2,1)S(1)} %get-tuple-element.111), channel_id=1, source_target_pairs={{0,16},{4,20},{8,24},{12,28},{16,0},{20,4},{24,8},{28,12},{1,17},{... | collective-permute-start | bytes 442376 | tf_op jit(solution)/shard_map/ppermute | solution.py:486
  146.4 17.8 %collective-permute-start.56 = (bf16[96,768]{1,0:T(8,128)(2,1)S(1)}, bf16[96,768]{1,0:T(8,128)(2,1)S(1)}, u32[]{:S(2)}, u32[]{:S(2)}) collective-permute-start(bf16[96,768]{1,0:T(8,128)(2,1)S(1)} %get-tuple-element.110), channel_id=1, source_target_pairs={{0,24},{4,28},{8,0},{12,4},{16,8},{20,12},{24,16},{28,20},{1,25},{... | collective-permute-start | bytes 442376 | tf_op jit(solution)/shard_map/ppermute | solution.py:486
  150.3 15.9 %collective-permute-start.33 = (bf16[256,768]{1,0:T(8,128)(2,1)S(1)}, bf16[256,768]{1,0:T(8,128)(2,1)S(1)}, u32[]{:S(2)}, u32[]{:S(2)}) collective-permute-start(bf16[256,768]{1,0:T(8,128)(2,1)S(1)} %get-tuple-element.61.near_ref), channel_id=1, source_target_pairs={{0,1},{1,0},{2,3},{3,2},{4,5},{5,4},{6,7},{7,6},{8,9},{9,8},{10,11... | collective-permute-start | bytes 1179656 | tf_op jit(solution)/shard_map/ppermute | solution.py:465
  153.9 19.5 %collective-permute-start.49 = (bf16[96,768]{1,0:T(8,128)(2,1)S(1)}, bf16[96,768]{1,0:T(8,128)(2,1)S(1)}, u32[]{:S(2)}, u32[]{:S(2)}) collective-permute-start(bf16[96,768]{1,0:T(8,128)(2,1)S(1)} %get-tuple-element.112), channel_id=1, source_target_pairs={{0,8},{4,12},{8,16},{12,20},{16,24},{20,28},{24,0},{28,4},{1,9},{5... | collective-permute-start | bytes 442376 | tf_op jit(solution)/shard_map/ppermute | solution.py:486
  155.3 18.2 %collective-permute-start.50 = (bf16[96,768]{1,0:T(8,128)(2,1)S(1)}, bf16[96,768]{1,0:T(8,128)(2,1)S(1)}, u32[]{:S(2)}, u32[]{:S(2)}) collective-permute-start(bf16[96,768]{1,0:T(8,128)(2,1)S(1)} %get-tuple-element.114), channel_id=1, source_target_pairs={{0,16},{4,20},{8,24},{12,28},{16,0},{20,4},{24,8},{28,12},{1,17},{... | collective-permute-start | bytes 442376 | tf_op jit(solution)/shard_map/ppermute | solution.py:486
  158.9 14.6 %collective-permute-start.51 = (bf16[96,768]{1,0:T(8,128)(2,1)S(1)}, bf16[96,768]{1,0:T(8,128)(2,1)S(1)}, u32[]{:S(2)}, u32[]{:S(2)}) collective-permute-start(bf16[96,768]{1,0:T(8,128)(2,1)S(1)} %get-tuple-element.113), channel_id=1, source_target_pairs={{0,24},{4,28},{8,0},{12,4},{16,8},{20,12},{24,16},{28,20},{1,25},{... | collective-permute-start | bytes 442376 | tf_op jit(solution)/shard_map/ppermute | solution.py:486
  165.4 19.4 %collective-permute-start.57 = (bf16[96,768]{1,0:T(8,128)(2,1)S(1)}, bf16[96,768]{1,0:T(8,128)(2,1)S(1)}, u32[]{:S(2)}, u32[]{:S(2)}) collective-permute-start(bf16[96,768]{1,0:T(8,128)(2,1)S(1)} %fusion.16), channel_id=1, source_target_pairs={{0,2},{2,0},{1,3},{3,1},{4,6},{6,4},{5,7},{7,5},{8,10},{10,8},{9,1... | collective-permute-start | bytes 442376 | tf_op jit(solution)/shard_map/ppermute | solution.py:468
  173.6 15.3 %collective-permute-start.52 = (bf16[96,768]{1,0:T(8,128)(2,1)S(1)}, bf16[96,768]{1,0:T(8,128)(2,1)S(1)}, u32[]{:S(2)}, u32[]{:S(2)}) collective-permute-start(bf16[96,768]{1,0:T(8,128)(2,1)S(1)} %fusion.19), channel_id=1, source_target_pairs={{0,2},{2,0},{1,3},{3,1},{4,6},{6,4},{5,7},{7,5},{8,10},{10,8},{9,1... | collective-permute-start | bytes 442376 | tf_op jit(solution)/shard_map/ppermute | solution.py:468
  189.8 11.6 %collective-permute-start.38 = (bf16[4,96,640]{2,1,0:T(8,128)(2,1)S(1)}, bf16[4,96,640]{2,1,0:T(8,128)(2,1)S(1)}, u32[]{:S(2)}, u32[]{:S(2)}) collective-permute-start(bf16[4,96,640]{2,1,0:T(8,128)(2,1)S(1)} %get-tuple-element.68), channel_id=1, source_target_pairs={{0,4},{4,0},{8,12},{12,8},{16,20},{20,16},{24,28},{28,24},{1,5},{5... | collective-permute-start | bytes 1474568 | tf_op jit(solution)/shard_map/ppermute | solution.py:482
  192.6 13.0 %collective-permute-start.36 = (bf16[128,768]{1,0:T(8,128)(2,1)S(1)}, bf16[128,768]{1,0:T(8,128)(2,1)S(1)}, u32[]{:S(2)}, u32[]{:S(2)}) collective-permute-start(bf16[128,768]{1,0:T(8,128)(2,1)S(1)} %dynamic-slice_bitcast_fusion), channel_id=1, source_target_pairs={{0,2},{2,0},{1,3},{3,1},{4,6},{6,4},{5,7},{7,5},{8,10},{10,8},{9,1... | collective-permute-start | bytes 589832 | tf_op jit(solution)/shard_map/ppermute | solution.py:468
  205.7 13.2 %collective-permute-start.37 = (bf16[128,768]{1,0:T(8,128)(2,1)S(1)}, bf16[128,768]{1,0:T(8,128)(2,1)S(1)}, u32[]{:S(2)}, u32[]{:S(2)}) collective-permute-start(bf16[128,768]{1,0:T(8,128)(2,1)S(1)} %fusion.12), channel_id=1, source_target_pairs={{0,1},{1,0},{2,3},{3,2},{4,5},{5,4},{6,7},{7,6},{8,9},{9,8},{10,11... | collective-permute-start | bytes 589832 | tf_op jit(solution)/shard_map/ppermute | solution.py:465
  (52 other events, 386.9 us)

commit v3 on v2

--- a/solution.py
+++ b/solution.py
@@ -233,18 +233,19 @@
     return lax.dot_general(left, right, dims, preferred_element_type=jnp.float32)
 
 
-def call(body, outs, *args, scratch=(), flops=0):
-    specs = [pl.BlockSpec(memory_space=pltpu.SMEM)] + [pl.BlockSpec(memory_space=pltpu.VMEM)] * (len(args) - 1)
+def call(body, outs, *args, scratch=(), copies=0, spec=None, room=32, flops=0):
+    spec = spec or pl.BlockSpec(memory_space=pltpu.VMEM)
+    specs = [spec] * len(args)
     shapes = [jax.ShapeDtypeStruct(shape, dtype) for shape, dtype in outs]
-    size = sum(math.prod(a.shape) * a.dtype.itemsize for a in list(args) + shapes)
     return pl.pallas_call(
         body,
         out_shape=shapes,
         in_specs=specs,
         out_specs=[pl.BlockSpec(memory_space=pltpu.VMEM)] * len(shapes),
-        scratch_shapes=[pltpu.VMEM(shape, dtype) for shape, dtype in scratch],
-        compiler_params=pltpu.CompilerParams(vmem_limit_bytes=48 << 20),
-        cost_estimate=pl.CostEstimate(flops=flops, bytes_accessed=size, transcendentals=0),
+        scratch_shapes=[pltpu.VMEM(shape, dtype) for shape, dtype in scratch]
+        + ([pltpu.SemaphoreType.DMA((copies,))] if copies else []),
+        compiler_params=pltpu.CompilerParams(vmem_limit_bytes=room << 20),
+        cost_estimate=pl.CostEstimate(flops=flops, bytes_accessed=0, transcendentals=0),
     )(*args)
 
 
@@ -265,9 +266,70 @@
     )
 
 
-def attend_body(at, x_ref, w_ref, bias_ref, o_ref, qkv_ref, lse_ref, vec_ref, p_scr, v_scr):
+def place(pieces, all_ref, window):
+    index = 0
+    shard, width = pieces[0].shape
+    for piece in pieces:
+        parts = [piece] if len(piece.shape) == 2 else [piece.at[i] for i in range(piece.shape[0])]
+        for part in parts:
+            owner = lax.axis_index("dp") ^ (2 * (index % 4) + index // 4)
+            start = window if part.shape[1] != width else 0
+            all_ref[pl.ds(pl.multiple_of(owner * shard, 32), shard), :] = part[:, start : start + width]
+            index += 1
+
+
+def fetch(pairs, sems):
+    copies = [pltpu.make_async_copy(src, dst, sems.at[i]) for i, (src, dst) in enumerate(pairs)]
+    for copy in copies:
+        copy.start()
+    for copy in copies:
+        copy.wait()
+
+
+def own_half(src, dst):
+    n = dst.shape[1]
+    dst[...] = jnp.where(lax.axis_index("ctx") == 0, src[:, :n], src[:, n:])
+
+
+def pack_first_body(qkv_hbm, gain_hbm, bias_hbm, out_hbm, w_ref, out_ref, pack_ref, qkv, gain, bias, out, sems):
+    fetch(((qkv_hbm, qkv), (gain_hbm, gain), (bias_hbm, bias), (out_hbm, out)), sems)
+    c = lax.axis_index("ctx")
+    n = qkv.shape[2] // 2
+    for i in range(3):
+        w_ref[:, i * n : (i + 1) * n] = jnp.where(c == 0, qkv[i, :, :n], qkv[i, :, n:])
+    first = w_ref.shape[1]
+    extra = first - 3 * n
+    row = lax.broadcasted_iota(jnp.int32, (2, extra), 0)
+    lane = lax.broadcasted_iota(jnp.int32, (2, extra), 1)
+    cols = mul(gain[...], (row == lane).astype(jnp.bfloat16), 0, 0)
+    cols = cols + mul(bias[...], (row + 2 == lane).astype(jnp.bfloat16), 0, 0)
+    w_ref[:, 3 * n :] = cols.astype(jnp.bfloat16)
+    own_half(out, out_ref)
+    pack_ref[:, 0:first] = w_ref[...]
+    pack_ref[:, first:] = out_ref[...]
+
+
+def pack_second_body(up_hbm, down_hbm, up_ref, down_ref, pack_ref, up, down, sems):
+    fetch(((up_hbm, up), (down_hbm, down)), sems)
+    own_half(up, up_ref)
+    own_half(down, down_ref)
+    n = up_ref.shape[1]
+    pack_ref[:, 0:n] = up_ref[...]
+    pack_ref[:, n:] = down_ref[...]
+
+
+def attend_body(
+    own_ref, far_ref, w0, w1, w2, w3, w4, w5, w6, bias_ref,
+    o_ref, qkv_ref, lse_ref, vec_ref, x_ref, w_ref, p_scr, v_scr,
+):
     width = o_ref.shape[1]
     rows = x_ref.shape[0]
+    part = far_ref.shape[0] // 2
+    c = lax.axis_index("ctx")
+    for t in range(2):
+        x_ref[pl.ds((2 * t + c) * part, part), :] = own_ref[t * part : (t + 1) * part, :]
+        x_ref[pl.ds((2 * t + 1 - c) * part, part), :] = far_ref[t * part : (t + 1) * part, :]
+    place((w0, w1, w2, w3, w4, w5, w6), w_ref, 0)
     scale = 1.0 / math.sqrt(HD)
     w = w_ref[...]
     qkv = mul(x_ref[...], w, 1, 0).astype(jnp.bfloat16)
@@ -291,15 +353,20 @@
     o_ref[...] = mul(p_scr[...], v_scr[...], 0, 0).astype(jnp.bfloat16)
 
 
-def split_rows(at, value_of, mine_ref, theirs_ref):
+def split_rows(value_of, mine_ref, theirs_ref):
     half = mine_ref.shape[0]
-    t = at[3]
+    t = lax.axis_index("tp")
     theirs_ref[...] = value_of(pl.ds((1 - t) * half, half)).astype(theirs_ref.dtype)
     mine_ref[...] = value_of(pl.ds(t * half, half))
 
 
-def project_body(at, o_ref, w_ref, mine_ref, theirs_ref):
-    split_rows(at, lambda rows: mul(o_ref[rows, :], w_ref[...], 1, 1), mine_ref, theirs_ref)
+def project_body(window, o_ref, w0, w1, w2, w3, w4, w5, mine_ref, theirs_ref, w_ref):
+    place((w0, w1, w2, w3, w4, w5), w_ref, window)
+    split_rows(lambda rows: mul(o_ref[rows, :], w_ref[...], 1, 1), mine_ref, theirs_ref)
+
+
+def add_tp_body(mine_ref, both_ref, sum_ref):
+    sum_ref[...] = (mine_ref[...] + both_ref[1 - lax.axis_index("tp")].astype(jnp.float32)).astype(jnp.bfloat16)
 
 
 def norm_parts(z):
@@ -312,9 +379,9 @@
     return r * (e2 - jnp.mean(e2, axis=1, keepdims=True) - n * jnp.mean(e2 * n, axis=1, keepdims=True))
 
 
-def norm_one_body(at, x_ref, a_ref, far_ref, vec_ref, n_ref, r_ref, low_ref):
+def norm_one_body(x_ref, a_ref, far_ref, vec_ref, n_ref, r_ref, low_ref):
     half = n_ref.shape[0]
-    z = x_ref[pl.ds(at[3] * half, half), :].astype(jnp.float32)
+    z = x_ref[pl.ds(lax.axis_index("tp") * half, half), :].astype(jnp.float32)
     z = z + (a_ref[...].astype(jnp.float32) + far_ref[...].astype(jnp.float32))
     n, r = norm_parts(z)
     n_ref[...] = n
@@ -322,15 +389,8 @@
     low_ref[...] = (n * vec_ref[0:1, :] + vec_ref[2:3, :]).astype(jnp.bfloat16)
 
 
-def join(at, near_ref, far_ref, all_ref):
-    half = near_ref.shape[0]
-    t = at[3]
-    all_ref[pl.ds(t * half, half), :] = near_ref[...]
-    all_ref[pl.ds((1 - t) * half, half), :] = far_ref[...]
-
-
-def ffn_body(at, near_ref, far_ref, up_ref, down_ref, y_ref, u_ref, slope_ref, mine_ref, theirs_ref):
-    join(at, near_ref, far_ref, y_ref)
+def ffn_body(window, y_ref, w0, w1, w2, w3, w4, w5, u_ref, slope_ref, up_ref):
+    place((w0, w1, w2, w3, w4, w5), up_ref, window)
     hid = mul(y_ref[...], up_ref[...], 1, 0)
     root = math.sqrt(2.0 / math.pi)
     square = hid * hid
@@ -338,14 +398,13 @@
     u_ref[...] = (0.5 * hid * (1.0 + bent)).astype(jnp.bfloat16)
     slope = 0.5 * (1.0 + bent) + 0.5 * hid * (1.0 - bent * bent) * (root * (1.0 + 3 * 0.044715 * square))
     slope_ref[...] = slope.astype(jnp.bfloat16)
-    split_rows(at, lambda rows: mul(u_ref[rows, :], down_ref[...], 1, 1), mine_ref, theirs_ref)
-
-
-def norm_two_body(at, n1_ref, m_ref, far_ref, e_ref, e_far_ref, vec_ref, out_ref, dz_ref, low_ref, grad_ref, e_scr, out_scr):
-    part = e_far_ref.shape[0]
-    c, t = at[2], at[3]
+
+
+def norm_two_body(n1_ref, m_ref, far_ref, e_ref, e_far_ref, vec_ref, out_ref, dz_ref, low_ref, grad_ref, e_scr, out_scr):
+    part = out_ref.shape[0]
+    c, t = lax.axis_index("ctx"), lax.axis_index("tp")
     e_scr[pl.ds(c * part, part), :] = e_ref[pl.ds(t * part, part), :].astype(jnp.float32)
-    e_scr[pl.ds((1 - c) * part, part), :] = e_far_ref[...].astype(jnp.float32)
+    e_scr[pl.ds((1 - c) * part, part), :] = e_far_ref[pl.ds(t * part, part), :].astype(jnp.float32)
     y1 = n1_ref[...] * vec_ref[0:1, :] + vec_ref[2:3, :]
     z = y1 + (m_ref[...].astype(jnp.float32) + far_ref[...].astype(jnp.float32))
     n, r = norm_parts(z)
@@ -360,48 +419,77 @@
     grad_ref[3:4, :] = jnp.sum(e, axis=0, keepdims=True)
 
 
-def ffn_back_body(at, near_ref, far_ref, slope_ref, down_ref, up_ref, dm_ref, dhid_ref, mine_ref, theirs_ref):
-    join(at, near_ref, far_ref, dm_ref)
+def ffn_back_body(dm_ref, slope_ref, down_ref, up_ref, dhid_ref, mine_ref, theirs_ref):
     du = mul(dm_ref[...], down_ref[...], 1, 0)
     dhid_ref[...] = (du * slope_ref[...].astype(jnp.float32)).astype(jnp.bfloat16)
-    split_rows(at, lambda rows: mul(dhid_ref[rows, :], up_ref[...], 1, 1), mine_ref, theirs_ref)
-
-
-def deal(at, grad, own_ref, away_ref, scr):
-    shard = own_ref.shape[1]
-    scr[...] = grad
-    x = at[1]
-    for i in range(own_ref.shape[0]):
-        away_ref[i] = scr[pl.ds((2 * i + 1 - x) * shard, shard), :].astype(away_ref.dtype)
-        own_ref[i] = scr[pl.ds((2 * i + x) * shard, shard), :].astype(own_ref.dtype)
-
-
-def grad_body(at, left_ref, right_ref, own_ref, away_ref, scr):
-    deal(at, mul(left_ref[...], right_ref[...], 0, 0), own_ref, away_ref, scr)
-
-
-def norm_one_back_body(at, dz2_ref, d_ref, far_ref, n_ref, r_ref, vec_ref, grad2_ref, dz_ref, low_ref, grad_ref):
+    split_rows(lambda rows: mul(dhid_ref[rows, :], up_ref[...], 1, 1), mine_ref, theirs_ref)
+
+
+def deal(own_ref, away_ref, scr, order, start=0):
+    one, two, three = order
+    shard, width = own_ref.shape[1:]
+    dp = lax.axis_index("dp")
+    for i, bits in enumerate((0, three, two, two ^ three)):
+        for ref, owner in ((own_ref, dp ^ bits), (away_ref, dp ^ bits ^ one)):
+            part = scr[pl.ds(pl.multiple_of(owner * shard, 32), shard), start : start + width]
+            ref[i] = part.astype(ref.dtype)
+
+
+def grad_body(order, left_ref, right_ref, own_ref, away_ref, scr):
+    scr[...] = mul(left_ref[...], right_ref[...], 0, 0)
+    deal(own_ref, away_ref, scr, order)
+
+
+def fold_pair(own_ref, got_ref, keep_ref, send_ref):
+    half = keep_ref.shape[0]
+    keep_ref[...] = own_ref[0:half] + got_ref[0:half].astype(jnp.float32)
+    send_ref[...] = (own_ref[half:] + got_ref[half:].astype(jnp.float32)).astype(jnp.bfloat16)
+
+
+def fold_body(own_ref, got_ref, keep_ref, send_ref):
+    fold_pair(own_ref, got_ref, keep_ref, send_ref)
+
+
+def fold_two_body(own_ref, got_ref, own2_ref, got2_ref, keep_ref, send_ref, keep2_ref, send2_ref):
+    fold_pair(own_ref, got_ref, keep_ref, send_ref)
+    fold_pair(own2_ref, got2_ref, keep2_ref, send2_ref)
+
+
+def fold_join_body(own_ref, got_ref, own2_ref, got2_ref, keep_ref, send_ref):
+    width = own_ref.shape[2]
+    for own, got, lanes in ((own_ref, got_ref, slice(0, width)), (own2_ref, got2_ref, slice(width, keep_ref.shape[2]))):
+        keep_ref[0, :, lanes] = own[0] + got[0].astype(jnp.float32)
+        send_ref[0, :, lanes] = (own[1] + got[1].astype(jnp.float32)).astype(jnp.bfloat16)
+
+
+def fold_last_body(own_ref, got_ref, sum_ref):
+    sum_ref[...] = (own_ref[0] + got_ref[0].astype(jnp.float32)).astype(jnp.bfloat16)
+
+
+def norm_one_back_body(dz2_ref, d_ref, far_ref, n_ref, r_ref, vec_ref, grad2_ref, dz_ref, low_ref):
     dy = dz2_ref[...] + (d_ref[...].astype(jnp.float32) + far_ref[...].astype(jnp.float32))
     n = n_ref[...]
     dz = norm_back(dy * vec_ref[0:1, :], n, r_ref[:, 0:1])
     dz_ref[...] = dz
-    low_ref[...] = dz.astype(jnp.bfloat16)
-    grad_ref[...] = grad2_ref[...]
-    grad_ref[0:1, :] = jnp.sum(dy * n, axis=0, keepdims=True)
-    grad_ref[2:3, :] = jnp.sum(dy, axis=0, keepdims=True)
+    half = dz.shape[0]
+    low_ref[0:half, :] = dz.astype(jnp.bfloat16)
+    sums = [
+        jnp.sum(dy * n, axis=0, keepdims=True), grad2_ref[1:2, :],
+        jnp.sum(dy, axis=0, keepdims=True), grad2_ref[3:4, :], jnp.zeros((12, dz.shape[1]), jnp.float32),
+    ]
+    low_ref[half : half + 16, :] = jnp.concatenate(sums, axis=0).astype(jnp.bfloat16)
 
 
 def attend_back_body(
-    at, near_ref, far_ref, w_out_ref, w_ref, qkv_ref, o_ref, lse_ref, bias_ref, x_ref, vec_ref, vec_far_ref,
-    own_ref, away_ref, own_o_ref, away_o_ref, mine_ref, theirs_ref,
-    da_scr, p_scr, dr_scr, q_scr, do_scr, all_scr, grad_scr, grad_o_scr,
+    da_ref, w_out_ref, w_ref, qkv_ref, o_ref, lse_ref, bias_ref, x_ref,
+    own_ref, away_ref, own2_ref, away2_ref, mine_ref, theirs_ref,
+    p_scr, dr_scr, q_scr, do_scr, all_scr, grad_scr,
 ):
     width = o_ref.shape[1]
     rows = x_ref.shape[0]
     scale = 1.0 / math.sqrt(HD)
-    join(at, near_ref, far_ref, da_scr)
-    da = da_scr[...]
-    deal(at, mul(da, o_ref[...], 0, 0), own_o_ref, away_o_ref, grad_o_scr)
+    half = rows // 2
+    da = jnp.concatenate([da_ref[0, 0:half, :], da_ref[1, 0:half, :]], axis=0)
     do = mul(da, w_out_ref[...], 1, 0).astype(jnp.bfloat16)
     q, k, v = [qkv_ref[:, i * width : (i + 1) * width] for i in range(3)]
     blocks = bias_ref.shape[0] // (width // HD)
@@ -422,15 +510,46 @@
     all_scr[:, 0:width] = dq.astype(jnp.bfloat16)
     all_scr[:, width : 2 * width] = mul(dr_scr[...], q_scr[...], 1, 0).astype(jnp.bfloat16)
     all_scr[:, 2 * width : 3 * width] = mul(p_scr[...], do_scr[...], 1, 0).astype(jnp.bfloat16)
-    vec = (vec_ref[...] + vec_far_ref[...]).astype(jnp.bfloat16)
-    extra = grad_scr.shape[1] - 3 * width
+    vec = sum(da_ref[i, half : half + 16, :].astype(jnp.float32) for i in range(2)).astype(jnp.bfloat16)
+    extra = w_ref.shape[1] - 3 * width
     unit = (
-        lax.broadcasted_iota(jnp.int32, (8, extra), 0) == lax.broadcasted_iota(jnp.int32, (8, extra), 1)
+        lax.broadcasted_iota(jnp.int32, (16, extra), 0) == lax.broadcasted_iota(jnp.int32, (16, extra), 1)
     ).astype(jnp.bfloat16)
-    grad = jnp.concatenate([mul(x_ref[...], all_scr[...], 0, 0), mul(vec, unit, 0, 0)], axis=1)
-    deal(at, grad, own_ref, away_ref, grad_scr)
+    grad_scr[...] = jnp.concatenate(
+        [mul(x_ref[...], all_scr[...], 0, 0), mul(vec, unit, 0, 0), mul(da, o_ref[...], 0, 0)], axis=1
+    )
+    deal(own_ref, away_ref, grad_scr, (1, 2, 4))
+    deal(own2_ref, away2_ref, grad_scr, (2, 1, 4), own_ref.shape[2])
     w = w_ref[:, 0 : 3 * width]
-    split_rows(at, lambda r: mul(all_scr[r, :], w, 1, 1), mine_ref, theirs_ref)
+    split_rows(lambda r: mul(all_scr[r, :], w, 1, 1), mine_ref, theirs_ref)
+
+
+def fold_input_body(mine_ref, both_ref, dz_ref, keep_ref, send_ref):
+    part = keep_ref.shape[0]
+    c, far = lax.axis_index("ctx"), 1 - lax.axis_index("tp")
+    own, other = pl.ds(c * part, part), pl.ds((1 - c) * part, part)
+    send_ref[...] = (mine_ref[other, :] + both_ref[far, other, :].astype(jnp.float32)).astype(jnp.bfloat16)
+    keep_ref[...] = dz_ref[own, :] + (mine_ref[own, :] + both_ref[far, own, :].astype(jnp.float32))
+
+
+def last_input_body(keep_ref, got_ref, out_ref):
+    out_ref[...] = (keep_ref[...] + got_ref[...].astype(jnp.float32)).astype(jnp.bfloat16)
+
+
+def finish_body(near_ref, far_ref, qkv_ref, out_ref, gain_ref, bias_ref):
+    c = lax.axis_index("ctx")
+    n = qkv_ref.shape[2] // 2
+    m = out_ref.shape[1] // 2
+    near, far = near_ref[...].astype(jnp.float32), far_ref[...].astype(jnp.float32)
+    low, high = jnp.where(c == 0, near, far), jnp.where(c == 0, far, near)
+    for i in range(3):
+        qkv_ref[i] = jnp.concatenate([low[:, i * n : (i + 1) * n], high[:, i * n : (i + 1) * n]], axis=1)
+    out_ref[...] = jnp.concatenate([low[:, low.shape[1] - m :], high[:, high.shape[1] - m :]], axis=1)
+    vec = near_ref[:, 3 * n : near_ref.shape[1] - m]
+    row = lax.broadcasted_iota(jnp.int32, (2, vec.shape[1]), 0)
+    lane = lax.broadcasted_iota(jnp.int32, (2, vec.shape[1]), 1)
+    gain_ref[...] = mul((row == lane).astype(jnp.bfloat16), vec, 1, 1)
+    bias_ref[...] = mul((row + 2 == lane).astype(jnp.bfloat16), vec, 1, 1)
 
 
 def rows_device(
@@ -448,47 +567,27 @@
 ):
     n_dp = dims["dp"]
     n_out = n_dp // 2
-    dp = lax.axis_index("dp")
     c = lax.axis_index("ctx")
-    t = lax.axis_index("tp")
-    z = dp // 2
-    x = dp % 2
-    at = jnp.stack([z, x, c, t]).astype(jnp.int32)
     f32, bf16 = jnp.float32, jnp.bfloat16
     pair = [(0, 1), (1, 0)]
-    across_x = [(i, i ^ 1) for i in range(n_dp)]
-
-    def across_z(s):
-        return [(i, ((i // 2 + s) % n_out) * 2 + i % 2) for i in range(n_dp)]
-
-    def swap_tp(v):
-        return lax.ppermute(v, "tp", pair)
+
+    def both_tp(v, tiled=False):
+        return lax.all_gather(v, "tp", axis=0, tiled=tiled)
 
     def swap_ctx(v):
         return lax.ppermute(v, "ctx", pair)
 
-    def gather_dp(v):
-        near = [v] + [lax.ppermute(v, "dp", across_z(s)) for s in range(1, n_out)]
-        order = [0] + [n_out - s for s in range(1, n_out)]
-        first = lax.ppermute(v, "dp", across_x)
-        near = jnp.stack([near[s] for s in order])
-        rest = lax.ppermute(near[1:], "dp", across_x)
-        far = jnp.concatenate([first[None], rest])
-        both = jnp.stack([jnp.where(x == 0, near, far), jnp.where(x == 0, far, near)], axis=1)
-        both = jnp.roll(both, z, axis=0)
-        return both.reshape(n_dp * v.shape[0], v.shape[1])
-
-    def scatter_dp(own, away):
-        half = (own.astype(f32) + lax.ppermute(away, "dp", across_x).astype(f32)).astype(bf16)
-        total = lax.dynamic_index_in_dim(half, z, 0, False).astype(f32)
-        for s in range(1, n_out):
-            piece = lax.dynamic_index_in_dim(half, (z + s) % n_out, 0, False)
-            total = total + lax.ppermute(piece, "dp", across_z(s)).astype(f32)
-        return total.astype(bf16)
-
-    rows = inputs.shape[0]
+    def swap_dp(v, bits):
+        return lax.ppermute(v, "dp", [(i, i ^ bits) for i in range(n_dp)])
+
+    def after(v, *others):
+        return lax.optimization_barrier((v,) + others)[0]
+
+    def all_after(vs, *others):
+        return list(lax.optimization_barrier(tuple(vs) + others)[: len(vs)])
+
+    rows, width = inputs.shape
     part = rows // 2
-    width = inputs.shape[1]
     shard = qkv_weight.shape[1]
     cols = qkv_weight.shape[2] // 2
     units = up_weight.shape[1] // 2
@@ -496,34 +595,40 @@
     own_blocks = rows // BLOCK
     per = own_blocks // 2
     total_rows = 2 * rows
-    pad = -(3 * cols + 4) % 128
-
-    def own_cols(w):
-        n = w.shape[-1] // 2
-        return lax.dynamic_slice_in_dim(w, c * n, n, w.ndim - 1)
-
-    small = jnp.concatenate([norm_gains, norm_biases], axis=0)
-    w1 = jnp.concatenate([own_cols(qkv_weight[i]) for i in range(3)] + [jnp.pad(small.T, ((0, 0), (0, pad)))], axis=1)
-    w_out_t = own_cols(out_weight.T)
-    w_up = own_cols(up_weight)
-    w_down_t = own_cols(down_weight.T)
-    w1 = gather_dp(w1)
-    w_out_t = gather_dp(w_out_t)
-    w_up = gather_dp(w_up)
-    w_down_t = gather_dp(w_down_t)
-
-    halves = inputs.reshape(2, part, width)
-    near = swap_ctx(lax.dynamic_index_in_dim(halves, t, 0, False))
-    far = swap_tp(near)
-    other = jnp.where(t == 0, jnp.stack([near, far]), jnp.stack([far, near]))
-    x_all = jnp.where(c == 0, jnp.stack([halves, other], 1), jnp.stack([other, halves], 1)).reshape(total_rows, width)
-    e_far = swap_ctx(lax.dynamic_index_in_dim(out_grad.reshape(2, part, width), t, 0, False))
-
-    picks = random_blocks.reshape(own_blocks, 2, heads, 3)
-    picks_own = lax.dynamic_index_in_dim(picks, c, 1, False)
-    picks_far = swap_ctx(lax.dynamic_index_in_dim(picks, 1 - c, 1, False))
-    picks = jnp.where(c == 0, jnp.stack([picks_own, picks_far]), jnp.stack([picks_far, picks_own]))
-    picks = picks.reshape(2 * own_blocks, heads, 3)
+    first = 3 * cols + 4 + (-(3 * cols + 4)) % 128
+
+    half = ((part, width), bf16)
+    hbm = pl.BlockSpec(memory_space=pltpu.HBM)
+
+    def packed(body, widths, *given):
+        return call(
+            body, [((shard, n), bf16) for n in widths], *given,
+            scratch=[(w.shape, bf16) for w in given], copies=len(given), spec=hbm, room=60,
+        )
+
+    def near_of(v):
+        return [v] + [swap_dp(v, 2 * k) for k in range(1, n_out)]
+
+    def far_rest(near):
+        return swap_dp(jnp.stack(near), 1)
+
+    x_far = swap_ctx(inputs)
+    w1, w_out, pack_one = packed(
+        pack_first_body, (first, cols, first + cols), qkv_weight, norm_gains, norm_biases, out_weight.T
+    )
+    w1_near = near_of(w1)
+    far_one = swap_dp(pack_one, 1)
+    w_up, w_down, pack_two = packed(pack_second_body, (units, units, 2 * units), up_weight, down_weight.T)
+    picks_far = swap_ctx(random_blocks)
+    w1_pieces = w1_near + [far_one, swap_dp(after(w1_near[1], far_one), 1), far_rest(w1_near[2:])]
+    out_near = near_of(after(w_out, *w1_near[1:]))
+    out_pieces = out_near + [far_one, far_rest(out_near[1:])]
+    up_near = near_of(after(w_up, *w1_near[1:]))
+    far_two = swap_dp(after(pack_two, *w1_near[1:]), 1)
+    e_far = swap_ctx(after(out_grad, x_far))
+
+    picks = jnp.where(c == 0, jnp.stack([random_blocks, picks_far]), jnp.stack([picks_far, random_blocks]))
+    picks = lax.dynamic_slice_in_dim(picks.reshape(2 * own_blocks, 2 * heads, 3), c * heads, heads, 1)
     blocks = jnp.arange(2 * own_blocks, dtype=jnp.int32)
     table, usable = block_table(blocks, lengths[0], picks)
     named = (table[..., None] == blocks) & usable[:, None, :, None]
@@ -535,97 +640,121 @@
 
     low = [((rows, width), bf16)]
     wide = [((rows, width), f32)]
-    o, qkv, lse, vecs = call(
+    small = [((8, width), f32)]
+    o, qkv, lse, vecs, x_all, w1_all = call(
         attend_body,
-        [((total_rows, cols), bf16), ((total_rows, 3 * cols), bf16), ((8, total_rows), f32), ((8, width), f32)],
-        at, x_all, w1, bias,
+        [
+            ((total_rows, cols), bf16), ((total_rows, 3 * cols), bf16), ((8, total_rows), f32), ((8, width), f32),
+            ((total_rows, width), bf16), ((width, first), bf16),
+        ],
+        inputs, after(x_far, e_far), *w1_pieces, bias,
         scratch=[((heads * total_rows, total_rows), bf16), ((heads * total_rows, cols), bf16)],
-        flops=10**9,
-    )
-
-    def sum_row(mine, theirs):
-        s = (mine + swap_tp(theirs).astype(f32)).astype(bf16)
-        return s, swap_ctx(s)
-
-    a, a_far = sum_row(*call(project_body, wide + low, at, o, w_out_t))
-    n1, r1, y_low = call(norm_one_body, wide + [((rows, 128), f32)] + low, at, x_all, a, a_far, vecs)
+        flops=2 * 10**10,
+    )
+
+    def sum_tp(mine, theirs):
+        return call(add_tp_body, low, mine, both_tp(theirs))[0]
+
+    mine, theirs, w_out_all = call(functools.partial(project_body, first), wide + low + [((width, cols), bf16)], o, *out_pieces)
+    a = after(sum_tp(mine, theirs), *up_near[1:])
+    a_far = swap_ctx(a)
+    up_near = up_near[:1] + all_after(up_near[1:], a)
+    up_pieces = up_near + [far_two, far_rest(up_near[1:])]
+    down_near = near_of(after(w_down, a))
+    n1, r1, y_low = call(norm_one_body, wide + [((rows, 128), f32)] + low, x_all, a, a_far, vecs)
     flat = [((total_rows, units), bf16)]
-    y_all, u, slope, mine, theirs = call(
-        ffn_body, [((total_rows, width), bf16)] + flat * 2 + wide + low, at, y_low, swap_tp(y_low), w_up, w_down_t,
-        flops=10**9,
-    )
-    m, m_far = sum_row(mine, theirs)
+    square = [((width, units), bf16)]
+    y_all = both_tp(y_low, True)
+    down_near = down_near[:1] + all_after(down_near[1:], y_all)
+    down_pieces = down_near + [far_two, far_rest(down_near[1:])]
+    u, slope, w_up_all = call(functools.partial(ffn_body, 0), flat * 2 + square, y_all, *up_pieces)
+    mine, theirs, w_down_all = call(functools.partial(project_body, units), wide + low + square, u, *down_pieces)
+    m = sum_tp(mine, theirs)
+    m_far = swap_ctx(m)
     out, dz2, dm_low, grad2 = call(
         norm_two_body,
-        [((part, width), bf16)] + wide + low + [((8, width), f32)],
-        at, n1, m, m_far, out_grad, e_far, vecs,
+        [((part, width), bf16)] + wide + low + small,
+        n1, m, m_far, out_grad, e_far, vecs,
         scratch=wide * 2,
     )
-    dm_all, dhid, mine, theirs = call(
-        ffn_back_body, [((total_rows, width), bf16)] + flat + wide + low,
-        at, dm_low, swap_tp(dm_low), slope, w_down_t, w_up,
-        flops=10**9,
-    )
-    d, d_far = sum_row(mine, theirs)
 
     def dealt(n):
         return [((n_out, shard, n), f32), ((n_out, shard, n), bf16)]
 
-    down_own, down_away = call(grad_body, dealt(units), at, dm_all, u, scratch=[((width, units), f32)])
-    up_own, up_away = call(grad_body, dealt(units), at, y_all, dhid, scratch=[((width, units), f32)])
-    dz1, da_low, grad1 = call(
-        norm_one_back_body, wide + low + [((8, width), f32)], at, dz2, d, d_far, n1, r1, vecs, grad2
-    )
-    qkv_own, qkv_away, o_own, o_away, mine, theirs = call(
+    def kept(k, n):
+        return [((k, shard, n), f32), ((k, shard, n), bf16)]
+
+    def fold(own, got):
+        return call(fold_body, kept(own.shape[0] // 2, own.shape[2]), own, got)
+
+    def last_sum(keep, send, bits):
+        total = call(fold_last_body, [(keep.shape[1:], bf16)], keep, swap_dp(send, bits))[0]
+        return total, swap_ctx(total)
+
+    down_order, up_order = (2, 1, 4), (1, 2, 4)
+    dm_all = both_tp(dm_low, True)
+    down_own, down_away = call(functools.partial(grad_body, down_order), dealt(units), dm_all, u, scratch=[((width, units), f32)])
+    dm_all = after(dm_all, down_away)
+    dhid, mine, theirs = call(
+        ffn_back_body, flat + wide + low, dm_all, slope, w_down_all, w_up_all
+    )
+    d = sum_tp(mine, theirs)
+    d_far = swap_ctx(d)
+    y_late, dhid = lax.optimization_barrier((y_all, dhid, d))[:2]
+    up_own, up_away = call(functools.partial(grad_body, up_order), dealt(units), y_late, dhid, scratch=[((width, units), f32)])
+    dz1, da_low = call(
+        norm_one_back_body, wide + [((rows + 16, width), bf16)], dz2, d, after(d_far, up_away), n1, r1, vecs, grad2
+    )
+    down_keep, down_send = fold(down_own, swap_dp(down_away, down_order[0]))
+    last = first + cols
+    left = last // 256 * 128
+    own, away, own2, away2, mine, theirs = call(
         attend_back_body,
-        dealt(w1.shape[1]) + dealt(cols) + wide + low,
-        at, da_low, swap_tp(da_low), w_out_t, w1, qkv, o, lse, bias, x_all, grad1, swap_tp(grad1),
+        dealt(left) + dealt(last - left) + wide + low,
+        after(both_tp(da_low), down_send), w_out_all, w1_all, qkv, o, lse, bias, x_all,
         scratch=[
-            ((total_rows, width), bf16),
             ((total_rows, heads * total_rows), bf16),
             ((total_rows, heads * total_rows), bf16),
             ((heads * total_rows, cols), bf16),
             ((heads * total_rows, cols), bf16),
             ((total_rows, 3 * cols), bf16),
-            ((width, w1.shape[1]), f32),
-            ((width, cols), f32),
+            ((width, last), f32),
         ],
-        flops=2 * 10**9,
-    )
-    dx = (mine + swap_tp(theirs).astype(f32)).astype(bf16).reshape(2, part, width)
-    dx_own = lax.dynamic_index_in_dim(dx, c, 0, False).astype(f32)
-    dx_far = swap_ctx(lax.dynamic_index_in_dim(dx, 1 - c, 0, False)).astype(f32)
-    dz1_own = lax.dynamic_index_in_dim(dz1.reshape(2, part, width), c, 0, False)
-    dx = (dz1_own + dx_own + dx_far).astype(bf16)
-
-    def both_tp(near):
-        far = swap_tp(near)
-        return jnp.where(t == 0, jnp.concatenate([near, far]), jnp.concatenate([far, near]))
-
-    output = both_tp(out)
-    input_grad = both_tp(dx)
-
-    def both_ctx(g):
-        far = swap_ctx(g)
-        return jnp.where(c == 0, jnp.concatenate([g, far], 1), jnp.concatenate([far, g], 1))
-
-    grad_down = both_ctx(scatter_dp(down_own, down_away)).astype(f32).T
-    grad_up = both_ctx(scatter_dp(up_own, up_away)).astype(f32)
-    grad_out = both_ctx(scatter_dp(o_own, o_away)).astype(f32).T
-    grad_1 = scatter_dp(qkv_own, qkv_away)
-    far_1 = swap_ctx(grad_1)
-    lo = jnp.where(c == 0, grad_1, far_1).astype(f32)
-    hi = jnp.where(c == 0, far_1, grad_1).astype(f32)
-    grad_qkv = jnp.stack(
-        [jnp.concatenate([lo[:, i * cols : (i + 1) * cols], hi[:, i * cols : (i + 1) * cols]], 1) for i in range(3)]
-    )
-    vec = grad_1[:, 3 * cols : 3 * cols + 4].astype(f32).T
-    return (output, input_grad, grad_qkv, grad_out, grad_up, grad_down, vec[:2], vec[2:])
+    )
+    up_own = after(up_own, theirs)
+    keep, send = call(fold_input_body, [((part, width), f32), half], mine, both_tp(theirs), dz1)
+    up_keep, up_send = fold(up_own, swap_dp(up_away, up_order[0]))
+    down_keep, down_send = fold(down_keep, swap_dp(down_send, down_order[1]))
+    keep1, send1, keep2, send2 = call(
+        fold_two_body, kept(2, left) + kept(2, last - left),
+        own, swap_dp(away, 1), own2, swap_dp(away2, 2),
+    )
+    up_keep, up_send = fold(up_keep, swap_dp(up_send, up_order[1]))
+    keep1, send1 = call(
+        fold_join_body, kept(1, last), keep1, swap_dp(send1, 2), keep2, swap_dp(send2, 1)
+    )
+    grad_down, down_far = last_sum(down_keep, down_send, 4)
+    grad_up, up_far = last_sum(up_keep, up_send, 4)
+    grad_1, far_1 = last_sum(keep1, send1, 4)
+    dx = call(last_input_body, [half], keep, swap_ctx(send))[0]
+    output, input_grad = both_tp(out, True), both_tp(dx, True)
+
+    def both_ctx(g, far):
+        return jnp.where(c == 0, jnp.concatenate([g, far], 1), jnp.concatenate([far, g], 1)).astype(f32)
+
+    grad_qkv, grad_out, gains, biases = call(
+        finish_body,
+        [((3, shard, 2 * cols), f32), ((shard, 2 * cols), f32), ((2, shard), f32), ((2, shard), f32)],
+        grad_1, far_1,
+    )
+    return (
+        output, input_grad, grad_qkv, grad_out.T, both_ctx(grad_up, up_far), both_ctx(grad_down, down_far).T, gains, biases
+    )
 
 
 def solution(mesh):
     dims = dict(mesh.shape)
-    fast = dims["ctx"] == 2 and dims["tp"] == 2 and dims["dp"] % 2 == 0
+    fast = dims["ctx"] == 2 and dims["tp"] == 2 and dims["dp"] == 8
     step = functools.partial(rows_device, dims) if fast else per_device
     return jax.shard_map(
         step,

time: 220 us -> 172 us (0.78)
  blocking collectives: 0 us -> 21.1 us
  waiting for transfers between devices: 91.1 us -> 70 us
  starting transfers between devices: 71.3 us -> 50.7 us
  other arithmetic: 15 us -> 3.24 us
  local copies, waits for them, and re-layouts: 13.9 us -> 2.88 us
  Pallas kernels: 26.4 us -> 21.8 us
    ppermute x47 -> x30, waiting for transfers between devices: 73.7 us -> 46.5 us  [swap_dp(): return lax.ppermute(v, 'dp', [(i, i ^ bits) for i in range(n_dp)])]
    all_gather x0 -> x9, blocking collectives: none -> 21.1 us  [both_tp(): return lax.all_gather(v, 'tp', axis=0, tiled=tiled)]
    ppermute x47 -> x30, starting transfers between devices: 59.1 us -> 40.9 us  [swap_dp(): return lax.ppermute(v, 'dp', [(i, i ^ bits) for i in range(n_dp)])]
    unnamed x55 -> x16, local copies, waits for them, and re-layouts: 7.84 us -> 1.76 us
    ppermute x11 -> x10, waiting for transfers between devices: 17.4 us -> 23.5 us  [swap_ctx(): return lax.ppermute(v, 'ctx', pair)]
    pallas_call x10 -> x28, Pallas kernels: 26.4 us -> 21.8 us  [call(): pl.pallas_call(body, out_shape=shapes, in_specs=specs, out_specs=[pl.Bloc...]
    convert_element_type x15 -> x1, other arithmetic: 4.2 us -> 0.92 us  [both_ctx(): jnp.where(c == 0, jnp.concatenate([g, far], 1), jnp.concatenate([far, g],...]
    concatenate x4 -> x0, other arithmetic: 2.95 us -> none  [the longest x3 2.21 us: gather_dp(): both = jnp.roll(both, z, axis=0)]
  transfers between devices with their start and end apart: 58 -> 40, of which waited for: 24 -> 16; matrix products, arithmetic and copies ran while one was open for 9% -> 3% of each run, Pallas kernels for 8% -> 9%
where the time goes in v3:
time: 172 us; the launch traced here: 171 us
  waiting for transfers between devices  70 us (41%)
  starting transfers between devices  50.7 us (29%)
  Pallas kernels  21.8 us (13%)
  blocking collectives  21.1 us (12%)
  other arithmetic  3.24 us (2%)
  local copies, waits for them, and re-layouts  2.88 us (2%)
    ppermute x30, waiting for transfers between devices, swap_dp(): return lax.ppermute(v, 'dp', [(i, i ^ bits) for i in range(n_dp)])  46.5 us
    ppermute x30, starting transfers between devices, swap_dp(): return lax.ppermute(v, 'dp', [(i, i ^ bits) for i in range(n_dp)])  40.9 us
    ppermute x10, waiting for transfers between devices, swap_ctx(): return lax.ppermute(v, 'ctx', pair)  23.5 us
    pallas_call x28, Pallas kernels, call(): pl.pallas_call(body, out_shape=shapes, in_specs=specs, out_specs=[pl.Bloc...  21.8 us
    all_gather x9, blocking collectives, both_tp(): return lax.all_gather(v, 'tp', axis=0, tiled=tiled)  21.1 us
    ppermute x10, starting transfers between devices, swap_ctx(): return lax.ppermute(v, 'ctx', pair)  9.81 us
  transfers between devices with their start and end apart: 40, of which 16 were waited for; matrix products, arithmetic and copies ran while one was open for 3% of the time, Pallas kernels for 9%

profile of v3, /device:TPU:0, one launch (start us, length us, event | category | flops | bytes accessed | tf_op | source)
XLA Modules:
  0.0 171.4 jit_solution(3826912796228832189)
XLA Ops:
  0.6 2.1 %shard_map.161 = (bf16[96,640]{1,0:T(8,128)(2,1)}, bf16[96,192]{1,0:T(8,128)(2,1)}, bf16[96,832]{1,0:T(8,128)(2,1)}) custom-call(bf16[3,96,384]{2,1,0:T(8,128)(2,1)} %qkv_hbm.1, bf16[2,96]{1,0:T(2,128)(2,1)} %gain_hbm.1, bf16[2,96]{1,0:T(2,128)(2,1)} %bias_hbm.1, bf16[96,384]{1,0:T(8,128)(2,1)} %bitcast.50), custom_call_target="tpu_custom_call" | custom-call | tf_op jit(solution)/shard_map/pallas_call | solution.py:240
  2.8 4.1 %collective-permute-start.3 = (bf16[96,640]{1,0:T(8,128)(2,1)}, bf16[96,640]{1,0:T(8,128)(2,1)S(1)}, u32[]{:S(2)}, u32[]{:S(2)}) collective-permute-start(bf16[96,640]{1,0:T(8,128)(2,1)} %get-tuple-element.93.w0), channel_id=1, source_target_pairs={{0,16},{4,20},{8,24},{12,28},{16,0},{20,4},{24,8},{28,12},{1,17},{... | collective-permute-start | bytes 368648 | tf_op jit(solution)/shard_map/ppermute | solution.py:581
  12.2 1.9 %shard_map.165 = (bf16[96,768]{1,0:T(8,128)(2,1)}, bf16[96,768]{1,0:T(8,128)(2,1)}, bf16[96,1536]{1,0:T(8,128)(2,1)}) custom-call(bf16[96,1536]{1,0:T(8,128)(2,1)} %up_hbm.1, bf16[96,1536]{1,0:T(8,128)(2,1)} %bitcast.48), custom_call_target="tpu_custom_call" | custom-call | tf_op jit(solution)/shard_map/pallas_call | solution.py:240
  17.1 3.5 %collective-permute-start.11 = (bf16[96,192]{1,0:T(8,128)(2,1)}, bf16[96,192]{1,0:T(8,128)(2,1)S(1)}, u32[]{:S(2)}, u32[]{:S(2)}) collective-permute-start(bf16[96,192]{1,0:T(8,128)(2,1)} %get-tuple-element.99.w0), channel_id=1, source_target_pairs={{0,24},{4,28},{8,16},{12,20},{16,8},{20,12},{24,0},{28,4},{1,25},{... | collective-permute-start | bytes 110600 | tf_op jit(solution)/shard_map/ppermute | solution.py:581
  21.6 2.7 %collective-permute-done.far_ref = bf16[256,768]{1,0:T(8,128)(2,1)S(1)} collective-permute-done((bf16[256,768]{1,0:T(8,128)(2,1)}, bf16[256,768]{1,0:T(8,128)(2,1)S(1)}, u32[]{:S(2)}, u32[]{:S(2)}) %collective-permute-start) | collective-permute-done | bytes 393248 | tf_op jit(solution)/shard_map/ppermute | solution.py:578
  27.8 1.6 collective-permute-start.13
  29.4 1.7 collective-permute-start.14
  31.1 2.0 %collective-permute-done.1.e_far_ref = bf16[256,768]{1,0:T(8,128)(2,1)S(1)} collective-permute-done((bf16[256,768]{1,0:T(8,128)(2,1)S(1)}, bf16[256,768]{1,0:T(8,128)(2,1)S(1)}, u32[]{:S(2)}, u32[]{:S(2)}) %collective-permute-start.1) | collective-permute-done | bytes 393248 | tf_op jit(solution)/shard_map/ppermute | solution.py:578
  33.1 2.4 %collective-permute-start.15 = (bf16[96,768]{1,0:T(8,128)(2,1)S(1)}, bf16[96,768]{1,0:T(8,128)(2,1)S(1)}, u32[]{:S(2)}, u32[]{:S(2)}) collective-permute-start(bf16[96,768]{1,0:T(8,128)(2,1)S(1)} %copy-done.2), channel_id=1, source_target_pairs={{0,24},{4,28},{8,16},{12,20},{16,8},{20,12},{24,0},{28,4},{1,25},{... | collective-permute-start | bytes 442376 | tf_op jit(solution)/shard_map/ppermute | solution.py:581
  36.0 2.8 %shard_map.162 = (bf16[512,192]{1,0:T(8,128)(2,1)S(1)}, bf16[512,576]{1,0:T(8,128)(2,1)S(1)}, f32[8,512]{1,0:T(8,128)S(1)}, f32[8,768]{1,0:T(8,128)S(1)}, bf16[5...) custom-call(bf16[256,768]{1,0:T(8,128)(2,1)S(1)} %copy-done.4, bf16[256,768]{1,0:T(8,128)(2,1)S(1)} %collective-permute-done.far_ref, ...), custom_call_target="tpu_custom_call" | custom-call | flops 20000000000 | tf_op jit(solution)/shard_map/pallas_call | solution.py:240
  38.8 1.8 %collective-permute-done.12.w5 = bf16[3,96,192]{2,1,0:T(8,128)(2,1)S(1)} collective-permute-done((bf16[3,96,192]{2,1,0:T(8,128)(2,1)S(1)}, bf16[3,96,192]{2,1,0:T(8,128)(2,1)S(1)}, u32[]{:S(2)}, u32[]{:S(2)}) %collective-permute-start.12) | collective-permute-done | bytes 110624 | tf_op jit(solution)/shard_map/ppermute | solution.py:581
  41.0 2.4 %all-gather = bf16[512,768]{1,0:T(8,128)(2,1)S(1)} all-gather(bf16[256,768]{1,0:T(8,128)(2,1)S(1)} %get-tuple-element.101), channel_id=2, replica_groups=mesh['dp'=8,'ctx'=2,'tp'=2] {'tp'}, dimensions={0}, use_global_device_ids=true | all-gather | bytes 1179648 | tf_op jit(solution)/shard_map/all_gather | solution.py:575
  46.3 2.4 %collective-permute-start.21 = (bf16[96,768]{1,0:T(8,128)(2,1)S(1)}, bf16[96,768]{1,0:T(8,128)(2,1)S(1)}, u32[]{:S(2)}, u32[]{:S(2)}) collective-permute-start(bf16[96,768]{1,0:T(8,128)(2,1)S(1)} %copy-done.1), channel_id=1, source_target_pairs={{0,24},{4,28},{8,16},{12,20},{16,8},{20,12},{24,0},{28,4},{1,25},{... | collective-permute-start | bytes 442376 | tf_op jit(solution)/shard_map/ppermute | solution.py:581
  50.1 4.7 %collective-permute-done.16.far_ref = bf16[256,768]{1,0:T(8,128)(2,1)S(1)} collective-permute-done((bf16[256,768]{1,0:T(8,128)(2,1)S(1)}, bf16[256,768]{1,0:T(8,128)(2,1)S(1)}, u32[]{:S(2)}, u32[]{:S(2)}) %collective-permute-start.16) | collective-permute-done | bytes 393248 | tf_op jit(solution)/shard_map/ppermute | solution.py:578
  55.1 2.5 %all_gather.44.y_ref.left_ref = bf16[512,768]{1,0:T(8,128)(2,1)S(1)} all-gather(bf16[256,768]{1,0:T(8,128)(2,1)S(1)} %get-tuple-element.107), channel_id=1, replica_groups=mesh['dp'=8,'ctx'=2,'tp'=2] {'tp'}, dimensions={0}, use_global_device_ids=true | all-gather | bytes 1179648 | tf_op jit(solution)/shard_map/all_gather | solution.py:575
  60.9 15.4 %collective-permute-done.17.w4 = bf16[96,1536]{1,0:T(8,128)(2,1)S(1)} collective-permute-done((bf16[96,1536]{1,0:T(8,128)(2,1)S(1)}, bf16[96,1536]{1,0:T(8,128)(2,1)S(1)}, u32[]{:S(2)}, u32[]{:S(2)}) %collective-permute-start.17) | collective-permute-done | bytes 294944 | tf_op jit(solution)/shard_map/ppermute | solution.py:581
  78.8 2.4 %all-gather.1 = bf16[512,768]{1,0:T(8,128)(2,1)S(1)} all-gather(bf16[256,768]{1,0:T(8,128)(2,1)S(1)} %get-tuple-element.120), channel_id=3, replica_groups=mesh['dp'=8,'ctx'=2,'tp'=2] {'tp'}, dimensions={0}, use_global_device_ids=true | all-gather | bytes 1179648 | tf_op jit(solution)/shard_map/all_gather | solution.py:575
  82.0 10.4 %collective-permute-done.23.far_ref = bf16[256,768]{1,0:T(8,128)(2,1)S(1)} collective-permute-done((bf16[256,768]{1,0:T(8,128)(2,1)S(1)}, bf16[256,768]{1,0:T(8,128)(2,1)S(1)}, u32[]{:S(2)}, u32[]{:S(2)}) %collective-permute-start.23) | collective-permute-done | bytes 393248 | tf_op jit(solution)/shard_map/ppermute | solution.py:578
  93.4 2.5 %all_gather.48.left_ref.dm_ref = bf16[512,768]{1,0:T(8,128)(2,1)S(1)} all-gather(bf16[256,768]{1,0:T(8,128)(2,1)S(1)} %get-tuple-element.123), channel_id=1, replica_groups=mesh['dp'=8,'ctx'=2,'tp'=2] {'tp'}, dimensions={0}, use_global_device_ids=true | all-gather | bytes 1179648 | tf_op jit(solution)/shard_map/all_gather | solution.py:575
  96.9 2.7 %collective-permute-start.25 = (bf16[4,96,768]{2,1,0:T(8,128)(2,1)S(1)}, bf16[4,96,768]{2,1,0:T(8,128)(2,1)S(1)}, u32[]{:S(2)}, u32[]{:S(2)}) collective-permute-start(bf16[4,96,768]{2,1,0:T(8,128)(2,1)S(1)} %get-tuple-element.124), channel_id=1, source_target_pairs={{0,8},{4,12},{8,0},{12,4},{16,24},{20,28},{24,16},{28,20},{1,9},{5... | collective-permute-start | bytes 1769480 | tf_op jit(solution)/shard_map/ppermute | solution.py:581
  99.5 1.8 %shard_map.172 = (bf16[512,768]{1,0:T(8,128)(2,1)S(1)}, f32[256,768]{1,0:T(8,128)S(1)}, bf16[256,768]{1,0:T(8,128)(2,1)S(1)}) custom-call(bf16[512,768]{1,0:T(8,128)(2,1)S(1)} %all_gather.48.left_ref.dm_ref, bf16[512,768]{1,0:T(8,128)(2,1)S(1)} %get-tuple-element.126.slope_ref, bf16[768,768]{1,0:T(8,128)(2,1)S(1)} %get-tuple-element.127.down_ref, ...), custom_call_target="tpu_custom_call" | custom-call | tf_op jit(solution)/shard_map/pallas_call | solution.py:240
  101.3 2.4 %all-gather.2 = bf16[512,768]{1,0:T(8,128)(2,1)S(1)} all-gather(bf16[256,768]{1,0:T(8,128)(2,1)S(1)} %get-tuple-element.130), channel_id=4, replica_groups=mesh['dp'=8,'ctx'=2,'tp'=2] {'tp'}, dimensions={0}, use_global_device_ids=true | all-gather | bytes 1179648 | tf_op jit(solution)/shard_map/all_gather | solution.py:575
  105.7 1.7 %collective-permute-start.33 = (bf16[4,96,768]{2,1,0:T(8,128)(2,1)S(1)}, bf16[4,96,768]{2,1,0:T(8,128)(2,1)S(1)}, u32[]{:S(2)}, u32[]{:S(2)}) collective-permute-start(bf16[4,96,768]{2,1,0:T(8,128)(2,1)S(1)} %get-tuple-element.134), channel_id=1, source_target_pairs={{0,4},{4,0},{8,12},{12,8},{16,20},{20,16},{24,28},{28,24},{1,5},{5... | collective-permute-start | bytes 1769480 | tf_op jit(solution)/shard_map/ppermute | solution.py:581
  107.5 5.7 %collective-permute-done.25.got_ref = bf16[4,96,768]{2,1,0:T(8,128)(2,1)S(1)} collective-permute-done((bf16[4,96,768]{2,1,0:T(8,128)(2,1)S(1)}, bf16[4,96,768]{2,1,0:T(8,128)(2,1)S(1)}, u32[]{:S(2)}, u32[]{:S(2)}) %collective-permute-start.25) | collective-permute-done | bytes 589856 | tf_op jit(solution)/shard_map/ppermute | solution.py:581
  115.5 2.4 %all-gather.3 = bf16[544,768]{1,0:T(8,128)(2,1)S(1)} all-gather(bf16[272,768]{1,0:T(8,128)(2,1)S(1)} %get-tuple-element.138), channel_id=5, replica_groups=mesh['dp'=8,'ctx'=2,'tp'=2] {'tp'}, dimensions={0}, use_global_device_ids=true | all-gather | bytes 1253376 | tf_op jit(solution)/shard_map/all_gather | solution.py:575
  117.9 4.7 %shard_map.177 = (f32[4,96,384]{2,1,0:T(8,128)S(1)}, bf16[4,96,384]{2,1,0:T(8,128)(2,1)S(1)}, f32[4,96,448]{2,1,0:T(8,128)S(1)}, bf16[4,96,448]{2,1,0:T(8,128)(2...) custom-call(bf16[2,272,768]{2,1,0:T(8,128)(2,1)S(1)} %bitcast.32, ...), custom_call_target="tpu_custom_call" | custom-call | tf_op jit(solution)/shard_map/pallas_call | solution.py:240
  127.4 2.4 %all-gather.4 = bf16[512,768]{1,0:T(8,128)(2,1)S(1)} all-gather(bf16[256,768]{1,0:T(8,128)(2,1)S(1)} %get-tuple-element.147), channel_id=6, replica_groups=mesh['dp'=8,'ctx'=2,'tp'=2] {'tp'}, dimensions={0}, use_global_device_ids=true | all-gather | bytes 1179648 | tf_op jit(solution)/shard_map/all_gather | solution.py:575
  131.1 12.2 %collective-permute-done.34.got_ref = bf16[2,96,768]{2,1,0:T(8,128)(2,1)S(1)} collective-permute-done((bf16[2,96,768]{2,1,0:T(8,128)(2,1)S(1)}, bf16[2,96,768]{2,1,0:T(8,128)(2,1)S(1)}, u32[]{:S(2)}, u32[]{:S(2)}) %collective-permute-start.34) | collective-permute-done | bytes 294944 | tf_op jit(solution)/shard_map/ppermute | solution.py:581
  147.4 2.1 %all_gather.47 = bf16[256,768]{1,0:T(8,128)(2,1)S(1)} all-gather(bf16[128,768]{1,0:T(8,128)(2,1)S(1)} %get-tuple-element.121), channel_id=1, replica_groups=mesh['dp'=8,'ctx'=2,'tp'=2] {'tp'}, dimensions={0}, use_global_device_ids=true | all-gather | bytes 589824 | tf_op jit(solution)/shard_map/all_gather | solution.py:575
  149.5 2.1 %all_gather.55 = bf16[256,768]{1,0:T(8,128)(2,1)S(1)} all-gather(bf16[128,768]{1,0:T(8,128)(2,1)S(1)} %shard_map.179), channel_id=1, replica_groups=mesh['dp'=8,'ctx'=2,'tp'=2] {'tp'}, dimensions={0}, use_global_device_ids=true | all-gather | bytes 589824 | tf_op jit(solution)/shard_map/all_gather | solution.py:575
  155.5 7.9 %collective-permute-done.31.got_ref = bf16[1,96,832]{2,1,0:T(8,128)(2,1)S(1)} collective-permute-done((bf16[1,96,832]{2,1,0:T(8,128)(2,1)S(1)}, bf16[1,96,832]{2,1,0:T(8,128)(2,1)S(1)}, u32[]{:S(2)}, u32[]{:S(2)}) %collective-permute-start.31) | collective-permute-done | bytes 159776 | tf_op jit(solution)/shard_map/ppermute | solution.py:581
  165.6 3.3 %collective-permute-done.32.far_ref = bf16[96,832]{1,0:T(8,128)(2,1)S(1)} collective-permute-done((bf16[96,832]{1,0:T(8,128)(2,1)S(1)}, bf16[96,832]{1,0:T(8,128)(2,1)S(1)}, u32[]{:S(2)}, u32[]{:S(2)}) %collective-permute-start.32) | collective-permute-done | bytes 159776 | tf_op jit(solution)/shard_map/ppermute | solution.py:578
  (132 shorter events, 49.1 us)
Async XLA Ops:
  2.8 13.8 %collective-permute-start.3 = (bf16[96,640]{1,0:T(8,128)(2,1)}, bf16[96,640]{1,0:T(8,128)(2,1)S(1)}, u32[]{:S(2)}, u32[]{:S(2)}) collective-permute-start(bf16[96,640]{1,0:T(8,128)(2,1)} %get-tuple-element.93.w0), channel_id=1, source_target_pairs={{0,16},{4,20},{8,24},{12,28},{16,0},{20,4},{24,8},{28,12},{1,17},{... | collective-permute-start | bytes 368648 | tf_op jit(solution)/shard_map/ppermute | solution.py:581
  6.9 9.7 %collective-permute-start.4 = (bf16[96,640]{1,0:T(8,128)(2,1)}, bf16[96,640]{1,0:T(8,128)(2,1)S(1)}, u32[]{:S(2)}, u32[]{:S(2)}) collective-permute-start(bf16[96,640]{1,0:T(8,128)(2,1)} %get-tuple-element.93.w0), channel_id=1, source_target_pairs={{0,24},{4,28},{8,16},{12,20},{16,8},{20,12},{24,0},{28,4},{1,25},{... | collective-permute-start | bytes 368648 | tf_op jit(solution)/shard_map/ppermute | solution.py:581
  8.2 8.8 %collective-permute-start.2 = (bf16[96,640]{1,0:T(8,128)(2,1)}, bf16[96,640]{1,0:T(8,128)(2,1)S(1)}, u32[]{:S(2)}, u32[]{:S(2)}) collective-permute-start(bf16[96,640]{1,0:T(8,128)(2,1)} %get-tuple-element.93.w0), channel_id=1, source_target_pairs={{0,8},{4,12},{8,0},{12,4},{16,24},{20,28},{24,16},{28,20},{1,9},{5... | collective-permute-start | bytes 368648 | tf_op jit(solution)/shard_map/ppermute | solution.py:581
  10.0 14.8 %collective-permute-start.5 = (bf16[96,832]{1,0:T(8,128)(2,1)}, bf16[96,832]{1,0:T(8,128)(2,1)S(1)}, u32[]{:S(2)}, u32[]{:S(2)}) collective-permute-start(bf16[96,832]{1,0:T(8,128)(2,1)} %get-tuple-element.94), channel_id=1, source_target_pairs={{0,4},{4,0},{8,12},{12,8},{16,20},{20,16},{24,28},{28,24},{1,5},{5... | collective-permute-start | bytes 479240 | tf_op jit(solution)/shard_map/ppermute | solution.py:581
  14.3 10.0 %collective-permute-start = (bf16[256,768]{1,0:T(8,128)(2,1)}, bf16[256,768]{1,0:T(8,128)(2,1)S(1)}, u32[]{:S(2)}, u32[]{:S(2)}) collective-permute-start(bf16[256,768]{1,0:T(8,128)(2,1)} %own_ref.1), channel_id=1, source_target_pairs={{0,2},{2,0},{1,3},{3,1},{4,6},{6,4},{5,7},{7,5},{8,10},{10,8},{9,1... | collective-permute-start | bytes 1179656 | tf_op jit(solution)/shard_map/ppermute | solution.py:578
  24.3 8.8 %collective-permute-start.1 = (bf16[256,768]{1,0:T(8,128)(2,1)S(1)}, bf16[256,768]{1,0:T(8,128)(2,1)S(1)}, u32[]{:S(2)}, u32[]{:S(2)}) collective-permute-start(bf16[256,768]{1,0:T(8,128)(2,1)S(1)} %copy-done), channel_id=1, source_target_pairs={{0,2},{2,0},{1,3},{3,1},{4,6},{6,4},{5,7},{7,5},{8,10},{10,8},{9,1... | collective-permute-start | bytes 1179656 | tf_op jit(solution)/shard_map/ppermute | solution.py:578
  24.8 11.2 %collective-permute-start.7 = (bf16[2,96,640]{2,1,0:T(8,128)(2,1)S(1)}, bf16[2,96,640]{2,1,0:T(8,128)(2,1)S(1)}, u32[]{:S(2)}, u32[]{:S(2)}) collective-permute-start(bf16[2,96,640]{2,1,0:T(8,128)(2,1)S(1)} %pad_maximum_fusion.2), channel_id=1, source_target_pairs={{0,4},{4,0},{8,12},{12,8},{16,20},{20,16},{24,28},{28,24},{1,5},{5... | collective-permute-start | bytes 737288 | tf_op jit(solution)/shard_map/ppermute | solution.py:581
  25.4 10.0 %collective-permute-start.6 = (bf16[96,640]{1,0:T(8,128)(2,1)S(1)}, bf16[96,640]{1,0:T(8,128)(2,1)S(1)}, u32[]{:S(2)}, u32[]{:S(2)}) collective-permute-start(bf16[96,640]{1,0:T(8,128)(2,1)S(1)} %collective-permute-done.2.w1), channel_id=1, source_target_pairs={{0,4},{4,0},{8,12},{12,8},{16,20},{20,16},{24,28},{28,24},{1,5},{5... | collective-permute-start | bytes 368648 | tf_op jit(solution)/shard_map/ppermute | solution.py:581
  27.8 15.7 %collective-permute-start.13 = (bf16[96,768]{1,0:T(8,128)(2,1)S(1)}, bf16[96,768]{1,0:T(8,128)(2,1)S(1)}, u32[]{:S(2)}, u32[]{:S(2)}) collective-permute-start(bf16[96,768]{1,0:T(8,128)(2,1)S(1)} %copy-done.2), channel_id=1, source_target_pairs={{0,8},{4,12},{8,0},{12,4},{16,24},{20,28},{24,16},{28,20},{1,9},{5... | collective-permute-start | bytes 442376 | tf_op jit(solution)/shard_map/ppermute | solution.py:581
  29.4 14.1 %collective-permute-start.14 = (bf16[96,768]{1,0:T(8,128)(2,1)S(1)}, bf16[96,768]{1,0:T(8,128)(2,1)S(1)}, u32[]{:S(2)}, u32[]{:S(2)}) collective-permute-start(bf16[96,768]{1,0:T(8,128)(2,1)S(1)} %copy-done.2), channel_id=1, source_target_pairs={{0,16},{4,20},{8,24},{12,28},{16,0},{20,4},{24,8},{28,12},{1,17},{... | collective-permute-start | bytes 442376 | tf_op jit(solution)/shard_map/ppermute | solution.py:581
  33.1 10.4 %collective-permute-start.15 = (bf16[96,768]{1,0:T(8,128)(2,1)S(1)}, bf16[96,768]{1,0:T(8,128)(2,1)S(1)}, u32[]{:S(2)}, u32[]{:S(2)}) collective-permute-start(bf16[96,768]{1,0:T(8,128)(2,1)S(1)} %copy-done.2), channel_id=1, source_target_pairs={{0,24},{4,28},{8,16},{12,20},{16,8},{20,12},{24,0},{28,4},{1,25},{... | collective-permute-start | bytes 442376 | tf_op jit(solution)/shard_map/ppermute | solution.py:581
  43.5 11.2 %collective-permute-start.16 = (bf16[256,768]{1,0:T(8,128)(2,1)S(1)}, bf16[256,768]{1,0:T(8,128)(2,1)S(1)}, u32[]{:S(2)}, u32[]{:S(2)}) collective-permute-start(bf16[256,768]{1,0:T(8,128)(2,1)S(1)} %shard_map.164.a_ref), channel_id=1, source_target_pairs={{0,2},{2,0},{1,3},{3,1},{4,6},{6,4},{5,7},{7,5},{8,10},{10,8},{9,1... | collective-permute-start | bytes 1179656 | tf_op jit(solution)/shard_map/ppermute | solution.py:578
  44.3 13.3 %collective-permute-start.19 = (bf16[96,768]{1,0:T(8,128)(2,1)S(1)}, bf16[96,768]{1,0:T(8,128)(2,1)S(1)}, u32[]{:S(2)}, u32[]{:S(2)}) collective-permute-start(bf16[96,768]{1,0:T(8,128)(2,1)S(1)} %copy-done.1), channel_id=1, source_target_pairs={{0,8},{4,12},{8,0},{12,4},{16,24},{20,28},{24,16},{28,20},{1,9},{5... | collective-permute-start | bytes 442376 | tf_op jit(solution)/shard_map/ppermute | solution.py:581
  44.9 13.8 %collective-permute-start.20 = (bf16[96,768]{1,0:T(8,128)(2,1)S(1)}, bf16[96,768]{1,0:T(8,128)(2,1)S(1)}, u32[]{:S(2)}, u32[]{:S(2)}) collective-permute-start(bf16[96,768]{1,0:T(8,128)(2,1)S(1)} %copy-done.1), channel_id=1, source_target_pairs={{0,16},{4,20},{8,24},{12,28},{16,0},{20,4},{24,8},{28,12},{1,17},{... | collective-permute-start | bytes 442376 | tf_op jit(solution)/shard_map/ppermute | solution.py:581
  46.3 12.4 %collective-permute-start.21 = (bf16[96,768]{1,0:T(8,128)(2,1)S(1)}, bf16[96,768]{1,0:T(8,128)(2,1)S(1)}, u32[]{:S(2)}, u32[]{:S(2)}) collective-permute-start(bf16[96,768]{1,0:T(8,128)(2,1)S(1)} %copy-done.1), channel_id=1, source_target_pairs={{0,24},{4,28},{8,16},{12,20},{16,8},{20,12},{24,0},{28,4},{1,25},{... | collective-permute-start | bytes 442376 | tf_op jit(solution)/shard_map/ppermute | solution.py:581
  48.8 27.5 %collective-permute-start.18 = (bf16[3,96,768]{2,1,0:T(8,128)(2,1)S(1)}, bf16[3,96,768]{2,1,0:T(8,128)(2,1)S(1)}, u32[]{:S(2)}, u32[]{:S(2)}) collective-permute-start(bf16[3,96,768]{2,1,0:T(8,128)(2,1)S(1)} %pad_maximum_fusion), channel_id=1, source_target_pairs={{0,4},{4,0},{8,12},{12,8},{16,20},{20,16},{24,28},{28,24},{1,5},{5... | collective-permute-start | bytes 1327112 | tf_op jit(solution)/shard_map/ppermute | solution.py:581
  58.8 19.0 %collective-permute-start.22 = (bf16[3,96,768]{2,1,0:T(8,128)(2,1)S(1)}, bf16[3,96,768]{2,1,0:T(8,128)(2,1)S(1)}, u32[]{:S(2)}, u32[]{:S(2)}) collective-permute-start(bf16[3,96,768]{2,1,0:T(8,128)(2,1)S(1)} %pad_maximum_fusion.1), channel_id=1, source_target_pairs={{0,4},{4,0},{8,12},{12,8},{16,20},{20,16},{24,28},{28,24},{1,5},{5... | collective-permute-start | bytes 1327112 | tf_op jit(solution)/shard_map/ppermute | solution.py:581
  60.1 16.2 %collective-permute-start.17 = (bf16[96,1536]{1,0:T(8,128)(2,1)S(1)}, bf16[96,1536]{1,0:T(8,128)(2,1)S(1)}, u32[]{:S(2)}, u32[]{:S(2)}) collective-permute-start(bf16[96,1536]{1,0:T(8,128)(2,1)S(1)} %copy-done.6), channel_id=1, source_target_pairs={{0,4},{4,0},{8,12},{12,8},{16,20},{20,16},{24,28},{28,24},{1,5},{5... | collective-permute-start | bytes 884744 | tf_op jit(solution)/shard_map/ppermute | solution.py:581
  81.2 11.2 %collective-permute-start.23 = (bf16[256,768]{1,0:T(8,128)(2,1)S(1)}, bf16[256,768]{1,0:T(8,128)(2,1)S(1)}, u32[]{:S(2)}, u32[]{:S(2)}) collective-permute-start(bf16[256,768]{1,0:T(8,128)(2,1)S(1)} %shard_map.169.m_ref), channel_id=1, source_target_pairs={{0,2},{2,0},{1,3},{3,1},{4,6},{6,4},{5,7},{7,5},{8,10},{10,8},{9,1... | collective-permute-start | bytes 1179656 | tf_op jit(solution)/shard_map/ppermute | solution.py:578
  96.9 16.3 %collective-permute-start.25 = (bf16[4,96,768]{2,1,0:T(8,128)(2,1)S(1)}, bf16[4,96,768]{2,1,0:T(8,128)(2,1)S(1)}, u32[]{:S(2)}, u32[]{:S(2)}) collective-permute-start(bf16[4,96,768]{2,1,0:T(8,128)(2,1)S(1)} %get-tuple-element.124), channel_id=1, source_target_pairs={{0,8},{4,12},{8,0},{12,4},{16,24},{20,28},{24,16},{28,20},{1,9},{5... | collective-permute-start | bytes 1769480 | tf_op jit(solution)/shard_map/ppermute | solution.py:581
  103.8 11.2 %collective-permute-start.24 = (bf16[256,768]{1,0:T(8,128)(2,1)S(1)}, bf16[256,768]{1,0:T(8,128)(2,1)S(1)}, u32[]{:S(2)}, u32[]{:S(2)}) collective-permute-start(bf16[256,768]{1,0:T(8,128)(2,1)S(1)} %shard_map.173.d_ref), channel_id=1, source_target_pairs={{0,2},{2,0},{1,3},{3,1},{4,6},{6,4},{5,7},{7,5},{8,10},{10,8},{9,1... | collective-permute-start | bytes 1179656 | tf_op jit(solution)/shard_map/ppermute | solution.py:578
  105.7 18.4 %collective-permute-start.33 = (bf16[4,96,768]{2,1,0:T(8,128)(2,1)S(1)}, bf16[4,96,768]{2,1,0:T(8,128)(2,1)S(1)}, u32[]{:S(2)}, u32[]{:S(2)}) collective-permute-start(bf16[4,96,768]{2,1,0:T(8,128)(2,1)S(1)} %get-tuple-element.134), channel_id=1, source_target_pairs={{0,4},{4,0},{8,12},{12,8},{16,20},{20,16},{24,28},{28,24},{1,5},{5... | collective-permute-start | bytes 1769480 | tf_op jit(solution)/shard_map/ppermute | solution.py:581
  113.2 14.0 %collective-permute-start.37 = (bf16[2,96,768]{2,1,0:T(8,128)(2,1)S(1)}, bf16[2,96,768]{2,1,0:T(8,128)(2,1)S(1)}, u32[]{:S(2)}, u32[]{:S(2)}) collective-permute-start(bf16[2,96,768]{2,1,0:T(8,128)(2,1)S(1)} %get-tuple-element.140), channel_id=1, source_target_pairs={{0,4},{4,0},{8,12},{12,8},{16,20},{20,16},{24,28},{28,24},{1,5},{5... | collective-permute-start | bytes 884744 | tf_op jit(solution)/shard_map/ppermute | solution.py:581
  122.7 20.8 %collective-permute-start.28 = (bf16[4,96,448]{2,1,0:T(8,128)(2,1)S(1)}, bf16[4,96,448]{2,1,0:T(8,128)(2,1)S(1)}, u32[]{:S(2)}, u32[]{:S(2)}) collective-permute-start(bf16[4,96,448]{2,1,0:T(8,128)(2,1)S(1)} %get-tuple-element.154), channel_id=1, source_target_pairs={{0,8},{4,12},{8,0},{12,4},{16,24},{20,28},{24,16},{28,20},{1,9},{5... | collective-permute-start | bytes 1032200 | tf_op jit(solution)/shard_map/ppermute | solution.py:581
  124.2 19.1 %collective-permute-start.34 = (bf16[2,96,768]{2,1,0:T(8,128)(2,1)S(1)}, bf16[2,96,768]{2,1,0:T(8,128)(2,1)S(1)}, u32[]{:S(2)}, u32[]{:S(2)}) collective-permute-start(bf16[2,96,768]{2,1,0:T(8,128)(2,1)S(1)} %get-tuple-element.166), channel_id=1, source_target_pairs={{0,8},{4,12},{8,0},{12,4},{16,24},{20,28},{24,16},{28,20},{1,9},{5... | collective-permute-start | bytes 884744 | tf_op jit(solution)/shard_map/ppermute | solution.py:581
  124.9 18.6 %collective-permute-start.27 = (bf16[4,96,384]{2,1,0:T(8,128)(2,1)S(1)}, bf16[4,96,384]{2,1,0:T(8,128)(2,1)S(1)}, u32[]{:S(2)}, u32[]{:S(2)}) collective-permute-start(bf16[4,96,384]{2,1,0:T(8,128)(2,1)S(1)} %get-tuple-element.152), channel_id=1, source_target_pairs={{0,4},{4,0},{8,12},{12,8},{16,20},{20,16},{24,28},{28,24},{1,5},{5... | collective-permute-start | bytes 884744 | tf_op jit(solution)/shard_map/ppermute | solution.py:581
  127.3 18.8 %collective-permute-start.38 = (bf16[1,96,768]{2,1,0:T(8,128)(2,1)S(1)}, bf16[1,96,768]{2,1,0:T(8,128)(2,1)S(1)}, u32[]{:S(2)}, u32[]{:S(2)}) collective-permute-start(bf16[1,96,768]{2,1,0:T(8,128)(2,1)S(1)} %get-tuple-element.171), channel_id=1, source_target_pairs={{0,16},{4,20},{8,24},{12,28},{16,0},{20,4},{24,8},{28,12},{1,17},{... | collective-permute-start | bytes 442376 | tf_op jit(solution)/shard_map/ppermute | solution.py:581
  129.8 19.7 %collective-permute-start.26 = (bf16[128,768]{1,0:T(8,128)(2,1)S(1)}, bf16[128,768]{1,0:T(8,128)(2,1)S(1)}, u32[]{:S(2)}, u32[]{:S(2)}) collective-permute-start(bf16[128,768]{1,0:T(8,128)(2,1)S(1)} %get-tuple-element.150), channel_id=1, source_target_pairs={{0,2},{2,0},{1,3},{3,1},{4,6},{6,4},{5,7},{7,5},{8,10},{10,8},{9,1... | collective-permute-start | bytes 589832 | tf_op jit(solution)/shard_map/ppermute | solution.py:578
  143.6 9.5 %collective-permute-start.30 = (bf16[2,96,448]{2,1,0:T(8,128)(2,1)S(1)}, bf16[2,96,448]{2,1,0:T(8,128)(2,1)S(1)}, u32[]{:S(2)}, u32[]{:S(2)}) collective-permute-start(bf16[2,96,448]{2,1,0:T(8,128)(2,1)S(1)} %get-tuple-element.158), channel_id=1, source_target_pairs={{0,4},{4,0},{8,12},{12,8},{16,20},{20,16},{24,28},{28,24},{1,5},{5... | collective-permute-start | bytes 516104 | tf_op jit(solution)/shard_map/ppermute | solution.py:581
  146.1 8.5 %collective-permute-start.39 = (bf16[96,768]{1,0:T(8,128)(2,1)S(1)}, bf16[96,768]{1,0:T(8,128)(2,1)S(1)}, u32[]{:S(2)}, u32[]{:S(2)}) collective-permute-start(bf16[96,768]{1,0:T(8,128)(2,1)S(1)} %shard_map.188), channel_id=1, source_target_pairs={{0,2},{2,0},{1,3},{3,1},{4,6},{6,4},{5,7},{7,5},{8,10},{10,8},{9,1... | collective-permute-start | bytes 442376 | tf_op jit(solution)/shard_map/ppermute | solution.py:578
  151.7 13.0 %collective-permute-start.36 = (bf16[96,768]{1,0:T(8,128)(2,1)S(1)}, bf16[96,768]{1,0:T(8,128)(2,1)S(1)}, u32[]{:S(2)}, u32[]{:S(2)}) collective-permute-start(bf16[96,768]{1,0:T(8,128)(2,1)S(1)} %shard_map.186), channel_id=1, source_target_pairs={{0,2},{2,0},{1,3},{3,1},{4,6},{6,4},{5,7},{7,5},{8,10},{10,8},{9,1... | collective-permute-start | bytes 442376 | tf_op jit(solution)/shard_map/ppermute | solution.py:578
  153.2 10.1 %collective-permute-start.31 = (bf16[1,96,832]{2,1,0:T(8,128)(2,1)S(1)}, bf16[1,96,832]{2,1,0:T(8,128)(2,1)S(1)}, u32[]{:S(2)}, u32[]{:S(2)}) collective-permute-start(bf16[1,96,832]{2,1,0:T(8,128)(2,1)S(1)} %get-tuple-element.160), channel_id=1, source_target_pairs={{0,16},{4,20},{8,24},{12,28},{16,0},{20,4},{24,8},{28,12},{1,17},{... | collective-permute-start | bytes 479240 | tf_op jit(solution)/shard_map/ppermute | solution.py:581
  (15 other events, 175.5 us)

commit v4 on v3

--- a/solution.py
+++ b/solution.py
@@ -266,16 +266,22 @@
     )
 
 
-def place(pieces, all_ref, window):
-    index = 0
-    shard, width = pieces[0].shape
+DIRECT = (0, 2, 4, 6, 1, 3, 5, 7)
+OUT_WAYS = (0, 1, 4, 5, 2, 3, 6, 7)
+UP_WAYS = (0, 4, 2, 6, 1, 5, 3, 7)
+DOWN_WAYS = (0, 4, 1, 5, 2, 6, 3, 7)
+
+
+def place(pieces, all_ref, ways, window=0):
+    width = all_ref.shape[1]
+    parts = []
     for piece in pieces:
-        parts = [piece] if len(piece.shape) == 2 else [piece.at[i] for i in range(piece.shape[0])]
-        for part in parts:
-            owner = lax.axis_index("dp") ^ (2 * (index % 4) + index // 4)
-            start = window if part.shape[1] != width else 0
-            all_ref[pl.ds(pl.multiple_of(owner * shard, 32), shard), :] = part[:, start : start + width]
-            index += 1
+        parts += [piece] if len(piece.shape) == 2 else [piece.at[i] for i in range(piece.shape[0])]
+    for part, bits in zip(parts, ways, strict=True):
+        shard = part.shape[0]
+        owner = lax.axis_index("dp") ^ bits
+        start = window if part.shape[1] > width else 0
+        all_ref[pl.ds(pl.multiple_of(owner * shard, 32), shard), :] = part[:, start : start + width]
 
 
 def fetch(pairs, sems):
@@ -291,35 +297,31 @@
     dst[...] = jnp.where(lax.axis_index("ctx") == 0, src[:, :n], src[:, n:])
 
 
-def pack_first_body(qkv_hbm, gain_hbm, bias_hbm, out_hbm, w_ref, out_ref, pack_ref, qkv, gain, bias, out, sems):
+def pack_first_body(qkv_hbm, gain_hbm, bias_hbm, out_hbm, w_ref, pack_ref, qkv, gain, bias, out, sems):
     fetch(((qkv_hbm, qkv), (gain_hbm, gain), (bias_hbm, bias), (out_hbm, out)), sems)
     c = lax.axis_index("ctx")
     n = qkv.shape[2] // 2
     for i in range(3):
         w_ref[:, i * n : (i + 1) * n] = jnp.where(c == 0, qkv[i, :, :n], qkv[i, :, n:])
     first = w_ref.shape[1]
-    extra = first - 3 * n
-    row = lax.broadcasted_iota(jnp.int32, (2, extra), 0)
-    lane = lax.broadcasted_iota(jnp.int32, (2, extra), 1)
+    row = lax.broadcasted_iota(jnp.int32, (2, first - 3 * n), 0)
+    lane = lax.broadcasted_iota(jnp.int32, (2, first - 3 * n), 1)
     cols = mul(gain[...], (row == lane).astype(jnp.bfloat16), 0, 0)
     cols = cols + mul(bias[...], (row + 2 == lane).astype(jnp.bfloat16), 0, 0)
     w_ref[:, 3 * n :] = cols.astype(jnp.bfloat16)
-    own_half(out, out_ref)
+    m = out.shape[1] // 2
     pack_ref[:, 0:first] = w_ref[...]
-    pack_ref[:, first:] = out_ref[...]
-
-
-def pack_second_body(up_hbm, down_hbm, up_ref, down_ref, pack_ref, up, down, sems):
+    pack_ref[:, first:] = jnp.where(c == 0, out[:, :m], out[:, m:])
+
+
+def pack_second_body(up_hbm, down_hbm, up_ref, down_ref, up, down, sems):
     fetch(((up_hbm, up), (down_hbm, down)), sems)
     own_half(up, up_ref)
     own_half(down, down_ref)
-    n = up_ref.shape[1]
-    pack_ref[:, 0:n] = up_ref[...]
-    pack_ref[:, n:] = down_ref[...]
 
 
 def attend_body(
-    own_ref, far_ref, w0, w1, w2, w3, w4, w5, w6, bias_ref,
+    own_ref, far_ref, w0, w1, w2, w3, w4, w5, bias_ref,
     o_ref, qkv_ref, lse_ref, vec_ref, x_ref, w_ref, p_scr, v_scr,
 ):
     width = o_ref.shape[1]
@@ -329,7 +331,7 @@
     for t in range(2):
         x_ref[pl.ds((2 * t + c) * part, part), :] = own_ref[t * part : (t + 1) * part, :]
         x_ref[pl.ds((2 * t + 1 - c) * part, part), :] = far_ref[t * part : (t + 1) * part, :]
-    place((w0, w1, w2, w3, w4, w5, w6), w_ref, 0)
+    place((w0, w1, w2, w3, w4, w5), w_ref, DIRECT)
     scale = 1.0 / math.sqrt(HD)
     w = w_ref[...]
     qkv = mul(x_ref[...], w, 1, 0).astype(jnp.bfloat16)
@@ -360,8 +362,9 @@
     mine_ref[...] = value_of(pl.ds(t * half, half))
 
 
-def project_body(window, o_ref, w0, w1, w2, w3, w4, w5, mine_ref, theirs_ref, w_ref):
-    place((w0, w1, w2, w3, w4, w5), w_ref, window)
+def project_body(ways, window, o_ref, *refs):
+    *pieces, mine_ref, theirs_ref, w_ref = refs
+    place(pieces, w_ref, ways, window)
     split_rows(lambda rows: mul(o_ref[rows, :], w_ref[...], 1, 1), mine_ref, theirs_ref)
 
 
@@ -389,8 +392,8 @@
     low_ref[...] = (n * vec_ref[0:1, :] + vec_ref[2:3, :]).astype(jnp.bfloat16)
 
 
-def ffn_body(window, y_ref, w0, w1, w2, w3, w4, w5, u_ref, slope_ref, up_ref):
-    place((w0, w1, w2, w3, w4, w5), up_ref, window)
+def ffn_body(y_ref, w0, w1, w2, w3, u_ref, slope_ref, up_ref):
+    place((w0, w1, w2, w3), up_ref, UP_WAYS)
     hid = mul(y_ref[...], up_ref[...], 1, 0)
     root = math.sqrt(2.0 / math.pi)
     square = hid * hid
@@ -536,6 +539,10 @@
     out_ref[...] = (keep_ref[...] + got_ref[...].astype(jnp.float32)).astype(jnp.bfloat16)
 
 
+def copy_body(in_ref, out_ref):
+    out_ref[...] = in_ref[...]
+
+
 def finish_body(near_ref, far_ref, qkv_ref, out_ref, gain_ref, bias_ref):
     c = lax.axis_index("ctx")
     n = qkv_ref.shape[2] // 2
@@ -606,26 +613,24 @@
             scratch=[(w.shape, bf16) for w in given], copies=len(given), spec=hbm, room=60,
         )
 
-    def near_of(v):
-        return [v] + [swap_dp(v, 2 * k) for k in range(1, n_out)]
-
-    def far_rest(near):
-        return swap_dp(jnp.stack(near), 1)
-
     x_far = swap_ctx(inputs)
-    w1, w_out, pack_one = packed(
-        pack_first_body, (first, cols, first + cols), qkv_weight, norm_gains, norm_biases, out_weight.T
-    )
-    w1_near = near_of(w1)
+    w1, pack_one = packed(
+        pack_first_body, (first, first + cols), qkv_weight, norm_gains, norm_biases, out_weight.T
+    )
+    w1_near = [swap_dp(w1, 2 * k) for k in range(1, n_out)]
     far_one = swap_dp(pack_one, 1)
-    w_up, w_down, pack_two = packed(pack_second_body, (units, units, 2 * units), up_weight, down_weight.T)
+    w_up, w_down = packed(pack_second_body, (units, units), up_weight, down_weight.T)
     picks_far = swap_ctx(random_blocks)
-    w1_pieces = w1_near + [far_one, swap_dp(after(w1_near[1], far_one), 1), far_rest(w1_near[2:])]
-    out_near = near_of(after(w_out, *w1_near[1:]))
-    out_pieces = out_near + [far_one, far_rest(out_near[1:])]
-    up_near = near_of(after(w_up, *w1_near[1:]))
-    far_two = swap_dp(after(pack_two, *w1_near[1:]), 1)
-    e_far = swap_ctx(after(out_grad, x_far))
+    w1_near = all_after(w1_near, far_one)
+    w1_pieces = [w1, *w1_near, far_one, swap_dp(jnp.stack(w1_near), 1)]
+    out_pieces = [jnp.stack([pack_one[:, first:], far_one[:, first:]])]
+    out_pieces[0] = after(out_pieces[0], *w1_near)
+    out_pieces.append(swap_dp(out_pieces[0], 4))
+    out_pieces.append(swap_dp(jnp.concatenate(out_pieces), 2))
+    up_pieces, down_pieces = all_after([w_up[None], w_down[None]], out_pieces[1])
+    up_pieces = [up_pieces, swap_dp(up_pieces, 4)]
+    down_pieces = [down_pieces, swap_dp(down_pieces, 4)]
+    e_far = swap_ctx(after(out_grad, *w1_near))
 
     picks = jnp.where(c == 0, jnp.stack([random_blocks, picks_far]), jnp.stack([picks_far, random_blocks]))
     picks = lax.dynamic_slice_in_dim(picks.reshape(2 * own_blocks, 2 * heads, 3), c * heads, heads, 1)
@@ -647,28 +652,30 @@
             ((total_rows, cols), bf16), ((total_rows, 3 * cols), bf16), ((8, total_rows), f32), ((8, width), f32),
             ((total_rows, width), bf16), ((width, first), bf16),
         ],
-        inputs, after(x_far, e_far), *w1_pieces, bias,
+        inputs, x_far, *w1_pieces, bias,
         scratch=[((heads * total_rows, total_rows), bf16), ((heads * total_rows, cols), bf16)],
-        flops=2 * 10**10,
+        flops=0,
     )
 
     def sum_tp(mine, theirs):
         return call(add_tp_body, low, mine, both_tp(theirs))[0]
 
-    mine, theirs, w_out_all = call(functools.partial(project_body, first), wide + low + [((width, cols), bf16)], o, *out_pieces)
-    a = after(sum_tp(mine, theirs), *up_near[1:])
+    mine, theirs, w_out_all = call(
+        functools.partial(project_body, OUT_WAYS, 0), wide + low + [((width, cols), bf16)], o, *out_pieces
+    )
+    theirs, up_pieces[1], down_pieces[1] = all_after([theirs, up_pieces[1], down_pieces[1]])
+    up_pieces.append(swap_dp(jnp.concatenate(up_pieces), 2))
+    down_pieces.append(swap_dp(jnp.concatenate(down_pieces), 1))
+    a = after(sum_tp(mine, theirs), e_far)
     a_far = swap_ctx(a)
-    up_near = up_near[:1] + all_after(up_near[1:], a)
-    up_pieces = up_near + [far_two, far_rest(up_near[1:])]
-    down_near = near_of(after(w_down, a))
+    up_pieces.append(swap_dp(jnp.concatenate(up_pieces), 1))
+    down_pieces.append(swap_dp(jnp.concatenate(down_pieces), 2))
     n1, r1, y_low = call(norm_one_body, wide + [((rows, 128), f32)] + low, x_all, a, a_far, vecs)
     flat = [((total_rows, units), bf16)]
     square = [((width, units), bf16)]
     y_all = both_tp(y_low, True)
-    down_near = down_near[:1] + all_after(down_near[1:], y_all)
-    down_pieces = down_near + [far_two, far_rest(down_near[1:])]
-    u, slope, w_up_all = call(functools.partial(ffn_body, 0), flat * 2 + square, y_all, *up_pieces)
-    mine, theirs, w_down_all = call(functools.partial(project_body, units), wide + low + square, u, *down_pieces)
+    u, slope, w_up_all = call(ffn_body, flat * 2 + square, y_all, *up_pieces)
+    mine, theirs, w_down_all = call(functools.partial(project_body, DOWN_WAYS, 0), wide + low + square, u, *down_pieces)
     m = sum_tp(mine, theirs)
     m_far = swap_ctx(m)
     out, dz2, dm_low, grad2 = call(
@@ -723,21 +730,21 @@
     )
     up_own = after(up_own, theirs)
     keep, send = call(fold_input_body, [((part, width), f32), half], mine, both_tp(theirs), dz1)
-    up_keep, up_send = fold(up_own, swap_dp(up_away, up_order[0]))
     down_keep, down_send = fold(down_keep, swap_dp(down_send, down_order[1]))
     keep1, send1, keep2, send2 = call(
         fold_two_body, kept(2, left) + kept(2, last - left),
         own, swap_dp(away, 1), own2, swap_dp(away2, 2),
     )
-    up_keep, up_send = fold(up_keep, swap_dp(up_send, up_order[1]))
+    up_keep, up_send = fold(after(up_own, keep1), swap_dp(up_away, up_order[0]))
     keep1, send1 = call(
         fold_join_body, kept(1, last), keep1, swap_dp(send1, 2), keep2, swap_dp(send2, 1)
     )
+    up_keep, up_send = fold(after(up_keep, keep1), swap_dp(up_send, up_order[1]))
     grad_down, down_far = last_sum(down_keep, down_send, 4)
     grad_up, up_far = last_sum(up_keep, up_send, 4)
     grad_1, far_1 = last_sum(keep1, send1, 4)
     dx = call(last_input_body, [half], keep, swap_ctx(send))[0]
-    output, input_grad = both_tp(out, True), both_tp(dx, True)
+    output, input_grad = [call(copy_body, low, both_tp(v, True))[0] for v in (out, dx)]
 
     def both_ctx(g, far):
         return jnp.where(c == 0, jnp.concatenate([g, far], 1), jnp.concatenate([far, g], 1)).astype(f32)

time: 172 us -> 159 us (0.924)
  waiting for transfers between devices: 70 us -> 61 us
  starting transfers between devices: 50.7 us -> 45.4 us
    ppermute x30 -> x24, waiting for transfers between devices: 46.5 us -> 35.9 us  [swap_dp(): return lax.ppermute(v, 'dp', [(i, i ^ bits) for i in range(n_dp)])]
    ppermute x30 -> x24, starting transfers between devices: 40.9 us -> 34 us  [swap_dp(): return lax.ppermute(v, 'dp', [(i, i ^ bits) for i in range(n_dp)])]
    unnamed x16 -> x10, local copies, waits for them, and re-layouts: 1.76 us -> 0.03 us
    pallas_call x28 -> x30, Pallas kernels: 21.8 us -> 23.3 us  [call(): pl.pallas_call(body, out_shape=shapes, in_specs=specs, out_specs=[pl.Bloc...]
  transfers between devices with their start and end apart: 40 -> 34, of which waited for: 16 -> 18; matrix products, arithmetic and copies ran while one was open for 3% -> 3% of each run, Pallas kernels for 9% -> 10%
where the time goes in v4:
time: 159 us; the launch traced here: 158 us
  waiting for transfers between devices  61 us (38%)
  starting transfers between devices  45.4 us (29%)
  Pallas kernels  23.3 us (15%)
  blocking collectives  20.9 us (13%)
  other arithmetic  4.1 us (3%)
  local copies, waits for them, and re-layouts  1.95 us (1%)
  between operations  1.67 us (1%)
    ppermute x24, waiting for transfers between devices, swap_dp(): return lax.ppermute(v, 'dp', [(i, i ^ bits) for i in range(n_dp)])  35.9 us
    ppermute x24, starting transfers between devices, swap_dp(): return lax.ppermute(v, 'dp', [(i, i ^ bits) for i in range(n_dp)])  34 us
    ppermute x10, waiting for transfers between devices, swap_ctx(): return lax.ppermute(v, 'ctx', pair)  25 us
    pallas_call x30, Pallas kernels, call(): pl.pallas_call(body, out_shape=shapes, in_specs=specs, out_specs=[pl.Bloc...  23.3 us
    all_gather x9, blocking collectives, both_tp(): return lax.all_gather(v, 'tp', axis=0, tiled=tiled)  20.9 us
    ppermute x10, starting transfers between devices, swap_ctx(): return lax.ppermute(v, 'ctx', pair)  11.4 us
  transfers between devices with their start and end apart: 34, of which 18 were waited for; matrix products, arithmetic and copies ran while one was open for 3% of the time, Pallas kernels for 10%

profile of v4, /device:TPU:0, one launch (start us, length us, event | category | flops | bytes accessed | tf_op | source)
XLA Modules:
  0.0 158.3 jit_solution(10747948812912898010)
XLA Ops:
  0.6 2.1 %shard_map.161 = (bf16[96,640]{1,0:T(8,128)(2,1)}, bf16[96,832]{1,0:T(8,128)(2,1)}) custom-call(bf16[3,96,384]{2,1,0:T(8,128)(2,1)} %qkv_hbm.1, bf16[2,96]{1,0:T(2,128)(2,1)} %gain_hbm.1, bf16[2,96]{1,0:T(2,128)(2,1)} %bias_hbm.1, bf16[96,384]{1,0:T(8,128)(2,1)} %bitcast.48), custom_call_target="tpu_custom_call" | custom-call | tf_op jit(solution)/shard_map/pallas_call | solution.py:240
  2.7 3.1 %collective-permute-start.1 = (bf16[96,640]{1,0:T(8,128)(2,1)}, bf16[96,640]{1,0:T(8,128)(2,1)S(1)}, u32[]{:S(2)}, u32[]{:S(2)}) collective-permute-start(bf16[96,640]{1,0:T(8,128)(2,1)} %get-tuple-element.88.w0), channel_id=1, source_target_pairs={{0,8},{4,12},{8,0},{12,4},{16,24},{20,28},{24,16},{28,20},{1,9},{5... | collective-permute-start | bytes 368648 | tf_op jit(solution)/shard_map/ppermute | solution.py:588
  5.8 2.6 %collective-permute-start.2 = (bf16[96,640]{1,0:T(8,128)(2,1)}, bf16[96,640]{1,0:T(8,128)(2,1)S(1)}, u32[]{:S(2)}, u32[]{:S(2)}) collective-permute-start(bf16[96,640]{1,0:T(8,128)(2,1)} %get-tuple-element.88.w0), channel_id=1, source_target_pairs={{0,16},{4,20},{8,24},{12,28},{16,0},{20,4},{24,8},{28,12},{1,17},{... | collective-permute-start | bytes 368648 | tf_op jit(solution)/shard_map/ppermute | solution.py:588
  20.6 2.9 %collective-permute-start.7 = (bf16[2,96,192]{2,1,0:T(8,128)(2,1)S(1)}, bf16[2,96,192]{2,1,0:T(8,128)(2,1)S(1)}, u32[]{:S(2)}, u32[]{:S(2)}) collective-permute-start(bf16[2,96,192]{2,1,0:T(8,128)(2,1)S(1)} %pad_maximum_fusion.6.refs_0_), channel_id=1, source_target_pairs={{0,16},{4,20},{8,24},{12,28},{16,0},{20,4},{24,8},{28,12},{1,17},{... | collective-permute-start | bytes 221192 | tf_op jit(solution)/shard_map/ppermute | solution.py:588
  23.7 2.5 %collective-permute-done.7.refs_1_ = bf16[2,96,192]{2,1,0:T(8,128)(2,1)S(1)} collective-permute-done((bf16[2,96,192]{2,1,0:T(8,128)(2,1)S(1)}, bf16[2,96,192]{2,1,0:T(8,128)(2,1)S(1)}, u32[]{:S(2)}, u32[]{:S(2)}) %collective-permute-start.7) | collective-permute-done | bytes 73760 | tf_op jit(solution)/shard_map/ppermute | solution.py:588
  26.3 1.9 %collective-permute-start.8 = (bf16[4,96,192]{2,1,0:T(8,128)(2,1)S(1)}, bf16[4,96,192]{2,1,0:T(8,128)(2,1)S(1)}, u32[]{:S(2)}, u32[]{:S(2)}) collective-permute-start(bf16[4,96,192]{2,1,0:T(8,128)(2,1)S(1)} %pad_maximum_fusion.5), channel_id=1, source_target_pairs={{0,8},{4,12},{8,0},{12,4},{16,24},{20,28},{24,16},{28,20},{1,9},{5... | collective-permute-start | bytes 442376 | tf_op jit(solution)/shard_map/ppermute | solution.py:588
  33.6 2.8 %shard_map.162 = (bf16[512,192]{1,0:T(8,128)(2,1)S(1)}, bf16[512,576]{1,0:T(8,128)(2,1)S(1)}, f32[8,512]{1,0:T(8,128)S(1)}, f32[8,768]{1,0:T(8,128)S(1)}, bf16[5...) custom-call(bf16[256,768]{1,0:T(8,128)(2,1)S(1)} %copy-done.2, bf16[256,768]{1,0:T(8,128)(2,1)S(1)} %collective-permute-done.far_ref, ...), custom_call_target="tpu_custom_call" | custom-call | tf_op jit(solution)/shard_map/pallas_call | solution.py:240
  36.9 3.0 %collective-permute-done.10.refs_1_ = bf16[1,96,768]{2,1,0:T(8,128)(2,1)S(1)} collective-permute-done((bf16[1,96,768]{2,1,0:T(8,128)(2,1)S(1)}, bf16[1,96,768]{2,1,0:T(8,128)(2,1)S(1)}, u32[]{:S(2)}, u32[]{:S(2)}) %collective-permute-start.10) | collective-permute-done | bytes 147488 | tf_op jit(solution)/shard_map/ppermute | solution.py:588
  42.2 2.4 %all-gather = bf16[512,768]{1,0:T(8,128)(2,1)S(1)} all-gather(bf16[256,768]{1,0:T(8,128)(2,1)S(1)} %get-tuple-element.102), channel_id=2, replica_groups=mesh['dp'=8,'ctx'=2,'tp'=2] {'tp'}, dimensions={0}, use_global_device_ids=true | all-gather | bytes 1179648 | tf_op jit(solution)/shard_map/all_gather | solution.py:582
  46.3 2.1 %collective-permute-done.13.w2 = bf16[2,96,768]{2,1,0:T(8,128)(2,1)S(1)} collective-permute-done((bf16[2,96,768]{2,1,0:T(8,128)(2,1)S(1)}, bf16[2,96,768]{2,1,0:T(8,128)(2,1)S(1)}, u32[]{:S(2)}, u32[]{:S(2)}) %collective-permute-start.13) | collective-permute-done | bytes 294944 | tf_op jit(solution)/shard_map/ppermute | solution.py:588
  50.7 5.2 %collective-permute-done.12.far_ref = bf16[256,768]{1,0:T(8,128)(2,1)S(1)} collective-permute-done((bf16[256,768]{1,0:T(8,128)(2,1)S(1)}, bf16[256,768]{1,0:T(8,128)(2,1)S(1)}, u32[]{:S(2)}, u32[]{:S(2)}) %collective-permute-start.12) | collective-permute-done | bytes 393248 | tf_op jit(solution)/shard_map/ppermute | solution.py:585
  56.2 2.4 %all_gather.44.y_ref.left_ref = bf16[512,768]{1,0:T(8,128)(2,1)S(1)} all-gather(bf16[256,768]{1,0:T(8,128)(2,1)S(1)} %get-tuple-element.107), channel_id=1, replica_groups=mesh['dp'=8,'ctx'=2,'tp'=2] {'tp'}, dimensions={0}, use_global_device_ids=true | all-gather | bytes 1179648 | tf_op jit(solution)/shard_map/all_gather | solution.py:582
  58.6 3.0 %collective-permute-done.14.w3 = bf16[4,96,768]{2,1,0:T(8,128)(2,1)S(1)} collective-permute-done((bf16[4,96,768]{2,1,0:T(8,128)(2,1)S(1)}, bf16[4,96,768]{2,1,0:T(8,128)(2,1)S(1)}, u32[]{:S(2)}, u32[]{:S(2)}) %collective-permute-start.14) | collective-permute-done | bytes 589856 | tf_op jit(solution)/shard_map/ppermute | solution.py:588
  64.1 2.4 %all-gather.1 = bf16[512,768]{1,0:T(8,128)(2,1)S(1)} all-gather(bf16[256,768]{1,0:T(8,128)(2,1)S(1)} %get-tuple-element.112), channel_id=3, replica_groups=mesh['dp'=8,'ctx'=2,'tp'=2] {'tp'}, dimensions={0}, use_global_device_ids=true | all-gather | bytes 1179648 | tf_op jit(solution)/shard_map/all_gather | solution.py:582
  67.7 10.1 %collective-permute-done.17.far_ref = bf16[256,768]{1,0:T(8,128)(2,1)S(1)} collective-permute-done((bf16[256,768]{1,0:T(8,128)(2,1)S(1)}, bf16[256,768]{1,0:T(8,128)(2,1)S(1)}, u32[]{:S(2)}, u32[]{:S(2)}) %collective-permute-start.17) | collective-permute-done | bytes 393248 | tf_op jit(solution)/shard_map/ppermute | solution.py:585
  78.7 2.4 %all_gather.48.left_ref.dm_ref = bf16[512,768]{1,0:T(8,128)(2,1)S(1)} all-gather(bf16[256,768]{1,0:T(8,128)(2,1)S(1)} %get-tuple-element.115), channel_id=1, replica_groups=mesh['dp'=8,'ctx'=2,'tp'=2] {'tp'}, dimensions={0}, use_global_device_ids=true | all-gather | bytes 1179648 | tf_op jit(solution)/shard_map/all_gather | solution.py:582
  83.8 2.5 %all-gather.2 = bf16[512,768]{1,0:T(8,128)(2,1)S(1)} all-gather(bf16[256,768]{1,0:T(8,128)(2,1)S(1)} %get-tuple-element.122), channel_id=4, replica_groups=mesh['dp'=8,'ctx'=2,'tp'=2] {'tp'}, dimensions={0}, use_global_device_ids=true | all-gather | bytes 1179648 | tf_op jit(solution)/shard_map/all_gather | solution.py:582
  87.6 2.0 %collective-permute-start.19 = (bf16[4,96,768]{2,1,0:T(8,128)(2,1)S(1)}, bf16[4,96,768]{2,1,0:T(8,128)(2,1)S(1)}, u32[]{:S(2)}, u32[]{:S(2)}) collective-permute-start(bf16[4,96,768]{2,1,0:T(8,128)(2,1)S(1)} %get-tuple-element.116), channel_id=1, source_target_pairs={{0,8},{4,12},{8,0},{12,4},{16,24},{20,28},{24,16},{28,20},{1,9},{5... | collective-permute-start | bytes 1769480 | tf_op jit(solution)/shard_map/ppermute | solution.py:588
  91.5 6.1 %collective-permute-done.18.far_ref = bf16[256,768]{1,0:T(8,128)(2,1)S(1)} collective-permute-done((bf16[256,768]{1,0:T(8,128)(2,1)S(1)}, bf16[256,768]{1,0:T(8,128)(2,1)S(1)}, u32[]{:S(2)}, u32[]{:S(2)}) %collective-permute-start.18) | collective-permute-done | bytes 393248 | tf_op jit(solution)/shard_map/ppermute | solution.py:585
  98.2 2.4 %all-gather.3 = bf16[544,768]{1,0:T(8,128)(2,1)S(1)} all-gather(bf16[272,768]{1,0:T(8,128)(2,1)S(1)} %get-tuple-element.130), channel_id=5, replica_groups=mesh['dp'=8,'ctx'=2,'tp'=2] {'tp'}, dimensions={0}, use_global_device_ids=true | all-gather | bytes 1253376 | tf_op jit(solution)/shard_map/all_gather | solution.py:582
  100.6 2.4 %collective-permute-done.19.got_ref = bf16[4,96,768]{2,1,0:T(8,128)(2,1)S(1)} collective-permute-done((bf16[4,96,768]{2,1,0:T(8,128)(2,1)S(1)}, bf16[4,96,768]{2,1,0:T(8,128)(2,1)S(1)}, u32[]{:S(2)}, u32[]{:S(2)}) %collective-permute-start.19) | collective-permute-done | bytes 589856 | tf_op jit(solution)/shard_map/ppermute | solution.py:588
  103.1 4.8 %shard_map.178 = (f32[4,96,384]{2,1,0:T(8,128)S(1)}, bf16[4,96,384]{2,1,0:T(8,128)(2,1)S(1)}, f32[4,96,448]{2,1,0:T(8,128)S(1)}, bf16[4,96,448]{2,1,0:T(8,128)(2...) custom-call(bf16[2,272,768]{2,1,0:T(8,128)(2,1)S(1)} %bitcast.30, ...), custom_call_target="tpu_custom_call" | custom-call | tf_op jit(solution)/shard_map/pallas_call | solution.py:240
  107.9 1.8 %collective-permute-start.22 = (bf16[4,96,448]{2,1,0:T(8,128)(2,1)S(1)}, bf16[4,96,448]{2,1,0:T(8,128)(2,1)S(1)}, u32[]{:S(2)}, u32[]{:S(2)}) collective-permute-start(bf16[4,96,448]{2,1,0:T(8,128)(2,1)S(1)} %get-tuple-element.146), channel_id=1, source_target_pairs={{0,8},{4,12},{8,0},{12,4},{16,24},{20,28},{24,16},{28,20},{1,9},{5... | collective-permute-start | bytes 1032200 | tf_op jit(solution)/shard_map/ppermute | solution.py:588
  111.7 7.9 %collective-permute-done.31.got_ref = bf16[2,96,768]{2,1,0:T(8,128)(2,1)S(1)} collective-permute-done((bf16[2,96,768]{2,1,0:T(8,128)(2,1)S(1)}, bf16[2,96,768]{2,1,0:T(8,128)(2,1)S(1)}, u32[]{:S(2)}, u32[]{:S(2)}) %collective-permute-start.31) | collective-permute-done | bytes 294944 | tf_op jit(solution)/shard_map/ppermute | solution.py:588
  121.5 2.1 %collective-permute-done.21.got_ref = bf16[4,96,384]{2,1,0:T(8,128)(2,1)S(1)} collective-permute-done((bf16[4,96,384]{2,1,0:T(8,128)(2,1)S(1)}, bf16[4,96,384]{2,1,0:T(8,128)(2,1)S(1)}, u32[]{:S(2)}, u32[]{:S(2)}) %collective-permute-start.21) | collective-permute-done | bytes 294944 | tf_op jit(solution)/shard_map/ppermute | solution.py:588
  126.9 2.4 %all-gather.4 = bf16[512,768]{1,0:T(8,128)(2,1)S(1)} all-gather(bf16[256,768]{1,0:T(8,128)(2,1)S(1)} %get-tuple-element.139), channel_id=6, replica_groups=mesh['dp'=8,'ctx'=2,'tp'=2] {'tp'}, dimensions={0}, use_global_device_ids=true | all-gather | bytes 1179648 | tf_op jit(solution)/shard_map/all_gather | solution.py:582
  131.5 3.9 %collective-permute-done.23.got_ref = bf16[2,96,384]{2,1,0:T(8,128)(2,1)S(1)} collective-permute-done((bf16[2,96,384]{2,1,0:T(8,128)(2,1)S(1)}, bf16[2,96,384]{2,1,0:T(8,128)(2,1)S(1)}, u32[]{:S(2)}, u32[]{:S(2)}) %collective-permute-start.23) | collective-permute-done | bytes 147488 | tf_op jit(solution)/shard_map/ppermute | solution.py:588
  136.4 2.2 %collective-permute-start.29 = (bf16[1,96,768]{2,1,0:T(8,128)(2,1)S(1)}, bf16[1,96,768]{2,1,0:T(8,128)(2,1)S(1)}, u32[]{:S(2)}, u32[]{:S(2)}) collective-permute-start(bf16[1,96,768]{2,1,0:T(8,128)(2,1)S(1)} %get-tuple-element.162), channel_id=1, source_target_pairs={{0,16},{4,20},{8,24},{12,28},{16,0},{20,4},{24,8},{28,12},{1,17},{... | collective-permute-start | bytes 442376 | tf_op jit(solution)/shard_map/ppermute | solution.py:588
  138.5 2.1 %all_gather.47.in_ref = bf16[256,768]{1,0:T(8,128)(2,1)S(1)} all-gather(bf16[128,768]{1,0:T(8,128)(2,1)S(1)} %get-tuple-element.113), channel_id=1, replica_groups=mesh['dp'=8,'ctx'=2,'tp'=2] {'tp'}, dimensions={0}, use_global_device_ids=true | all-gather | bytes 589824 | tf_op jit(solution)/shard_map/all_gather | solution.py:582
  141.4 2.1 %all_gather.55.in_ref = bf16[256,768]{1,0:T(8,128)(2,1)S(1)} all-gather(bf16[128,768]{1,0:T(8,128)(2,1)S(1)} %shard_map.180), channel_id=1, replica_groups=mesh['dp'=8,'ctx'=2,'tp'=2] {'tp'}, dimensions={0}, use_global_device_ids=true | all-gather | bytes 589824 | tf_op jit(solution)/shard_map/all_gather | solution.py:582
  144.3 4.4 %collective-permute-done.25.got_ref = bf16[1,96,832]{2,1,0:T(8,128)(2,1)S(1)} collective-permute-done((bf16[1,96,832]{2,1,0:T(8,128)(2,1)S(1)}, bf16[1,96,832]{2,1,0:T(8,128)(2,1)S(1)}, u32[]{:S(2)}, u32[]{:S(2)}) %collective-permute-start.25) | collective-permute-done | bytes 159776 | tf_op jit(solution)/shard_map/ppermute | solution.py:588
  152.8 2.5 %collective-permute-done.26.far_ref = bf16[96,832]{1,0:T(8,128)(2,1)S(1)} collective-permute-done((bf16[96,832]{1,0:T(8,128)(2,1)S(1)}, bf16[96,832]{1,0:T(8,128)(2,1)S(1)}, u32[]{:S(2)}, u32[]{:S(2)}) %collective-permute-start.26) | collective-permute-done | bytes 159776 | tf_op jit(solution)/shard_map/ppermute | solution.py:585
  (121 shorter events, 54.3 us)
Async XLA Ops:
  2.7 14.2 %collective-permute-start.1 = (bf16[96,640]{1,0:T(8,128)(2,1)}, bf16[96,640]{1,0:T(8,128)(2,1)S(1)}, u32[]{:S(2)}, u32[]{:S(2)}) collective-permute-start(bf16[96,640]{1,0:T(8,128)(2,1)} %get-tuple-element.88.w0), channel_id=1, source_target_pairs={{0,8},{4,12},{8,0},{12,4},{16,24},{20,28},{24,16},{28,20},{1,9},{5... | collective-permute-start | bytes 368648 | tf_op jit(solution)/shard_map/ppermute | solution.py:588
  5.8 12.5 %collective-permute-start.2 = (bf16[96,640]{1,0:T(8,128)(2,1)}, bf16[96,640]{1,0:T(8,128)(2,1)S(1)}, u32[]{:S(2)}, u32[]{:S(2)}) collective-permute-start(bf16[96,640]{1,0:T(8,128)(2,1)} %get-tuple-element.88.w0), channel_id=1, source_target_pairs={{0,16},{4,20},{8,24},{12,28},{16,0},{20,4},{24,8},{28,12},{1,17},{... | collective-permute-start | bytes 368648 | tf_op jit(solution)/shard_map/ppermute | solution.py:588
  8.4 10.0 %collective-permute-start.3 = (bf16[96,640]{1,0:T(8,128)(2,1)}, bf16[96,640]{1,0:T(8,128)(2,1)S(1)}, u32[]{:S(2)}, u32[]{:S(2)}) collective-permute-start(bf16[96,640]{1,0:T(8,128)(2,1)} %get-tuple-element.88.w0), channel_id=1, source_target_pairs={{0,24},{4,28},{8,16},{12,20},{16,8},{20,12},{24,0},{28,4},{1,25},{... | collective-permute-start | bytes 368648 | tf_op jit(solution)/shard_map/ppermute | solution.py:588
  8.4 10.0 %collective-permute-start.4 = (bf16[96,832]{1,0:T(8,128)(2,1)}, bf16[96,832]{1,0:T(8,128)(2,1)S(1)}, u32[]{:S(2)}, u32[]{:S(2)}) collective-permute-start(bf16[96,832]{1,0:T(8,128)(2,1)} %get-tuple-element.89), channel_id=1, source_target_pairs={{0,4},{4,0},{8,12},{12,8},{16,20},{20,16},{24,28},{28,24},{1,5},{5... | collective-permute-start | bytes 479240 | tf_op jit(solution)/shard_map/ppermute | solution.py:588
  15.2 16.8 %collective-permute-start = (bf16[256,768]{1,0:T(8,128)(2,1)}, bf16[256,768]{1,0:T(8,128)(2,1)S(1)}, u32[]{:S(2)}, u32[]{:S(2)}) collective-permute-start(bf16[256,768]{1,0:T(8,128)(2,1)} %own_ref.1), channel_id=1, source_target_pairs={{0,2},{2,0},{1,3},{3,1},{4,6},{6,4},{5,7},{7,5},{8,10},{10,8},{9,1... | collective-permute-start | bytes 1179656 | tf_op jit(solution)/shard_map/ppermute | solution.py:585
  19.1 14.4 %collective-permute-start.5 = (bf16[3,96,640]{2,1,0:T(8,128)(2,1)}, bf16[3,96,640]{2,1,0:T(8,128)(2,1)S(1)}, u32[]{:S(2)}, u32[]{:S(2)}) collective-permute-start(bf16[3,96,640]{2,1,0:T(8,128)(2,1)} %pad_maximum_fusion.2), channel_id=1, source_target_pairs={{0,4},{4,0},{8,12},{12,8},{16,20},{20,16},{24,28},{28,24},{1,5},{5... | collective-permute-start | bytes 1105928 | tf_op jit(solution)/shard_map/ppermute | solution.py:588
  26.3 10.2 %collective-permute-start.8 = (bf16[4,96,192]{2,1,0:T(8,128)(2,1)S(1)}, bf16[4,96,192]{2,1,0:T(8,128)(2,1)S(1)}, u32[]{:S(2)}, u32[]{:S(2)}) collective-permute-start(bf16[4,96,192]{2,1,0:T(8,128)(2,1)S(1)} %pad_maximum_fusion.5), channel_id=1, source_target_pairs={{0,8},{4,12},{8,0},{12,4},{16,24},{20,28},{24,16},{28,20},{1,9},{5... | collective-permute-start | bytes 442376 | tf_op jit(solution)/shard_map/ppermute | solution.py:588
  28.2 11.7 %collective-permute-start.10 = (bf16[1,96,768]{2,1,0:T(8,128)(2,1)S(1)}, bf16[1,96,768]{2,1,0:T(8,128)(2,1)S(1)}, u32[]{:S(2)}, u32[]{:S(2)}) collective-permute-start(bf16[1,96,768]{2,1,0:T(8,128)(2,1)S(1)} %bitcast.35), channel_id=1, source_target_pairs={{0,16},{4,20},{8,24},{12,28},{16,0},{20,4},{24,8},{28,12},{1,17},{... | collective-permute-start | bytes 442376 | tf_op jit(solution)/shard_map/ppermute | solution.py:588
  29.3 12.2 %collective-permute-start.9 = (bf16[1,96,768]{2,1,0:T(8,128)(2,1)S(1)}, bf16[1,96,768]{2,1,0:T(8,128)(2,1)S(1)}, u32[]{:S(2)}, u32[]{:S(2)}) collective-permute-start(bf16[1,96,768]{2,1,0:T(8,128)(2,1)S(1)} %bitcast.39), channel_id=1, source_target_pairs={{0,16},{4,20},{8,24},{12,28},{16,0},{20,4},{24,8},{28,12},{1,17},{... | collective-permute-start | bytes 442376 | tf_op jit(solution)/shard_map/ppermute | solution.py:588
  32.0 12.6 %collective-permute-start.11 = (bf16[256,768]{1,0:T(8,128)(2,1)S(1)}, bf16[256,768]{1,0:T(8,128)(2,1)S(1)}, u32[]{:S(2)}, u32[]{:S(2)}) collective-permute-start(bf16[256,768]{1,0:T(8,128)(2,1)S(1)} %copy-done.3), channel_id=1, source_target_pairs={{0,2},{2,0},{1,3},{3,1},{4,6},{6,4},{5,7},{7,5},{8,10},{10,8},{9,1... | collective-permute-start | bytes 1179656 | tf_op jit(solution)/shard_map/ppermute | solution.py:585
  41.6 6.8 %collective-permute-start.13 = (bf16[2,96,768]{2,1,0:T(8,128)(2,1)S(1)}, bf16[2,96,768]{2,1,0:T(8,128)(2,1)S(1)}, u32[]{:S(2)}, u32[]{:S(2)}) collective-permute-start(bf16[2,96,768]{2,1,0:T(8,128)(2,1)S(1)} %pad_maximum_fusion.3), channel_id=1, source_target_pairs={{0,8},{4,12},{8,0},{12,4},{16,24},{20,28},{24,16},{28,20},{1,9},{5... | collective-permute-start | bytes 884744 | tf_op jit(solution)/shard_map/ppermute | solution.py:588
  41.7 7.2 %collective-permute-start.15 = (bf16[2,96,768]{2,1,0:T(8,128)(2,1)S(1)}, bf16[2,96,768]{2,1,0:T(8,128)(2,1)S(1)}, u32[]{:S(2)}, u32[]{:S(2)}) collective-permute-start(bf16[2,96,768]{2,1,0:T(8,128)(2,1)S(1)} %pad_maximum_fusion.4), channel_id=1, source_target_pairs={{0,4},{4,0},{8,12},{12,8},{16,20},{20,16},{24,28},{28,24},{1,5},{5... | collective-permute-start | bytes 884744 | tf_op jit(solution)/shard_map/ppermute | solution.py:588
  44.6 11.2 %collective-permute-start.12 = (bf16[256,768]{1,0:T(8,128)(2,1)S(1)}, bf16[256,768]{1,0:T(8,128)(2,1)S(1)}, u32[]{:S(2)}, u32[]{:S(2)}) collective-permute-start(bf16[256,768]{1,0:T(8,128)(2,1)S(1)} %shard_map.165.a_ref), channel_id=1, source_target_pairs={{0,2},{2,0},{1,3},{3,1},{4,6},{6,4},{5,7},{7,5},{8,10},{10,8},{9,1... | collective-permute-start | bytes 1179656 | tf_op jit(solution)/shard_map/ppermute | solution.py:585
  48.5 13.1 %collective-permute-start.14 = (bf16[4,96,768]{2,1,0:T(8,128)(2,1)S(1)}, bf16[4,96,768]{2,1,0:T(8,128)(2,1)S(1)}, u32[]{:S(2)}, u32[]{:S(2)}) collective-permute-start(bf16[4,96,768]{2,1,0:T(8,128)(2,1)S(1)} %pad_maximum_fusion), channel_id=1, source_target_pairs={{0,4},{4,0},{8,12},{12,8},{16,20},{20,16},{24,28},{28,24},{1,5},{5... | collective-permute-start | bytes 1769480 | tf_op jit(solution)/shard_map/ppermute | solution.py:588
  49.0 14.2 %collective-permute-start.16 = (bf16[4,96,768]{2,1,0:T(8,128)(2,1)S(1)}, bf16[4,96,768]{2,1,0:T(8,128)(2,1)S(1)}, u32[]{:S(2)}, u32[]{:S(2)}) collective-permute-start(bf16[4,96,768]{2,1,0:T(8,128)(2,1)S(1)} %pad_maximum_fusion.1), channel_id=1, source_target_pairs={{0,8},{4,12},{8,0},{12,4},{16,24},{20,28},{24,16},{28,20},{1,9},{5... | collective-permute-start | bytes 1769480 | tf_op jit(solution)/shard_map/ppermute | solution.py:588
  66.5 11.2 %collective-permute-start.17 = (bf16[256,768]{1,0:T(8,128)(2,1)S(1)}, bf16[256,768]{1,0:T(8,128)(2,1)S(1)}, u32[]{:S(2)}, u32[]{:S(2)}) collective-permute-start(bf16[256,768]{1,0:T(8,128)(2,1)S(1)} %shard_map.169.m_ref), channel_id=1, source_target_pairs={{0,2},{2,0},{1,3},{3,1},{4,6},{6,4},{5,7},{7,5},{8,10},{10,8},{9,1... | collective-permute-start | bytes 1179656 | tf_op jit(solution)/shard_map/ppermute | solution.py:585
  86.5 11.2 %collective-permute-start.18 = (bf16[256,768]{1,0:T(8,128)(2,1)S(1)}, bf16[256,768]{1,0:T(8,128)(2,1)S(1)}, u32[]{:S(2)}, u32[]{:S(2)}) collective-permute-start(bf16[256,768]{1,0:T(8,128)(2,1)S(1)} %shard_map.174.d_ref), channel_id=1, source_target_pairs={{0,2},{2,0},{1,3},{3,1},{4,6},{6,4},{5,7},{7,5},{8,10},{10,8},{9,1... | collective-permute-start | bytes 1179656 | tf_op jit(solution)/shard_map/ppermute | solution.py:585
  87.6 15.4 %collective-permute-start.19 = (bf16[4,96,768]{2,1,0:T(8,128)(2,1)S(1)}, bf16[4,96,768]{2,1,0:T(8,128)(2,1)S(1)}, u32[]{:S(2)}, u32[]{:S(2)}) collective-permute-start(bf16[4,96,768]{2,1,0:T(8,128)(2,1)S(1)} %get-tuple-element.116), channel_id=1, source_target_pairs={{0,8},{4,12},{8,0},{12,4},{16,24},{20,28},{24,16},{28,20},{1,9},{5... | collective-permute-start | bytes 1769480 | tf_op jit(solution)/shard_map/ppermute | solution.py:588
  90.6 33.2 %collective-permute-start.27 = (bf16[4,96,768]{2,1,0:T(8,128)(2,1)S(1)}, bf16[4,96,768]{2,1,0:T(8,128)(2,1)S(1)}, u32[]{:S(2)}, u32[]{:S(2)}) collective-permute-start(bf16[4,96,768]{2,1,0:T(8,128)(2,1)S(1)} %get-tuple-element.126), channel_id=1, source_target_pairs={{0,4},{4,0},{8,12},{12,8},{16,20},{20,16},{24,28},{28,24},{1,5},{5... | collective-permute-start | bytes 1769480 | tf_op jit(solution)/shard_map/ppermute | solution.py:588
  107.9 15.8 %collective-permute-start.22 = (bf16[4,96,448]{2,1,0:T(8,128)(2,1)S(1)}, bf16[4,96,448]{2,1,0:T(8,128)(2,1)S(1)}, u32[]{:S(2)}, u32[]{:S(2)}) collective-permute-start(bf16[4,96,448]{2,1,0:T(8,128)(2,1)S(1)} %get-tuple-element.146), channel_id=1, source_target_pairs={{0,8},{4,12},{8,0},{12,4},{16,24},{20,28},{24,16},{28,20},{1,9},{5... | collective-permute-start | bytes 1032200 | tf_op jit(solution)/shard_map/ppermute | solution.py:588
  109.7 9.9 %collective-permute-start.31 = (bf16[2,96,768]{2,1,0:T(8,128)(2,1)S(1)}, bf16[2,96,768]{2,1,0:T(8,128)(2,1)S(1)}, u32[]{:S(2)}, u32[]{:S(2)}) collective-permute-start(bf16[2,96,768]{2,1,0:T(8,128)(2,1)S(1)} %get-tuple-element.132), channel_id=1, source_target_pairs={{0,4},{4,0},{8,12},{12,8},{16,20},{20,16},{24,28},{28,24},{1,5},{5... | collective-permute-start | bytes 884744 | tf_op jit(solution)/shard_map/ppermute | solution.py:588
  110.6 13.0 %collective-permute-start.21 = (bf16[4,96,384]{2,1,0:T(8,128)(2,1)S(1)}, bf16[4,96,384]{2,1,0:T(8,128)(2,1)S(1)}, u32[]{:S(2)}, u32[]{:S(2)}) collective-permute-start(bf16[4,96,384]{2,1,0:T(8,128)(2,1)S(1)} %get-tuple-element.144), channel_id=1, source_target_pairs={{0,4},{4,0},{8,12},{12,8},{16,20},{20,16},{24,28},{28,24},{1,5},{5... | collective-permute-start | bytes 884744 | tf_op jit(solution)/shard_map/ppermute | solution.py:588
  119.7 11.2 %collective-permute-start.32 = (bf16[1,96,768]{2,1,0:T(8,128)(2,1)S(1)}, bf16[1,96,768]{2,1,0:T(8,128)(2,1)S(1)}, u32[]{:S(2)}, u32[]{:S(2)}) collective-permute-start(bf16[1,96,768]{2,1,0:T(8,128)(2,1)S(1)} %get-tuple-element.165), channel_id=1, source_target_pairs={{0,16},{4,20},{8,24},{12,28},{16,0},{20,4},{24,8},{28,12},{1,17},{... | collective-permute-start | bytes 442376 | tf_op jit(solution)/shard_map/ppermute | solution.py:588
  123.9 12.5 %collective-permute-start.28 = (bf16[2,96,768]{2,1,0:T(8,128)(2,1)S(1)}, bf16[2,96,768]{2,1,0:T(8,128)(2,1)S(1)}, u32[]{:S(2)}, u32[]{:S(2)}) collective-permute-start(bf16[2,96,768]{2,1,0:T(8,128)(2,1)S(1)} %get-tuple-element.160), channel_id=1, source_target_pairs={{0,8},{4,12},{8,0},{12,4},{16,24},{20,28},{24,16},{28,20},{1,9},{5... | collective-permute-start | bytes 884744 | tf_op jit(solution)/shard_map/ppermute | solution.py:588
  124.5 10.8 %collective-permute-start.24 = (bf16[2,96,448]{2,1,0:T(8,128)(2,1)S(1)}, bf16[2,96,448]{2,1,0:T(8,128)(2,1)S(1)}, u32[]{:S(2)}, u32[]{:S(2)}) collective-permute-start(bf16[2,96,448]{2,1,0:T(8,128)(2,1)S(1)} %get-tuple-element.150), channel_id=1, source_target_pairs={{0,4},{4,0},{8,12},{12,8},{16,20},{20,16},{24,28},{28,24},{1,5},{5... | collective-permute-start | bytes 516104 | tf_op jit(solution)/shard_map/ppermute | solution.py:588
  125.4 9.9 %collective-permute-start.23 = (bf16[2,96,384]{2,1,0:T(8,128)(2,1)S(1)}, bf16[2,96,384]{2,1,0:T(8,128)(2,1)S(1)}, u32[]{:S(2)}, u32[]{:S(2)}) collective-permute-start(bf16[2,96,384]{2,1,0:T(8,128)(2,1)S(1)} %get-tuple-element.148), channel_id=1, source_target_pairs={{0,8},{4,12},{8,0},{12,4},{16,24},{20,28},{24,16},{28,20},{1,9},{5... | collective-permute-start | bytes 442376 | tf_op jit(solution)/shard_map/ppermute | solution.py:588
  129.3 12.1 %collective-permute-start.20 = (bf16[128,768]{1,0:T(8,128)(2,1)S(1)}, bf16[128,768]{1,0:T(8,128)(2,1)S(1)}, u32[]{:S(2)}, u32[]{:S(2)}) collective-permute-start(bf16[128,768]{1,0:T(8,128)(2,1)S(1)} %get-tuple-element.142), channel_id=1, source_target_pairs={{0,2},{2,0},{1,3},{3,1},{4,6},{6,4},{5,7},{7,5},{8,10},{10,8},{9,1... | collective-permute-start | bytes 589832 | tf_op jit(solution)/shard_map/ppermute | solution.py:585
  130.9 21.0 %collective-permute-start.33 = (bf16[96,768]{1,0:T(8,128)(2,1)S(1)}, bf16[96,768]{1,0:T(8,128)(2,1)S(1)}, u32[]{:S(2)}, u32[]{:S(2)}) collective-permute-start(bf16[96,768]{1,0:T(8,128)(2,1)S(1)} %shard_map.190), channel_id=1, source_target_pairs={{0,2},{2,0},{1,3},{3,1},{4,6},{6,4},{5,7},{7,5},{8,10},{10,8},{9,1... | collective-permute-start | bytes 442376 | tf_op jit(solution)/shard_map/ppermute | solution.py:585
  135.4 13.3 %collective-permute-start.25 = (bf16[1,96,832]{2,1,0:T(8,128)(2,1)S(1)}, bf16[1,96,832]{2,1,0:T(8,128)(2,1)S(1)}, u32[]{:S(2)}, u32[]{:S(2)}) collective-permute-start(bf16[1,96,832]{2,1,0:T(8,128)(2,1)S(1)} %get-tuple-element.152), channel_id=1, source_target_pairs={{0,16},{4,20},{8,24},{12,28},{16,0},{20,4},{24,8},{28,12},{1,17},{... | collective-permute-start | bytes 479240 | tf_op jit(solution)/shard_map/ppermute | solution.py:588
  136.4 14.7 %collective-permute-start.29 = (bf16[1,96,768]{2,1,0:T(8,128)(2,1)S(1)}, bf16[1,96,768]{2,1,0:T(8,128)(2,1)S(1)}, u32[]{:S(2)}, u32[]{:S(2)}) collective-permute-start(bf16[1,96,768]{2,1,0:T(8,128)(2,1)S(1)} %get-tuple-element.162), channel_id=1, source_target_pairs={{0,16},{4,20},{8,24},{12,28},{16,0},{20,4},{24,8},{28,12},{1,17},{... | collective-permute-start | bytes 442376 | tf_op jit(solution)/shard_map/ppermute | solution.py:588
  148.7 6.6 %collective-permute-start.26 = (bf16[96,832]{1,0:T(8,128)(2,1)S(1)}, bf16[96,832]{1,0:T(8,128)(2,1)S(1)}, u32[]{:S(2)}, u32[]{:S(2)}) collective-permute-start(bf16[96,832]{1,0:T(8,128)(2,1)S(1)} %shard_map.184.near_ref), channel_id=1, source_target_pairs={{0,2},{2,0},{1,3},{3,1},{4,6},{6,4},{5,7},{7,5},{8,10},{10,8},{9,1... | collective-permute-start | bytes 479240 | tf_op jit(solution)/shard_map/ppermute | solution.py:585
  151.1 6.2 %collective-permute-start.30 = (bf16[96,768]{1,0:T(8,128)(2,1)S(1)}, bf16[96,768]{1,0:T(8,128)(2,1)S(1)}, u32[]{:S(2)}, u32[]{:S(2)}) collective-permute-start(bf16[96,768]{1,0:T(8,128)(2,1)S(1)} %shard_map.188), channel_id=1, source_target_pairs={{0,2},{2,0},{1,3},{3,1},{4,6},{6,4},{5,7},{7,5},{8,10},{10,8},{9,1... | collective-permute-start | bytes 442376 | tf_op jit(solution)/shard_map/ppermute | solution.py:585
  (7 other events, 92.6 us)

commit v5 on v4

--- a/solution.py
+++ b/solution.py
@@ -303,15 +303,15 @@
     n = qkv.shape[2] // 2
     for i in range(3):
         w_ref[:, i * n : (i + 1) * n] = jnp.where(c == 0, qkv[i, :, :n], qkv[i, :, n:])
-    first = w_ref.shape[1]
-    row = lax.broadcasted_iota(jnp.int32, (2, first - 3 * n), 0)
-    lane = lax.broadcasted_iota(jnp.int32, (2, first - 3 * n), 1)
+    m = out.shape[1] // 2
+    extra = pack_ref.shape[1] - 3 * n - m
+    row = lax.broadcasted_iota(jnp.int32, (2, extra), 0)
+    lane = lax.broadcasted_iota(jnp.int32, (2, extra), 1)
     cols = mul(gain[...], (row == lane).astype(jnp.bfloat16), 0, 0)
     cols = cols + mul(bias[...], (row + 2 == lane).astype(jnp.bfloat16), 0, 0)
-    w_ref[:, 3 * n :] = cols.astype(jnp.bfloat16)
-    m = out.shape[1] // 2
-    pack_ref[:, 0:first] = w_ref[...]
-    pack_ref[:, first:] = jnp.where(c == 0, out[:, :m], out[:, m:])
+    pack_ref[:, 0:m] = jnp.where(c == 0, out[:, :m], out[:, m:])
+    pack_ref[:, m : m + extra] = cols.astype(jnp.bfloat16)
+    pack_ref[:, m + extra :] = w_ref[...]
 
 
 def pack_second_body(up_hbm, down_hbm, up_ref, down_ref, up, down, sems):
@@ -322,7 +322,7 @@
 
 def attend_body(
     own_ref, far_ref, w0, w1, w2, w3, w4, w5, bias_ref,
-    o_ref, qkv_ref, lse_ref, vec_ref, x_ref, w_ref, p_scr, v_scr,
+    o_ref, qkv_ref, lse_ref, x_ref, w_ref, p_scr, v_scr,
 ):
     width = o_ref.shape[1]
     rows = x_ref.shape[0]
@@ -331,16 +331,11 @@
     for t in range(2):
         x_ref[pl.ds((2 * t + c) * part, part), :] = own_ref[t * part : (t + 1) * part, :]
         x_ref[pl.ds((2 * t + 1 - c) * part, part), :] = far_ref[t * part : (t + 1) * part, :]
-    place((w0, w1, w2, w3, w4, w5), w_ref, DIRECT)
+    place((w0, w1, w2, w3, w4, w5), w_ref, DIRECT, w4.shape[1] - w_ref.shape[1])
     scale = 1.0 / math.sqrt(HD)
     w = w_ref[...]
     qkv = mul(x_ref[...], w, 1, 0).astype(jnp.bfloat16)
-    qkv_ref[...] = qkv[:, : 3 * width]
-    vec = w[:, 3 * width :]
-    unit = (
-        lax.broadcasted_iota(jnp.int32, (8, vec.shape[1]), 0) == lax.broadcasted_iota(jnp.int32, (8, vec.shape[1]), 1)
-    ).astype(jnp.bfloat16)
-    vec_ref[...] = mul(unit, vec, 1, 1)
+    qkv_ref[...] = qkv
     q, k, v = [qkv[:, i * width : (i + 1) * width] for i in range(3)]
     lse_ref[...] = jnp.zeros_like(lse_ref)
     blocks = bias_ref.shape[0] // (width // HD)
@@ -362,9 +357,22 @@
     mine_ref[...] = value_of(pl.ds(t * half, half))
 
 
-def project_body(ways, window, o_ref, *refs):
+def project_body(ways, o_ref, *refs):
     *pieces, mine_ref, theirs_ref, w_ref = refs
-    place(pieces, w_ref, ways, window)
+    place(pieces, w_ref, ways)
+    split_rows(lambda rows: mul(o_ref[rows, :], w_ref[...], 1, 1), mine_ref, theirs_ref)
+
+
+def project_out_body(ways, o_ref, *refs):
+    *pieces, mine_ref, theirs_ref, w_ref, vec_ref, scr = refs
+    place(pieces, scr, ways)
+    n = w_ref.shape[1]
+    w_ref[...] = scr[:, 0:n]
+    extra = scr.shape[1] - n
+    unit = (
+        lax.broadcasted_iota(jnp.int32, (8, extra), 0) == lax.broadcasted_iota(jnp.int32, (8, extra), 1)
+    ).astype(jnp.bfloat16)
+    vec_ref[...] = mul(unit, scr[:, n:], 1, 1)
     split_rows(lambda rows: mul(o_ref[rows, :], w_ref[...], 1, 1), mine_ref, theirs_ref)
 
 
@@ -443,6 +451,11 @@
     deal(own_ref, away_ref, scr, order)
 
 
+def deal_two(own_ref, away_ref, own2_ref, away2_ref, scr):
+    deal(own_ref, away_ref, scr, (1, 2, 4))
+    deal(own2_ref, away2_ref, scr, (2, 1, 4), own_ref.shape[2])
+
+
 def fold_pair(own_ref, got_ref, keep_ref, send_ref):
     half = keep_ref.shape[0]
     keep_ref[...] = own_ref[0:half] + got_ref[0:half].astype(jnp.float32)
@@ -484,9 +497,9 @@
 
 
 def attend_back_body(
-    da_ref, w_out_ref, w_ref, qkv_ref, o_ref, lse_ref, bias_ref, x_ref,
-    own_ref, away_ref, own2_ref, away2_ref, mine_ref, theirs_ref,
-    p_scr, dr_scr, q_scr, do_scr, all_scr, grad_scr,
+    da_ref, w_out_ref, qkv_ref, o_ref, lse_ref, bias_ref, x_ref,
+    own_ref, away_ref, own2_ref, away2_ref, all_scr,
+    p_scr, dr_scr, q_scr, do_scr, grad_scr,
 ):
     width = o_ref.shape[1]
     rows = x_ref.shape[0]
@@ -514,17 +527,18 @@
     all_scr[:, width : 2 * width] = mul(dr_scr[...], q_scr[...], 1, 0).astype(jnp.bfloat16)
     all_scr[:, 2 * width : 3 * width] = mul(p_scr[...], do_scr[...], 1, 0).astype(jnp.bfloat16)
     vec = sum(da_ref[i, half : half + 16, :].astype(jnp.float32) for i in range(2)).astype(jnp.bfloat16)
-    extra = w_ref.shape[1] - 3 * width
+    extra = grad_scr.shape[1] - 4 * width
     unit = (
         lax.broadcasted_iota(jnp.int32, (16, extra), 0) == lax.broadcasted_iota(jnp.int32, (16, extra), 1)
     ).astype(jnp.bfloat16)
     grad_scr[...] = jnp.concatenate(
         [mul(x_ref[...], all_scr[...], 0, 0), mul(vec, unit, 0, 0), mul(da, o_ref[...], 0, 0)], axis=1
     )
-    deal(own_ref, away_ref, grad_scr, (1, 2, 4))
-    deal(own2_ref, away2_ref, grad_scr, (2, 1, 4), own_ref.shape[2])
-    w = w_ref[:, 0 : 3 * width]
-    split_rows(lambda r: mul(all_scr[r, :], w, 1, 1), mine_ref, theirs_ref)
+    deal_two(own_ref, away_ref, own2_ref, away2_ref, grad_scr)
+
+
+def input_body(grad_ref, w_ref, mine_ref, theirs_ref):
+    split_rows(lambda rows: mul(grad_ref[rows, :], w_ref[...], 1, 1), mine_ref, theirs_ref)
 
 
 def fold_input_body(mine_ref, both_ref, dz_ref, keep_ref, send_ref):
@@ -602,7 +616,7 @@
     own_blocks = rows // BLOCK
     per = own_blocks // 2
     total_rows = 2 * rows
-    first = 3 * cols + 4 + (-(3 * cols + 4)) % 128
+    extra = 4 + (-(4 * cols + 4)) % 64
 
     half = ((part, width), bf16)
     hbm = pl.BlockSpec(memory_space=pltpu.HBM)
@@ -615,16 +629,17 @@
 
     x_far = swap_ctx(inputs)
     w1, pack_one = packed(
-        pack_first_body, (first, first + cols), qkv_weight, norm_gains, norm_biases, out_weight.T
+        pack_first_body, (3 * cols, 4 * cols + extra), qkv_weight, norm_gains, norm_biases, out_weight.T
     )
     w1_near = [swap_dp(w1, 2 * k) for k in range(1, n_out)]
     far_one = swap_dp(pack_one, 1)
     w_up, w_down = packed(pack_second_body, (units, units), up_weight, down_weight.T)
     picks_far = swap_ctx(random_blocks)
     w1_near = all_after(w1_near, far_one)
-    w1_pieces = [w1, *w1_near, far_one, swap_dp(jnp.stack(w1_near), 1)]
-    out_pieces = [jnp.stack([pack_one[:, first:], far_one[:, first:]])]
-    out_pieces[0] = after(out_pieces[0], *w1_near)
+    w1_rest = jnp.stack(w1_near)
+    w1_pieces = [w1, *w1_near, far_one, swap_dp(w1_rest, 1)]
+    out_pieces = [jnp.stack([pack_one[:, : cols + extra], far_one[:, : cols + extra]])]
+    out_pieces[0] = after(out_pieces[0], w1_rest)
     out_pieces.append(swap_dp(out_pieces[0], 4))
     out_pieces.append(swap_dp(jnp.concatenate(out_pieces), 2))
     up_pieces, down_pieces = all_after([w_up[None], w_down[None]], out_pieces[1])
@@ -646,11 +661,11 @@
     low = [((rows, width), bf16)]
     wide = [((rows, width), f32)]
     small = [((8, width), f32)]
-    o, qkv, lse, vecs, x_all, w1_all = call(
+    o, qkv, lse, x_all, w1_all = call(
         attend_body,
         [
-            ((total_rows, cols), bf16), ((total_rows, 3 * cols), bf16), ((8, total_rows), f32), ((8, width), f32),
-            ((total_rows, width), bf16), ((width, first), bf16),
+            ((total_rows, cols), bf16), ((total_rows, 3 * cols), bf16), ((8, total_rows), f32),
+            ((total_rows, width), bf16), ((width, 3 * cols), bf16),
         ],
         inputs, x_far, *w1_pieces, bias,
         scratch=[((heads * total_rows, total_rows), bf16), ((heads * total_rows, cols), bf16)],
@@ -660,8 +675,9 @@
     def sum_tp(mine, theirs):
         return call(add_tp_body, low, mine, both_tp(theirs))[0]
 
-    mine, theirs, w_out_all = call(
-        functools.partial(project_body, OUT_WAYS, 0), wide + low + [((width, cols), bf16)], o, *out_pieces
+    mine, theirs, w_out_all, vecs = call(
+        functools.partial(project_out_body, OUT_WAYS), wide + low + [((width, cols), bf16)] + small, o, *out_pieces,
+        scratch=[((width, cols + extra), bf16)],
     )
     theirs, up_pieces[1], down_pieces[1] = all_after([theirs, up_pieces[1], down_pieces[1]])
     up_pieces.append(swap_dp(jnp.concatenate(up_pieces), 2))
@@ -675,7 +691,7 @@
     square = [((width, units), bf16)]
     y_all = both_tp(y_low, True)
     u, slope, w_up_all = call(ffn_body, flat * 2 + square, y_all, *up_pieces)
-    mine, theirs, w_down_all = call(functools.partial(project_body, DOWN_WAYS, 0), wide + low + square, u, *down_pieces)
+    mine, theirs, w_down_all = call(functools.partial(project_body, DOWN_WAYS), wide + low + square, u, *down_pieces)
     m = sum_tp(mine, theirs)
     m_far = swap_ctx(m)
     out, dz2, dm_low, grad2 = call(
@@ -685,22 +701,27 @@
         scratch=wide * 2,
     )
 
-    def dealt(n):
-        return [((n_out, shard, n), f32), ((n_out, shard, n), bf16)]
-
-    def kept(k, n):
-        return [((k, shard, n), f32), ((k, shard, n), bf16)]
+    def pairs(k, *widths):
+        return [((k, shard, n), dtype) for n in widths for dtype in (f32, bf16)]
+
+    def cut(n):
+        most = n * 2 // 3 // 128 * 128
+        return most, n - most
 
     def fold(own, got):
-        return call(fold_body, kept(own.shape[0] // 2, own.shape[2]), own, got)
-
-    def last_sum(keep, send, bits):
+        return call(fold_body, pairs(own.shape[0] // 2, own.shape[2]), own, got)
+
+    def fold_first(own, away, own2, away2):
+        return call(fold_two_body, pairs(2, own.shape[2], own2.shape[2]), own, swap_dp(away, 1), own2, swap_dp(away2, 2))
+
+    def fold_third(keep, send, bits):
         total = call(fold_last_body, [(keep.shape[1:], bf16)], keep, swap_dp(send, bits))[0]
         return total, swap_ctx(total)
 
-    down_order, up_order = (2, 1, 4), (1, 2, 4)
     dm_all = both_tp(dm_low, True)
-    down_own, down_away = call(functools.partial(grad_body, down_order), dealt(units), dm_all, u, scratch=[((width, units), f32)])
+    down_own, down_away = call(
+        functools.partial(grad_body, (2, 1, 4)), pairs(n_out, units), dm_all, u, scratch=[((width, units), f32)]
+    )
     dm_all = after(dm_all, down_away)
     dhid, mine, theirs = call(
         ffn_back_body, flat + wide + low, dm_all, slope, w_down_all, w_up_all
@@ -708,43 +729,45 @@
     d = sum_tp(mine, theirs)
     d_far = swap_ctx(d)
     y_late, dhid = lax.optimization_barrier((y_all, dhid, d))[:2]
-    up_own, up_away = call(functools.partial(grad_body, up_order), dealt(units), y_late, dhid, scratch=[((width, units), f32)])
+    up = call(
+        functools.partial(grad_body, (1, 4, 2)), pairs(n_out, units), y_late, dhid, scratch=[((width, units), f32)]
+    )
+    down_keep, down_send = fold(down_own, swap_dp(down_away, 2))
+    output = call(copy_body, low, both_tp(after(out, up[1]), True))[0]
     dz1, da_low = call(
-        norm_one_back_body, wide + [((rows + 16, width), bf16)], dz2, d, after(d_far, up_away), n1, r1, vecs, grad2
-    )
-    down_keep, down_send = fold(down_own, swap_dp(down_away, down_order[0]))
-    last = first + cols
-    left = last // 256 * 128
-    own, away, own2, away2, mine, theirs = call(
+        norm_one_back_body, wide + [((rows + 16, width), bf16)], dz2, d, after(d_far, up[1], down_send, output), n1, r1, vecs, grad2
+    )
+    last = 4 * cols + extra
+    *tail, dqkv = call(
         attend_back_body,
-        dealt(left) + dealt(last - left) + wide + low,
-        after(both_tp(da_low), down_send), w_out_all, w1_all, qkv, o, lse, bias, x_all,
+        pairs(n_out, *cut(last)) + [((total_rows, 3 * cols), bf16)],
+        after(both_tp(da_low), down_send), w_out_all, qkv, o, lse, bias, x_all,
+        flops=2 * 10**10,
         scratch=[
             ((total_rows, heads * total_rows), bf16),
             ((total_rows, heads * total_rows), bf16),
             ((heads * total_rows, cols), bf16),
             ((heads * total_rows, cols), bf16),
-            ((total_rows, 3 * cols), bf16),
             ((width, last), f32),
         ],
     )
-    up_own = after(up_own, theirs)
+    mine, theirs = call(input_body, wide + low, dqkv, w1_all)
+    down = fold(after(down_keep, theirs), swap_dp(down_send, 1))
+    theirs = after(theirs, down[1])
     keep, send = call(fold_input_body, [((part, width), f32), half], mine, both_tp(theirs), dz1)
-    down_keep, down_send = fold(down_keep, swap_dp(down_send, down_order[1]))
-    keep1, send1, keep2, send2 = call(
-        fold_two_body, kept(2, left) + kept(2, last - left),
-        own, swap_dp(away, 1), own2, swap_dp(away2, 2),
-    )
-    up_keep, up_send = fold(after(up_own, keep1), swap_dp(up_away, up_order[0]))
-    keep1, send1 = call(
-        fold_join_body, kept(1, last), keep1, swap_dp(send1, 2), keep2, swap_dp(send2, 1)
-    )
-    up_keep, up_send = fold(after(up_keep, keep1), swap_dp(up_send, up_order[1]))
-    grad_down, down_far = last_sum(down_keep, down_send, 4)
-    grad_up, up_far = last_sum(up_keep, up_send, 4)
-    grad_1, far_1 = last_sum(keep1, send1, 4)
-    dx = call(last_input_body, [half], keep, swap_ctx(send))[0]
-    output, input_grad = [call(copy_body, low, both_tp(v, True))[0] for v in (out, dx)]
+    up = fold(after(up[0], mine), swap_dp(up[1], 1))
+    keep1, send1, keep2, send2 = fold_first(*all_after(tail[:1], send), *tail[1:])
+    got1, got2 = swap_dp(send1, 2), swap_dp(send2, 1)
+    dx_far = swap_ctx(send)
+    up = fold(after(up[0], keep1), swap_dp(up[1], 4))
+    grad_down, down_far = fold_third(*all_after(down[:1], keep1), down[1], 4)
+    keep1 = after(keep1, dx_far, up[1], grad_down)
+    tail = call(fold_join_body, pairs(1, last), keep1, got1, keep2, got2)
+    grad_1, far_1 = fold_third(*tail, 4)
+    grad_up, up_far = fold_third(*all_after(up[:1], grad_1), up[1], 2)
+    dx = call(last_input_body, [half], keep, after(dx_far, grad_1))[0]
+    input_grad = call(copy_body, low, both_tp(dx, True))[0]
+    grad_1 = after(grad_1, input_grad)
 
     def both_ctx(g, far):
         return jnp.where(c == 0, jnp.concatenate([g, far], 1), jnp.concatenate([far, g], 1)).astype(f32)

time: 159 us -> 152 us (0.956)
  waiting for transfers between devices: 61 us -> 53.8 us
    ppermute x10, waiting for transfers between devices: 25 us -> 20.2 us  [swap_ctx(): return lax.ppermute(v, 'ctx', pair)]
    ppermute x24, waiting for transfers between devices: 35.9 us -> 33.6 us  [swap_dp(): return lax.ppermute(v, 'dp', [(i, i ^ bits) for i in range(n_dp)])]
    pallas_call x30 -> x31, Pallas kernels: 23.3 us -> 23.8 us  [call(): pl.pallas_call(body, out_shape=shapes, in_specs=specs, out_specs=[pl.Bloc...]
  transfers between devices with their start and end apart: 34 -> 34, of which waited for: 18 -> 17; matrix products, arithmetic and copies ran while one was open for 3% -> 4% of each run, Pallas kernels for 10% -> 12%
where the time goes in v5:
time: 152 us; the launch traced here: 151 us
  waiting for transfers between devices  53.8 us (35%)
  starting transfers between devices  45 us (30%)
  Pallas kernels  23.8 us (16%)
  blocking collectives  20.9 us (14%)
  other arithmetic  4.08 us (3%)
  local copies, waits for them, and re-layouts  1.95 us (1%)
  between operations  1.74 us (1%)
    ppermute x24, starting transfers between devices, swap_dp(): return lax.ppermute(v, 'dp', [(i, i ^ bits) for i in range(n_dp)])  33.8 us
    ppermute x24, waiting for transfers between devices, swap_dp(): return lax.ppermute(v, 'dp', [(i, i ^ bits) for i in range(n_dp)])  33.6 us
    pallas_call x31, Pallas kernels, call(): pl.pallas_call(body, out_shape=shapes, in_specs=specs, out_specs=[pl.Bloc...  23.8 us
    all_gather x9, blocking collectives, both_tp(): return lax.all_gather(v, 'tp', axis=0, tiled=tiled)  20.9 us
    ppermute x10, waiting for transfers between devices, swap_ctx(): return lax.ppermute(v, 'ctx', pair)  20.2 us
    ppermute x10, starting transfers between devices, swap_ctx(): return lax.ppermute(v, 'ctx', pair)  11.2 us
  transfers between devices with their start and end apart: 34, of which 17 were waited for; matrix products, arithmetic and copies ran while one was open for 4% of the time, Pallas kernels for 12%

profile of v5, /device:TPU:0, one launch (start us, length us, event | category | flops | bytes accessed | tf_op | source)
XLA Modules:
  0.0 151.3 jit_solution(10881372375686728614)
XLA Ops:
  0.6 2.0 %shard_map.161 = (bf16[96,576]{1,0:T(8,128)(2,1)}, bf16[96,832]{1,0:T(8,128)(2,1)}) custom-call(bf16[3,96,384]{2,1,0:T(8,128)(2,1)} %qkv_hbm.1, bf16[2,96]{1,0:T(2,128)(2,1)} %gain_hbm.1, bf16[2,96]{1,0:T(2,128)(2,1)} %bias_hbm.1, bf16[96,384]{1,0:T(8,128)(2,1)} %bitcast.48), custom_call_target="tpu_custom_call" | custom-call | tf_op jit(solution)/shard_map/pallas_call | solution.py:240
  2.6 3.1 %collective-permute-start.1 = (bf16[96,576]{1,0:T(8,128)(2,1)}, bf16[96,576]{1,0:T(8,128)(2,1)S(1)}, u32[]{:S(2)}, u32[]{:S(2)}) collective-permute-start(bf16[96,576]{1,0:T(8,128)(2,1)} %get-tuple-element.97.w0), channel_id=1, source_target_pairs={{0,8},{4,12},{8,0},{12,4},{16,24},{20,28},{24,16},{28,20},{1,9},{5... | collective-permute-start | bytes 331784 | tf_op jit(solution)/shard_map/ppermute | solution.py:602
  5.7 2.6 %collective-permute-start.2 = (bf16[96,576]{1,0:T(8,128)(2,1)}, bf16[96,576]{1,0:T(8,128)(2,1)S(1)}, u32[]{:S(2)}, u32[]{:S(2)}) collective-permute-start(bf16[96,576]{1,0:T(8,128)(2,1)} %get-tuple-element.97.w0), channel_id=1, source_target_pairs={{0,16},{4,20},{8,24},{12,28},{16,0},{20,4},{24,8},{28,12},{1,17},{... | collective-permute-start | bytes 331784 | tf_op jit(solution)/shard_map/ppermute | solution.py:602
  8.3 1.7 %collective-permute-start.4 = (bf16[96,832]{1,0:T(8,128)(2,1)}, bf16[96,832]{1,0:T(8,128)(2,1)S(1)}, u32[]{:S(2)}, u32[]{:S(2)}) collective-permute-start(bf16[96,832]{1,0:T(8,128)(2,1)} %get-tuple-element.98), channel_id=1, source_target_pairs={{0,4},{4,0},{8,12},{12,8},{16,20},{20,16},{24,28},{28,24},{1,5},{5... | collective-permute-start | bytes 479240 | tf_op jit(solution)/shard_map/ppermute | solution.py:602
  13.1 1.8 %shard_map.164 = (bf16[96,768]{1,0:T(8,128)(2,1)}, bf16[96,768]{1,0:T(8,128)(2,1)}) custom-call(bf16[96,1536]{1,0:T(8,128)(2,1)} %up_hbm.1, bf16[96,1536]{1,0:T(8,128)(2,1)} %bitcast.46), custom_call_target="tpu_custom_call" | custom-call | tf_op jit(solution)/shard_map/pallas_call | solution.py:240
  19.1 2.9 %collective-permute-start.7 = (bf16[2,96,256]{2,1,0:T(8,128)(2,1)S(1)}, bf16[2,96,256]{2,1,0:T(8,128)(2,1)S(1)}, u32[]{:S(2)}, u32[]{:S(2)}) collective-permute-start(bf16[2,96,256]{2,1,0:T(8,128)(2,1)S(1)} %pad_maximum_fusion.6.refs_0_), channel_id=1, source_target_pairs={{0,16},{4,20},{8,24},{12,28},{16,0},{20,4},{24,8},{28,12},{1,17},{... | collective-permute-start | bytes 294920 | tf_op jit(solution)/shard_map/ppermute | solution.py:602
  24.9 1.7 %collective-permute-start.8 = (bf16[4,96,256]{2,1,0:T(8,128)(2,1)S(1)}, bf16[4,96,256]{2,1,0:T(8,128)(2,1)S(1)}, u32[]{:S(2)}, u32[]{:S(2)}) collective-permute-start(bf16[4,96,256]{2,1,0:T(8,128)(2,1)S(1)} %pad_maximum_fusion.5), channel_id=1, source_target_pairs={{0,8},{4,12},{8,0},{12,4},{16,24},{20,28},{24,16},{28,20},{1,9},{5... | collective-permute-start | bytes 589832 | tf_op jit(solution)/shard_map/ppermute | solution.py:602
  32.0 2.9 %shard_map.162 = (bf16[512,192]{1,0:T(8,128)(2,1)S(1)}, bf16[512,576]{1,0:T(8,128)(2,1)S(1)}, f32[8,512]{1,0:T(8,128)S(1)}, bf16[512,768]{1,0:T(8,128)(2,1)S(1)}, bf16[768,576]{1,0:T(8,128)(2,1)S(1)}) custom-call(bf16[256,768]{1,0:T(8,128)(2,1)S(1)} %copy-done.2, bf16[256,768]{1,0:T(8,128)(2,1)S(1)} %collective-permute-done.far_ref, ...), custom_call_target="tpu_custom_call" | custom-call | tf_op jit(solution)/shard_map/pallas_call | solution.py:240
  35.4 3.4 %collective-permute-done.10.refs_1_ = bf16[1,96,768]{2,1,0:T(8,128)(2,1)S(1)} collective-permute-done((bf16[1,96,768]{2,1,0:T(8,128)(2,1)S(1)}, bf16[1,96,768]{2,1,0:T(8,128)(2,1)S(1)}, u32[]{:S(2)}, u32[]{:S(2)}) %collective-permute-start.10) | collective-permute-done | bytes 147488 | tf_op jit(solution)/shard_map/ppermute | solution.py:602
  42.0 2.4 %all-gather = bf16[512,768]{1,0:T(8,128)(2,1)S(1)} all-gather(bf16[256,768]{1,0:T(8,128)(2,1)S(1)} %get-tuple-element.111), channel_id=2, replica_groups=mesh['dp'=8,'ctx'=2,'tp'=2] {'tp'}, dimensions={0}, use_global_device_ids=true | all-gather | bytes 1179648 | tf_op jit(solution)/shard_map/all_gather | solution.py:596
  49.6 6.0 %collective-permute-done.12.far_ref = bf16[256,768]{1,0:T(8,128)(2,1)S(1)} collective-permute-done((bf16[256,768]{1,0:T(8,128)(2,1)S(1)}, bf16[256,768]{1,0:T(8,128)(2,1)S(1)}, u32[]{:S(2)}, u32[]{:S(2)}) %collective-permute-start.12) | collective-permute-done | bytes 393248 | tf_op jit(solution)/shard_map/ppermute | solution.py:599
  56.0 2.4 %all_gather.44.y_ref.left_ref = bf16[512,768]{1,0:T(8,128)(2,1)S(1)} all-gather(bf16[256,768]{1,0:T(8,128)(2,1)S(1)} %get-tuple-element.116), channel_id=1, replica_groups=mesh['dp'=8,'ctx'=2,'tp'=2] {'tp'}, dimensions={0}, use_global_device_ids=true | all-gather | bytes 1179648 | tf_op jit(solution)/shard_map/all_gather | solution.py:596
  58.4 2.8 %collective-permute-done.14.w3 = bf16[4,96,768]{2,1,0:T(8,128)(2,1)S(1)} collective-permute-done((bf16[4,96,768]{2,1,0:T(8,128)(2,1)S(1)}, bf16[4,96,768]{2,1,0:T(8,128)(2,1)S(1)}, u32[]{:S(2)}, u32[]{:S(2)}) %collective-permute-start.14) | collective-permute-done | bytes 589856 | tf_op jit(solution)/shard_map/ppermute | solution.py:602
  63.7 2.4 %all-gather.1 = bf16[512,768]{1,0:T(8,128)(2,1)S(1)} all-gather(bf16[256,768]{1,0:T(8,128)(2,1)S(1)} %get-tuple-element.121), channel_id=3, replica_groups=mesh['dp'=8,'ctx'=2,'tp'=2] {'tp'}, dimensions={0}, use_global_device_ids=true | all-gather | bytes 1179648 | tf_op jit(solution)/shard_map/all_gather | solution.py:596
  66.7 10.6 %collective-permute-done.17.far_ref = bf16[256,768]{1,0:T(8,128)(2,1)S(1)} collective-permute-done((bf16[256,768]{1,0:T(8,128)(2,1)S(1)}, bf16[256,768]{1,0:T(8,128)(2,1)S(1)}, u32[]{:S(2)}, u32[]{:S(2)}) %collective-permute-start.17) | collective-permute-done | bytes 393248 | tf_op jit(solution)/shard_map/ppermute | solution.py:599
  78.3 2.4 %all_gather.47.left_ref.dm_ref = bf16[512,768]{1,0:T(8,128)(2,1)S(1)} all-gather(bf16[256,768]{1,0:T(8,128)(2,1)S(1)} %get-tuple-element.123), channel_id=1, replica_groups=mesh['dp'=8,'ctx'=2,'tp'=2] {'tp'}, dimensions={0}, use_global_device_ids=true | all-gather | bytes 1179648 | tf_op jit(solution)/shard_map/all_gather | solution.py:596
  81.6 2.1 %collective-permute-start.19 = (bf16[4,96,768]{2,1,0:T(8,128)(2,1)S(1)}, bf16[4,96,768]{2,1,0:T(8,128)(2,1)S(1)}, u32[]{:S(2)}, u32[]{:S(2)}) collective-permute-start(bf16[4,96,768]{2,1,0:T(8,128)(2,1)S(1)} %get-tuple-element.124), channel_id=1, source_target_pairs={{0,8},{4,12},{8,0},{12,4},{16,24},{20,28},{24,16},{28,20},{1,9},{5... | collective-permute-start | bytes 1769480 | tf_op jit(solution)/shard_map/ppermute | solution.py:602
  83.7 1.8 %shard_map.172 = (bf16[512,768]{1,0:T(8,128)(2,1)S(1)}, f32[256,768]{1,0:T(8,128)S(1)}, bf16[256,768]{1,0:T(8,128)(2,1)S(1)}) custom-call(bf16[512,768]{1,0:T(8,128)(2,1)S(1)} %all_gather.47.left_ref.dm_ref, bf16[512,768]{1,0:T(8,128)(2,1)S(1)} %get-tuple-element.126.slope_ref, bf16[768,768]{1,0:T(8,128)(2,1)S(1)} %get-tuple-element.127.down_ref, ...), custom_call_target="tpu_custom_call" | custom-call | tf_op jit(solution)/shard_map/pallas_call | solution.py:240
  85.5 2.5 %all-gather.2 = bf16[512,768]{1,0:T(8,128)(2,1)S(1)} all-gather(bf16[256,768]{1,0:T(8,128)(2,1)S(1)} %get-tuple-element.131), channel_id=4, replica_groups=mesh['dp'=8,'ctx'=2,'tp'=2] {'tp'}, dimensions={0}, use_global_device_ids=true | all-gather | bytes 1179648 | tf_op jit(solution)/shard_map/all_gather | solution.py:596
  90.9 2.1 %all_gather.50.in_ref = bf16[256,768]{1,0:T(8,128)(2,1)S(1)} all-gather(bf16[128,768]{1,0:T(8,128)(2,1)S(1)} %get-tuple-element.135), channel_id=1, replica_groups=mesh['dp'=8,'ctx'=2,'tp'=2] {'tp'}, dimensions={0}, use_global_device_ids=true | all-gather | bytes 589824 | tf_op jit(solution)/shard_map/all_gather | solution.py:596
  93.7 3.6 %collective-permute-done.19.got_ref = bf16[4,96,768]{2,1,0:T(8,128)(2,1)S(1)} collective-permute-done((bf16[4,96,768]{2,1,0:T(8,128)(2,1)S(1)}, bf16[4,96,768]{2,1,0:T(8,128)(2,1)S(1)}, u32[]{:S(2)}, u32[]{:S(2)}) %collective-permute-start.19) | collective-permute-done | bytes 589856 | tf_op jit(solution)/shard_map/ppermute | solution.py:602
  99.8 2.4 %all-gather.3 = bf16[544,768]{1,0:T(8,128)(2,1)S(1)} all-gather(bf16[272,768]{1,0:T(8,128)(2,1)S(1)} %get-tuple-element.142), channel_id=5, replica_groups=mesh['dp'=8,'ctx'=2,'tp'=2] {'tp'}, dimensions={0}, use_global_device_ids=true | all-gather | bytes 1253376 | tf_op jit(solution)/shard_map/all_gather | solution.py:596
  102.3 4.4 %shard_map.178 = (f32[4,96,512]{2,1,0:T(8,128)S(1)}, bf16[4,96,512]{2,1,0:T(8,128)(2,1)S(1)}, f32[4,96,320]{2,1,0:T(8,128)S(1)}, bf16[4,96,320]{2,1,0:T(8,128)(2,1)S(1)}, bf16[512,576]{1,0:T(8,128)(2,1)S(1)}) custom-call(bf16[2,272,768]{2,1,0:T(8,128)(2,1)S(1)} %bitcast.42, bf16[768,192]{1,0:T(8,128)(2,1)S(1)} %get-tuple-element.144.w_out_ref, ...), custom_call_target="tpu_custom_call" | custom-call | flops 20000000000 | tf_op jit(solution)/shard_map/pallas_call | solution.py:240
  109.5 1.7 %collective-permute-start.25 = (bf16[2,96,768]{2,1,0:T(8,128)(2,1)S(1)}, bf16[2,96,768]{2,1,0:T(8,128)(2,1)S(1)}, u32[]{:S(2)}, u32[]{:S(2)}) collective-permute-start(bf16[2,96,768]{2,1,0:T(8,128)(2,1)S(1)} %get-tuple-element.168), channel_id=1, source_target_pairs={{0,16},{4,20},{8,24},{12,28},{16,0},{20,4},{24,8},{28,12},{1,17},{... | collective-permute-start | bytes 884744 | tf_op jit(solution)/shard_map/ppermute | solution.py:602
  112.3 2.4 %all-gather.4 = bf16[512,768]{1,0:T(8,128)(2,1)S(1)} all-gather(bf16[256,768]{1,0:T(8,128)(2,1)S(1)} %get-tuple-element.154), channel_id=6, replica_groups=mesh['dp'=8,'ctx'=2,'tp'=2] {'tp'}, dimensions={0}, use_global_device_ids=true | all-gather | bytes 1179648 | tf_op jit(solution)/shard_map/all_gather | solution.py:596
  116.3 4.8 %collective-permute-done.23.got2_ref = bf16[4,96,320]{2,1,0:T(8,128)(2,1)S(1)} collective-permute-done((bf16[4,96,320]{2,1,0:T(8,128)(2,1)S(1)}, bf16[4,96,320]{2,1,0:T(8,128)(2,1)S(1)}, u32[]{:S(2)}, u32[]{:S(2)}) %collective-permute-start.23) | collective-permute-done | bytes 245792 | tf_op jit(solution)/shard_map/ppermute | solution.py:602
  121.4 1.9 %collective-permute-start.26 = (bf16[1,96,768]{2,1,0:T(8,128)(2,1)S(1)}, bf16[1,96,768]{2,1,0:T(8,128)(2,1)S(1)}, u32[]{:S(2)}, u32[]{:S(2)}) collective-permute-start(bf16[1,96,768]{2,1,0:T(8,128)(2,1)S(1)} %get-tuple-element.153), channel_id=1, source_target_pairs={{0,16},{4,20},{8,24},{12,28},{16,0},{20,4},{24,8},{28,12},{1,17},{... | collective-permute-start | bytes 442376 | tf_op jit(solution)/shard_map/ppermute | solution.py:602
  126.2 5.5 %collective-permute-done.26.got_ref = bf16[1,96,768]{2,1,0:T(8,128)(2,1)S(1)} collective-permute-done((bf16[1,96,768]{2,1,0:T(8,128)(2,1)S(1)}, bf16[1,96,768]{2,1,0:T(8,128)(2,1)S(1)}, u32[]{:S(2)}, u32[]{:S(2)}) %collective-permute-start.26) | collective-permute-done | bytes 147488 | tf_op jit(solution)/shard_map/ppermute | solution.py:602
  132.3 2.6 %collective-permute-start.31 = (bf16[1,96,768]{2,1,0:T(8,128)(2,1)S(1)}, bf16[1,96,768]{2,1,0:T(8,128)(2,1)S(1)}, u32[]{:S(2)}, u32[]{:S(2)}) collective-permute-start(bf16[1,96,768]{2,1,0:T(8,128)(2,1)S(1)} %get-tuple-element.169), channel_id=1, source_target_pairs={{0,8},{4,12},{8,0},{12,4},{16,24},{20,28},{24,16},{28,20},{1,9},{5... | collective-permute-start | bytes 442376 | tf_op jit(solution)/shard_map/ppermute | solution.py:602
  136.1 5.2 %collective-permute-done.29.got_ref = bf16[1,96,832]{2,1,0:T(8,128)(2,1)S(1)} collective-permute-done((bf16[1,96,832]{2,1,0:T(8,128)(2,1)S(1)}, bf16[1,96,832]{2,1,0:T(8,128)(2,1)S(1)}, u32[]{:S(2)}, u32[]{:S(2)}) %collective-permute-start.29) | collective-permute-done | bytes 159776 | tf_op jit(solution)/shard_map/ppermute | solution.py:602
  144.5 2.1 %all_gather.55.in_ref = bf16[256,768]{1,0:T(8,128)(2,1)S(1)} all-gather(bf16[128,768]{1,0:T(8,128)(2,1)S(1)} %shard_map.188), channel_id=1, replica_groups=mesh['dp'=8,'ctx'=2,'tp'=2] {'tp'}, dimensions={0}, use_global_device_ids=true | all-gather | bytes 589824 | tf_op jit(solution)/shard_map/all_gather | solution.py:596
  148.7 1.7 %collective-permute-done.30.far_ref = bf16[96,832]{1,0:T(8,128)(2,1)S(1)} collective-permute-done((bf16[96,832]{1,0:T(8,128)(2,1)S(1)}, bf16[96,832]{1,0:T(8,128)(2,1)S(1)}, u32[]{:S(2)}, u32[]{:S(2)}) %collective-permute-start.30) | collective-permute-done | bytes 159776 | tf_op jit(solution)/shard_map/ppermute | solution.py:599
  (122 shorter events, 51.7 us)
Async XLA Ops:
  2.6 14.2 %collective-permute-start.1 = (bf16[96,576]{1,0:T(8,128)(2,1)}, bf16[96,576]{1,0:T(8,128)(2,1)S(1)}, u32[]{:S(2)}, u32[]{:S(2)}) collective-permute-start(bf16[96,576]{1,0:T(8,128)(2,1)} %get-tuple-element.97.w0), channel_id=1, source_target_pairs={{0,8},{4,12},{8,0},{12,4},{16,24},{20,28},{24,16},{28,20},{1,9},{5... | collective-permute-start | bytes 331784 | tf_op jit(solution)/shard_map/ppermute | solution.py:602
  5.7 12.5 %collective-permute-start.2 = (bf16[96,576]{1,0:T(8,128)(2,1)}, bf16[96,576]{1,0:T(8,128)(2,1)S(1)}, u32[]{:S(2)}, u32[]{:S(2)}) collective-permute-start(bf16[96,576]{1,0:T(8,128)(2,1)} %get-tuple-element.97.w0), channel_id=1, source_target_pairs={{0,16},{4,20},{8,24},{12,28},{16,0},{20,4},{24,8},{28,12},{1,17},{... | collective-permute-start | bytes 331784 | tf_op jit(solution)/shard_map/ppermute | solution.py:602
  8.3 10.0 %collective-permute-start.3 = (bf16[96,576]{1,0:T(8,128)(2,1)}, bf16[96,576]{1,0:T(8,128)(2,1)S(1)}, u32[]{:S(2)}, u32[]{:S(2)}) collective-permute-start(bf16[96,576]{1,0:T(8,128)(2,1)} %get-tuple-element.97.w0), channel_id=1, source_target_pairs={{0,24},{4,28},{8,16},{12,20},{16,8},{20,12},{24,0},{28,4},{1,25},{... | collective-permute-start | bytes 331784 | tf_op jit(solution)/shard_map/ppermute | solution.py:602
  8.3 10.0 %collective-permute-start.4 = (bf16[96,832]{1,0:T(8,128)(2,1)}, bf16[96,832]{1,0:T(8,128)(2,1)S(1)}, u32[]{:S(2)}, u32[]{:S(2)}) collective-permute-start(bf16[96,832]{1,0:T(8,128)(2,1)} %get-tuple-element.98), channel_id=1, source_target_pairs={{0,4},{4,0},{8,12},{12,8},{16,20},{20,16},{24,28},{28,24},{1,5},{5... | collective-permute-start | bytes 479240 | tf_op jit(solution)/shard_map/ppermute | solution.py:602
  15.2 15.2 %collective-permute-start = (bf16[256,768]{1,0:T(8,128)(2,1)}, bf16[256,768]{1,0:T(8,128)(2,1)S(1)}, u32[]{:S(2)}, u32[]{:S(2)}) collective-permute-start(bf16[256,768]{1,0:T(8,128)(2,1)} %own_ref.1), channel_id=1, source_target_pairs={{0,2},{2,0},{1,3},{3,1},{4,6},{6,4},{5,7},{7,5},{8,10},{10,8},{9,1... | collective-permute-start | bytes 1179656 | tf_op jit(solution)/shard_map/ppermute | solution.py:599
  22.1 9.8 %collective-permute-start.5 = (bf16[3,96,576]{2,1,0:T(8,128)(2,1)}, bf16[3,96,576]{2,1,0:T(8,128)(2,1)S(1)}, u32[]{:S(2)}, u32[]{:S(2)}) collective-permute-start(bf16[3,96,576]{2,1,0:T(8,128)(2,1)} %pad_maximum_fusion.2), channel_id=1, source_target_pairs={{0,4},{4,0},{8,12},{12,8},{16,20},{20,16},{24,28},{28,24},{1,5},{5... | collective-permute-start | bytes 995336 | tf_op jit(solution)/shard_map/ppermute | solution.py:602
  24.9 10.0 %collective-permute-start.8 = (bf16[4,96,256]{2,1,0:T(8,128)(2,1)S(1)}, bf16[4,96,256]{2,1,0:T(8,128)(2,1)S(1)}, u32[]{:S(2)}, u32[]{:S(2)}) collective-permute-start(bf16[4,96,256]{2,1,0:T(8,128)(2,1)S(1)} %pad_maximum_fusion.5), channel_id=1, source_target_pairs={{0,8},{4,12},{8,0},{12,4},{16,24},{20,28},{24,16},{28,20},{1,9},{5... | collective-permute-start | bytes 589832 | tf_op jit(solution)/shard_map/ppermute | solution.py:602
  26.6 12.3 %collective-permute-start.10 = (bf16[1,96,768]{2,1,0:T(8,128)(2,1)S(1)}, bf16[1,96,768]{2,1,0:T(8,128)(2,1)S(1)}, u32[]{:S(2)}, u32[]{:S(2)}) collective-permute-start(bf16[1,96,768]{2,1,0:T(8,128)(2,1)S(1)} %bitcast.34), channel_id=1, source_target_pairs={{0,16},{4,20},{8,24},{12,28},{16,0},{20,4},{24,8},{28,12},{1,17},{... | collective-permute-start | bytes 442376 | tf_op jit(solution)/shard_map/ppermute | solution.py:602
  28.0 12.4 %collective-permute-start.9 = (bf16[1,96,768]{2,1,0:T(8,128)(2,1)S(1)}, bf16[1,96,768]{2,1,0:T(8,128)(2,1)S(1)}, u32[]{:S(2)}, u32[]{:S(2)}) collective-permute-start(bf16[1,96,768]{2,1,0:T(8,128)(2,1)S(1)} %bitcast.38), channel_id=1, source_target_pairs={{0,16},{4,20},{8,24},{12,28},{16,0},{20,4},{24,8},{28,12},{1,17},{... | collective-permute-start | bytes 442376 | tf_op jit(solution)/shard_map/ppermute | solution.py:602
  30.4 14.0 %collective-permute-start.11 = (bf16[256,768]{1,0:T(8,128)(2,1)S(1)}, bf16[256,768]{1,0:T(8,128)(2,1)S(1)}, u32[]{:S(2)}, u32[]{:S(2)}) collective-permute-start(bf16[256,768]{1,0:T(8,128)(2,1)S(1)} %copy-done.3), channel_id=1, source_target_pairs={{0,2},{2,0},{1,3},{3,1},{4,6},{6,4},{5,7},{7,5},{8,10},{10,8},{9,1... | collective-permute-start | bytes 1179656 | tf_op jit(solution)/shard_map/ppermute | solution.py:599
  40.5 7.1 %collective-permute-start.13 = (bf16[2,96,768]{2,1,0:T(8,128)(2,1)S(1)}, bf16[2,96,768]{2,1,0:T(8,128)(2,1)S(1)}, u32[]{:S(2)}, u32[]{:S(2)}) collective-permute-start(bf16[2,96,768]{2,1,0:T(8,128)(2,1)S(1)} %pad_maximum_fusion.3), channel_id=1, source_target_pairs={{0,8},{4,12},{8,0},{12,4},{16,24},{20,28},{24,16},{28,20},{1,9},{5... | collective-permute-start | bytes 884744 | tf_op jit(solution)/shard_map/ppermute | solution.py:602
  40.6 8.1 %collective-permute-start.15 = (bf16[2,96,768]{2,1,0:T(8,128)(2,1)S(1)}, bf16[2,96,768]{2,1,0:T(8,128)(2,1)S(1)}, u32[]{:S(2)}, u32[]{:S(2)}) collective-permute-start(bf16[2,96,768]{2,1,0:T(8,128)(2,1)S(1)} %pad_maximum_fusion.4), channel_id=1, source_target_pairs={{0,4},{4,0},{8,12},{12,8},{16,20},{20,16},{24,28},{28,24},{1,5},{5... | collective-permute-start | bytes 884744 | tf_op jit(solution)/shard_map/ppermute | solution.py:602
  44.4 11.2 %collective-permute-start.12 = (bf16[256,768]{1,0:T(8,128)(2,1)S(1)}, bf16[256,768]{1,0:T(8,128)(2,1)S(1)}, u32[]{:S(2)}, u32[]{:S(2)}) collective-permute-start(bf16[256,768]{1,0:T(8,128)(2,1)S(1)} %shard_map.165.a_ref), channel_id=1, source_target_pairs={{0,2},{2,0},{1,3},{3,1},{4,6},{6,4},{5,7},{7,5},{8,10},{10,8},{9,1... | collective-permute-start | bytes 1179656 | tf_op jit(solution)/shard_map/ppermute | solution.py:599
  47.7 13.5 %collective-permute-start.14 = (bf16[4,96,768]{2,1,0:T(8,128)(2,1)S(1)}, bf16[4,96,768]{2,1,0:T(8,128)(2,1)S(1)}, u32[]{:S(2)}, u32[]{:S(2)}) collective-permute-start(bf16[4,96,768]{2,1,0:T(8,128)(2,1)S(1)} %pad_maximum_fusion), channel_id=1, source_target_pairs={{0,4},{4,0},{8,12},{12,8},{16,20},{20,16},{24,28},{28,24},{1,5},{5... | collective-permute-start | bytes 1769480 | tf_op jit(solution)/shard_map/ppermute | solution.py:602
  48.8 14.0 %collective-permute-start.16 = (bf16[4,96,768]{2,1,0:T(8,128)(2,1)S(1)}, bf16[4,96,768]{2,1,0:T(8,128)(2,1)S(1)}, u32[]{:S(2)}, u32[]{:S(2)}) collective-permute-start(bf16[4,96,768]{2,1,0:T(8,128)(2,1)S(1)} %pad_maximum_fusion.1), channel_id=1, source_target_pairs={{0,8},{4,12},{8,0},{12,4},{16,24},{20,28},{24,16},{28,20},{1,9},{5... | collective-permute-start | bytes 1769480 | tf_op jit(solution)/shard_map/ppermute | solution.py:602
  66.1 11.2 %collective-permute-start.17 = (bf16[256,768]{1,0:T(8,128)(2,1)S(1)}, bf16[256,768]{1,0:T(8,128)(2,1)S(1)}, u32[]{:S(2)}, u32[]{:S(2)}) collective-permute-start(bf16[256,768]{1,0:T(8,128)(2,1)S(1)} %shard_map.169.m_ref), channel_id=1, source_target_pairs={{0,2},{2,0},{1,3},{3,1},{4,6},{6,4},{5,7},{7,5},{8,10},{10,8},{9,1... | collective-permute-start | bytes 1179656 | tf_op jit(solution)/shard_map/ppermute | solution.py:599
  81.6 15.7 %collective-permute-start.19 = (bf16[4,96,768]{2,1,0:T(8,128)(2,1)S(1)}, bf16[4,96,768]{2,1,0:T(8,128)(2,1)S(1)}, u32[]{:S(2)}, u32[]{:S(2)}) collective-permute-start(bf16[4,96,768]{2,1,0:T(8,128)(2,1)S(1)} %get-tuple-element.124), channel_id=1, source_target_pairs={{0,8},{4,12},{8,0},{12,4},{16,24},{20,28},{24,16},{28,20},{1,9},{5... | collective-permute-start | bytes 1769480 | tf_op jit(solution)/shard_map/ppermute | solution.py:602
  88.1 11.2 %collective-permute-start.18 = (bf16[256,768]{1,0:T(8,128)(2,1)S(1)}, bf16[256,768]{1,0:T(8,128)(2,1)S(1)}, u32[]{:S(2)}, u32[]{:S(2)}) collective-permute-start(bf16[256,768]{1,0:T(8,128)(2,1)S(1)} %shard_map.173.d_ref), channel_id=1, source_target_pairs={{0,2},{2,0},{1,3},{3,1},{4,6},{6,4},{5,7},{7,5},{8,10},{10,8},{9,1... | collective-permute-start | bytes 1179656 | tf_op jit(solution)/shard_map/ppermute | solution.py:599
  89.7 19.7 %collective-permute-start.24 = (bf16[4,96,768]{2,1,0:T(8,128)(2,1)S(1)}, bf16[4,96,768]{2,1,0:T(8,128)(2,1)S(1)}, u32[]{:S(2)}, u32[]{:S(2)}) collective-permute-start(bf16[4,96,768]{2,1,0:T(8,128)(2,1)S(1)} %get-tuple-element.134), channel_id=1, source_target_pairs={{0,4},{4,0},{8,12},{12,8},{16,20},{20,16},{24,28},{28,24},{1,5},{5... | collective-permute-start | bytes 1769480 | tf_op jit(solution)/shard_map/ppermute | solution.py:602
  97.4 14.9 %collective-permute-start.20 = (bf16[2,96,768]{2,1,0:T(8,128)(2,1)S(1)}, bf16[2,96,768]{2,1,0:T(8,128)(2,1)S(1)}, u32[]{:S(2)}, u32[]{:S(2)}) collective-permute-start(bf16[2,96,768]{2,1,0:T(8,128)(2,1)S(1)} %get-tuple-element.138), channel_id=1, source_target_pairs={{0,4},{4,0},{8,12},{12,8},{16,20},{20,16},{24,28},{28,24},{1,5},{5... | collective-permute-start | bytes 884744 | tf_op jit(solution)/shard_map/ppermute | solution.py:602
  106.6 14.5 %collective-permute-start.22 = (bf16[4,96,512]{2,1,0:T(8,128)(2,1)S(1)}, bf16[4,96,512]{2,1,0:T(8,128)(2,1)S(1)}, u32[]{:S(2)}, u32[]{:S(2)}) collective-permute-start(bf16[4,96,512]{2,1,0:T(8,128)(2,1)S(1)} %get-tuple-element.160), channel_id=1, source_target_pairs={{0,4},{4,0},{8,12},{12,8},{16,20},{20,16},{24,28},{28,24},{1,5},{5... | collective-permute-start | bytes 1179656 | tf_op jit(solution)/shard_map/ppermute | solution.py:602
  107.2 13.9 %collective-permute-start.23 = (bf16[4,96,320]{2,1,0:T(8,128)(2,1)S(1)}, bf16[4,96,320]{2,1,0:T(8,128)(2,1)S(1)}, u32[]{:S(2)}, u32[]{:S(2)}) collective-permute-start(bf16[4,96,320]{2,1,0:T(8,128)(2,1)S(1)} %get-tuple-element.162), channel_id=1, source_target_pairs={{0,8},{4,12},{8,0},{12,4},{16,24},{20,28},{24,16},{28,20},{1,9},{5... | collective-permute-start | bytes 737288 | tf_op jit(solution)/shard_map/ppermute | solution.py:602
  109.5 16.6 %collective-permute-start.25 = (bf16[2,96,768]{2,1,0:T(8,128)(2,1)S(1)}, bf16[2,96,768]{2,1,0:T(8,128)(2,1)S(1)}, u32[]{:S(2)}, u32[]{:S(2)}) collective-permute-start(bf16[2,96,768]{2,1,0:T(8,128)(2,1)S(1)} %get-tuple-element.168), channel_id=1, source_target_pairs={{0,16},{4,20},{8,24},{12,28},{16,0},{20,4},{24,8},{28,12},{1,17},{... | collective-permute-start | bytes 884744 | tf_op jit(solution)/shard_map/ppermute | solution.py:602
  114.8 17.0 %collective-permute-start.21 = (bf16[128,768]{1,0:T(8,128)(2,1)S(1)}, bf16[128,768]{1,0:T(8,128)(2,1)S(1)}, u32[]{:S(2)}, u32[]{:S(2)}) collective-permute-start(bf16[128,768]{1,0:T(8,128)(2,1)S(1)} %get-tuple-element.157), channel_id=1, source_target_pairs={{0,2},{2,0},{1,3},{3,1},{4,6},{6,4},{5,7},{7,5},{8,10},{10,8},{9,1... | collective-permute-start | bytes 589832 | tf_op jit(solution)/shard_map/ppermute | solution.py:599
  121.3 10.5 %collective-permute-start.27 = (bf16[2,96,512]{2,1,0:T(8,128)(2,1)S(1)}, bf16[2,96,512]{2,1,0:T(8,128)(2,1)S(1)}, u32[]{:S(2)}, u32[]{:S(2)}) collective-permute-start(bf16[2,96,512]{2,1,0:T(8,128)(2,1)S(1)} %get-tuple-element.173), channel_id=1, source_target_pairs={{0,8},{4,12},{8,0},{12,4},{16,24},{20,28},{24,16},{28,20},{1,9},{5... | collective-permute-start | bytes 589832 | tf_op jit(solution)/shard_map/ppermute | solution.py:602
  121.4 10.3 %collective-permute-start.26 = (bf16[1,96,768]{2,1,0:T(8,128)(2,1)S(1)}, bf16[1,96,768]{2,1,0:T(8,128)(2,1)S(1)}, u32[]{:S(2)}, u32[]{:S(2)}) collective-permute-start(bf16[1,96,768]{2,1,0:T(8,128)(2,1)S(1)} %get-tuple-element.153), channel_id=1, source_target_pairs={{0,16},{4,20},{8,24},{12,28},{16,0},{20,4},{24,8},{28,12},{1,17},{... | collective-permute-start | bytes 442376 | tf_op jit(solution)/shard_map/ppermute | solution.py:602
  123.3 8.4 %collective-permute-start.28 = (bf16[2,96,320]{2,1,0:T(8,128)(2,1)S(1)}, bf16[2,96,320]{2,1,0:T(8,128)(2,1)S(1)}, u32[]{:S(2)}, u32[]{:S(2)}) collective-permute-start(bf16[2,96,320]{2,1,0:T(8,128)(2,1)S(1)} %get-tuple-element.175), channel_id=1, source_target_pairs={{0,4},{4,0},{8,12},{12,8},{16,20},{20,16},{24,28},{28,24},{1,5},{5... | collective-permute-start | bytes 368648 | tf_op jit(solution)/shard_map/ppermute | solution.py:602
  131.8 9.5 %collective-permute-start.29 = (bf16[1,96,832]{2,1,0:T(8,128)(2,1)S(1)}, bf16[1,96,832]{2,1,0:T(8,128)(2,1)S(1)}, u32[]{:S(2)}, u32[]{:S(2)}) collective-permute-start(bf16[1,96,832]{2,1,0:T(8,128)(2,1)S(1)} %get-tuple-element.177), channel_id=1, source_target_pairs={{0,16},{4,20},{8,24},{12,28},{16,0},{20,4},{24,8},{28,12},{1,17},{... | collective-permute-start | bytes 479240 | tf_op jit(solution)/shard_map/ppermute | solution.py:602
  132.3 9.1 %collective-permute-start.31 = (bf16[1,96,768]{2,1,0:T(8,128)(2,1)S(1)}, bf16[1,96,768]{2,1,0:T(8,128)(2,1)S(1)}, u32[]{:S(2)}, u32[]{:S(2)}) collective-permute-start(bf16[1,96,768]{2,1,0:T(8,128)(2,1)S(1)} %get-tuple-element.169), channel_id=1, source_target_pairs={{0,8},{4,12},{8,0},{12,4},{16,24},{20,28},{24,16},{28,20},{1,9},{5... | collective-permute-start | bytes 442376 | tf_op jit(solution)/shard_map/ppermute | solution.py:602
  134.9 8.1 %collective-permute-start.33 = (bf16[96,768]{1,0:T(8,128)(2,1)S(1)}, bf16[96,768]{1,0:T(8,128)(2,1)S(1)}, u32[]{:S(2)}, u32[]{:S(2)}) collective-permute-start(bf16[96,768]{1,0:T(8,128)(2,1)S(1)} %shard_map.185), channel_id=1, source_target_pairs={{0,2},{2,0},{1,3},{3,1},{4,6},{6,4},{5,7},{7,5},{8,10},{10,8},{9,1... | collective-permute-start | bytes 442376 | tf_op jit(solution)/shard_map/ppermute | solution.py:599
  141.4 6.4 %collective-permute-start.32 = (bf16[96,768]{1,0:T(8,128)(2,1)S(1)}, bf16[96,768]{1,0:T(8,128)(2,1)S(1)}, u32[]{:S(2)}, u32[]{:S(2)}) collective-permute-start(bf16[96,768]{1,0:T(8,128)(2,1)S(1)} %shard_map.191), channel_id=1, source_target_pairs={{0,2},{2,0},{1,3},{3,1},{4,6},{6,4},{5,7},{7,5},{8,10},{10,8},{9,1... | collective-permute-start | bytes 442376 | tf_op jit(solution)/shard_map/ppermute | solution.py:599
  143.9 6.5 %collective-permute-start.30 = (bf16[96,832]{1,0:T(8,128)(2,1)S(1)}, bf16[96,832]{1,0:T(8,128)(2,1)S(1)}, u32[]{:S(2)}, u32[]{:S(2)}) collective-permute-start(bf16[96,832]{1,0:T(8,128)(2,1)S(1)} %shard_map.187.near_ref), channel_id=1, source_target_pairs={{0,2},{2,0},{1,3},{3,1},{4,6},{6,4},{5,7},{7,5},{8,10},{10,8},{9,1... | collective-permute-start | bytes 479240 | tf_op jit(solution)/shard_map/ppermute | solution.py:599
  (7 other events, 85.3 us)

commit v6 on v5

--- a/solution.py
+++ b/solution.py
@@ -258,12 +258,10 @@
     return jnp.where(mask, values, jnp.zeros_like(values))
 
 
-def biased(raw, bias, scale):
+def biased(raw, bias):
     blocks = bias.shape[0]
     size = raw.shape[0] // blocks
-    return jnp.concatenate(
-        [raw[j * size : (j + 1) * size] * scale + bias[j : j + 1] for j in range(blocks)], axis=0
-    )
+    return jnp.concatenate([raw[j * size : (j + 1) * size] + bias[j : j + 1] for j in range(blocks)], axis=0)
 
 
 DIRECT = (0, 2, 4, 6, 1, 3, 5, 7)
@@ -332,15 +330,16 @@
         x_ref[pl.ds((2 * t + c) * part, part), :] = own_ref[t * part : (t + 1) * part, :]
         x_ref[pl.ds((2 * t + 1 - c) * part, part), :] = far_ref[t * part : (t + 1) * part, :]
     place((w0, w1, w2, w3, w4, w5), w_ref, DIRECT, w4.shape[1] - w_ref.shape[1])
-    scale = 1.0 / math.sqrt(HD)
+    scale = jnp.bfloat16(1.0 / math.sqrt(HD))
     w = w_ref[...]
     qkv = mul(x_ref[...], w, 1, 0).astype(jnp.bfloat16)
     qkv_ref[...] = qkv
     q, k, v = [qkv[:, i * width : (i + 1) * width] for i in range(3)]
+    q = q * scale
     lse_ref[...] = jnp.zeros_like(lse_ref)
     blocks = bias_ref.shape[0] // (width // HD)
     for h, mask in enumerate(head_masks(width)):
-        s = biased(mul(k, only(q, mask), 1, 1), bias_ref[h * blocks : (h + 1) * blocks, :], scale)
+        s = biased(mul(k, only(q, mask), 1, 1), bias_ref[h * blocks : (h + 1) * blocks, :])
         top = jnp.max(s, axis=0, keepdims=True)
         e = jnp.exp(s - top)
         total = jnp.sum(e, axis=0, keepdims=True)
@@ -358,9 +357,10 @@
 
 
 def project_body(ways, o_ref, *refs):
-    *pieces, mine_ref, theirs_ref, w_ref = refs
+    *pieces, theirs_ref, w_ref = refs
     place(pieces, w_ref, ways)
-    split_rows(lambda rows: mul(o_ref[rows, :], w_ref[...], 1, 1), mine_ref, theirs_ref)
+    rows = part_rows(theirs_ref.shape[0], False)
+    theirs_ref[...] = mul(o_ref[rows, :], w_ref[...], 1, 1).astype(jnp.bfloat16)
 
 
 def project_out_body(ways, o_ref, *refs):
@@ -430,10 +430,31 @@
     grad_ref[3:4, :] = jnp.sum(e, axis=0, keepdims=True)
 
 
-def ffn_back_body(dm_ref, slope_ref, down_ref, up_ref, dhid_ref, mine_ref, theirs_ref):
+def join(near_ref, far_ref, all_ref):
+    half = near_ref.shape[0]
+    t = lax.axis_index("tp")
+    all_ref[pl.ds(t * half, half), :] = near_ref[...]
+    all_ref[pl.ds((1 - t) * half, half), :] = far_ref[...]
+
+
+def part_rows(half, mine):
+    t = lax.axis_index("tp")
+    return pl.ds((t if mine else 1 - t) * half, half)
+
+
+def ffn_back_body(near_ref, far_ref, slope_ref, down_ref, up_ref, dm_ref, dhid_ref, theirs_ref):
+    join(near_ref, far_ref, dm_ref)
     du = mul(dm_ref[...], down_ref[...], 1, 0)
     dhid_ref[...] = (du * slope_ref[...].astype(jnp.float32)).astype(jnp.bfloat16)
-    split_rows(lambda rows: mul(dhid_ref[rows, :], up_ref[...], 1, 1), mine_ref, theirs_ref)
+    theirs_ref[...] = mul(dhid_ref[part_rows(near_ref.shape[0], False), :], up_ref[...], 1, 1).astype(jnp.bfloat16)
+
+
+def part_body(rows_ref, w_ref, mine_ref):
+    mine_ref[...] = mul(rows_ref[part_rows(mine_ref.shape[0], True), :], w_ref[...], 1, 1)
+
+
+def add_far_body(mine_ref, far_ref, sum_ref):
+    sum_ref[...] = (mine_ref[...] + far_ref[...].astype(jnp.float32)).astype(jnp.bfloat16)
 
 
 def deal(own_ref, away_ref, scr, order, start=0):
@@ -447,7 +468,7 @@
 
 
 def grad_body(order, left_ref, right_ref, own_ref, away_ref, scr):
-    scr[...] = mul(left_ref[...], right_ref[...], 0, 0)
+    scr[...] = mul(left_ref[...], right_ref[...], 0, 0).astype(scr.dtype)
     deal(own_ref, away_ref, scr, order)
 
 
@@ -458,8 +479,8 @@
 
 def fold_pair(own_ref, got_ref, keep_ref, send_ref):
     half = keep_ref.shape[0]
-    keep_ref[...] = own_ref[0:half] + got_ref[0:half].astype(jnp.float32)
-    send_ref[...] = (own_ref[half:] + got_ref[half:].astype(jnp.float32)).astype(jnp.bfloat16)
+    keep_ref[...] = own_ref[0:half].astype(jnp.float32) + got_ref[0:half].astype(jnp.float32)
+    send_ref[...] = (own_ref[half:].astype(jnp.float32) + got_ref[half:].astype(jnp.float32)).astype(jnp.bfloat16)
 
 
 def fold_body(own_ref, got_ref, keep_ref, send_ref):
@@ -503,26 +524,28 @@
 ):
     width = o_ref.shape[1]
     rows = x_ref.shape[0]
-    scale = 1.0 / math.sqrt(HD)
+    scale = jnp.bfloat16(1.0 / math.sqrt(HD))
     half = rows // 2
     da = jnp.concatenate([da_ref[0, 0:half, :], da_ref[1, 0:half, :]], axis=0)
     do = mul(da, w_out_ref[...], 1, 0).astype(jnp.bfloat16)
     q, k, v = [qkv_ref[:, i * width : (i + 1) * width] for i in range(3)]
+    q = q * scale
+    k_scaled = k * scale
     blocks = bias_ref.shape[0] // (width // HD)
     dq = jnp.zeros((rows, width), jnp.float32)
     for h, mask in enumerate(head_masks(width)):
         q_h, do_h = only(q, mask), only(do, mask)
-        s = biased(mul(k, q_h, 1, 1), bias_ref[h * blocks : (h + 1) * blocks, :], scale)
+        s = biased(mul(k, q_h, 1, 1), bias_ref[h * blocks : (h + 1) * blocks, :])
         p = jnp.exp(s - lse_ref[h : h + 1, :])
         dp = mul(v, do_h, 1, 1)
         pd = p * dp
         ds = pd - p * jnp.sum(pd, axis=0, keepdims=True)
-        dr = (ds * scale).astype(jnp.bfloat16)
+        dr = ds.astype(jnp.bfloat16)
         p_scr[:, h * rows : (h + 1) * rows] = p.astype(jnp.bfloat16)
         dr_scr[:, h * rows : (h + 1) * rows] = dr
         q_scr[h * rows : (h + 1) * rows, :] = q_h
         do_scr[h * rows : (h + 1) * rows, :] = do_h
-        dq = dq + mul(dr, only(k, mask), 0, 0)
+        dq = dq + mul(dr, only(k_scaled, mask), 0, 0)
     all_scr[:, 0:width] = dq.astype(jnp.bfloat16)
     all_scr[:, width : 2 * width] = mul(dr_scr[...], q_scr[...], 1, 0).astype(jnp.bfloat16)
     all_scr[:, 2 * width : 3 * width] = mul(p_scr[...], do_scr[...], 1, 0).astype(jnp.bfloat16)
@@ -533,7 +556,7 @@
     ).astype(jnp.bfloat16)
     grad_scr[...] = jnp.concatenate(
         [mul(x_ref[...], all_scr[...], 0, 0), mul(vec, unit, 0, 0), mul(da, o_ref[...], 0, 0)], axis=1
-    )
+    ).astype(grad_scr.dtype)
     deal_two(own_ref, away_ref, own2_ref, away2_ref, grad_scr)
 
 
@@ -592,6 +615,9 @@
     f32, bf16 = jnp.float32, jnp.bfloat16
     pair = [(0, 1), (1, 0)]
 
+    def swap_tp(v):
+        return lax.ppermute(v, "tp", pair)
+
     def both_tp(v, tiled=False):
         return lax.all_gather(v, "tp", axis=0, tiled=tiled)
 
@@ -635,14 +661,14 @@
     far_one = swap_dp(pack_one, 1)
     w_up, w_down = packed(pack_second_body, (units, units), up_weight, down_weight.T)
     picks_far = swap_ctx(random_blocks)
-    w1_near = all_after(w1_near, far_one)
+    out_first = jnp.stack([pack_one[:, : cols + extra], far_one[:, : cols + extra]])
+    out_next = swap_dp(out_first, 4)
+    w1_near = all_after(w1_near, far_one, out_first)
     w1_rest = jnp.stack(w1_near)
     w1_pieces = [w1, *w1_near, far_one, swap_dp(w1_rest, 1)]
-    out_pieces = [jnp.stack([pack_one[:, : cols + extra], far_one[:, : cols + extra]])]
-    out_pieces[0] = after(out_pieces[0], w1_rest)
-    out_pieces.append(swap_dp(out_pieces[0], 4))
+    out_pieces = [out_first, out_next]
     out_pieces.append(swap_dp(jnp.concatenate(out_pieces), 2))
-    up_pieces, down_pieces = all_after([w_up[None], w_down[None]], out_pieces[1])
+    up_pieces, down_pieces = all_after([w_up[None], w_down[None]], w1_rest)
     up_pieces = [up_pieces, swap_dp(up_pieces, 4)]
     down_pieces = [down_pieces, swap_dp(down_pieces, 4)]
     e_far = swap_ctx(after(out_grad, *w1_near))
@@ -691,8 +717,9 @@
     square = [((width, units), bf16)]
     y_all = both_tp(y_low, True)
     u, slope, w_up_all = call(ffn_body, flat * 2 + square, y_all, *up_pieces)
-    mine, theirs, w_down_all = call(functools.partial(project_body, DOWN_WAYS), wide + low + square, u, *down_pieces)
-    m = sum_tp(mine, theirs)
+    theirs, w_down_all = call(functools.partial(project_body, DOWN_WAYS), low + square, u, *down_pieces)
+    mine = call(part_body, wide, u, w_down_all)[0]
+    m = call(add_far_body, low, mine, swap_tp(theirs))[0]
     m_far = swap_ctx(m)
     out, dz2, dm_low, grad2 = call(
         norm_two_body,
@@ -718,29 +745,28 @@
         total = call(fold_last_body, [(keep.shape[1:], bf16)], keep, swap_dp(send, bits))[0]
         return total, swap_ctx(total)
 
-    dm_all = both_tp(dm_low, True)
+    dm_all, dhid, theirs = call(
+        ffn_back_body, [((total_rows, width), bf16)] + flat + low, dm_low, swap_tp(dm_low), slope, w_down_all, w_up_all
+    )
     down_own, down_away = call(
-        functools.partial(grad_body, (2, 1, 4)), pairs(n_out, units), dm_all, u, scratch=[((width, units), f32)]
-    )
-    dm_all = after(dm_all, down_away)
-    dhid, mine, theirs = call(
-        ffn_back_body, flat + wide + low, dm_all, slope, w_down_all, w_up_all
-    )
-    d = sum_tp(mine, theirs)
+        functools.partial(grad_body, (2, 1, 4)), [((n_out, shard, units), bf16)] * 2, dm_all, u, scratch=[((width, units), bf16)]
+    )
+    mine = call(part_body, wide, dhid, w_up_all)[0]
+    d = call(add_far_body, low, after(mine, down_away), swap_tp(theirs))[0]
     d_far = swap_ctx(d)
     y_late, dhid = lax.optimization_barrier((y_all, dhid, d))[:2]
     up = call(
-        functools.partial(grad_body, (1, 4, 2)), pairs(n_out, units), y_late, dhid, scratch=[((width, units), f32)]
-    )
-    down_keep, down_send = fold(down_own, swap_dp(down_away, 2))
+        functools.partial(grad_body, (1, 4, 2)), [((n_out, shard, units), bf16)] * 2, y_late, dhid, scratch=[((width, units), bf16)]
+    )
     output = call(copy_body, low, both_tp(after(out, up[1]), True))[0]
     dz1, da_low = call(
-        norm_one_back_body, wide + [((rows + 16, width), bf16)], dz2, d, after(d_far, up[1], down_send, output), n1, r1, vecs, grad2
-    )
+        norm_one_back_body, wide + [((rows + 16, width), bf16)], dz2, d, after(d_far, up[1], output), n1, r1, vecs, grad2
+    )
+    down_keep, down_send = fold(after(down_own, da_low), swap_dp(down_away, 2))
     last = 4 * cols + extra
     *tail, dqkv = call(
         attend_back_body,
-        pairs(n_out, *cut(last)) + [((total_rows, 3 * cols), bf16)],
+        [((n_out, shard, n), bf16) for n in cut(last) for _ in range(2)] + [((total_rows, 3 * cols), bf16)],
         after(both_tp(da_low), down_send), w_out_all, qkv, o, lse, bias, x_all,
         flops=2 * 10**10,
         scratch=[
@@ -748,7 +774,7 @@
             ((total_rows, heads * total_rows), bf16),
             ((heads * total_rows, cols), bf16),
             ((heads * total_rows, cols), bf16),
-            ((width, last), f32),
+            ((width, last), bf16),
         ],
     )
     mine, theirs = call(input_body, wide + low, dqkv, w1_all)
@@ -760,12 +786,13 @@
     got1, got2 = swap_dp(send1, 2), swap_dp(send2, 1)
     dx_far = swap_ctx(send)
     up = fold(after(up[0], keep1), swap_dp(up[1], 4))
-    grad_down, down_far = fold_third(*all_after(down[:1], keep1), down[1], 4)
-    keep1 = after(keep1, dx_far, up[1], grad_down)
+    keep1 = after(keep1, dx_far, up[1])
     tail = call(fold_join_body, pairs(1, last), keep1, got1, keep2, got2)
-    grad_1, far_1 = fold_third(*tail, 4)
+    grad_down, down_far = fold_third(*all_after(down[:1], tail[0]), down[1], 4)
+    grad_1, far_1 = fold_third(after(tail[0], grad_down), tail[1], 4)
     grad_up, up_far = fold_third(*all_after(up[:1], grad_1), up[1], 2)
-    dx = call(last_input_body, [half], keep, after(dx_far, grad_1))[0]
+    down_far = after(down_far, grad_up)
+    dx = call(last_input_body, [half], keep, after(dx_far, grad_up))[0]
     input_grad = call(copy_body, low, both_tp(dx, True))[0]
     grad_1 = after(grad_1, input_grad)
 

time: 152 us -> 144 us (0.947)
  blocking collectives: 20.9 us -> 14.1 us
  waiting for transfers between devices: 53.8 us -> 51.4 us
  starting transfers between devices: 45 us -> 46.8 us
    all_gather x9 -> x6, blocking collectives: 20.9 us -> 14.1 us  [both_tp(): return lax.all_gather(v, 'tp', axis=0, tiled=tiled)]
    ppermute x24, waiting for transfers between devices: 33.6 us -> 28.3 us  [swap_dp(): return lax.ppermute(v, 'dp', [(i, i ^ bits) for i in range(n_dp)])]
    ppermute x0 -> x3, waiting for transfers between devices: none -> 3.09 us  [swap_tp(): return lax.ppermute(v, 'tp', pair)]
    pallas_call x31 -> x33, Pallas kernels: 23.8 us -> 23.8 us  [call(): pl.pallas_call(body, out_shape=shapes, in_specs=specs, out_specs=[pl.Bloc...]
  transfers between devices with their start and end apart: 34 -> 37, of which waited for: 17 -> 19; matrix products, arithmetic and copies ran while one was open for 4% -> 4% of each run, Pallas kernels for 12% -> 12%
where the time goes in v6:
time: 144 us
  waiting for transfers between devices  51.4 us (36%)
  starting transfers between devices  46.8 us (32%)
  Pallas kernels  23.8 us (17%)
  blocking collectives  14.1 us (10%)
  other arithmetic  4.1 us (3%)
  local copies, waits for them, and re-layouts  1.99 us (1%)
  between operations  1.79 us (1%)
    ppermute x24, starting transfers between devices, swap_dp(): return lax.ppermute(v, 'dp', [(i, i ^ bits) for i in range(n_dp)])  34 us
    ppermute x24, waiting for transfers between devices, swap_dp(): return lax.ppermute(v, 'dp', [(i, i ^ bits) for i in range(n_dp)])  28.3 us
    pallas_call x33, Pallas kernels, call(): pl.pallas_call(body, out_shape=shapes, in_specs=specs, out_specs=[pl.Bloc...  23.8 us
    ppermute x10, waiting for transfers between devices, swap_ctx(): return lax.ppermute(v, 'ctx', pair)  20 us
    all_gather x6, blocking collectives, both_tp(): return lax.all_gather(v, 'tp', axis=0, tiled=tiled)  14.1 us
    ppermute x10, starting transfers between devices, swap_ctx(): return lax.ppermute(v, 'ctx', pair)  12.5 us
    ppermute x3, waiting for transfers between devices, swap_tp(): return lax.ppermute(v, 'tp', pair)  3.09 us
  transfers between devices with their start and end apart: 37, of which 19 were waited for; matrix products, arithmetic and copies ran while one was open for 4% of the time, Pallas kernels for 12%

profile of v6, /device:TPU:0, one launch (start us, length us, event | category | flops | bytes accessed | tf_op | source)
XLA Modules:
  0.0 143.9 jit_solution(14992857433493409366)
XLA Ops:
  0.6 2.0 %shard_map.161 = (bf16[96,576]{1,0:T(8,128)(2,1)}, bf16[96,832]{1,0:T(8,128)(2,1)}) custom-call(bf16[3,96,384]{2,1,0:T(8,128)(2,1)} %qkv_hbm.1, bf16[2,96]{1,0:T(2,128)(2,1)} %gain_hbm.1, bf16[2,96]{1,0:T(2,128)(2,1)} %bias_hbm.1, bf16[96,384]{1,0:T(8,128)(2,1)} %bitcast.44), custom_call_target="tpu_custom_call" | custom-call | tf_op jit(solution)/shard_map/pallas_call | solution.py:240
  2.6 5.1 %collective-permute-start.3 = (bf16[96,576]{1,0:T(8,128)(2,1)}, bf16[96,576]{1,0:T(8,128)(2,1)S(1)}, u32[]{:S(2)}, u32[]{:S(2)}) collective-permute-start(bf16[96,576]{1,0:T(8,128)(2,1)} %get-tuple-element.98.w0), channel_id=1, source_target_pairs={{0,24},{4,28},{8,16},{12,20},{16,8},{20,12},{24,0},{28,4},{1,25},{... | collective-permute-start | bytes 331784 | tf_op jit(solution)/shard_map/ppermute | solution.py:628
  13.1 1.8 %shard_map.164 = (bf16[96,768]{1,0:T(8,128)(2,1)}, bf16[96,768]{1,0:T(8,128)(2,1)}) custom-call(bf16[96,1536]{1,0:T(8,128)(2,1)} %up_hbm.1, bf16[96,1536]{1,0:T(8,128)(2,1)} %bitcast.42), custom_call_target="tpu_custom_call" | custom-call | tf_op jit(solution)/shard_map/pallas_call | solution.py:240
  17.1 2.2 %collective-permute-start.7 = (bf16[2,96,256]{2,1,0:T(8,128)(2,1)S(1)}, bf16[2,96,256]{2,1,0:T(8,128)(2,1)S(1)}, u32[]{:S(2)}, u32[]{:S(2)}) collective-permute-start(bf16[2,96,256]{2,1,0:T(8,128)(2,1)S(1)} %pad_maximum_fusion.6.refs_0_), channel_id=1, source_target_pairs={{0,16},{4,20},{8,24},{12,28},{16,0},{20,4},{24,8},{28,12},{1,17},{... | collective-permute-start | bytes 294920 | tf_op jit(solution)/shard_map/ppermute | solution.py:628
  21.3 2.5 %collective-permute-start.10 = (bf16[1,96,768]{2,1,0:T(8,128)(2,1)S(1)}, bf16[1,96,768]{2,1,0:T(8,128)(2,1)S(1)}, u32[]{:S(2)}, u32[]{:S(2)}) collective-permute-start(bf16[1,96,768]{2,1,0:T(8,128)(2,1)S(1)} %bitcast.30), channel_id=1, source_target_pairs={{0,16},{4,20},{8,24},{12,28},{16,0},{20,4},{24,8},{28,12},{1,17},{... | collective-permute-start | bytes 442376 | tf_op jit(solution)/shard_map/ppermute | solution.py:628
  23.9 3.7 %collective-permute-done.7.refs_1_ = bf16[2,96,256]{2,1,0:T(8,128)(2,1)S(1)} collective-permute-done((bf16[2,96,256]{2,1,0:T(8,128)(2,1)S(1)}, bf16[2,96,256]{2,1,0:T(8,128)(2,1)S(1)}, u32[]{:S(2)}, u32[]{:S(2)}) %collective-permute-start.7) | collective-permute-done | bytes 98336 | tf_op jit(solution)/shard_map/ppermute | solution.py:628
  27.6 3.2 %collective-permute-start.8 = (bf16[4,96,256]{2,1,0:T(8,128)(2,1)S(1)}, bf16[4,96,256]{2,1,0:T(8,128)(2,1)S(1)}, u32[]{:S(2)}, u32[]{:S(2)}) collective-permute-start(bf16[4,96,256]{2,1,0:T(8,128)(2,1)S(1)} %pad_maximum_fusion.5), channel_id=1, source_target_pairs={{0,8},{4,12},{8,0},{12,4},{16,24},{20,28},{24,16},{28,20},{1,9},{5... | collective-permute-start | bytes 589832 | tf_op jit(solution)/shard_map/ppermute | solution.py:628
  33.3 2.9 %shard_map.162 = (bf16[512,192]{1,0:T(8,128)(2,1)S(1)}, bf16[512,576]{1,0:T(8,128)(2,1)S(1)}, f32[8,512]{1,0:T(8,128)S(1)}, bf16[512,768]{1,0:T(8,128)(2,1)S(1)}, bf16[768,576]{1,0:T(8,128)(2,1)S(1)}) custom-call(bf16[256,768]{1,0:T(8,128)(2,1)S(1)} %copy-done.2, bf16[256,768]{1,0:T(8,128)(2,1)S(1)} %collective-permute-done.far_ref, ...), custom_call_target="tpu_custom_call" | custom-call | tf_op jit(solution)/shard_map/pallas_call | solution.py:240
  36.2 2.3 %collective-permute-done.8.refs_2_ = bf16[4,96,256]{2,1,0:T(8,128)(2,1)S(1)} collective-permute-done((bf16[4,96,256]{2,1,0:T(8,128)(2,1)S(1)}, bf16[4,96,256]{2,1,0:T(8,128)(2,1)S(1)}, u32[]{:S(2)}, u32[]{:S(2)}) %collective-permute-start.8) | collective-permute-done | bytes 196640 | tf_op jit(solution)/shard_map/ppermute | solution.py:628
  39.3 2.4 %all-gather = bf16[512,768]{1,0:T(8,128)(2,1)S(1)} all-gather(bf16[256,768]{1,0:T(8,128)(2,1)S(1)} %get-tuple-element.111), channel_id=2, replica_groups=mesh['dp'=8,'ctx'=2,'tp'=2] {'tp'}, dimensions={0}, use_global_device_ids=true | all-gather | bytes 1179648 | tf_op jit(solution)/shard_map/all_gather | solution.py:622
  43.4 2.5 %collective-permute-done.13.w2 = bf16[2,96,768]{2,1,0:T(8,128)(2,1)S(1)} collective-permute-done((bf16[2,96,768]{2,1,0:T(8,128)(2,1)S(1)}, bf16[2,96,768]{2,1,0:T(8,128)(2,1)S(1)}, u32[]{:S(2)}, u32[]{:S(2)}) %collective-permute-start.13) | collective-permute-done | bytes 294944 | tf_op jit(solution)/shard_map/ppermute | solution.py:628
  46.1 2.0 %collective-permute-start.16 = (bf16[4,96,768]{2,1,0:T(8,128)(2,1)S(1)}, bf16[4,96,768]{2,1,0:T(8,128)(2,1)S(1)}, u32[]{:S(2)}, u32[]{:S(2)}) collective-permute-start(bf16[4,96,768]{2,1,0:T(8,128)(2,1)S(1)} %pad_maximum_fusion.1), channel_id=1, source_target_pairs={{0,8},{4,12},{8,0},{12,4},{16,24},{20,28},{24,16},{28,20},{1,9},{5... | collective-permute-start | bytes 1769480 | tf_op jit(solution)/shard_map/ppermute | solution.py:628
  48.1 4.8 %collective-permute-done.12.far_ref = bf16[256,768]{1,0:T(8,128)(2,1)S(1)} collective-permute-done((bf16[256,768]{1,0:T(8,128)(2,1)S(1)}, bf16[256,768]{1,0:T(8,128)(2,1)S(1)}, u32[]{:S(2)}, u32[]{:S(2)}) %collective-permute-start.12) | collective-permute-done | bytes 393248 | tf_op jit(solution)/shard_map/ppermute | solution.py:625
  53.4 2.5 %all_gather.29.y_ref.left_ref = bf16[512,768]{1,0:T(8,128)(2,1)S(1)} all-gather(bf16[256,768]{1,0:T(8,128)(2,1)S(1)} %get-tuple-element.116), channel_id=1, replica_groups=mesh['dp'=8,'ctx'=2,'tp'=2] {'tp'}, dimensions={0}, use_global_device_ids=true | all-gather | bytes 1179648 | tf_op jit(solution)/shard_map/all_gather | solution.py:622
  55.9 2.9 %collective-permute-done.14.w3 = bf16[4,96,768]{2,1,0:T(8,128)(2,1)S(1)} collective-permute-done((bf16[4,96,768]{2,1,0:T(8,128)(2,1)S(1)}, bf16[4,96,768]{2,1,0:T(8,128)(2,1)S(1)}, u32[]{:S(2)}, u32[]{:S(2)}) %collective-permute-start.14) | collective-permute-done | bytes 589856 | tf_op jit(solution)/shard_map/ppermute | solution.py:628
  64.3 10.1 %collective-permute-done.18.far_ref = bf16[256,768]{1,0:T(8,128)(2,1)S(1)} collective-permute-done((bf16[256,768]{1,0:T(8,128)(2,1)S(1)}, bf16[256,768]{1,0:T(8,128)(2,1)S(1)}, u32[]{:S(2)}, u32[]{:S(2)}) %collective-permute-start.18) | collective-permute-done | bytes 393248 | tf_op jit(solution)/shard_map/ppermute | solution.py:625
  75.4 1.7 %collective-permute-done.19.far_ref = bf16[256,768]{1,0:T(8,128)(2,1)S(1)} collective-permute-done((bf16[256,768]{1,0:T(8,128)(2,1)S(1)}, bf16[256,768]{1,0:T(8,128)(2,1)S(1)}, u32[]{:S(2)}, u32[]{:S(2)}) %collective-permute-start.19) | collective-permute-done | bytes 393248 | tf_op jit(solution)/shard_map/ppermute | solution.py:619
  81.4 2.0 %collective-permute-start.22 = (bf16[4,96,768]{2,1,0:T(8,128)(2,1)S(1)}, bf16[4,96,768]{2,1,0:T(8,128)(2,1)S(1)}, u32[]{:S(2)}, u32[]{:S(2)}) collective-permute-start(bf16[4,96,768]{2,1,0:T(8,128)(2,1)S(1)} %get-tuple-element.128), channel_id=1, source_target_pairs={{0,8},{4,12},{8,0},{12,4},{16,24},{20,28},{24,16},{28,20},{1,9},{5... | collective-permute-start | bytes 1769480 | tf_op jit(solution)/shard_map/ppermute | solution.py:628
  85.3 2.1 %all_gather.30.in_ref = bf16[256,768]{1,0:T(8,128)(2,1)S(1)} all-gather(bf16[128,768]{1,0:T(8,128)(2,1)S(1)} %get-tuple-element.134), channel_id=1, replica_groups=mesh['dp'=8,'ctx'=2,'tp'=2] {'tp'}, dimensions={0}, use_global_device_ids=true | all-gather | bytes 589824 | tf_op jit(solution)/shard_map/all_gather | solution.py:622
  88.2 3.4 %collective-permute-done.21.far_ref = bf16[256,768]{1,0:T(8,128)(2,1)S(1)} collective-permute-done((bf16[256,768]{1,0:T(8,128)(2,1)S(1)}, bf16[256,768]{1,0:T(8,128)(2,1)S(1)}, u32[]{:S(2)}, u32[]{:S(2)}) %collective-permute-start.21) | collective-permute-done | bytes 393248 | tf_op jit(solution)/shard_map/ppermute | solution.py:625
  92.1 2.6 %all-gather.1 = bf16[544,768]{1,0:T(8,128)(2,1)S(1)} all-gather(bf16[272,768]{1,0:T(8,128)(2,1)S(1)} %get-tuple-element.139), channel_id=3, replica_groups=mesh['dp'=8,'ctx'=2,'tp'=2] {'tp'}, dimensions={0}, use_global_device_ids=true | all-gather | bytes 1253376 | tf_op jit(solution)/shard_map/all_gather | solution.py:622
  94.7 2.1 %collective-permute-done.22.got_ref = bf16[4,96,768]{2,1,0:T(8,128)(2,1)S(1)} collective-permute-done((bf16[4,96,768]{2,1,0:T(8,128)(2,1)S(1)}, bf16[4,96,768]{2,1,0:T(8,128)(2,1)S(1)}, u32[]{:S(2)}, u32[]{:S(2)}) %collective-permute-start.22) | collective-permute-done | bytes 589856 | tf_op jit(solution)/shard_map/ppermute | solution.py:628
  98.0 4.2 %shard_map.180 = (bf16[4,96,512]{2,1,0:T(8,128)(2,1)S(1)}, bf16[4,96,512]{2,1,0:T(8,128)(2,1)S(1)}, bf16[4,96,320]{2,1,0:T(8,128)(2,1)S(1)}, bf16[4,96,320]{2,1,0:T(8,128)(2,1)S(1)}, bf16[512,576]{1,0:T(8,128)(2,1)S(1)}) custom-call(bf16[2,272,768]{2,1,0:T(8,128)(2,1)S(1)} %bitcast.38, bf16[768,192]{1,0:T(8,128)(2,1)S(1)} %get-tuple-element.144.w_out_ref, ...), custom_call_target="tpu_custom_call" | custom-call | flops 20000000000 | tf_op jit(solution)/shard_map/pallas_call | solution.py:240
  103.4 1.7 %collective-permute-start.27 = (bf16[4,96,320]{2,1,0:T(8,128)(2,1)S(1)}, bf16[4,96,320]{2,1,0:T(8,128)(2,1)S(1)}, u32[]{:S(2)}, u32[]{:S(2)}) collective-permute-start(bf16[4,96,320]{2,1,0:T(8,128)(2,1)S(1)} %get-tuple-element.165), channel_id=1, source_target_pairs={{0,8},{4,12},{8,0},{12,4},{16,24},{20,28},{24,16},{28,20},{1,9},{5... | collective-permute-start | bytes 737288 | tf_op jit(solution)/shard_map/ppermute | solution.py:628
  106.1 1.8 %collective-permute-start.28 = (bf16[2,96,768]{2,1,0:T(8,128)(2,1)S(1)}, bf16[2,96,768]{2,1,0:T(8,128)(2,1)S(1)}, u32[]{:S(2)}, u32[]{:S(2)}) collective-permute-start(bf16[2,96,768]{2,1,0:T(8,128)(2,1)S(1)} %get-tuple-element.168), channel_id=1, source_target_pairs={{0,16},{4,20},{8,24},{12,28},{16,0},{20,4},{24,8},{28,12},{1,17},{... | collective-permute-start | bytes 884744 | tf_op jit(solution)/shard_map/ppermute | solution.py:628
  107.9 2.4 %all-gather.2 = bf16[512,768]{1,0:T(8,128)(2,1)S(1)} all-gather(bf16[256,768]{1,0:T(8,128)(2,1)S(1)} %get-tuple-element.154), channel_id=4, replica_groups=mesh['dp'=8,'ctx'=2,'tp'=2] {'tp'}, dimensions={0}, use_global_device_ids=true | all-gather | bytes 1179648 | tf_op jit(solution)/shard_map/all_gather | solution.py:622
  111.6 5.8 %collective-permute-done.27.got2_ref = bf16[4,96,320]{2,1,0:T(8,128)(2,1)S(1)} collective-permute-done((bf16[4,96,320]{2,1,0:T(8,128)(2,1)S(1)}, bf16[4,96,320]{2,1,0:T(8,128)(2,1)S(1)}, u32[]{:S(2)}, u32[]{:S(2)}) %collective-permute-start.27) | collective-permute-done | bytes 245792 | tf_op jit(solution)/shard_map/ppermute | solution.py:628
  120.6 2.9 %collective-permute-done.30.got2_ref = bf16[2,96,320]{2,1,0:T(8,128)(2,1)S(1)} collective-permute-done((bf16[2,96,320]{2,1,0:T(8,128)(2,1)S(1)}, bf16[2,96,320]{2,1,0:T(8,128)(2,1)S(1)}, u32[]{:S(2)}, u32[]{:S(2)}) %collective-permute-start.30) | collective-permute-done | bytes 122912 | tf_op jit(solution)/shard_map/ppermute | solution.py:628
  123.6 2.3 %collective-permute-done.29.got_ref = bf16[2,96,512]{2,1,0:T(8,128)(2,1)S(1)} collective-permute-done((bf16[2,96,512]{2,1,0:T(8,128)(2,1)S(1)}, bf16[2,96,512]{2,1,0:T(8,128)(2,1)S(1)}, u32[]{:S(2)}, u32[]{:S(2)}) %collective-permute-start.29) | collective-permute-done | bytes 196640 | tf_op jit(solution)/shard_map/ppermute | solution.py:628
  126.7 4.1 %collective-permute-start.33 = (bf16[1,96,768]{2,1,0:T(8,128)(2,1)S(1)}, bf16[1,96,768]{2,1,0:T(8,128)(2,1)S(1)}, u32[]{:S(2)}, u32[]{:S(2)}) collective-permute-start(bf16[1,96,768]{2,1,0:T(8,128)(2,1)S(1)} %get-tuple-element.170), channel_id=1, source_target_pairs={{0,8},{4,12},{8,0},{12,4},{16,24},{20,28},{24,16},{28,20},{1,9},{5... | collective-permute-start | bytes 442376 | tf_op jit(solution)/shard_map/ppermute | solution.py:628
  132.3 2.1 %collective-permute-done.32.got_ref = bf16[1,96,832]{2,1,0:T(8,128)(2,1)S(1)} collective-permute-done((bf16[1,96,832]{2,1,0:T(8,128)(2,1)S(1)}, bf16[1,96,832]{2,1,0:T(8,128)(2,1)S(1)}, u32[]{:S(2)}, u32[]{:S(2)}) %collective-permute-start.32) | collective-permute-done | bytes 159776 | tf_op jit(solution)/shard_map/ppermute | solution.py:628
  137.7 2.1 %all_gather.35.in_ref = bf16[256,768]{1,0:T(8,128)(2,1)S(1)} all-gather(bf16[128,768]{1,0:T(8,128)(2,1)S(1)} %shard_map.191), channel_id=1, replica_groups=mesh['dp'=8,'ctx'=2,'tp'=2] {'tp'}, dimensions={0}, use_global_device_ids=true | all-gather | bytes 589824 | tf_op jit(solution)/shard_map/all_gather | solution.py:622
  (127 shorter events, 45.7 us)
Async XLA Ops:
  2.6 16.7 %collective-permute-start.3 = (bf16[96,576]{1,0:T(8,128)(2,1)}, bf16[96,576]{1,0:T(8,128)(2,1)S(1)}, u32[]{:S(2)}, u32[]{:S(2)}) collective-permute-start(bf16[96,576]{1,0:T(8,128)(2,1)} %get-tuple-element.98.w0), channel_id=1, source_target_pairs={{0,24},{4,28},{8,16},{12,20},{16,8},{20,12},{24,0},{28,4},{1,25},{... | collective-permute-start | bytes 331784 | tf_op jit(solution)/shard_map/ppermute | solution.py:628
  7.8 11.6 %collective-permute-start.2 = (bf16[96,576]{1,0:T(8,128)(2,1)}, bf16[96,576]{1,0:T(8,128)(2,1)S(1)}, u32[]{:S(2)}, u32[]{:S(2)}) collective-permute-start(bf16[96,576]{1,0:T(8,128)(2,1)} %get-tuple-element.98.w0), channel_id=1, source_target_pairs={{0,16},{4,20},{8,24},{12,28},{16,0},{20,4},{24,8},{28,12},{1,17},{... | collective-permute-start | bytes 331784 | tf_op jit(solution)/shard_map/ppermute | solution.py:628
  7.8 11.6 %collective-permute-start.1 = (bf16[96,576]{1,0:T(8,128)(2,1)}, bf16[96,576]{1,0:T(8,128)(2,1)S(1)}, u32[]{:S(2)}, u32[]{:S(2)}) collective-permute-start(bf16[96,576]{1,0:T(8,128)(2,1)} %get-tuple-element.98.w0), channel_id=1, source_target_pairs={{0,8},{4,12},{8,0},{12,4},{16,24},{20,28},{24,16},{28,20},{1,9},{5... | collective-permute-start | bytes 331784 | tf_op jit(solution)/shard_map/ppermute | solution.py:628
  8.4 6.8 %collective-permute-start.6 = (s32[4,6,3]{1,0,2:T(4,128)}, s32[4,6,3]{1,0,2:T(4,128)S(1)}, u32[]{:S(2)}, u32[]{:S(2)}) collective-permute-start(s32[4,6,3]{1,0,2:T(4,128)} %param.18), channel_id=1, source_target_pairs={{0,2},{2,0},{1,3},{3,1},{4,6},{6,4},{5,7},{7,5},{8,10},{10,8},{9,1... | collective-permute-start | bytes 872 | tf_op jit(solution)/shard_map/ppermute | solution.py:625
  10.1 7.0 %collective-permute-start.4 = (bf16[96,832]{1,0:T(8,128)(2,1)}, bf16[96,832]{1,0:T(8,128)(2,1)S(1)}, u32[]{:S(2)}, u32[]{:S(2)}) collective-permute-start(bf16[96,832]{1,0:T(8,128)(2,1)} %get-tuple-element.99), channel_id=1, source_target_pairs={{0,4},{4,0},{8,12},{12,8},{16,20},{20,16},{24,28},{28,24},{1,5},{5... | collective-permute-start | bytes 479240 | tf_op jit(solution)/shard_map/ppermute | solution.py:628
  15.2 16.5 %collective-permute-start = (bf16[256,768]{1,0:T(8,128)(2,1)}, bf16[256,768]{1,0:T(8,128)(2,1)S(1)}, u32[]{:S(2)}, u32[]{:S(2)}) collective-permute-start(bf16[256,768]{1,0:T(8,128)(2,1)} %own_ref.1), channel_id=1, source_target_pairs={{0,2},{2,0},{1,3},{3,1},{4,6},{6,4},{5,7},{7,5},{8,10},{10,8},{9,1... | collective-permute-start | bytes 1179656 | tf_op jit(solution)/shard_map/ppermute | solution.py:625
  17.1 10.5 %collective-permute-start.7 = (bf16[2,96,256]{2,1,0:T(8,128)(2,1)S(1)}, bf16[2,96,256]{2,1,0:T(8,128)(2,1)S(1)}, u32[]{:S(2)}, u32[]{:S(2)}) collective-permute-start(bf16[2,96,256]{2,1,0:T(8,128)(2,1)S(1)} %pad_maximum_fusion.6.refs_0_), channel_id=1, source_target_pairs={{0,16},{4,20},{8,24},{12,28},{16,0},{20,4},{24,8},{28,12},{1,17},{... | collective-permute-start | bytes 294920 | tf_op jit(solution)/shard_map/ppermute | solution.py:628
  20.1 13.2 %collective-permute-start.5 = (bf16[3,96,576]{2,1,0:T(8,128)(2,1)}, bf16[3,96,576]{2,1,0:T(8,128)(2,1)S(1)}, u32[]{:S(2)}, u32[]{:S(2)}) collective-permute-start(bf16[3,96,576]{2,1,0:T(8,128)(2,1)} %pad_maximum_fusion.2), channel_id=1, source_target_pairs={{0,4},{4,0},{8,12},{12,8},{16,20},{20,16},{24,28},{28,24},{1,5},{5... | collective-permute-start | bytes 995336 | tf_op jit(solution)/shard_map/ppermute | solution.py:628
  20.9 18.1 %collective-permute-start.9 = (bf16[1,96,768]{2,1,0:T(8,128)(2,1)S(1)}, bf16[1,96,768]{2,1,0:T(8,128)(2,1)S(1)}, u32[]{:S(2)}, u32[]{:S(2)}) collective-permute-start(bf16[1,96,768]{2,1,0:T(8,128)(2,1)S(1)} %bitcast.34), channel_id=1, source_target_pairs={{0,16},{4,20},{8,24},{12,28},{16,0},{20,4},{24,8},{28,12},{1,17},{... | collective-permute-start | bytes 442376 | tf_op jit(solution)/shard_map/ppermute | solution.py:628
  21.3 17.7 %collective-permute-start.10 = (bf16[1,96,768]{2,1,0:T(8,128)(2,1)S(1)}, bf16[1,96,768]{2,1,0:T(8,128)(2,1)S(1)}, u32[]{:S(2)}, u32[]{:S(2)}) collective-permute-start(bf16[1,96,768]{2,1,0:T(8,128)(2,1)S(1)} %bitcast.30), channel_id=1, source_target_pairs={{0,16},{4,20},{8,24},{12,28},{16,0},{20,4},{24,8},{28,12},{1,17},{... | collective-permute-start | bytes 442376 | tf_op jit(solution)/shard_map/ppermute | solution.py:628
  27.6 10.9 %collective-permute-start.8 = (bf16[4,96,256]{2,1,0:T(8,128)(2,1)S(1)}, bf16[4,96,256]{2,1,0:T(8,128)(2,1)S(1)}, u32[]{:S(2)}, u32[]{:S(2)}) collective-permute-start(bf16[4,96,256]{2,1,0:T(8,128)(2,1)S(1)} %pad_maximum_fusion.5), channel_id=1, source_target_pairs={{0,8},{4,12},{8,0},{12,4},{16,24},{20,28},{24,16},{28,20},{1,9},{5... | collective-permute-start | bytes 589832 | tf_op jit(solution)/shard_map/ppermute | solution.py:628
  31.7 10.0 %collective-permute-start.11 = (bf16[256,768]{1,0:T(8,128)(2,1)S(1)}, bf16[256,768]{1,0:T(8,128)(2,1)S(1)}, u32[]{:S(2)}, u32[]{:S(2)}) collective-permute-start(bf16[256,768]{1,0:T(8,128)(2,1)S(1)} %copy-done.3), channel_id=1, source_target_pairs={{0,2},{2,0},{1,3},{3,1},{4,6},{6,4},{5,7},{7,5},{8,10},{10,8},{9,1... | collective-permute-start | bytes 1179656 | tf_op jit(solution)/shard_map/ppermute | solution.py:625
  39.1 6.8 %collective-permute-start.13 = (bf16[2,96,768]{2,1,0:T(8,128)(2,1)S(1)}, bf16[2,96,768]{2,1,0:T(8,128)(2,1)S(1)}, u32[]{:S(2)}, u32[]{:S(2)}) collective-permute-start(bf16[2,96,768]{2,1,0:T(8,128)(2,1)S(1)} %pad_maximum_fusion.3), channel_id=1, source_target_pairs={{0,8},{4,12},{8,0},{12,4},{16,24},{20,28},{24,16},{28,20},{1,9},{5... | collective-permute-start | bytes 884744 | tf_op jit(solution)/shard_map/ppermute | solution.py:628
  39.2 6.8 %collective-permute-start.15 = (bf16[2,96,768]{2,1,0:T(8,128)(2,1)S(1)}, bf16[2,96,768]{2,1,0:T(8,128)(2,1)S(1)}, u32[]{:S(2)}, u32[]{:S(2)}) collective-permute-start(bf16[2,96,768]{2,1,0:T(8,128)(2,1)S(1)} %pad_maximum_fusion.4), channel_id=1, source_target_pairs={{0,4},{4,0},{8,12},{12,8},{16,20},{20,16},{24,28},{28,24},{1,5},{5... | collective-permute-start | bytes 884744 | tf_op jit(solution)/shard_map/ppermute | solution.py:628
  41.8 11.2 %collective-permute-start.12 = (bf16[256,768]{1,0:T(8,128)(2,1)S(1)}, bf16[256,768]{1,0:T(8,128)(2,1)S(1)}, u32[]{:S(2)}, u32[]{:S(2)}) collective-permute-start(bf16[256,768]{1,0:T(8,128)(2,1)S(1)} %shard_map.165.a_ref), channel_id=1, source_target_pairs={{0,2},{2,0},{1,3},{3,1},{4,6},{6,4},{5,7},{7,5},{8,10},{10,8},{9,1... | collective-permute-start | bytes 1179656 | tf_op jit(solution)/shard_map/ppermute | solution.py:625
  46.0 12.9 %collective-permute-start.14 = (bf16[4,96,768]{2,1,0:T(8,128)(2,1)S(1)}, bf16[4,96,768]{2,1,0:T(8,128)(2,1)S(1)}, u32[]{:S(2)}, u32[]{:S(2)}) collective-permute-start(bf16[4,96,768]{2,1,0:T(8,128)(2,1)S(1)} %pad_maximum_fusion), channel_id=1, source_target_pairs={{0,4},{4,0},{8,12},{12,8},{16,20},{20,16},{24,28},{28,24},{1,5},{5... | collective-permute-start | bytes 1769480 | tf_op jit(solution)/shard_map/ppermute | solution.py:628
  46.1 14.6 %collective-permute-start.16 = (bf16[4,96,768]{2,1,0:T(8,128)(2,1)S(1)}, bf16[4,96,768]{2,1,0:T(8,128)(2,1)S(1)}, u32[]{:S(2)}, u32[]{:S(2)}) collective-permute-start(bf16[4,96,768]{2,1,0:T(8,128)(2,1)S(1)} %pad_maximum_fusion.1), channel_id=1, source_target_pairs={{0,8},{4,12},{8,0},{12,4},{16,24},{20,28},{24,16},{28,20},{1,9},{5... | collective-permute-start | bytes 1769480 | tf_op jit(solution)/shard_map/ppermute | solution.py:628
  63.1 11.2 %collective-permute-start.18 = (bf16[256,768]{1,0:T(8,128)(2,1)S(1)}, bf16[256,768]{1,0:T(8,128)(2,1)S(1)}, u32[]{:S(2)}, u32[]{:S(2)}) collective-permute-start(bf16[256,768]{1,0:T(8,128)(2,1)S(1)} %shard_map.170.m_ref), channel_id=1, source_target_pairs={{0,2},{2,0},{1,3},{3,1},{4,6},{6,4},{5,7},{7,5},{8,10},{10,8},{9,1... | collective-permute-start | bytes 1179656 | tf_op jit(solution)/shard_map/ppermute | solution.py:625
  80.3 11.3 %collective-permute-start.21 = (bf16[256,768]{1,0:T(8,128)(2,1)S(1)}, bf16[256,768]{1,0:T(8,128)(2,1)S(1)}, u32[]{:S(2)}, u32[]{:S(2)}) collective-permute-start(bf16[256,768]{1,0:T(8,128)(2,1)S(1)} %shard_map.175.d_ref), channel_id=1, source_target_pairs={{0,2},{2,0},{1,3},{3,1},{4,6},{6,4},{5,7},{7,5},{8,10},{10,8},{9,1... | collective-permute-start | bytes 1179656 | tf_op jit(solution)/shard_map/ppermute | solution.py:625
  81.4 15.4 %collective-permute-start.22 = (bf16[4,96,768]{2,1,0:T(8,128)(2,1)S(1)}, bf16[4,96,768]{2,1,0:T(8,128)(2,1)S(1)}, u32[]{:S(2)}, u32[]{:S(2)}) collective-permute-start(bf16[4,96,768]{2,1,0:T(8,128)(2,1)S(1)} %get-tuple-element.128), channel_id=1, source_target_pairs={{0,8},{4,12},{8,0},{12,4},{16,24},{20,28},{24,16},{28,20},{1,9},{5... | collective-permute-start | bytes 1769480 | tf_op jit(solution)/shard_map/ppermute | solution.py:628
  84.4 21.6 %collective-permute-start.25 = (bf16[4,96,768]{2,1,0:T(8,128)(2,1)S(1)}, bf16[4,96,768]{2,1,0:T(8,128)(2,1)S(1)}, u32[]{:S(2)}, u32[]{:S(2)}) collective-permute-start(bf16[4,96,768]{2,1,0:T(8,128)(2,1)S(1)} %get-tuple-element.133), channel_id=1, source_target_pairs={{0,4},{4,0},{8,12},{12,8},{16,20},{20,16},{24,28},{28,24},{1,5},{5... | collective-permute-start | bytes 1769480 | tf_op jit(solution)/shard_map/ppermute | solution.py:628
  97.0 10.9 %collective-permute-start.23 = (bf16[2,96,768]{2,1,0:T(8,128)(2,1)S(1)}, bf16[2,96,768]{2,1,0:T(8,128)(2,1)S(1)}, u32[]{:S(2)}, u32[]{:S(2)}) collective-permute-start(bf16[2,96,768]{2,1,0:T(8,128)(2,1)S(1)} %get-tuple-element.142), channel_id=1, source_target_pairs={{0,4},{4,0},{8,12},{12,8},{16,20},{20,16},{24,28},{28,24},{1,5},{5... | collective-permute-start | bytes 884744 | tf_op jit(solution)/shard_map/ppermute | solution.py:628
  102.2 15.2 %collective-permute-start.26 = (bf16[4,96,512]{2,1,0:T(8,128)(2,1)S(1)}, bf16[4,96,512]{2,1,0:T(8,128)(2,1)S(1)}, u32[]{:S(2)}, u32[]{:S(2)}) collective-permute-start(bf16[4,96,512]{2,1,0:T(8,128)(2,1)S(1)} %get-tuple-element.163), channel_id=1, source_target_pairs={{0,4},{4,0},{8,12},{12,8},{16,20},{20,16},{24,28},{28,24},{1,5},{5... | collective-permute-start | bytes 1179656 | tf_op jit(solution)/shard_map/ppermute | solution.py:628
  103.4 14.0 %collective-permute-start.27 = (bf16[4,96,320]{2,1,0:T(8,128)(2,1)S(1)}, bf16[4,96,320]{2,1,0:T(8,128)(2,1)S(1)}, u32[]{:S(2)}, u32[]{:S(2)}) collective-permute-start(bf16[4,96,320]{2,1,0:T(8,128)(2,1)S(1)} %get-tuple-element.165), channel_id=1, source_target_pairs={{0,8},{4,12},{8,0},{12,4},{16,24},{20,28},{24,16},{28,20},{1,9},{5... | collective-permute-start | bytes 737288 | tf_op jit(solution)/shard_map/ppermute | solution.py:628
  106.1 14.5 %collective-permute-start.28 = (bf16[2,96,768]{2,1,0:T(8,128)(2,1)S(1)}, bf16[2,96,768]{2,1,0:T(8,128)(2,1)S(1)}, u32[]{:S(2)}, u32[]{:S(2)}) collective-permute-start(bf16[2,96,768]{2,1,0:T(8,128)(2,1)S(1)} %get-tuple-element.168), channel_id=1, source_target_pairs={{0,16},{4,20},{8,24},{12,28},{16,0},{20,4},{24,8},{28,12},{1,17},{... | collective-permute-start | bytes 884744 | tf_op jit(solution)/shard_map/ppermute | solution.py:628
  110.4 10.3 %collective-permute-start.24 = (bf16[128,768]{1,0:T(8,128)(2,1)S(1)}, bf16[128,768]{1,0:T(8,128)(2,1)S(1)}, u32[]{:S(2)}, u32[]{:S(2)}) collective-permute-start(bf16[128,768]{1,0:T(8,128)(2,1)S(1)} %get-tuple-element.157), channel_id=1, source_target_pairs={{0,2},{2,0},{1,3},{3,1},{4,6},{6,4},{5,7},{7,5},{8,10},{10,8},{9,1... | collective-permute-start | bytes 589832 | tf_op jit(solution)/shard_map/ppermute | solution.py:625
  117.6 8.3 %collective-permute-start.29 = (bf16[2,96,512]{2,1,0:T(8,128)(2,1)S(1)}, bf16[2,96,512]{2,1,0:T(8,128)(2,1)S(1)}, u32[]{:S(2)}, u32[]{:S(2)}) collective-permute-start(bf16[2,96,512]{2,1,0:T(8,128)(2,1)S(1)} %get-tuple-element.172), channel_id=1, source_target_pairs={{0,8},{4,12},{8,0},{12,4},{16,24},{20,28},{24,16},{28,20},{1,9},{5... | collective-permute-start | bytes 589832 | tf_op jit(solution)/shard_map/ppermute | solution.py:628
  117.6 13.2 %collective-permute-start.31 = (bf16[1,96,768]{2,1,0:T(8,128)(2,1)S(1)}, bf16[1,96,768]{2,1,0:T(8,128)(2,1)S(1)}, u32[]{:S(2)}, u32[]{:S(2)}) collective-permute-start(bf16[1,96,768]{2,1,0:T(8,128)(2,1)S(1)} %get-tuple-element.153), channel_id=1, source_target_pairs={{0,16},{4,20},{8,24},{12,28},{16,0},{20,4},{24,8},{28,12},{1,17},{... | collective-permute-start | bytes 442376 | tf_op jit(solution)/shard_map/ppermute | solution.py:628
  125.9 8.5 %collective-permute-start.32 = (bf16[1,96,832]{2,1,0:T(8,128)(2,1)S(1)}, bf16[1,96,832]{2,1,0:T(8,128)(2,1)S(1)}, u32[]{:S(2)}, u32[]{:S(2)}) collective-permute-start(bf16[1,96,832]{2,1,0:T(8,128)(2,1)S(1)} %get-tuple-element.179), channel_id=1, source_target_pairs={{0,16},{4,20},{8,24},{12,28},{16,0},{20,4},{24,8},{28,12},{1,17},{... | collective-permute-start | bytes 479240 | tf_op jit(solution)/shard_map/ppermute | solution.py:628
  126.7 8.9 %collective-permute-start.33 = (bf16[1,96,768]{2,1,0:T(8,128)(2,1)S(1)}, bf16[1,96,768]{2,1,0:T(8,128)(2,1)S(1)}, u32[]{:S(2)}, u32[]{:S(2)}) collective-permute-start(bf16[1,96,768]{2,1,0:T(8,128)(2,1)S(1)} %get-tuple-element.170), channel_id=1, source_target_pairs={{0,8},{4,12},{8,0},{12,4},{16,24},{20,28},{24,16},{28,20},{1,9},{5... | collective-permute-start | bytes 442376 | tf_op jit(solution)/shard_map/ppermute | solution.py:628
  130.9 6.8 %collective-permute-start.36 = (bf16[96,768]{1,0:T(8,128)(2,1)S(1)}, bf16[96,768]{1,0:T(8,128)(2,1)S(1)}, u32[]{:S(2)}, u32[]{:S(2)}) collective-permute-start(bf16[96,768]{1,0:T(8,128)(2,1)S(1)} %shard_map.188), channel_id=1, source_target_pairs={{0,2},{2,0},{1,3},{3,1},{4,6},{6,4},{5,7},{7,5},{8,10},{10,8},{9,1... | collective-permute-start | bytes 442376 | tf_op jit(solution)/shard_map/ppermute | solution.py:625
  134.4 8.6 %collective-permute-start.34 = (bf16[96,832]{1,0:T(8,128)(2,1)S(1)}, bf16[96,832]{1,0:T(8,128)(2,1)S(1)}, u32[]{:S(2)}, u32[]{:S(2)}) collective-permute-start(bf16[96,832]{1,0:T(8,128)(2,1)S(1)} %shard_map.189.near_ref), channel_id=1, source_target_pairs={{0,2},{2,0},{1,3},{3,1},{4,6},{6,4},{5,7},{7,5},{8,10},{10,8},{9,1... | collective-permute-start | bytes 479240 | tf_op jit(solution)/shard_map/ppermute | solution.py:625
  (10 other events, 82.7 us)

commit v7 on v6

--- a/solution.py
+++ b/solution.py
@@ -762,12 +762,11 @@
     dz1, da_low = call(
         norm_one_back_body, wide + [((rows + 16, width), bf16)], dz2, d, after(d_far, up[1], output), n1, r1, vecs, grad2
     )
-    down_keep, down_send = fold(after(down_own, da_low), swap_dp(down_away, 2))
     last = 4 * cols + extra
     *tail, dqkv = call(
         attend_back_body,
         [((n_out, shard, n), bf16) for n in cut(last) for _ in range(2)] + [((total_rows, 3 * cols), bf16)],
-        after(both_tp(da_low), down_send), w_out_all, qkv, o, lse, bias, x_all,
+        both_tp(da_low), w_out_all, qkv, o, lse, bias, x_all,
         flops=2 * 10**10,
         scratch=[
             ((total_rows, heads * total_rows), bf16),
@@ -778,21 +777,21 @@
         ],
     )
     mine, theirs = call(input_body, wide + low, dqkv, w1_all)
+    down_keep, down_send = fold(after(down_own, tail[0]), swap_dp(down_away, 2))
     down = fold(after(down_keep, theirs), swap_dp(down_send, 1))
-    theirs = after(theirs, down[1])
     keep, send = call(fold_input_body, [((part, width), f32), half], mine, both_tp(theirs), dz1)
     up = fold(after(up[0], mine), swap_dp(up[1], 1))
     keep1, send1, keep2, send2 = fold_first(*all_after(tail[:1], send), *tail[1:])
     got1, got2 = swap_dp(send1, 2), swap_dp(send2, 1)
     dx_far = swap_ctx(send)
-    up = fold(after(up[0], keep1), swap_dp(up[1], 4))
-    keep1 = after(keep1, dx_far, up[1])
+    keep1 = after(keep1, dx_far)
     tail = call(fold_join_body, pairs(1, last), keep1, got1, keep2, got2)
+    up = fold(after(up[0], tail[0]), swap_dp(up[1], 4))
     grad_down, down_far = fold_third(*all_after(down[:1], tail[0]), down[1], 4)
-    grad_1, far_1 = fold_third(after(tail[0], grad_down), tail[1], 4)
-    grad_up, up_far = fold_third(*all_after(up[:1], grad_1), up[1], 2)
-    down_far = after(down_far, grad_up)
-    dx = call(last_input_body, [half], keep, after(dx_far, grad_up))[0]
+    grad_up, up_far = fold_third(*up, 2)
+    grad_1, far_1 = fold_third(after(tail[0], grad_down, grad_up), tail[1], 4)
+    down_far = after(down_far, grad_1)
+    dx = call(last_input_body, [half], keep, after(dx_far, grad_1))[0]
     input_grad = call(copy_body, low, both_tp(dx, True))[0]
     grad_1 = after(grad_1, input_grad)
 

time: 144 us -> 142 us (0.986)
    ppermute x10, starting transfers between devices: 12.5 us -> 11 us  [swap_ctx(): return lax.ppermute(v, 'ctx', pair)]
  transfers between devices with their start and end apart: 37 -> 37, of which waited for: 19 -> 18; matrix products, arithmetic and copies ran while one was open for 4% -> 4% of each run, Pallas kernels for 12% -> 13%
where the time goes in v7:
time: 142 us
  waiting for transfers between devices  50.5 us (36%)
  starting transfers between devices  45.4 us (32%)
  Pallas kernels  23.8 us (17%)
  blocking collectives  14.1 us (10%)
  other arithmetic  4.1 us (3%)
  local copies, waits for them, and re-layouts  1.99 us (1%)
  between operations  1.78 us (1%)
    ppermute x24, starting transfers between devices, swap_dp(): return lax.ppermute(v, 'dp', [(i, i ^ bits) for i in range(n_dp)])  34 us
    ppermute x24, waiting for transfers between devices, swap_dp(): return lax.ppermute(v, 'dp', [(i, i ^ bits) for i in range(n_dp)])  28.2 us
    pallas_call x33, Pallas kernels, call(): pl.pallas_call(body, out_shape=shapes, in_specs=specs, out_specs=[pl.Bloc...  23.8 us
    ppermute x10, waiting for transfers between devices, swap_ctx(): return lax.ppermute(v, 'ctx', pair)  19.2 us
    all_gather x6, blocking collectives, both_tp(): return lax.all_gather(v, 'tp', axis=0, tiled=tiled)  14.1 us
    ppermute x10, starting transfers between devices, swap_ctx(): return lax.ppermute(v, 'ctx', pair)  11 us
    ppermute x3, waiting for transfers between devices, swap_tp(): return lax.ppermute(v, 'tp', pair)  3.09 us
  transfers between devices with their start and end apart: 37, of which 18 were waited for; matrix products, arithmetic and copies ran while one was open for 4% of the time, Pallas kernels for 13%

profile of v7, /device:TPU:0, one launch (start us, length us, event | category | flops | bytes accessed | tf_op | source)
XLA Modules:
  0.0 141.6 jit_solution(8082988223909206855)
XLA Ops:
  0.6 2.0 %shard_map.161 = (bf16[96,576]{1,0:T(8,128)(2,1)}, bf16[96,832]{1,0:T(8,128)(2,1)}) custom-call(bf16[3,96,384]{2,1,0:T(8,128)(2,1)} %qkv_hbm.1, bf16[2,96]{1,0:T(2,128)(2,1)} %gain_hbm.1, bf16[2,96]{1,0:T(2,128)(2,1)} %bias_hbm.1, bf16[96,384]{1,0:T(8,128)(2,1)} %bitcast.44), custom_call_target="tpu_custom_call" | custom-call | tf_op jit(solution)/shard_map/pallas_call | solution.py:240
  2.6 5.1 %collective-permute-start.3 = (bf16[96,576]{1,0:T(8,128)(2,1)}, bf16[96,576]{1,0:T(8,128)(2,1)S(1)}, u32[]{:S(2)}, u32[]{:S(2)}) collective-permute-start(bf16[96,576]{1,0:T(8,128)(2,1)} %get-tuple-element.95.w0), channel_id=1, source_target_pairs={{0,24},{4,28},{8,16},{12,20},{16,8},{20,12},{24,0},{28,4},{1,25},{... | collective-permute-start | bytes 331784 | tf_op jit(solution)/shard_map/ppermute | solution.py:628
  8.4 1.7 %collective-permute-start.6 = (s32[4,6,3]{1,0,2:T(4,128)}, s32[4,6,3]{1,0,2:T(4,128)S(1)}, u32[]{:S(2)}, u32[]{:S(2)}) collective-permute-start(s32[4,6,3]{1,0,2:T(4,128)} %param.18), channel_id=1, source_target_pairs={{0,2},{2,0},{1,3},{3,1},{4,6},{6,4},{5,7},{7,5},{8,10},{10,8},{9,1... | collective-permute-start | bytes 872 | tf_op jit(solution)/shard_map/ppermute | solution.py:625
  13.1 1.8 %shard_map.164 = (bf16[96,768]{1,0:T(8,128)(2,1)}, bf16[96,768]{1,0:T(8,128)(2,1)}) custom-call(bf16[96,1536]{1,0:T(8,128)(2,1)} %up_hbm.1, bf16[96,1536]{1,0:T(8,128)(2,1)} %bitcast.42), custom_call_target="tpu_custom_call" | custom-call | tf_op jit(solution)/shard_map/pallas_call | solution.py:240
  17.1 2.2 %collective-permute-start.7 = (bf16[2,96,256]{2,1,0:T(8,128)(2,1)S(1)}, bf16[2,96,256]{2,1,0:T(8,128)(2,1)S(1)}, u32[]{:S(2)}, u32[]{:S(2)}) collective-permute-start(bf16[2,96,256]{2,1,0:T(8,128)(2,1)S(1)} %pad_maximum_fusion.6.refs_0_), channel_id=1, source_target_pairs={{0,16},{4,20},{8,24},{12,28},{16,0},{20,4},{24,8},{28,12},{1,17},{... | collective-permute-start | bytes 294920 | tf_op jit(solution)/shard_map/ppermute | solution.py:628
  21.3 2.5 %collective-permute-start.10 = (bf16[1,96,768]{2,1,0:T(8,128)(2,1)S(1)}, bf16[1,96,768]{2,1,0:T(8,128)(2,1)S(1)}, u32[]{:S(2)}, u32[]{:S(2)}) collective-permute-start(bf16[1,96,768]{2,1,0:T(8,128)(2,1)S(1)} %bitcast.30), channel_id=1, source_target_pairs={{0,16},{4,20},{8,24},{12,28},{16,0},{20,4},{24,8},{28,12},{1,17},{... | collective-permute-start | bytes 442376 | tf_op jit(solution)/shard_map/ppermute | solution.py:628
  23.9 3.7 %collective-permute-done.7.refs_1_ = bf16[2,96,256]{2,1,0:T(8,128)(2,1)S(1)} collective-permute-done((bf16[2,96,256]{2,1,0:T(8,128)(2,1)S(1)}, bf16[2,96,256]{2,1,0:T(8,128)(2,1)S(1)}, u32[]{:S(2)}, u32[]{:S(2)}) %collective-permute-start.7) | collective-permute-done | bytes 98336 | tf_op jit(solution)/shard_map/ppermute | solution.py:628
  27.6 3.2 %collective-permute-start.8 = (bf16[4,96,256]{2,1,0:T(8,128)(2,1)S(1)}, bf16[4,96,256]{2,1,0:T(8,128)(2,1)S(1)}, u32[]{:S(2)}, u32[]{:S(2)}) collective-permute-start(bf16[4,96,256]{2,1,0:T(8,128)(2,1)S(1)} %pad_maximum_fusion.5), channel_id=1, source_target_pairs={{0,8},{4,12},{8,0},{12,4},{16,24},{20,28},{24,16},{28,20},{1,9},{5... | collective-permute-start | bytes 589832 | tf_op jit(solution)/shard_map/ppermute | solution.py:628
  33.3 2.9 %shard_map.162 = (bf16[512,192]{1,0:T(8,128)(2,1)S(1)}, bf16[512,576]{1,0:T(8,128)(2,1)S(1)}, f32[8,512]{1,0:T(8,128)S(1)}, bf16[512,768]{1,0:T(8,128)(2,1)S(1)}, bf16[768,576]{1,0:T(8,128)(2,1)S(1)}) custom-call(bf16[256,768]{1,0:T(8,128)(2,1)S(1)} %copy-done.2, bf16[256,768]{1,0:T(8,128)(2,1)S(1)} %collective-permute-done.far_ref, ...), custom_call_target="tpu_custom_call" | custom-call | tf_op jit(solution)/shard_map/pallas_call | solution.py:240
  36.2 2.3 %collective-permute-done.8.refs_2_ = bf16[4,96,256]{2,1,0:T(8,128)(2,1)S(1)} collective-permute-done((bf16[4,96,256]{2,1,0:T(8,128)(2,1)S(1)}, bf16[4,96,256]{2,1,0:T(8,128)(2,1)S(1)}, u32[]{:S(2)}, u32[]{:S(2)}) %collective-permute-start.8) | collective-permute-done | bytes 196640 | tf_op jit(solution)/shard_map/ppermute | solution.py:628
  39.3 2.4 %all-gather = bf16[512,768]{1,0:T(8,128)(2,1)S(1)} all-gather(bf16[256,768]{1,0:T(8,128)(2,1)S(1)} %get-tuple-element.108), channel_id=2, replica_groups=mesh['dp'=8,'ctx'=2,'tp'=2] {'tp'}, dimensions={0}, use_global_device_ids=true | all-gather | bytes 1179648 | tf_op jit(solution)/shard_map/all_gather | solution.py:622
  43.4 2.5 %collective-permute-done.13.w2 = bf16[2,96,768]{2,1,0:T(8,128)(2,1)S(1)} collective-permute-done((bf16[2,96,768]{2,1,0:T(8,128)(2,1)S(1)}, bf16[2,96,768]{2,1,0:T(8,128)(2,1)S(1)}, u32[]{:S(2)}, u32[]{:S(2)}) %collective-permute-start.13) | collective-permute-done | bytes 294944 | tf_op jit(solution)/shard_map/ppermute | solution.py:628
  46.1 2.0 %collective-permute-start.16 = (bf16[4,96,768]{2,1,0:T(8,128)(2,1)S(1)}, bf16[4,96,768]{2,1,0:T(8,128)(2,1)S(1)}, u32[]{:S(2)}, u32[]{:S(2)}) collective-permute-start(bf16[4,96,768]{2,1,0:T(8,128)(2,1)S(1)} %pad_maximum_fusion.1), channel_id=1, source_target_pairs={{0,8},{4,12},{8,0},{12,4},{16,24},{20,28},{24,16},{28,20},{1,9},{5... | collective-permute-start | bytes 1769480 | tf_op jit(solution)/shard_map/ppermute | solution.py:628
  48.1 4.8 %collective-permute-done.12.far_ref = bf16[256,768]{1,0:T(8,128)(2,1)S(1)} collective-permute-done((bf16[256,768]{1,0:T(8,128)(2,1)S(1)}, bf16[256,768]{1,0:T(8,128)(2,1)S(1)}, u32[]{:S(2)}, u32[]{:S(2)}) %collective-permute-start.12) | collective-permute-done | bytes 393248 | tf_op jit(solution)/shard_map/ppermute | solution.py:625
  53.4 2.5 %all_gather.29.y_ref.left_ref = bf16[512,768]{1,0:T(8,128)(2,1)S(1)} all-gather(bf16[256,768]{1,0:T(8,128)(2,1)S(1)} %get-tuple-element.113), channel_id=1, replica_groups=mesh['dp'=8,'ctx'=2,'tp'=2] {'tp'}, dimensions={0}, use_global_device_ids=true | all-gather | bytes 1179648 | tf_op jit(solution)/shard_map/all_gather | solution.py:622
  55.9 2.9 %collective-permute-done.14.w3 = bf16[4,96,768]{2,1,0:T(8,128)(2,1)S(1)} collective-permute-done((bf16[4,96,768]{2,1,0:T(8,128)(2,1)S(1)}, bf16[4,96,768]{2,1,0:T(8,128)(2,1)S(1)}, u32[]{:S(2)}, u32[]{:S(2)}) %collective-permute-start.14) | collective-permute-done | bytes 589856 | tf_op jit(solution)/shard_map/ppermute | solution.py:628
  64.3 10.1 %collective-permute-done.18.far_ref = bf16[256,768]{1,0:T(8,128)(2,1)S(1)} collective-permute-done((bf16[256,768]{1,0:T(8,128)(2,1)S(1)}, bf16[256,768]{1,0:T(8,128)(2,1)S(1)}, u32[]{:S(2)}, u32[]{:S(2)}) %collective-permute-start.18) | collective-permute-done | bytes 393248 | tf_op jit(solution)/shard_map/ppermute | solution.py:625
  75.4 1.7 %collective-permute-done.19.far_ref = bf16[256,768]{1,0:T(8,128)(2,1)S(1)} collective-permute-done((bf16[256,768]{1,0:T(8,128)(2,1)S(1)}, bf16[256,768]{1,0:T(8,128)(2,1)S(1)}, u32[]{:S(2)}, u32[]{:S(2)}) %collective-permute-start.19) | collective-permute-done | bytes 393248 | tf_op jit(solution)/shard_map/ppermute | solution.py:619
  81.4 2.0 %collective-permute-start.27 = (bf16[4,96,768]{2,1,0:T(8,128)(2,1)S(1)}, bf16[4,96,768]{2,1,0:T(8,128)(2,1)S(1)}, u32[]{:S(2)}, u32[]{:S(2)}) collective-permute-start(bf16[4,96,768]{2,1,0:T(8,128)(2,1)S(1)} %get-tuple-element.125), channel_id=1, source_target_pairs={{0,8},{4,12},{8,0},{12,4},{16,24},{20,28},{24,16},{28,20},{1,9},{5... | collective-permute-start | bytes 1769480 | tf_op jit(solution)/shard_map/ppermute | solution.py:628
  85.3 2.1 %all_gather.30.in_ref = bf16[256,768]{1,0:T(8,128)(2,1)S(1)} all-gather(bf16[128,768]{1,0:T(8,128)(2,1)S(1)} %get-tuple-element.131), channel_id=1, replica_groups=mesh['dp'=8,'ctx'=2,'tp'=2] {'tp'}, dimensions={0}, use_global_device_ids=true | all-gather | bytes 589824 | tf_op jit(solution)/shard_map/all_gather | solution.py:622
  88.2 3.4 %collective-permute-done.21.far_ref = bf16[256,768]{1,0:T(8,128)(2,1)S(1)} collective-permute-done((bf16[256,768]{1,0:T(8,128)(2,1)S(1)}, bf16[256,768]{1,0:T(8,128)(2,1)S(1)}, u32[]{:S(2)}, u32[]{:S(2)}) %collective-permute-start.21) | collective-permute-done | bytes 393248 | tf_op jit(solution)/shard_map/ppermute | solution.py:625
  92.1 2.6 %all-gather.1 = bf16[544,768]{1,0:T(8,128)(2,1)S(1)} all-gather(bf16[272,768]{1,0:T(8,128)(2,1)S(1)} %get-tuple-element.136), channel_id=3, replica_groups=mesh['dp'=8,'ctx'=2,'tp'=2] {'tp'}, dimensions={0}, use_global_device_ids=true | all-gather | bytes 1253376 | tf_op jit(solution)/shard_map/all_gather | solution.py:622
  94.7 4.2 %shard_map.179 = (bf16[4,96,512]{2,1,0:T(8,128)(2,1)S(1)}, bf16[4,96,512]{2,1,0:T(8,128)(2,1)S(1)}, bf16[4,96,320]{2,1,0:T(8,128)(2,1)S(1)}, bf16[4,96,320]{2,1,0:T(8,128)(2,1)S(1)}, bf16[512,576]{1,0:T(8,128)(2,1)S(1)}) custom-call(bf16[2,272,768]{2,1,0:T(8,128)(2,1)S(1)} %bitcast.38, bf16[768,192]{1,0:T(8,128)(2,1)S(1)} %get-tuple-element.137.w_out_ref, ...), custom_call_target="tpu_custom_call" | custom-call | flops 20000000000 | tf_op jit(solution)/shard_map/pallas_call | solution.py:240
  100.5 2.0 %collective-permute-start.24 = (bf16[4,96,320]{2,1,0:T(8,128)(2,1)S(1)}, bf16[4,96,320]{2,1,0:T(8,128)(2,1)S(1)}, u32[]{:S(2)}, u32[]{:S(2)}) collective-permute-start(bf16[4,96,320]{2,1,0:T(8,128)(2,1)S(1)} %get-tuple-element.151), channel_id=1, source_target_pairs={{0,8},{4,12},{8,0},{12,4},{16,24},{20,28},{24,16},{28,20},{1,9},{5... | collective-permute-start | bytes 737288 | tf_op jit(solution)/shard_map/ppermute | solution.py:628
  103.9 2.0 %collective-permute-start.31 = (bf16[2,96,768]{2,1,0:T(8,128)(2,1)S(1)}, bf16[2,96,768]{2,1,0:T(8,128)(2,1)S(1)}, u32[]{:S(2)}, u32[]{:S(2)}) collective-permute-start(bf16[2,96,768]{2,1,0:T(8,128)(2,1)S(1)} %get-tuple-element.170), channel_id=1, source_target_pairs={{0,16},{4,20},{8,24},{12,28},{16,0},{20,4},{24,8},{28,12},{1,17},{... | collective-permute-start | bytes 884744 | tf_op jit(solution)/shard_map/ppermute | solution.py:628
  106.0 2.4 %all-gather.2 = bf16[512,768]{1,0:T(8,128)(2,1)S(1)} all-gather(bf16[256,768]{1,0:T(8,128)(2,1)S(1)} %get-tuple-element.143), channel_id=4, replica_groups=mesh['dp'=8,'ctx'=2,'tp'=2] {'tp'}, dimensions={0}, use_global_device_ids=true | all-gather | bytes 1179648 | tf_op jit(solution)/shard_map/all_gather | solution.py:622
  109.3 5.5 %collective-permute-done.24.got2_ref = bf16[4,96,320]{2,1,0:T(8,128)(2,1)S(1)} collective-permute-done((bf16[4,96,320]{2,1,0:T(8,128)(2,1)S(1)}, bf16[4,96,320]{2,1,0:T(8,128)(2,1)S(1)}, u32[]{:S(2)}, u32[]{:S(2)}) %collective-permute-start.24) | collective-permute-done | bytes 245792 | tf_op jit(solution)/shard_map/ppermute | solution.py:628
  116.5 3.7 %collective-permute-start.29 = (bf16[1,96,768]{2,1,0:T(8,128)(2,1)S(1)}, bf16[1,96,768]{2,1,0:T(8,128)(2,1)S(1)}, u32[]{:S(2)}, u32[]{:S(2)}) collective-permute-start(bf16[1,96,768]{2,1,0:T(8,128)(2,1)S(1)} %get-tuple-element.165), channel_id=1, source_target_pairs={{0,16},{4,20},{8,24},{12,28},{16,0},{20,4},{24,8},{28,12},{1,17},{... | collective-permute-start | bytes 442376 | tf_op jit(solution)/shard_map/ppermute | solution.py:628
  121.5 3.9 %collective-permute-done.26.got2_ref = bf16[2,96,320]{2,1,0:T(8,128)(2,1)S(1)} collective-permute-done((bf16[2,96,320]{2,1,0:T(8,128)(2,1)S(1)}, bf16[2,96,320]{2,1,0:T(8,128)(2,1)S(1)}, u32[]{:S(2)}, u32[]{:S(2)}) %collective-permute-start.26) | collective-permute-done | bytes 122912 | tf_op jit(solution)/shard_map/ppermute | solution.py:628
  127.0 2.0 %collective-permute-done.29.got_ref = bf16[1,96,768]{2,1,0:T(8,128)(2,1)S(1)} collective-permute-done((bf16[1,96,768]{2,1,0:T(8,128)(2,1)S(1)}, bf16[1,96,768]{2,1,0:T(8,128)(2,1)S(1)}, u32[]{:S(2)}, u32[]{:S(2)}) %collective-permute-start.29) | collective-permute-done | bytes 147488 | tf_op jit(solution)/shard_map/ppermute | solution.py:628
  129.8 1.9 %collective-permute-done.32.got_ref = bf16[1,96,768]{2,1,0:T(8,128)(2,1)S(1)} collective-permute-done((bf16[1,96,768]{2,1,0:T(8,128)(2,1)S(1)}, bf16[1,96,768]{2,1,0:T(8,128)(2,1)S(1)}, u32[]{:S(2)}, u32[]{:S(2)}) %collective-permute-start.32) | collective-permute-done | bytes 147488 | tf_op jit(solution)/shard_map/ppermute | solution.py:628
  135.1 2.1 %all_gather.35.in_ref = bf16[256,768]{1,0:T(8,128)(2,1)S(1)} all-gather(bf16[128,768]{1,0:T(8,128)(2,1)S(1)} %shard_map.191), channel_id=1, replica_groups=mesh['dp'=8,'ctx'=2,'tp'=2] {'tp'}, dimensions={0}, use_global_device_ids=true | all-gather | bytes 589824 | tf_op jit(solution)/shard_map/all_gather | solution.py:622
  (127 shorter events, 43.3 us)
Async XLA Ops:
  2.6 16.7 %collective-permute-start.3 = (bf16[96,576]{1,0:T(8,128)(2,1)}, bf16[96,576]{1,0:T(8,128)(2,1)S(1)}, u32[]{:S(2)}, u32[]{:S(2)}) collective-permute-start(bf16[96,576]{1,0:T(8,128)(2,1)} %get-tuple-element.95.w0), channel_id=1, source_target_pairs={{0,24},{4,28},{8,16},{12,20},{16,8},{20,12},{24,0},{28,4},{1,25},{... | collective-permute-start | bytes 331784 | tf_op jit(solution)/shard_map/ppermute | solution.py:628
  7.8 11.6 %collective-permute-start.2 = (bf16[96,576]{1,0:T(8,128)(2,1)}, bf16[96,576]{1,0:T(8,128)(2,1)S(1)}, u32[]{:S(2)}, u32[]{:S(2)}) collective-permute-start(bf16[96,576]{1,0:T(8,128)(2,1)} %get-tuple-element.95.w0), channel_id=1, source_target_pairs={{0,16},{4,20},{8,24},{12,28},{16,0},{20,4},{24,8},{28,12},{1,17},{... | collective-permute-start | bytes 331784 | tf_op jit(solution)/shard_map/ppermute | solution.py:628
  7.8 11.6 %collective-permute-start.1 = (bf16[96,576]{1,0:T(8,128)(2,1)}, bf16[96,576]{1,0:T(8,128)(2,1)S(1)}, u32[]{:S(2)}, u32[]{:S(2)}) collective-permute-start(bf16[96,576]{1,0:T(8,128)(2,1)} %get-tuple-element.95.w0), channel_id=1, source_target_pairs={{0,8},{4,12},{8,0},{12,4},{16,24},{20,28},{24,16},{28,20},{1,9},{5... | collective-permute-start | bytes 331784 | tf_op jit(solution)/shard_map/ppermute | solution.py:628
  8.4 6.8 %collective-permute-start.6 = (s32[4,6,3]{1,0,2:T(4,128)}, s32[4,6,3]{1,0,2:T(4,128)S(1)}, u32[]{:S(2)}, u32[]{:S(2)}) collective-permute-start(s32[4,6,3]{1,0,2:T(4,128)} %param.18), channel_id=1, source_target_pairs={{0,2},{2,0},{1,3},{3,1},{4,6},{6,4},{5,7},{7,5},{8,10},{10,8},{9,1... | collective-permute-start | bytes 872 | tf_op jit(solution)/shard_map/ppermute | solution.py:625
  10.1 7.0 %collective-permute-start.4 = (bf16[96,832]{1,0:T(8,128)(2,1)}, bf16[96,832]{1,0:T(8,128)(2,1)S(1)}, u32[]{:S(2)}, u32[]{:S(2)}) collective-permute-start(bf16[96,832]{1,0:T(8,128)(2,1)} %get-tuple-element.96), channel_id=1, source_target_pairs={{0,4},{4,0},{8,12},{12,8},{16,20},{20,16},{24,28},{28,24},{1,5},{5... | collective-permute-start | bytes 479240 | tf_op jit(solution)/shard_map/ppermute | solution.py:628
  15.2 16.5 %collective-permute-start = (bf16[256,768]{1,0:T(8,128)(2,1)}, bf16[256,768]{1,0:T(8,128)(2,1)S(1)}, u32[]{:S(2)}, u32[]{:S(2)}) collective-permute-start(bf16[256,768]{1,0:T(8,128)(2,1)} %own_ref.1), channel_id=1, source_target_pairs={{0,2},{2,0},{1,3},{3,1},{4,6},{6,4},{5,7},{7,5},{8,10},{10,8},{9,1... | collective-permute-start | bytes 1179656 | tf_op jit(solution)/shard_map/ppermute | solution.py:625
  17.1 10.5 %collective-permute-start.7 = (bf16[2,96,256]{2,1,0:T(8,128)(2,1)S(1)}, bf16[2,96,256]{2,1,0:T(8,128)(2,1)S(1)}, u32[]{:S(2)}, u32[]{:S(2)}) collective-permute-start(bf16[2,96,256]{2,1,0:T(8,128)(2,1)S(1)} %pad_maximum_fusion.6.refs_0_), channel_id=1, source_target_pairs={{0,16},{4,20},{8,24},{12,28},{16,0},{20,4},{24,8},{28,12},{1,17},{... | collective-permute-start | bytes 294920 | tf_op jit(solution)/shard_map/ppermute | solution.py:628
  20.1 13.2 %collective-permute-start.5 = (bf16[3,96,576]{2,1,0:T(8,128)(2,1)}, bf16[3,96,576]{2,1,0:T(8,128)(2,1)S(1)}, u32[]{:S(2)}, u32[]{:S(2)}) collective-permute-start(bf16[3,96,576]{2,1,0:T(8,128)(2,1)} %pad_maximum_fusion.2), channel_id=1, source_target_pairs={{0,4},{4,0},{8,12},{12,8},{16,20},{20,16},{24,28},{28,24},{1,5},{5... | collective-permute-start | bytes 995336 | tf_op jit(solution)/shard_map/ppermute | solution.py:628
  20.9 18.1 %collective-permute-start.9 = (bf16[1,96,768]{2,1,0:T(8,128)(2,1)S(1)}, bf16[1,96,768]{2,1,0:T(8,128)(2,1)S(1)}, u32[]{:S(2)}, u32[]{:S(2)}) collective-permute-start(bf16[1,96,768]{2,1,0:T(8,128)(2,1)S(1)} %bitcast.34), channel_id=1, source_target_pairs={{0,16},{4,20},{8,24},{12,28},{16,0},{20,4},{24,8},{28,12},{1,17},{... | collective-permute-start | bytes 442376 | tf_op jit(solution)/shard_map/ppermute | solution.py:628
  21.3 17.7 %collective-permute-start.10 = (bf16[1,96,768]{2,1,0:T(8,128)(2,1)S(1)}, bf16[1,96,768]{2,1,0:T(8,128)(2,1)S(1)}, u32[]{:S(2)}, u32[]{:S(2)}) collective-permute-start(bf16[1,96,768]{2,1,0:T(8,128)(2,1)S(1)} %bitcast.30), channel_id=1, source_target_pairs={{0,16},{4,20},{8,24},{12,28},{16,0},{20,4},{24,8},{28,12},{1,17},{... | collective-permute-start | bytes 442376 | tf_op jit(solution)/shard_map/ppermute | solution.py:628
  27.6 10.9 %collective-permute-start.8 = (bf16[4,96,256]{2,1,0:T(8,128)(2,1)S(1)}, bf16[4,96,256]{2,1,0:T(8,128)(2,1)S(1)}, u32[]{:S(2)}, u32[]{:S(2)}) collective-permute-start(bf16[4,96,256]{2,1,0:T(8,128)(2,1)S(1)} %pad_maximum_fusion.5), channel_id=1, source_target_pairs={{0,8},{4,12},{8,0},{12,4},{16,24},{20,28},{24,16},{28,20},{1,9},{5... | collective-permute-start | bytes 589832 | tf_op jit(solution)/shard_map/ppermute | solution.py:628
  31.7 10.0 %collective-permute-start.11 = (bf16[256,768]{1,0:T(8,128)(2,1)S(1)}, bf16[256,768]{1,0:T(8,128)(2,1)S(1)}, u32[]{:S(2)}, u32[]{:S(2)}) collective-permute-start(bf16[256,768]{1,0:T(8,128)(2,1)S(1)} %copy-done.3), channel_id=1, source_target_pairs={{0,2},{2,0},{1,3},{3,1},{4,6},{6,4},{5,7},{7,5},{8,10},{10,8},{9,1... | collective-permute-start | bytes 1179656 | tf_op jit(solution)/shard_map/ppermute | solution.py:625
  39.1 6.8 %collective-permute-start.13 = (bf16[2,96,768]{2,1,0:T(8,128)(2,1)S(1)}, bf16[2,96,768]{2,1,0:T(8,128)(2,1)S(1)}, u32[]{:S(2)}, u32[]{:S(2)}) collective-permute-start(bf16[2,96,768]{2,1,0:T(8,128)(2,1)S(1)} %pad_maximum_fusion.3), channel_id=1, source_target_pairs={{0,8},{4,12},{8,0},{12,4},{16,24},{20,28},{24,16},{28,20},{1,9},{5... | collective-permute-start | bytes 884744 | tf_op jit(solution)/shard_map/ppermute | solution.py:628
  39.2 6.8 %collective-permute-start.15 = (bf16[2,96,768]{2,1,0:T(8,128)(2,1)S(1)}, bf16[2,96,768]{2,1,0:T(8,128)(2,1)S(1)}, u32[]{:S(2)}, u32[]{:S(2)}) collective-permute-start(bf16[2,96,768]{2,1,0:T(8,128)(2,1)S(1)} %pad_maximum_fusion.4), channel_id=1, source_target_pairs={{0,4},{4,0},{8,12},{12,8},{16,20},{20,16},{24,28},{28,24},{1,5},{5... | collective-permute-start | bytes 884744 | tf_op jit(solution)/shard_map/ppermute | solution.py:628
  41.8 11.2 %collective-permute-start.12 = (bf16[256,768]{1,0:T(8,128)(2,1)S(1)}, bf16[256,768]{1,0:T(8,128)(2,1)S(1)}, u32[]{:S(2)}, u32[]{:S(2)}) collective-permute-start(bf16[256,768]{1,0:T(8,128)(2,1)S(1)} %shard_map.165.a_ref), channel_id=1, source_target_pairs={{0,2},{2,0},{1,3},{3,1},{4,6},{6,4},{5,7},{7,5},{8,10},{10,8},{9,1... | collective-permute-start | bytes 1179656 | tf_op jit(solution)/shard_map/ppermute | solution.py:625
  46.0 12.9 %collective-permute-start.14 = (bf16[4,96,768]{2,1,0:T(8,128)(2,1)S(1)}, bf16[4,96,768]{2,1,0:T(8,128)(2,1)S(1)}, u32[]{:S(2)}, u32[]{:S(2)}) collective-permute-start(bf16[4,96,768]{2,1,0:T(8,128)(2,1)S(1)} %pad_maximum_fusion), channel_id=1, source_target_pairs={{0,4},{4,0},{8,12},{12,8},{16,20},{20,16},{24,28},{28,24},{1,5},{5... | collective-permute-start | bytes 1769480 | tf_op jit(solution)/shard_map/ppermute | solution.py:628
  46.1 14.6 %collective-permute-start.16 = (bf16[4,96,768]{2,1,0:T(8,128)(2,1)S(1)}, bf16[4,96,768]{2,1,0:T(8,128)(2,1)S(1)}, u32[]{:S(2)}, u32[]{:S(2)}) collective-permute-start(bf16[4,96,768]{2,1,0:T(8,128)(2,1)S(1)} %pad_maximum_fusion.1), channel_id=1, source_target_pairs={{0,8},{4,12},{8,0},{12,4},{16,24},{20,28},{24,16},{28,20},{1,9},{5... | collective-permute-start | bytes 1769480 | tf_op jit(solution)/shard_map/ppermute | solution.py:628
  63.1 11.2 %collective-permute-start.18 = (bf16[256,768]{1,0:T(8,128)(2,1)S(1)}, bf16[256,768]{1,0:T(8,128)(2,1)S(1)}, u32[]{:S(2)}, u32[]{:S(2)}) collective-permute-start(bf16[256,768]{1,0:T(8,128)(2,1)S(1)} %shard_map.170.m_ref), channel_id=1, source_target_pairs={{0,2},{2,0},{1,3},{3,1},{4,6},{6,4},{5,7},{7,5},{8,10},{10,8},{9,1... | collective-permute-start | bytes 1179656 | tf_op jit(solution)/shard_map/ppermute | solution.py:625
  80.3 11.3 %collective-permute-start.21 = (bf16[256,768]{1,0:T(8,128)(2,1)S(1)}, bf16[256,768]{1,0:T(8,128)(2,1)S(1)}, u32[]{:S(2)}, u32[]{:S(2)}) collective-permute-start(bf16[256,768]{1,0:T(8,128)(2,1)S(1)} %shard_map.175.d_ref), channel_id=1, source_target_pairs={{0,2},{2,0},{1,3},{3,1},{4,6},{6,4},{5,7},{7,5},{8,10},{10,8},{9,1... | collective-permute-start | bytes 1179656 | tf_op jit(solution)/shard_map/ppermute | solution.py:625
  81.4 21.0 %collective-permute-start.27 = (bf16[4,96,768]{2,1,0:T(8,128)(2,1)S(1)}, bf16[4,96,768]{2,1,0:T(8,128)(2,1)S(1)}, u32[]{:S(2)}, u32[]{:S(2)}) collective-permute-start(bf16[4,96,768]{2,1,0:T(8,128)(2,1)S(1)} %get-tuple-element.125), channel_id=1, source_target_pairs={{0,8},{4,12},{8,0},{12,4},{16,24},{20,28},{24,16},{28,20},{1,9},{5... | collective-permute-start | bytes 1769480 | tf_op jit(solution)/shard_map/ppermute | solution.py:628
  84.4 19.4 %collective-permute-start.30 = (bf16[4,96,768]{2,1,0:T(8,128)(2,1)S(1)}, bf16[4,96,768]{2,1,0:T(8,128)(2,1)S(1)}, u32[]{:S(2)}, u32[]{:S(2)}) collective-permute-start(bf16[4,96,768]{2,1,0:T(8,128)(2,1)S(1)} %get-tuple-element.130), channel_id=1, source_target_pairs={{0,4},{4,0},{8,12},{12,8},{16,20},{20,16},{24,28},{28,24},{1,5},{5... | collective-permute-start | bytes 1769480 | tf_op jit(solution)/shard_map/ppermute | solution.py:628
  98.9 15.9 %collective-permute-start.23 = (bf16[4,96,512]{2,1,0:T(8,128)(2,1)S(1)}, bf16[4,96,512]{2,1,0:T(8,128)(2,1)S(1)}, u32[]{:S(2)}, u32[]{:S(2)}) collective-permute-start(bf16[4,96,512]{2,1,0:T(8,128)(2,1)S(1)} %get-tuple-element.149), channel_id=1, source_target_pairs={{0,4},{4,0},{8,12},{12,8},{16,20},{20,16},{24,28},{28,24},{1,5},{5... | collective-permute-start | bytes 1179656 | tf_op jit(solution)/shard_map/ppermute | solution.py:628
  100.5 14.4 %collective-permute-start.24 = (bf16[4,96,320]{2,1,0:T(8,128)(2,1)S(1)}, bf16[4,96,320]{2,1,0:T(8,128)(2,1)S(1)}, u32[]{:S(2)}, u32[]{:S(2)}) collective-permute-start(bf16[4,96,320]{2,1,0:T(8,128)(2,1)S(1)} %get-tuple-element.151), channel_id=1, source_target_pairs={{0,8},{4,12},{8,0},{12,4},{16,24},{20,28},{24,16},{28,20},{1,9},{5... | collective-permute-start | bytes 737288 | tf_op jit(solution)/shard_map/ppermute | solution.py:628
  102.6 13.9 %collective-permute-start.28 = (bf16[2,96,768]{2,1,0:T(8,128)(2,1)S(1)}, bf16[2,96,768]{2,1,0:T(8,128)(2,1)S(1)}, u32[]{:S(2)}, u32[]{:S(2)}) collective-permute-start(bf16[2,96,768]{2,1,0:T(8,128)(2,1)S(1)} %get-tuple-element.162), channel_id=1, source_target_pairs={{0,4},{4,0},{8,12},{12,8},{16,20},{20,16},{24,28},{28,24},{1,5},{5... | collective-permute-start | bytes 884744 | tf_op jit(solution)/shard_map/ppermute | solution.py:628
  103.9 21.7 %collective-permute-start.31 = (bf16[2,96,768]{2,1,0:T(8,128)(2,1)S(1)}, bf16[2,96,768]{2,1,0:T(8,128)(2,1)S(1)}, u32[]{:S(2)}, u32[]{:S(2)}) collective-permute-start(bf16[2,96,768]{2,1,0:T(8,128)(2,1)S(1)} %get-tuple-element.170), channel_id=1, source_target_pairs={{0,16},{4,20},{8,24},{12,28},{16,0},{20,4},{24,8},{28,12},{1,17},{... | collective-permute-start | bytes 884744 | tf_op jit(solution)/shard_map/ppermute | solution.py:628
  108.4 13.1 %collective-permute-start.22 = (bf16[128,768]{1,0:T(8,128)(2,1)S(1)}, bf16[128,768]{1,0:T(8,128)(2,1)S(1)}, u32[]{:S(2)}, u32[]{:S(2)}) collective-permute-start(bf16[128,768]{1,0:T(8,128)(2,1)S(1)} %get-tuple-element.146), channel_id=1, source_target_pairs={{0,2},{2,0},{1,3},{3,1},{4,6},{6,4},{5,7},{7,5},{8,10},{10,8},{9,1... | collective-permute-start | bytes 589832 | tf_op jit(solution)/shard_map/ppermute | solution.py:625
  115.0 10.4 %collective-permute-start.25 = (bf16[2,96,512]{2,1,0:T(8,128)(2,1)S(1)}, bf16[2,96,512]{2,1,0:T(8,128)(2,1)S(1)}, u32[]{:S(2)}, u32[]{:S(2)}) collective-permute-start(bf16[2,96,512]{2,1,0:T(8,128)(2,1)S(1)} %get-tuple-element.154), channel_id=1, source_target_pairs={{0,8},{4,12},{8,0},{12,4},{16,24},{20,28},{24,16},{28,20},{1,9},{5... | collective-permute-start | bytes 589832 | tf_op jit(solution)/shard_map/ppermute | solution.py:628
  116.5 12.5 %collective-permute-start.29 = (bf16[1,96,768]{2,1,0:T(8,128)(2,1)S(1)}, bf16[1,96,768]{2,1,0:T(8,128)(2,1)S(1)}, u32[]{:S(2)}, u32[]{:S(2)}) collective-permute-start(bf16[1,96,768]{2,1,0:T(8,128)(2,1)S(1)} %get-tuple-element.165), channel_id=1, source_target_pairs={{0,16},{4,20},{8,24},{12,28},{16,0},{20,4},{24,8},{28,12},{1,17},{... | collective-permute-start | bytes 442376 | tf_op jit(solution)/shard_map/ppermute | solution.py:628
  125.5 8.7 %collective-permute-start.33 = (bf16[1,96,832]{2,1,0:T(8,128)(2,1)S(1)}, bf16[1,96,832]{2,1,0:T(8,128)(2,1)S(1)}, u32[]{:S(2)}, u32[]{:S(2)}) collective-permute-start(bf16[1,96,832]{2,1,0:T(8,128)(2,1)S(1)} %get-tuple-element.174), channel_id=1, source_target_pairs={{0,16},{4,20},{8,24},{12,28},{16,0},{20,4},{24,8},{28,12},{1,17},{... | collective-permute-start | bytes 479240 | tf_op jit(solution)/shard_map/ppermute | solution.py:628
  129.1 6.0 %collective-permute-start.36 = (bf16[96,768]{1,0:T(8,128)(2,1)S(1)}, bf16[96,768]{1,0:T(8,128)(2,1)S(1)}, u32[]{:S(2)}, u32[]{:S(2)}) collective-permute-start(bf16[96,768]{1,0:T(8,128)(2,1)S(1)} %shard_map.186), channel_id=1, source_target_pairs={{0,2},{2,0},{1,3},{3,1},{4,6},{6,4},{5,7},{7,5},{8,10},{10,8},{9,1... | collective-permute-start | bytes 442376 | tf_op jit(solution)/shard_map/ppermute | solution.py:625
  131.7 7.2 %collective-permute-start.35 = (bf16[96,768]{1,0:T(8,128)(2,1)S(1)}, bf16[96,768]{1,0:T(8,128)(2,1)S(1)}, u32[]{:S(2)}, u32[]{:S(2)}) collective-permute-start(bf16[96,768]{1,0:T(8,128)(2,1)S(1)} %shard_map.189), channel_id=1, source_target_pairs={{0,2},{2,0},{1,3},{3,1},{4,6},{6,4},{5,7},{7,5},{8,10},{10,8},{9,1... | collective-permute-start | bytes 442376 | tf_op jit(solution)/shard_map/ppermute | solution.py:625
  134.2 6.4 %collective-permute-start.34 = (bf16[96,832]{1,0:T(8,128)(2,1)S(1)}, bf16[96,832]{1,0:T(8,128)(2,1)S(1)}, u32[]{:S(2)}, u32[]{:S(2)}) collective-permute-start(bf16[96,832]{1,0:T(8,128)(2,1)S(1)} %shard_map.190.near_ref), channel_id=1, source_target_pairs={{0,2},{2,0},{1,3},{3,1},{4,6},{6,4},{5,7},{7,5},{8,10},{10,8},{9,1... | collective-permute-start | bytes 479240 | tf_op jit(solution)/shard_map/ppermute | solution.py:625
  (10 other events, 82.3 us)

commit v8 on v7

--- a/solution.py
+++ b/solution.py
@@ -668,10 +668,9 @@
     w1_pieces = [w1, *w1_near, far_one, swap_dp(w1_rest, 1)]
     out_pieces = [out_first, out_next]
     out_pieces.append(swap_dp(jnp.concatenate(out_pieces), 2))
-    up_pieces, down_pieces = all_after([w_up[None], w_down[None]], w1_rest)
+    up_pieces, down_pieces = all_after([w_up[None], w_down[None]], w1_rest, out_next)
     up_pieces = [up_pieces, swap_dp(up_pieces, 4)]
     down_pieces = [down_pieces, swap_dp(down_pieces, 4)]
-    e_far = swap_ctx(after(out_grad, *w1_near))
 
     picks = jnp.where(c == 0, jnp.stack([random_blocks, picks_far]), jnp.stack([picks_far, random_blocks]))
     picks = lax.dynamic_slice_in_dim(picks.reshape(2 * own_blocks, 2 * heads, 3), c * heads, heads, 1)
@@ -701,6 +700,7 @@
     def sum_tp(mine, theirs):
         return call(add_tp_body, low, mine, both_tp(theirs))[0]
 
+    e_far = swap_ctx(after(out_grad, o))
     mine, theirs, w_out_all, vecs = call(
         functools.partial(project_out_body, OUT_WAYS), wide + low + [((width, cols), bf16)] + small, o, *out_pieces,
         scratch=[((width, cols + extra), bf16)],

time: 142 us -> 140 us (0.986)
  starting transfers between devices: 45.4 us -> 43.7 us
    ppermute x24, starting transfers between devices: 34 us -> 28.7 us  [swap_dp(): return lax.ppermute(v, 'dp', [(i, i ^ bits) for i in range(n_dp)])]
    ppermute x10, starting transfers between devices: 11 us -> 14.6 us  [swap_ctx(): return lax.ppermute(v, 'ctx', pair)]
where the time goes in v8:
time: 140 us
  waiting for transfers between devices  50.3 us (36%)
  starting transfers between devices  43.7 us (31%)
  Pallas kernels  23.8 us (17%)
  blocking collectives  14 us (10%)
  other arithmetic  4.09 us (3%)
  local copies, waits for them, and re-layouts  1.99 us (1%)
  between operations  1.73 us (1%)
    ppermute x24, starting transfers between devices, swap_dp(): return lax.ppermute(v, 'dp', [(i, i ^ bits) for i in range(n_dp)])  28.7 us
    ppermute x24, waiting for transfers between devices, swap_dp(): return lax.ppermute(v, 'dp', [(i, i ^ bits) for i in range(n_dp)])  28.1 us
    pallas_call x33, Pallas kernels, call(): pl.pallas_call(body, out_shape=shapes, in_specs=specs, out_specs=[pl.Bloc...  23.8 us
    ppermute x10, waiting for transfers between devices, swap_ctx(): return lax.ppermute(v, 'ctx', pair)  19.1 us
    ppermute x10, starting transfers between devices, swap_ctx(): return lax.ppermute(v, 'ctx', pair)  14.6 us
    all_gather x6, blocking collectives, both_tp(): return lax.all_gather(v, 'tp', axis=0, tiled=tiled)  14 us
    ppermute x3, waiting for transfers between devices, swap_tp(): return lax.ppermute(v, 'tp', pair)  3.09 us
  transfers between devices with their start and end apart: 37, of which 18 were waited for; matrix products, arithmetic and copies ran while one was open for 4% of the time, Pallas kernels for 13%

profile of v8, /device:TPU:0, one launch (start us, length us, event | category | flops | bytes accessed | tf_op | source)
XLA Modules:
  0.0 139.6 jit_solution(7302317569912539809)
XLA Ops:
  0.6 2.0 %shard_map.161 = (bf16[96,576]{1,0:T(8,128)(2,1)}, bf16[96,832]{1,0:T(8,128)(2,1)}) custom-call(bf16[3,96,384]{2,1,0:T(8,128)(2,1)} %qkv_hbm.1, bf16[2,96]{1,0:T(2,128)(2,1)} %gain_hbm.1, bf16[2,96]{1,0:T(2,128)(2,1)} %bias_hbm.1, bf16[96,384]{1,0:T(8,128)(2,1)} %bitcast.44), custom_call_target="tpu_custom_call" | custom-call | tf_op jit(solution)/shard_map/pallas_call | solution.py:240
  2.6 5.1 %collective-permute-start.3 = (bf16[96,576]{1,0:T(8,128)(2,1)}, bf16[96,576]{1,0:T(8,128)(2,1)S(1)}, u32[]{:S(2)}, u32[]{:S(2)}) collective-permute-start(bf16[96,576]{1,0:T(8,128)(2,1)} %get-tuple-element.95.w0), channel_id=1, source_target_pairs={{0,24},{4,28},{8,16},{12,20},{16,8},{20,12},{24,0},{28,4},{1,25},{... | collective-permute-start | bytes 331784 | tf_op jit(solution)/shard_map/ppermute | solution.py:628
  8.4 1.7 %collective-permute-start.6 = (s32[4,6,3]{1,0,2:T(4,128)}, s32[4,6,3]{1,0,2:T(4,128)S(1)}, u32[]{:S(2)}, u32[]{:S(2)}) collective-permute-start(s32[4,6,3]{1,0,2:T(4,128)} %param.18), channel_id=1, source_target_pairs={{0,2},{2,0},{1,3},{3,1},{4,6},{6,4},{5,7},{7,5},{8,10},{10,8},{9,1... | collective-permute-start | bytes 872 | tf_op jit(solution)/shard_map/ppermute | solution.py:625
  13.1 1.8 %shard_map.164 = (bf16[96,768]{1,0:T(8,128)(2,1)}, bf16[96,768]{1,0:T(8,128)(2,1)}) custom-call(bf16[96,1536]{1,0:T(8,128)(2,1)} %up_hbm.1, bf16[96,1536]{1,0:T(8,128)(2,1)} %bitcast.42), custom_call_target="tpu_custom_call" | custom-call | tf_op jit(solution)/shard_map/pallas_call | solution.py:240
  17.1 2.2 %collective-permute-start.7 = (bf16[2,96,256]{2,1,0:T(8,128)(2,1)S(1)}, bf16[2,96,256]{2,1,0:T(8,128)(2,1)S(1)}, u32[]{:S(2)}, u32[]{:S(2)}) collective-permute-start(bf16[2,96,256]{2,1,0:T(8,128)(2,1)S(1)} %pad_maximum_fusion.6.refs_0_), channel_id=1, source_target_pairs={{0,16},{4,20},{8,24},{12,28},{16,0},{20,4},{24,8},{28,12},{1,17},{... | collective-permute-start | bytes 294920 | tf_op jit(solution)/shard_map/ppermute | solution.py:628
  20.9 2.8 %collective-permute-done.7.refs_1_ = bf16[2,96,256]{2,1,0:T(8,128)(2,1)S(1)} collective-permute-done((bf16[2,96,256]{2,1,0:T(8,128)(2,1)S(1)}, bf16[2,96,256]{2,1,0:T(8,128)(2,1)S(1)}, u32[]{:S(2)}, u32[]{:S(2)}) %collective-permute-start.7) | collective-permute-done | bytes 98336 | tf_op jit(solution)/shard_map/ppermute | solution.py:628
  24.1 3.3 %collective-permute-start.9 = (bf16[1,96,768]{2,1,0:T(8,128)(2,1)S(1)}, bf16[1,96,768]{2,1,0:T(8,128)(2,1)S(1)}, u32[]{:S(2)}, u32[]{:S(2)}) collective-permute-start(bf16[1,96,768]{2,1,0:T(8,128)(2,1)S(1)} %bitcast.34), channel_id=1, source_target_pairs={{0,16},{4,20},{8,24},{12,28},{16,0},{20,4},{24,8},{28,12},{1,17},{... | collective-permute-start | bytes 442376 | tf_op jit(solution)/shard_map/ppermute | solution.py:628
  29.0 2.9 %shard_map.162 = (bf16[512,192]{1,0:T(8,128)(2,1)S(1)}, bf16[512,576]{1,0:T(8,128)(2,1)S(1)}, f32[8,512]{1,0:T(8,128)S(1)}, bf16[512,768]{1,0:T(8,128)(2,1)S(1)}, bf16[768,576]{1,0:T(8,128)(2,1)S(1)}) custom-call(bf16[256,768]{1,0:T(8,128)(2,1)S(1)} %copy-done.2, bf16[256,768]{1,0:T(8,128)(2,1)S(1)} %collective-permute-done.far_ref, ...), custom_call_target="tpu_custom_call" | custom-call | tf_op jit(solution)/shard_map/pallas_call | solution.py:240
  31.9 1.6 %collective-permute-start.11 = (bf16[256,768]{1,0:T(8,128)(2,1)S(1)}, bf16[256,768]{1,0:T(8,128)(2,1)S(1)}, u32[]{:S(2)}, u32[]{:S(2)}) collective-permute-start(bf16[256,768]{1,0:T(8,128)(2,1)S(1)} %copy-done.3), channel_id=1, source_target_pairs={{0,2},{2,0},{1,3},{3,1},{4,6},{6,4},{5,7},{7,5},{8,10},{10,8},{9,1... | collective-permute-start | bytes 1179656 | tf_op jit(solution)/shard_map/ppermute | solution.py:625
  34.0 2.5 %collective-permute-done.9.w1 = bf16[1,96,768]{2,1,0:T(8,128)(2,1)S(1)} collective-permute-done((bf16[1,96,768]{2,1,0:T(8,128)(2,1)S(1)}, bf16[1,96,768]{2,1,0:T(8,128)(2,1)S(1)}, u32[]{:S(2)}, u32[]{:S(2)}) %collective-permute-start.9) | collective-permute-done | bytes 147488 | tf_op jit(solution)/shard_map/ppermute | solution.py:628
  36.6 1.6 %collective-permute-done.10.refs_1_ = bf16[1,96,768]{2,1,0:T(8,128)(2,1)S(1)} collective-permute-done((bf16[1,96,768]{2,1,0:T(8,128)(2,1)S(1)}, bf16[1,96,768]{2,1,0:T(8,128)(2,1)S(1)}, u32[]{:S(2)}, u32[]{:S(2)}) %collective-permute-start.10) | collective-permute-done | bytes 147488 | tf_op jit(solution)/shard_map/ppermute | solution.py:628
  38.9 2.4 %all-gather = bf16[512,768]{1,0:T(8,128)(2,1)S(1)} all-gather(bf16[256,768]{1,0:T(8,128)(2,1)S(1)} %get-tuple-element.108), channel_id=2, replica_groups=mesh['dp'=8,'ctx'=2,'tp'=2] {'tp'}, dimensions={0}, use_global_device_ids=true | all-gather | bytes 1179648 | tf_op jit(solution)/shard_map/all_gather | solution.py:622
  41.4 4.1 %collective-permute-done.13.w2 = bf16[2,96,768]{2,1,0:T(8,128)(2,1)S(1)} collective-permute-done((bf16[2,96,768]{2,1,0:T(8,128)(2,1)S(1)}, bf16[2,96,768]{2,1,0:T(8,128)(2,1)S(1)}, u32[]{:S(2)}, u32[]{:S(2)}) %collective-permute-start.13) | collective-permute-done | bytes 294944 | tf_op jit(solution)/shard_map/ppermute | solution.py:628
  48.4 5.8 %collective-permute-done.12.far_ref = bf16[256,768]{1,0:T(8,128)(2,1)S(1)} collective-permute-done((bf16[256,768]{1,0:T(8,128)(2,1)S(1)}, bf16[256,768]{1,0:T(8,128)(2,1)S(1)}, u32[]{:S(2)}, u32[]{:S(2)}) %collective-permute-start.12) | collective-permute-done | bytes 393248 | tf_op jit(solution)/shard_map/ppermute | solution.py:625
  54.6 2.5 %all_gather.29.y_ref.left_ref = bf16[512,768]{1,0:T(8,128)(2,1)S(1)} all-gather(bf16[256,768]{1,0:T(8,128)(2,1)S(1)} %get-tuple-element.113), channel_id=1, replica_groups=mesh['dp'=8,'ctx'=2,'tp'=2] {'tp'}, dimensions={0}, use_global_device_ids=true | all-gather | bytes 1179648 | tf_op jit(solution)/shard_map/all_gather | solution.py:622
  63.8 9.7 %collective-permute-done.18.far_ref = bf16[256,768]{1,0:T(8,128)(2,1)S(1)} collective-permute-done((bf16[256,768]{1,0:T(8,128)(2,1)S(1)}, bf16[256,768]{1,0:T(8,128)(2,1)S(1)}, u32[]{:S(2)}, u32[]{:S(2)}) %collective-permute-start.18) | collective-permute-done | bytes 393248 | tf_op jit(solution)/shard_map/ppermute | solution.py:625
  74.5 1.7 %collective-permute-done.19.far_ref = bf16[256,768]{1,0:T(8,128)(2,1)S(1)} collective-permute-done((bf16[256,768]{1,0:T(8,128)(2,1)S(1)}, bf16[256,768]{1,0:T(8,128)(2,1)S(1)}, u32[]{:S(2)}, u32[]{:S(2)}) %collective-permute-start.19) | collective-permute-done | bytes 393248 | tf_op jit(solution)/shard_map/ppermute | solution.py:619
  79.4 1.6 %collective-permute-start.21 = (bf16[256,768]{1,0:T(8,128)(2,1)S(1)}, bf16[256,768]{1,0:T(8,128)(2,1)S(1)}, u32[]{:S(2)}, u32[]{:S(2)}) collective-permute-start(bf16[256,768]{1,0:T(8,128)(2,1)S(1)} %shard_map.175.d_ref), channel_id=1, source_target_pairs={{0,2},{2,0},{1,3},{3,1},{4,6},{6,4},{5,7},{7,5},{8,10},{10,8},{9,1... | collective-permute-start | bytes 1179656 | tf_op jit(solution)/shard_map/ppermute | solution.py:625
  81.0 1.7 %collective-permute-start.27 = (bf16[4,96,768]{2,1,0:T(8,128)(2,1)S(1)}, bf16[4,96,768]{2,1,0:T(8,128)(2,1)S(1)}, u32[]{:S(2)}, u32[]{:S(2)}) collective-permute-start(bf16[4,96,768]{2,1,0:T(8,128)(2,1)S(1)} %get-tuple-element.125), channel_id=1, source_target_pairs={{0,8},{4,12},{8,0},{12,4},{16,24},{20,28},{24,16},{28,20},{1,9},{5... | collective-permute-start | bytes 1769480 | tf_op jit(solution)/shard_map/ppermute | solution.py:628
  84.2 2.1 %all_gather.30.in_ref = bf16[256,768]{1,0:T(8,128)(2,1)S(1)} all-gather(bf16[128,768]{1,0:T(8,128)(2,1)S(1)} %get-tuple-element.131), channel_id=1, replica_groups=mesh['dp'=8,'ctx'=2,'tp'=2] {'tp'}, dimensions={0}, use_global_device_ids=true | all-gather | bytes 589824 | tf_op jit(solution)/shard_map/all_gather | solution.py:622
  87.1 3.6 %collective-permute-done.21.far_ref = bf16[256,768]{1,0:T(8,128)(2,1)S(1)} collective-permute-done((bf16[256,768]{1,0:T(8,128)(2,1)S(1)}, bf16[256,768]{1,0:T(8,128)(2,1)S(1)}, u32[]{:S(2)}, u32[]{:S(2)}) %collective-permute-start.21) | collective-permute-done | bytes 393248 | tf_op jit(solution)/shard_map/ppermute | solution.py:625
  91.2 2.6 %all-gather.1 = bf16[544,768]{1,0:T(8,128)(2,1)S(1)} all-gather(bf16[272,768]{1,0:T(8,128)(2,1)S(1)} %get-tuple-element.136), channel_id=3, replica_groups=mesh['dp'=8,'ctx'=2,'tp'=2] {'tp'}, dimensions={0}, use_global_device_ids=true | all-gather | bytes 1253376 | tf_op jit(solution)/shard_map/all_gather | solution.py:622
  93.9 4.2 %shard_map.179 = (bf16[4,96,512]{2,1,0:T(8,128)(2,1)S(1)}, bf16[4,96,512]{2,1,0:T(8,128)(2,1)S(1)}, bf16[4,96,320]{2,1,0:T(8,128)(2,1)S(1)}, bf16[4,96,320]{2,1,0:T(8,128)(2,1)S(1)}, bf16[512,576]{1,0:T(8,128)(2,1)S(1)}) custom-call(bf16[2,272,768]{2,1,0:T(8,128)(2,1)S(1)} %bitcast.38, bf16[768,192]{1,0:T(8,128)(2,1)S(1)} %get-tuple-element.137.w_out_ref, ...), custom_call_target="tpu_custom_call" | custom-call | flops 20000000000 | tf_op jit(solution)/shard_map/pallas_call | solution.py:240
  104.1 2.4 %all-gather.2 = bf16[512,768]{1,0:T(8,128)(2,1)S(1)} all-gather(bf16[256,768]{1,0:T(8,128)(2,1)S(1)} %get-tuple-element.143), channel_id=4, replica_groups=mesh['dp'=8,'ctx'=2,'tp'=2] {'tp'}, dimensions={0}, use_global_device_ids=true | all-gather | bytes 1179648 | tf_op jit(solution)/shard_map/all_gather | solution.py:622
  107.9 4.0 %collective-permute-done.24.got2_ref = bf16[4,96,320]{2,1,0:T(8,128)(2,1)S(1)} collective-permute-done((bf16[4,96,320]{2,1,0:T(8,128)(2,1)S(1)}, bf16[4,96,320]{2,1,0:T(8,128)(2,1)S(1)}, u32[]{:S(2)}, u32[]{:S(2)}) %collective-permute-start.24) | collective-permute-done | bytes 245792 | tf_op jit(solution)/shard_map/ppermute | solution.py:628
  112.1 3.5 %collective-permute-done.28.got_ref = bf16[2,96,768]{2,1,0:T(8,128)(2,1)S(1)} collective-permute-done((bf16[2,96,768]{2,1,0:T(8,128)(2,1)S(1)}, bf16[2,96,768]{2,1,0:T(8,128)(2,1)S(1)}, u32[]{:S(2)}, u32[]{:S(2)}) %collective-permute-start.28) | collective-permute-done | bytes 294944 | tf_op jit(solution)/shard_map/ppermute | solution.py:628
  115.7 2.5 %collective-permute-start.29 = (bf16[1,96,768]{2,1,0:T(8,128)(2,1)S(1)}, bf16[1,96,768]{2,1,0:T(8,128)(2,1)S(1)}, u32[]{:S(2)}, u32[]{:S(2)}) collective-permute-start(bf16[1,96,768]{2,1,0:T(8,128)(2,1)S(1)} %get-tuple-element.165), channel_id=1, source_target_pairs={{0,16},{4,20},{8,24},{12,28},{16,0},{20,4},{24,8},{28,12},{1,17},{... | collective-permute-start | bytes 442376 | tf_op jit(solution)/shard_map/ppermute | solution.py:628
  118.7 4.6 %collective-permute-done.26.got2_ref = bf16[2,96,320]{2,1,0:T(8,128)(2,1)S(1)} collective-permute-done((bf16[2,96,320]{2,1,0:T(8,128)(2,1)S(1)}, bf16[2,96,320]{2,1,0:T(8,128)(2,1)S(1)}, u32[]{:S(2)}, u32[]{:S(2)}) %collective-permute-start.26) | collective-permute-done | bytes 122912 | tf_op jit(solution)/shard_map/ppermute | solution.py:628
  124.0 1.8 %collective-permute-start.32 = (bf16[1,96,768]{2,1,0:T(8,128)(2,1)S(1)}, bf16[1,96,768]{2,1,0:T(8,128)(2,1)S(1)}, u32[]{:S(2)}, u32[]{:S(2)}) collective-permute-start(bf16[1,96,768]{2,1,0:T(8,128)(2,1)S(1)} %get-tuple-element.172), channel_id=1, source_target_pairs={{0,8},{4,12},{8,0},{12,4},{16,24},{20,28},{24,16},{28,20},{1,9},{5... | collective-permute-start | bytes 442376 | tf_op jit(solution)/shard_map/ppermute | solution.py:628
  127.0 1.8 %collective-permute-start.36 = (bf16[96,768]{1,0:T(8,128)(2,1)S(1)}, bf16[96,768]{1,0:T(8,128)(2,1)S(1)}, u32[]{:S(2)}, u32[]{:S(2)}) collective-permute-start(bf16[96,768]{1,0:T(8,128)(2,1)S(1)} %shard_map.186), channel_id=1, source_target_pairs={{0,2},{2,0},{1,3},{3,1},{4,6},{6,4},{5,7},{7,5},{8,10},{10,8},{9,1... | collective-permute-start | bytes 442376 | tf_op jit(solution)/shard_map/ppermute | solution.py:625
  132.4 1.6 %collective-permute-start.34 = (bf16[96,832]{1,0:T(8,128)(2,1)S(1)}, bf16[96,832]{1,0:T(8,128)(2,1)S(1)}, u32[]{:S(2)}, u32[]{:S(2)}) collective-permute-start(bf16[96,832]{1,0:T(8,128)(2,1)S(1)} %shard_map.190.near_ref), channel_id=1, source_target_pairs={{0,2},{2,0},{1,3},{3,1},{4,6},{6,4},{5,7},{7,5},{8,10},{10,8},{9,1... | collective-permute-start | bytes 479240 | tf_op jit(solution)/shard_map/ppermute | solution.py:625
  134.0 2.1 %all_gather.35.in_ref = bf16[256,768]{1,0:T(8,128)(2,1)S(1)} all-gather(bf16[128,768]{1,0:T(8,128)(2,1)S(1)} %shard_map.191), channel_id=1, replica_groups=mesh['dp'=8,'ctx'=2,'tp'=2] {'tp'}, dimensions={0}, use_global_device_ids=true | all-gather | bytes 589824 | tf_op jit(solution)/shard_map/all_gather | solution.py:622
  (127 shorter events, 44.2 us)
Async XLA Ops:
  2.6 16.7 %collective-permute-start.3 = (bf16[96,576]{1,0:T(8,128)(2,1)}, bf16[96,576]{1,0:T(8,128)(2,1)S(1)}, u32[]{:S(2)}, u32[]{:S(2)}) collective-permute-start(bf16[96,576]{1,0:T(8,128)(2,1)} %get-tuple-element.95.w0), channel_id=1, source_target_pairs={{0,24},{4,28},{8,16},{12,20},{16,8},{20,12},{24,0},{28,4},{1,25},{... | collective-permute-start | bytes 331784 | tf_op jit(solution)/shard_map/ppermute | solution.py:628
  7.8 11.5 %collective-permute-start.2 = (bf16[96,576]{1,0:T(8,128)(2,1)}, bf16[96,576]{1,0:T(8,128)(2,1)S(1)}, u32[]{:S(2)}, u32[]{:S(2)}) collective-permute-start(bf16[96,576]{1,0:T(8,128)(2,1)} %get-tuple-element.95.w0), channel_id=1, source_target_pairs={{0,16},{4,20},{8,24},{12,28},{16,0},{20,4},{24,8},{28,12},{1,17},{... | collective-permute-start | bytes 331784 | tf_op jit(solution)/shard_map/ppermute | solution.py:628
  7.8 11.5 %collective-permute-start.1 = (bf16[96,576]{1,0:T(8,128)(2,1)}, bf16[96,576]{1,0:T(8,128)(2,1)S(1)}, u32[]{:S(2)}, u32[]{:S(2)}) collective-permute-start(bf16[96,576]{1,0:T(8,128)(2,1)} %get-tuple-element.95.w0), channel_id=1, source_target_pairs={{0,8},{4,12},{8,0},{12,4},{16,24},{20,28},{24,16},{28,20},{1,9},{5... | collective-permute-start | bytes 331784 | tf_op jit(solution)/shard_map/ppermute | solution.py:628
  8.4 6.8 %collective-permute-start.6 = (s32[4,6,3]{1,0,2:T(4,128)}, s32[4,6,3]{1,0,2:T(4,128)S(1)}, u32[]{:S(2)}, u32[]{:S(2)}) collective-permute-start(s32[4,6,3]{1,0,2:T(4,128)} %param.18), channel_id=1, source_target_pairs={{0,2},{2,0},{1,3},{3,1},{4,6},{6,4},{5,7},{7,5},{8,10},{10,8},{9,1... | collective-permute-start | bytes 872 | tf_op jit(solution)/shard_map/ppermute | solution.py:625
  10.1 7.0 %collective-permute-start.4 = (bf16[96,832]{1,0:T(8,128)(2,1)}, bf16[96,832]{1,0:T(8,128)(2,1)S(1)}, u32[]{:S(2)}, u32[]{:S(2)}) collective-permute-start(bf16[96,832]{1,0:T(8,128)(2,1)} %get-tuple-element.96), channel_id=1, source_target_pairs={{0,4},{4,0},{8,12},{12,8},{16,20},{20,16},{24,28},{28,24},{1,5},{5... | collective-permute-start | bytes 479240 | tf_op jit(solution)/shard_map/ppermute | solution.py:628
  15.2 13.2 %collective-permute-start = (bf16[256,768]{1,0:T(8,128)(2,1)}, bf16[256,768]{1,0:T(8,128)(2,1)S(1)}, u32[]{:S(2)}, u32[]{:S(2)}) collective-permute-start(bf16[256,768]{1,0:T(8,128)(2,1)} %own_ref.1), channel_id=1, source_target_pairs={{0,2},{2,0},{1,3},{3,1},{4,6},{6,4},{5,7},{7,5},{8,10},{10,8},{9,1... | collective-permute-start | bytes 1179656 | tf_op jit(solution)/shard_map/ppermute | solution.py:625
  17.1 6.7 %collective-permute-start.7 = (bf16[2,96,256]{2,1,0:T(8,128)(2,1)S(1)}, bf16[2,96,256]{2,1,0:T(8,128)(2,1)S(1)}, u32[]{:S(2)}, u32[]{:S(2)}) collective-permute-start(bf16[2,96,256]{2,1,0:T(8,128)(2,1)S(1)} %pad_maximum_fusion.6.refs_0_), channel_id=1, source_target_pairs={{0,16},{4,20},{8,24},{12,28},{16,0},{20,4},{24,8},{28,12},{1,17},{... | collective-permute-start | bytes 294920 | tf_op jit(solution)/shard_map/ppermute | solution.py:628
  20.1 8.9 %collective-permute-start.5 = (bf16[3,96,576]{2,1,0:T(8,128)(2,1)}, bf16[3,96,576]{2,1,0:T(8,128)(2,1)S(1)}, u32[]{:S(2)}, u32[]{:S(2)}) collective-permute-start(bf16[3,96,576]{2,1,0:T(8,128)(2,1)} %pad_maximum_fusion.2), channel_id=1, source_target_pairs={{0,4},{4,0},{8,12},{12,8},{16,20},{20,16},{24,28},{28,24},{1,5},{5... | collective-permute-start | bytes 995336 | tf_op jit(solution)/shard_map/ppermute | solution.py:628
  23.8 9.7 %collective-permute-start.8 = (bf16[4,96,256]{2,1,0:T(8,128)(2,1)S(1)}, bf16[4,96,256]{2,1,0:T(8,128)(2,1)S(1)}, u32[]{:S(2)}, u32[]{:S(2)}) collective-permute-start(bf16[4,96,256]{2,1,0:T(8,128)(2,1)S(1)} %pad_maximum_fusion.5), channel_id=1, source_target_pairs={{0,8},{4,12},{8,0},{12,4},{16,24},{20,28},{24,16},{28,20},{1,9},{5... | collective-permute-start | bytes 589832 | tf_op jit(solution)/shard_map/ppermute | solution.py:628
  24.1 12.5 %collective-permute-start.9 = (bf16[1,96,768]{2,1,0:T(8,128)(2,1)S(1)}, bf16[1,96,768]{2,1,0:T(8,128)(2,1)S(1)}, u32[]{:S(2)}, u32[]{:S(2)}) collective-permute-start(bf16[1,96,768]{2,1,0:T(8,128)(2,1)S(1)} %bitcast.34), channel_id=1, source_target_pairs={{0,16},{4,20},{8,24},{12,28},{16,0},{20,4},{24,8},{28,12},{1,17},{... | collective-permute-start | bytes 442376 | tf_op jit(solution)/shard_map/ppermute | solution.py:628
  27.4 10.7 %collective-permute-start.10 = (bf16[1,96,768]{2,1,0:T(8,128)(2,1)S(1)}, bf16[1,96,768]{2,1,0:T(8,128)(2,1)S(1)}, u32[]{:S(2)}, u32[]{:S(2)}) collective-permute-start(bf16[1,96,768]{2,1,0:T(8,128)(2,1)S(1)} %bitcast.30), channel_id=1, source_target_pairs={{0,16},{4,20},{8,24},{12,28},{16,0},{20,4},{24,8},{28,12},{1,17},{... | collective-permute-start | bytes 442376 | tf_op jit(solution)/shard_map/ppermute | solution.py:628
  31.9 14.2 %collective-permute-start.11 = (bf16[256,768]{1,0:T(8,128)(2,1)S(1)}, bf16[256,768]{1,0:T(8,128)(2,1)S(1)}, u32[]{:S(2)}, u32[]{:S(2)}) collective-permute-start(bf16[256,768]{1,0:T(8,128)(2,1)S(1)} %copy-done.3), channel_id=1, source_target_pairs={{0,2},{2,0},{1,3},{3,1},{4,6},{6,4},{5,7},{7,5},{8,10},{10,8},{9,1... | collective-permute-start | bytes 1179656 | tf_op jit(solution)/shard_map/ppermute | solution.py:625
  38.2 7.3 %collective-permute-start.13 = (bf16[2,96,768]{2,1,0:T(8,128)(2,1)S(1)}, bf16[2,96,768]{2,1,0:T(8,128)(2,1)S(1)}, u32[]{:S(2)}, u32[]{:S(2)}) collective-permute-start(bf16[2,96,768]{2,1,0:T(8,128)(2,1)S(1)} %pad_maximum_fusion.3), channel_id=1, source_target_pairs={{0,8},{4,12},{8,0},{12,4},{16,24},{20,28},{24,16},{28,20},{1,9},{5... | collective-permute-start | bytes 884744 | tf_op jit(solution)/shard_map/ppermute | solution.py:628
  38.3 9.3 %collective-permute-start.15 = (bf16[2,96,768]{2,1,0:T(8,128)(2,1)S(1)}, bf16[2,96,768]{2,1,0:T(8,128)(2,1)S(1)}, u32[]{:S(2)}, u32[]{:S(2)}) collective-permute-start(bf16[2,96,768]{2,1,0:T(8,128)(2,1)S(1)} %pad_maximum_fusion.4), channel_id=1, source_target_pairs={{0,4},{4,0},{8,12},{12,8},{16,20},{20,16},{24,28},{28,24},{1,5},{5... | collective-permute-start | bytes 884744 | tf_op jit(solution)/shard_map/ppermute | solution.py:628
  45.5 12.7 %collective-permute-start.14 = (bf16[4,96,768]{2,1,0:T(8,128)(2,1)S(1)}, bf16[4,96,768]{2,1,0:T(8,128)(2,1)S(1)}, u32[]{:S(2)}, u32[]{:S(2)}) collective-permute-start(bf16[4,96,768]{2,1,0:T(8,128)(2,1)S(1)} %pad_maximum_fusion), channel_id=1, source_target_pairs={{0,4},{4,0},{8,12},{12,8},{16,20},{20,16},{24,28},{28,24},{1,5},{5... | collective-permute-start | bytes 1769480 | tf_op jit(solution)/shard_map/ppermute | solution.py:628
  46.1 8.1 %collective-permute-start.12 = (bf16[256,768]{1,0:T(8,128)(2,1)S(1)}, bf16[256,768]{1,0:T(8,128)(2,1)S(1)}, u32[]{:S(2)}, u32[]{:S(2)}) collective-permute-start(bf16[256,768]{1,0:T(8,128)(2,1)S(1)} %shard_map.165.a_ref), channel_id=1, source_target_pairs={{0,2},{2,0},{1,3},{3,1},{4,6},{6,4},{5,7},{7,5},{8,10},{10,8},{9,1... | collective-permute-start | bytes 1179656 | tf_op jit(solution)/shard_map/ppermute | solution.py:625
  47.7 12.1 %collective-permute-start.16 = (bf16[4,96,768]{2,1,0:T(8,128)(2,1)S(1)}, bf16[4,96,768]{2,1,0:T(8,128)(2,1)S(1)}, u32[]{:S(2)}, u32[]{:S(2)}) collective-permute-start(bf16[4,96,768]{2,1,0:T(8,128)(2,1)S(1)} %pad_maximum_fusion.1), channel_id=1, source_target_pairs={{0,8},{4,12},{8,0},{12,4},{16,24},{20,28},{24,16},{28,20},{1,9},{5... | collective-permute-start | bytes 1769480 | tf_op jit(solution)/shard_map/ppermute | solution.py:628
  62.3 11.2 %collective-permute-start.18 = (bf16[256,768]{1,0:T(8,128)(2,1)S(1)}, bf16[256,768]{1,0:T(8,128)(2,1)S(1)}, u32[]{:S(2)}, u32[]{:S(2)}) collective-permute-start(bf16[256,768]{1,0:T(8,128)(2,1)S(1)} %shard_map.170.m_ref), channel_id=1, source_target_pairs={{0,2},{2,0},{1,3},{3,1},{4,6},{6,4},{5,7},{7,5},{8,10},{10,8},{9,1... | collective-permute-start | bytes 1179656 | tf_op jit(solution)/shard_map/ppermute | solution.py:625
  79.4 11.3 %collective-permute-start.21 = (bf16[256,768]{1,0:T(8,128)(2,1)S(1)}, bf16[256,768]{1,0:T(8,128)(2,1)S(1)}, u32[]{:S(2)}, u32[]{:S(2)}) collective-permute-start(bf16[256,768]{1,0:T(8,128)(2,1)S(1)} %shard_map.175.d_ref), channel_id=1, source_target_pairs={{0,2},{2,0},{1,3},{3,1},{4,6},{6,4},{5,7},{7,5},{8,10},{10,8},{9,1... | collective-permute-start | bytes 1179656 | tf_op jit(solution)/shard_map/ppermute | solution.py:625
  81.0 19.4 %collective-permute-start.27 = (bf16[4,96,768]{2,1,0:T(8,128)(2,1)S(1)}, bf16[4,96,768]{2,1,0:T(8,128)(2,1)S(1)}, u32[]{:S(2)}, u32[]{:S(2)}) collective-permute-start(bf16[4,96,768]{2,1,0:T(8,128)(2,1)S(1)} %get-tuple-element.125), channel_id=1, source_target_pairs={{0,8},{4,12},{8,0},{12,4},{16,24},{20,28},{24,16},{28,20},{1,9},{5... | collective-permute-start | bytes 1769480 | tf_op jit(solution)/shard_map/ppermute | solution.py:628
  83.6 19.2 %collective-permute-start.30 = (bf16[4,96,768]{2,1,0:T(8,128)(2,1)S(1)}, bf16[4,96,768]{2,1,0:T(8,128)(2,1)S(1)}, u32[]{:S(2)}, u32[]{:S(2)}) collective-permute-start(bf16[4,96,768]{2,1,0:T(8,128)(2,1)S(1)} %get-tuple-element.130), channel_id=1, source_target_pairs={{0,4},{4,0},{8,12},{12,8},{16,20},{20,16},{24,28},{28,24},{1,5},{5... | collective-permute-start | bytes 1769480 | tf_op jit(solution)/shard_map/ppermute | solution.py:628
  98.1 13.8 %collective-permute-start.23 = (bf16[4,96,512]{2,1,0:T(8,128)(2,1)S(1)}, bf16[4,96,512]{2,1,0:T(8,128)(2,1)S(1)}, u32[]{:S(2)}, u32[]{:S(2)}) collective-permute-start(bf16[4,96,512]{2,1,0:T(8,128)(2,1)S(1)} %get-tuple-element.149), channel_id=1, source_target_pairs={{0,4},{4,0},{8,12},{12,8},{16,20},{20,16},{24,28},{28,24},{1,5},{5... | collective-permute-start | bytes 1179656 | tf_op jit(solution)/shard_map/ppermute | solution.py:628
  99.6 12.3 %collective-permute-start.24 = (bf16[4,96,320]{2,1,0:T(8,128)(2,1)S(1)}, bf16[4,96,320]{2,1,0:T(8,128)(2,1)S(1)}, u32[]{:S(2)}, u32[]{:S(2)}) collective-permute-start(bf16[4,96,320]{2,1,0:T(8,128)(2,1)S(1)} %get-tuple-element.151), channel_id=1, source_target_pairs={{0,8},{4,12},{8,0},{12,4},{16,24},{20,28},{24,16},{28,20},{1,9},{5... | collective-permute-start | bytes 737288 | tf_op jit(solution)/shard_map/ppermute | solution.py:628
  100.5 15.1 %collective-permute-start.28 = (bf16[2,96,768]{2,1,0:T(8,128)(2,1)S(1)}, bf16[2,96,768]{2,1,0:T(8,128)(2,1)S(1)}, u32[]{:S(2)}, u32[]{:S(2)}) collective-permute-start(bf16[2,96,768]{2,1,0:T(8,128)(2,1)S(1)} %get-tuple-element.162), channel_id=1, source_target_pairs={{0,4},{4,0},{8,12},{12,8},{16,20},{20,16},{24,28},{28,24},{1,5},{5... | collective-permute-start | bytes 884744 | tf_op jit(solution)/shard_map/ppermute | solution.py:628
  103.0 20.9 %collective-permute-start.31 = (bf16[2,96,768]{2,1,0:T(8,128)(2,1)S(1)}, bf16[2,96,768]{2,1,0:T(8,128)(2,1)S(1)}, u32[]{:S(2)}, u32[]{:S(2)}) collective-permute-start(bf16[2,96,768]{2,1,0:T(8,128)(2,1)S(1)} %get-tuple-element.170), channel_id=1, source_target_pairs={{0,16},{4,20},{8,24},{12,28},{16,0},{20,4},{24,8},{28,12},{1,17},{... | collective-permute-start | bytes 884744 | tf_op jit(solution)/shard_map/ppermute | solution.py:628
  106.5 12.2 %collective-permute-start.22 = (bf16[128,768]{1,0:T(8,128)(2,1)S(1)}, bf16[128,768]{1,0:T(8,128)(2,1)S(1)}, u32[]{:S(2)}, u32[]{:S(2)}) collective-permute-start(bf16[128,768]{1,0:T(8,128)(2,1)S(1)} %get-tuple-element.146), channel_id=1, source_target_pairs={{0,2},{2,0},{1,3},{3,1},{4,6},{6,4},{5,7},{7,5},{8,10},{10,8},{9,1... | collective-permute-start | bytes 589832 | tf_op jit(solution)/shard_map/ppermute | solution.py:625
  112.0 11.3 %collective-permute-start.25 = (bf16[2,96,512]{2,1,0:T(8,128)(2,1)S(1)}, bf16[2,96,512]{2,1,0:T(8,128)(2,1)S(1)}, u32[]{:S(2)}, u32[]{:S(2)}) collective-permute-start(bf16[2,96,512]{2,1,0:T(8,128)(2,1)S(1)} %get-tuple-element.154), channel_id=1, source_target_pairs={{0,8},{4,12},{8,0},{12,4},{16,24},{20,28},{24,16},{28,20},{1,9},{5... | collective-permute-start | bytes 589832 | tf_op jit(solution)/shard_map/ppermute | solution.py:628
  115.7 11.3 %collective-permute-start.29 = (bf16[1,96,768]{2,1,0:T(8,128)(2,1)S(1)}, bf16[1,96,768]{2,1,0:T(8,128)(2,1)S(1)}, u32[]{:S(2)}, u32[]{:S(2)}) collective-permute-start(bf16[1,96,768]{2,1,0:T(8,128)(2,1)S(1)} %get-tuple-element.165), channel_id=1, source_target_pairs={{0,16},{4,20},{8,24},{12,28},{16,0},{20,4},{24,8},{28,12},{1,17},{... | collective-permute-start | bytes 442376 | tf_op jit(solution)/shard_map/ppermute | solution.py:628
  123.4 8.9 %collective-permute-start.33 = (bf16[1,96,832]{2,1,0:T(8,128)(2,1)S(1)}, bf16[1,96,832]{2,1,0:T(8,128)(2,1)S(1)}, u32[]{:S(2)}, u32[]{:S(2)}) collective-permute-start(bf16[1,96,832]{2,1,0:T(8,128)(2,1)S(1)} %get-tuple-element.174), channel_id=1, source_target_pairs={{0,16},{4,20},{8,24},{12,28},{16,0},{20,4},{24,8},{28,12},{1,17},{... | collective-permute-start | bytes 479240 | tf_op jit(solution)/shard_map/ppermute | solution.py:628
  127.0 6.9 %collective-permute-start.36 = (bf16[96,768]{1,0:T(8,128)(2,1)S(1)}, bf16[96,768]{1,0:T(8,128)(2,1)S(1)}, u32[]{:S(2)}, u32[]{:S(2)}) collective-permute-start(bf16[96,768]{1,0:T(8,128)(2,1)S(1)} %shard_map.186), channel_id=1, source_target_pairs={{0,2},{2,0},{1,3},{3,1},{4,6},{6,4},{5,7},{7,5},{8,10},{10,8},{9,1... | collective-permute-start | bytes 442376 | tf_op jit(solution)/shard_map/ppermute | solution.py:625
  129.7 8.0 %collective-permute-start.35 = (bf16[96,768]{1,0:T(8,128)(2,1)S(1)}, bf16[96,768]{1,0:T(8,128)(2,1)S(1)}, u32[]{:S(2)}, u32[]{:S(2)}) collective-permute-start(bf16[96,768]{1,0:T(8,128)(2,1)S(1)} %shard_map.189), channel_id=1, source_target_pairs={{0,2},{2,0},{1,3},{3,1},{4,6},{6,4},{5,7},{7,5},{8,10},{10,8},{9,1... | collective-permute-start | bytes 442376 | tf_op jit(solution)/shard_map/ppermute | solution.py:625
  132.4 6.3 %collective-permute-start.34 = (bf16[96,832]{1,0:T(8,128)(2,1)S(1)}, bf16[96,832]{1,0:T(8,128)(2,1)S(1)}, u32[]{:S(2)}, u32[]{:S(2)}) collective-permute-start(bf16[96,832]{1,0:T(8,128)(2,1)S(1)} %shard_map.190.near_ref), channel_id=1, source_target_pairs={{0,2},{2,0},{1,3},{3,1},{4,6},{6,4},{5,7},{7,5},{8,10},{10,8},{9,1... | collective-permute-start | bytes 479240 | tf_op jit(solution)/shard_map/ppermute | solution.py:625
  (10 other events, 70.4 us)
